TPU v7x, 256 devices: a whole 4x4x8 slice. The times are simulated.
256 devices in a mesh: dp: 4 (over y_hi, core), ctx: 64 (over y_lo, z, x).
Axes of the slice: x: 4, y: 4 (y_hi: 2, y_lo: 2; y = y_hi * 2 + y_lo), z: 8, core: 2. Of those that a mesh axis runs over, the one named last changes fastest.
Arguments:
- feat_clean: bfloat16 [4, 4096, 6144], P('dp', 'ctx'), may hold values from -6 to 6
- feat_pert: bfloat16 [4, 4096, 6144], P('dp', 'ctx'), may hold values from -6 to 6
- feat_teacher: bfloat16 [4, 4096, 6144], P('dp', 'ctx'), may hold values from -6 to 6
- short_taps: float32 [3, 6144], replicated, may hold values from -3 to 3
- residues: float32 [2048, 16], replicated, may hold values from -0.25914272 to 0.25914272
- decay_rate: float32 [2048, 16], replicated, may hold values from 2.4414063e-05 to 0.0333333333
- out_weight: bfloat16 [2048, 4096], P(None, 'dp'), may hold values from -0.125 to 0.125
- norm_gain: float32 [4096], replicated, may hold values from 0.1 to 1.9
Outputs:
- grad_clean: bfloat16 [4, 4096, 6144], P('dp', 'ctx')
- grad_pert: bfloat16 [4, 4096, 6144], P('dp', 'ctx')
All inputs are finite; a program needn't handle non-finite values.
Results may differ from a plain program's by a relative error of at most 0.018.
Values may be sent and summed in bfloat16 or wider, within the bound.
No kernel may reach another device: no remote copies, remote signals or barrier semaphores. Data moves between devices by JAX's collectives and lax.ppermute only.
A program may use at most 192 MiB of HBM per device.

v0:
```python
import math

import jax
import jax.numpy as jnp
from jax import lax
from jax.sharding import PartitionSpec as P

eps = 1e-06
teacher_weight = 0.5
highest = lax.Precision.HIGHEST


def passed_along(value, axis, steps):
    count = lax.axis_size(axis)
    first, last = (max(0, -steps), min(count, count - steps))
    return lax.ppermute(value, axis, [(source, source + steps) for source in range(first, last)])


def split_table(table):
    upper = table.astype(jnp.bfloat16)
    lower = (table - upper.astype(jnp.float32)).astype(jnp.bfloat16)
    return (upper, lower)


def split_product(form, table, data):
    upper, lower = split_table(table)
    return jnp.einsum(form, upper, data, preferred_element_type=jnp.float32) + jnp.einsum(
        form, lower, data, preferred_element_type=jnp.float32
    )


def modal_group(group_parts):
    group_data, group_res, group_decay_factor = group_parts
    streams, group_width, length = group_data.shape
    block = min(128, length)
    total_block_count = length // block
    positions = jnp.arange(block, dtype=jnp.float32)
    powers = jnp.exp(-group_decay_factor[:, :, None] * positions[None, None, :])
    kernel = jnp.einsum("gm,gmk->gk", group_res, powers, precision=highest)
    offset = jnp.arange(block)[:, None] - jnp.arange(block)[None, :]
    toeplitz = jnp.where(
        offset[None] >= 0, jnp.take(kernel, jnp.clip(offset, 0, block - 1), axis=1), 0.0
    )
    blocks = group_data.reshape(streams, group_width, total_block_count, block)
    within = split_product("gij,sgkj->sgki", toeplitz, blocks)
    tail_decay = jnp.exp(-group_decay_factor[:, :, None] * (block - 1.0 - positions)[None, None, :])
    block_ends = split_product("gmj,sgkj->sgkm", tail_decay, blocks)
    blocks_at = jnp.arange(total_block_count)
    block_lag = (blocks_at[:, None] - 1 - blocks_at[None, :]).astype(jnp.float32)
    carry_map = jnp.where(
        block_lag[None, None] >= 0.0,
        jnp.exp(
            -group_decay_factor[:, :, None, None] * block * jnp.maximum(block_lag, 0.0)[None, None]
        ),
        0.0,
    )
    states = jnp.einsum("gmab,sgbm->sgam", carry_map, block_ends, precision=highest)
    reach_map = group_res[:, :, None] * jnp.exp(
        -group_decay_factor[:, :, None] * (positions + 1.0)[None, None, :]
    )
    between = jnp.einsum("gmi,sgkm->sgki", reach_map, states, precision=highest)
    final_map = jnp.exp(
        -group_decay_factor[:, :, None]
        * block
        * (total_block_count - 1 - blocks_at).astype(jnp.float32)[None, None, :]
    )
    end_state = jnp.einsum("gmk,sgkm->sgm", final_map, block_ends, precision=highest)
    return ((within + between).reshape(streams, group_width, length), end_state)


def modal_conv(signal, residues, decay_rate):
    streams, channels, length = signal.shape
    group_width = math.gcd(channels, 64)
    groups = channels // group_width
    grouped = signal.reshape(streams, groups, group_width, length).transpose(1, 0, 2, 3)
    result, end_state = lax.map(
        modal_group,
        (
            grouped,
            residues.reshape(groups, group_width, -1),
            decay_rate.reshape(groups, group_width, -1),
        ),
    )
    result = result.transpose(1, 0, 2, 3).reshape(streams, channels, length)
    end_state = end_state.transpose(1, 0, 2, 3).reshape(streams, channels, -1)
    return (result, end_state)


def loss_slopes(mixer_outputs, squares, gain, full_width):
    inv_scale = lax.rsqrt(squares / full_width + eps)[..., None]
    normed = mixer_outputs * inv_scale * gain
    change = normed[:, 1] - normed[:, 0]
    clean_slope = -2.0 * change
    pert_slope = 2.0 * change + 2.0 * teacher_weight * (normed[:, 1] - normed[:, 2])
    return (jnp.stack([clean_slope, pert_slope], 1), inv_scale[:, :2])


def out_slopes(mixer_outputs, norm_slope, inv_scale, inner_sum, gain, full_width):
    value = (
        inv_scale * gain * norm_slope
        - mixer_outputs[:, :2] * inv_scale**3 * (inner_sum / full_width)[..., None]
    )
    return value.astype(jnp.bfloat16)


def per_device(
    feat_clean, feat_pert, feat_teacher, short_taps, residues, decay_rate, out_weight, norm_gain
):
    features = jnp.concatenate([feat_clean, feat_pert, feat_teacher], 0)
    prior = passed_along(features[:, -2:, :], "ctx", 1)
    extended = jnp.concatenate([prior, features], 1)
    rows = features.shape[1]
    width = features.shape[2] // 3

    def filtered(lower, upper):
        first_term = short_taps[0, lower:upper] * extended[:, 2:, lower:upper].astype(jnp.float32)
        second_term = short_taps[1, lower:upper] * extended[:, 1 : rows + 1, lower:upper].astype(
            jnp.float32
        )
        third_term = short_taps[2, lower:upper] * extended[:, :rows, lower:upper].astype(
            jnp.float32
        )
        return first_term + second_term + third_term

    query = filtered(0, width).astype(jnp.bfloat16)
    key_part = filtered(width, 2 * width)
    value_part = filtered(2 * width, 3 * width)
    gated = jnp.swapaxes((key_part * value_part).astype(jnp.bfloat16), 1, 2)
    devices = lax.axis_size("ctx")
    share = width // devices
    first = lax.axis_index("ctx") * share
    local_res = lax.dynamic_slice_in_dim(residues, first, share, 0)
    local_rate = lax.dynamic_slice_in_dim(decay_rate, first, share, 0)
    result, unused = modal_conv(
        lax.all_to_all(gated, "ctx", split_axis=1, concat_axis=2, tiled=True), local_res, local_rate
    )
    conv = lax.all_to_all(
        result.astype(jnp.bfloat16), "ctx", split_axis=2, concat_axis=1, tiled=True
    )
    convolved_rows = jnp.swapaxes(conv, 1, 2)
    gated_product = (query.astype(jnp.float32) * convolved_rows.astype(jnp.float32)).astype(
        jnp.bfloat16
    )
    full_width = norm_gain.shape[0]
    mixing_weight = lax.all_gather(out_weight, "dp", axis=1, tiled=True)
    mixer_outputs = jnp.einsum(
        "snc,cd->snd", gated_product, mixing_weight, preferred_element_type=jnp.float32
    )[None]
    squares = jnp.sum(mixer_outputs * mixer_outputs, -1)
    norm_slope, inv_scale = loss_slopes(mixer_outputs, squares, norm_gain, full_width)
    inner_sum = jnp.sum(norm_gain * norm_slope * mixer_outputs[:, :2], -1)
    output_gradient = out_slopes(
        mixer_outputs, norm_slope, inv_scale, inner_sum, norm_gain, full_width
    )
    product_gradient = jnp.einsum(
        "snd,cd->snc", output_gradient[0], mixing_weight, preferred_element_type=jnp.float32
    )
    conv_slope = jnp.swapaxes(
        (product_gradient * query[:2].astype(jnp.float32)).astype(jnp.bfloat16), 1, 2
    )
    query_slope = product_gradient * convolved_rows[:2].astype(jnp.float32)
    result, unused = modal_conv(
        jnp.flip(lax.all_to_all(conv_slope, "ctx", split_axis=1, concat_axis=2, tiled=True), 2),
        local_res,
        local_rate,
    )
    gated_slope = lax.all_to_all(
        jnp.flip(result, 2).astype(jnp.bfloat16), "ctx", split_axis=2, concat_axis=1, tiled=True
    )
    gated_rows = jnp.swapaxes(gated_slope, 1, 2).astype(jnp.float32)
    unit_slope = jnp.concatenate(
        [query_slope, gated_rows * value_part[:2], gated_rows * key_part[:2]], -1
    )
    after = passed_along(unit_slope[:, :2].astype(jnp.bfloat16), "ctx", -1).astype(jnp.float32)
    extended_slope = jnp.concatenate([unit_slope, after], 1)
    feature_slope = (
        short_taps[0] * extended_slope[:, :-2]
        + short_taps[1] * extended_slope[:, 1:-1]
        + short_taps[2] * extended_slope[:, 2:]
    )
    gradient = feature_slope.astype(jnp.bfloat16)
    return (gradient[0:1], gradient[1:2])


def solution(mesh):
    in_specs = (
        P("dp", "ctx", None),
        P("dp", "ctx", None),
        P("dp", "ctx", None),
        P(),
        P(),
        P(),
        P(None, "dp"),
        P(),
    )
    out_specs = (P("dp", "ctx", None), P("dp", "ctx", None))
    return jax.shard_map(
        per_device, mesh=mesh, in_specs=in_specs, out_specs=out_specs, check_vma=False
    )
```

profile of v0, /device:TPU:6, one launch (start us, length us, event | category | flops | bytes accessed | tf_op | source)
XLA Modules:
  0.0 366.9 jit_solution(5542178561489246472)
XLA Ops:
  9.6 3.7 %collective-permute-start = (bf16[3,2,6144]{2,1,0:T(2,128)(2,1)S(1)}, bf16[3,2,6144]{2,1,0:T(2,128)(2,1)S(1)}, u32[]{:S(2)}, u32[]{:S(2)}) collective-permute-start(bf16[3,2,6144]{2,1,0:T(2,128)(2,1)S(1)} %slice.150), channel_id=1, source_target_pairs={{0,1},{1,2},{2,3},{3,4},{4,5},{5,6},{6,7},{7,8},{8,9},{9,10},{10,1... | collective-permute-start | bytes 221192 | tf_op jit(solution)/shard_map/ppermute | solution.py:16
  22.2 13.8 %all-to-all-start = ((bf16[64,2,3072]{2,1,0:T(2,128)(2,1)}), bf16[64,2,3072]{2,1,0:T(2,128)(2,1)S(1)}, u32[]{:S(2)}, u32[]{:S(2)}) async-start(bf16[64,2,3072]{2,1,0:T(2,128)(2,1)} %reshape.280), calls=%async_computation | async-start | bytes 1572864 | tf_op jit(solution)/shard_map/all_to_all | solution.py:135
  37.5 54.4 %gather_fusion = f32[16384,32]{1,0:T(8,128)} fusion(f32[32,128]{0,1:T(8,128)S(1)} %copy.89, s32[16384]{0:T(1024)S(1)} %bitcast_clamp_fusion), kind=kCustom, calls=%fused_computation.clone | custom fusion | bytes 4259840 | tf_op jit(solution)/shard_map/while/body/eval_jaxpr/jit(_take)/gather | solution.py:42
  91.9 5.5 %copy.63 = f32[128,128,32]{1,0,2:T(8,128)S(1)} copy(f32[128,128,32]{2,1,0:T(8,128)} %bitcast.177) | data formatting | bytes 4194304 | tf_op jit(solution)/shard_map/while/body/eval_jaxpr/jit(_take)/gather | solution.py:42
  103.8 3.0 reshape.253
  110.5 28.6 %fusion.18 = f32[3,32,32,16]{2,0,3,1:T(4,128)S(1)} fusion(f32[32,32]{1,0:T(8,128)S(1)} %convert_maximum_fusion, f32[32,16]{1,0:T(8,128)S(1)} %copy.64, pred[32,32]{1,0:T(8,128)(4,1)S(1)} %convert_compare_fusion, f32[3,32,32,16]{2,3,0,1:T(8,128)S(1)} %fusion.21), kind=kOutput, calls=%fused_computation.48 | convolution fusion | flops 19922944 | bytes 400384 | tf_op jit(solution)/shard_map/while/body/eval_jaxpr/gmab,sgbm->sgam/dot_general | solution.py:57
  139.1 2.9 fusion.22
  142.0 3.6 copy.100
  145.6 7.2 %reshape.282 = bf16[64,2,3072]{2,1,0:T(2,128)(2,1)} reshape(bf16[4096,3,32]{2,1,0:T(4,128)(2,1)} %bitcast.175) | data formatting | bytes 1572864
  152.8 11.3 %all-to-all-start.1 = ((bf16[64,2,3072]{2,1,0:T(2,128)(2,1)}), bf16[64,2,3072]{2,1,0:T(2,128)(2,1)S(1)}, u32[]{:S(2)}, u32[]{:S(2)}) async-start(bf16[64,2,3072]{2,1,0:T(2,128)(2,1)} %reshape.282), calls=%async_computation.1 | async-start | bytes 1572864 | tf_op jit(solution)/shard_map/all_to_all | solution.py:137
  164.1 3.5 add_convert_fusion.1
  167.5 18.1 %all-to-all-done.1 = bf16[64,2,3072]{2,1,0:T(2,128)(2,1)S(1)} async-done(((bf16[64,2,3072]{2,1,0:T(2,128)(2,1)}), bf16[64,2,3072]{2,1,0:T(2,128)(2,1)S(1)}, u32[]{:S(2)}, u32[]{:S(2)}) %all-to-all-start.1) | async-done | bytes 786464 | tf_op jit(solution)/shard_map/all_to_all | solution.py:137
  185.7 4.8 %reshape.283 = bf16[4096,3,32]{2,1,0:T(4,128)(2,1)} reshape(bf16[64,2,3072]{2,1,0:T(2,128)(2,1)S(1)} %all-to-all-done.1) | data formatting | bytes 1572864
  190.5 6.3 %copy.98 = bf16[3,32,64,64]{3,1,2,0:T(8,128)(2,1)} copy(bf16[3,32,64,64]{1,0,3,2:T(4,128)(2,1)} %bitcast.176) | data formatting | bytes 1572864 | tf_op jit(solution)/shard_map/all_to_all | solution.py:137
  198.5 8.2 %multiply_reduce_fusion = (f32[3,64]{1,0:T(4,128)S(1)}, f32[3,64,4096]{2,1,0:T(8,128)S(1)}) fusion(bf16[2048,4096]{1,0:T(8,128)(2,1)} %all-gather.2.cloned.1.call-done, bf16[3,64,2048]{2,1,0:T(8,128)(2,1)} %add_convert_fusion.1, bf16[3,2048,64]{1,2,0:T(8,128)(2,1)S(1)} %copy.72), kind=kOutput, calls=%fused_computation.30 | convolution fusion | flops 3224370944 | bytes 21496576 | tf_op jit(solution)/shard_map/snc,cd->snd/dot_general | solution.py:146
  209.0 13.7 %convert_multiply_fusion = (f32[2,64,2048]{2,1,0:T(8,128)S(1)}, bf16[2,2048,64]{1,2,0:T(8,128)(2,1)}) fusion(bf16[3,64,2048]{2,1,0:T(8,128)(2,1)} %bitcast.193, bf16[3,64,2048]{2,1,0:T(8,128)(2,1)} %add_convert_fusion.1, bf16[2048,4096]{1,0:T(8,128)(2,1)} %all-gather.2.cloned.1.call-done, f32[2,64]{1,0:T(2,128)S(1)} %broadcast_multiply_fusion.2, ...), kind=kOutput, calls=%fused_computation.68 | convolution fusion | flops 2152464384 | bytes 23610880 | tf_op jit(solution)/shard_map/snd,cd->snc/dot_general | solution.py:155
  222.8 3.6 copy.73
  226.3 3.8 %reshape.284 = bf16[64,2,2048]{2,1,0:T(2,128)(2,1)} reshape(bf16[2048,2,64]{2,1,0:T(2,128)(2,1)} %bitcast.190) | data formatting | bytes 1048576
  230.1 21.9 %all_to_all.60 = bf16[64,2,2048]{2,1,0:T(2,128)(2,1)} all-to-all(bf16[64,2,2048]{2,1,0:T(2,128)(2,1)} %reshape.284), channel_id=1, replica_groups=mesh['dp'=4,'ctx'=64] {'ctx'}, dimensions={0} | all-to-all | bytes 1048576 | tf_op jit(solution)/shard_map/all_to_all | solution.py:163
  252.0 3.7 %reshape.285 = bf16[2048,2,64]{2,1,0:T(2,128)(2,1)} reshape(bf16[64,2,2048]{2,1,0:T(2,128)(2,1)} %all_to_all.60) | data formatting | bytes 1048576
  258.5 2.7 all_to_all.54
  261.2 16.0 %rev.8 = bf16[2,32,4096]{2,1,0:T(8,128)(2,1)} reverse(bf16[2,32,4096]{2,1,0:T(8,128)(2,1)} %all_to_all.54), dimensions={2} | reverse | bytes 1048576 | tf_op jit(solution)/shard_map/jit(_flip)/rev | solution.py:163
  280.0 13.7 %fusion.23 = f32[2,32,32,16]{2,0,3,1:T(2,128)S(1)} fusion(f32[32,32]{1,0:T(8,128)S(1)} %convert_maximum_fusion, f32[32,16]{1,0:T(8,128)S(1)} %copy.64, pred[32,32]{1,0:T(8,128)(4,1)S(1)} %convert_compare_fusion, f32[2,32,32,16]{2,3,0,1:T(8,128)S(1)} %fusion.24), kind=kOutput, calls=%fused_computation.56 | convolution fusion | flops 13631488 | bytes 269312 | tf_op jit(solution)/shard_map/while/body/eval_jaxpr/gmab,sgbm->sgam/dot_general | solution.py:57
  295.4 2.8 fusion.19
  298.2 3.3 copy.99
  301.4 2.7 reverse_bitcast_fusion
  304.1 5.2 %reshape.286 = bf16[64,2,2048]{2,1,0:T(2,128)(2,1)S(1)} reshape(bf16[4096,2,32]{2,1,0:T(2,128)(2,1)} %reverse_bitcast_fusion) | data formatting | bytes 1048576
  309.3 21.1 %all_to_all.61 = bf16[64,2,2048]{2,1,0:T(2,128)(2,1)} all-to-all(bf16[64,2,2048]{2,1,0:T(2,128)(2,1)S(1)} %reshape.286), channel_id=1, replica_groups=mesh['dp'=4,'ctx'=64] {'ctx'}, dimensions={0} | all-to-all | bytes 1048576 | tf_op jit(solution)/shard_map/all_to_all | solution.py:167
  330.5 5.1 %reshape.287 = bf16[4096,2,32]{2,1,0:T(2,128)(2,1)S(1)} reshape(bf16[64,2,2048]{2,1,0:T(2,128)(2,1)} %all_to_all.61) | data formatting | bytes 1048576
  335.6 3.7 %copy.83 = bf16[2,32,4096]{2,1,0:T(8,128)(2,1)} copy(bf16[2,32,4096]{1,0,2:T(2,128)(2,1)S(1)} %bitcast.182) | data formatting | bytes 1048576 | tf_op jit(solution)/shard_map/all_to_all | solution.py:167
  343.8 3.3 copy.85
  351.0 6.1 %collective-permute-done.1 = bf16[2,2,6144]{2,1,0:T(2,128)(2,1)S(1)} collective-permute-done((bf16[2,2,6144]{2,1,0:T(2,128)(2,1)S(1)}, bf16[2,2,6144]{2,1,0:T(2,128)(2,1)S(1)}, u32[]{:S(2)}, u32[]{:S(2)}) %collective-permute-start.1) | collective-permute-done | bytes 49184 | tf_op jit(solution)/shard_map/ppermute | solution.py:16
  (80 shorter events, 44.9 us)
Async XLA Ops:
  7.2 1.1 copy-start.6
  7.2 1.4 copy-start.7
  7.2 191.3 %all-gather.2.cloned.1.call-start = ((), (), s32[]{:S(2)}) async-start(), calls=%async_computation.4 | async-start | bytes 20971520 | tf_op jit(solution)/shard_map/all_gather | solution.py:145
  8.3 1.2 copy-start.8
  8.3 5.1 %copy-start.10 = (f32[3,6144]{1,0:T(4,128)S(1)}, f32[3,6144]{1,0:T(4,128)}, u32[]{:S(2)}) copy-start(f32[3,6144]{1,0:T(4,128)} %param.13) | copy-start | bytes 221188
  9.5 8.8 %copy-start = (bf16[3,64,6144]{2,1,0:T(8,128)(2,1)}, bf16[3,64,6144]{2,1,0:T(8,128)(2,1)S(1)}, u32[]{:S(2)}) copy-start(bf16[3,64,6144]{2,1,0:T(8,128)(2,1)S(1)} %constant_dynamic-update-slice_fusion) | copy-start | bytes 7077892
  9.6 6.2 %collective-permute-start = (bf16[3,2,6144]{2,1,0:T(2,128)(2,1)S(1)}, bf16[3,2,6144]{2,1,0:T(2,128)(2,1)S(1)}, u32[]{:S(2)}, u32[]{:S(2)}) collective-permute-start(bf16[3,2,6144]{2,1,0:T(2,128)(2,1)S(1)} %slice.150), channel_id=1, source_target_pairs={{0,1},{1,2},{2,3},{3,4},{4,5},{5,6},{6,7},{7,8},{8,9},{9,10},{10,1... | collective-permute-start | bytes 221192 | tf_op jit(solution)/shard_map/ppermute | solution.py:16
  22.2 75.4 %all-to-all-start = ((bf16[64,2,3072]{2,1,0:T(2,128)(2,1)}), bf16[64,2,3072]{2,1,0:T(2,128)(2,1)S(1)}, u32[]{:S(2)}, u32[]{:S(2)}) async-start(bf16[64,2,3072]{2,1,0:T(2,128)(2,1)} %reshape.280), calls=%async_computation | async-start | bytes 1572864 | tf_op jit(solution)/shard_map/all_to_all | solution.py:135
  152.8 32.9 %all-to-all-start.1 = ((bf16[64,2,3072]{2,1,0:T(2,128)(2,1)}), bf16[64,2,3072]{2,1,0:T(2,128)(2,1)S(1)}, u32[]{:S(2)}, u32[]{:S(2)}) async-start(bf16[64,2,3072]{2,1,0:T(2,128)(2,1)} %reshape.282), calls=%async_computation.1 | async-start | bytes 1572864 | tf_op jit(solution)/shard_map/all_to_all | solution.py:137
  198.5 8.2 %copy-start.5 = (bf16[3,2048,64]{1,2,0:T(8,128)(2,1)}, bf16[3,2048,64]{1,2,0:T(8,128)(2,1)S(1)}, u32[]{:S(2)}) copy-start(bf16[3,2048,64]{1,2,0:T(8,128)(2,1)S(1)} %copy.72) | copy-start | bytes 2359300
  198.5 8.2 %copy-start.9 = (f32[4096]{0:T(1024)S(1)}, f32[4096]{0:T(1024)}, u32[]{:S(2)}) copy-start(f32[4096]{0:T(1024)} %param.17) | copy-start | bytes 49156
  206.7 1.6 copy-start.1
  207.4 1.3 copy-start.2
  207.5 1.6 copy-start.3
  343.8 3.3 copy-start.4
  349.1 8.1 %collective-permute-start.1 = (bf16[2,2,6144]{2,1,0:T(2,128)(2,1)S(1)}, bf16[2,2,6144]{2,1,0:T(2,128)(2,1)S(1)}, u32[]{:S(2)}, u32[]{:S(2)}) collective-permute-start(bf16[2,2,6144]{2,1,0:T(2,128)(2,1)S(1)} %slice.255), channel_id=1, source_target_pairs={{1,0},{2,1},{3,2},{4,3},{5,4},{6,5},{7,6},{8,7},{9,8},{10,9},{11,1... | collective-permute-start | bytes 147464 | tf_op jit(solution)/shard_map/ppermute | solution.py:16
Sparse Core Ops, SparseCore 0:
  9.8 123.8 all-gather.1
where the time goes:
time: 374 us; the launch traced here: 367 us
  local copies, waits for them, and re-layouts  162 us (43%)
  matrix products  76.9 us (21%)
  blocking collectives  43 us (11%)
  starting transfers between devices  30.8 us (8%)
  waiting for transfers between devices  27.4 us (7%)
  between operations  14.7 us (4%)
  other arithmetic  11.6 us (3%)
    gather x2, local copies, waits for them, and re-layouts, modal_group(): jnp.take(kernel, jnp.clip(offset, 0, block - 1), axis=1)  59.9 us
    dot_general x2, matrix products, modal_group(): jnp.einsum('gmab,sgbm->sgam', carry_map, block_ends, precision=highest)  42.3 us
    unnamed x35, local copies, waits for them, and re-layouts  41.6 us
    all_to_all x1, blocking collectives, per_device(): lax.all_to_all(conv_slope, 'ctx', split_axis=1, concat_axis=2, tiled=True)  21.9 us
    all_to_all x1, blocking collectives, per_device(): lax.all_to_all(jnp.flip(result, 2).astype(jnp.bfloat16), 'ctx', split_axi...  21.1 us
    all_to_all x1, waiting for transfers between devices, per_device(): lax.all_to_all(result.astype(jnp.bfloat16), 'ctx', split_axis=2, concat_a...  18.1 us
    rev x1, local copies, waits for them, and re-layouts, per_device(): jnp.flip(lax.all_to_all(conv_slope, 'ctx', split_axis=1, concat_axis=2, t...  16 us
    all_to_all x1, starting transfers between devices, per_device(): lax.all_to_all(gated, 'ctx', split_axis=1, concat_axis=2, tiled=True)  13.8 us
  transfers between devices with their start and end apart: 5, of which 3 were waited for; matrix products, arithmetic and copies ran while one was open for 38% of the time, Pallas kernels for 0%

commit v1 on v0

v1 whole, which is shorter than its diff:
```python
import functools

import jax
import jax.numpy as jnp
from jax import lax
from jax.experimental import pallas as pl
from jax.experimental.pallas import tpu as pltpu
from jax.sharding import PartitionSpec as P

eps = 1e-06
teacher_weight = 0.5
f32 = jnp.float32
bf16 = jnp.bfloat16

ROWS = 64
C = 2048
M = 16
D = 4096
LANES = 128
TILES = C // LANES
QUARTER = 4


def tile_lanes(tile, branch=0):
    return pl.ds(pl.multiple_of(branch * C + tile * LANES, LANES), LANES)


def sublane_index():
    return lax.broadcasted_iota(jnp.int32, (8, LANES), 0).astype(f32)


def row(value, index):
    return jnp.broadcast_to(value[index : index + 1], (8, LANES))


def whole(count):
    return [pl.BlockSpec(memory_space=pltpu.VMEM)] * count


def params(mib):
    return pltpu.CompilerParams(vmem_limit_bytes=mib * 2**20)


def gate_kernel(clean, pert, teacher, halo, taps, rate, query, gated, states, ext):
    def one_tile(tile, carry):
        lanes = tile_lanes(tile)
        decay = rate[:, lanes]
        step8 = jnp.exp(-8.0 * decay)
        back = 7.0 - sublane_index()
        step8_rows = [row(step8, m) for m in range(M)]
        weights = [jnp.exp(-row(decay, m) * back) for m in range(M)]
        for s, features in enumerate((clean, pert, teacher)):
            parts = []
            for branch in range(3):
                columns = tile_lanes(tile, branch)
                slot = s * 3 + branch
                ext[slot, 8 : 8 + ROWS, :] = features[:, columns].astype(f32)
                ext[slot, 6:8, :] = halo[s, :, columns].astype(f32)
                tap = taps[:, columns]
                parts.append(
                    tap[0:1] * ext[slot, 8 : 8 + ROWS, :]
                    + tap[1:2] * ext[slot, 7 : 7 + ROWS, :]
                    + tap[2:3] * ext[slot, 6 : 6 + ROWS, :]
                )
            query[s, :, lanes] = parts[0].astype(bf16)
            rounded = (parts[1] * parts[2]).astype(bf16)
            gated[s, :, lanes] = rounded
            x = rounded.astype(f32)
            for m in range(M):
                state = x[0:8]
                for i in range(1, 8):
                    state = state * step8_rows[m] + x[8 * i : 8 * i + 8]
                state = jnp.sum(state * weights[m], axis=0, keepdims=True)
                states[m, tile // QUARTER, s, pl.ds(tile % QUARTER, 1), :] = state
        return carry

    lax.fori_loop(0, TILES, one_tile, 0)


def within_kernel(streams, reverse, data, rate, res, out, held, near):
    def one_tile(tile, carry):
        lanes = tile_lanes(tile)
        decay = rate[:, lanes]
        weight = res[:, lanes]
        place = sublane_index()
        step1 = jnp.exp(-decay)
        scaled = weight * step1
        short = jnp.zeros((8, LANES), f32)
        for m in range(M):
            powers = jnp.exp(-row(decay, m) * place)
            near[pl.ds(8 * m, 8), :] = row(scaled, m) * powers
            short = short + row(weight, m) * powers
        near[pl.ds(8 * M, 8), :] = short
        hops = []
        for hop in (1, 2, 4):
            inside = place < 8.0 - hop if reverse else place >= float(hop)
            hops.append((hop, jnp.exp(-8.0 * hop * decay), inside))

        def moved(value, hop):
            return pltpu.roll(value, 8 - hop if reverse else hop, 0)

        for s in range(streams):
            held[s] = data[s, :, lanes].astype(f32)
            x = [held[s, pl.ds(i, 8, stride=8), :] for i in range(8)]
            if reverse:
                x = x[::-1]
            total = [row(short, 0) * x[n] for n in range(8)]
            for n in range(8):
                for lag in range(1, n + 1):
                    total[n] = total[n] + row(short, lag) * x[n - lag]
            for m in range(M):
                local = x[0]
                for n in range(1, 8):
                    local = local * row(step1, m) + x[n]
                state = jnp.where(hops[0][2], moved(local, 1), 0.0)
                for hop, power, inside in hops:
                    state = state + jnp.where(inside, row(power, m), 0.0) * moved(state, hop)
                for n in range(8):
                    total[n] = total[n] + near[pl.ds(8 * m + n, 1), :] * state
            for n in range(8):
                i = 7 - n if reverse else n
                held[s, pl.ds(i, 8, stride=8), :] = total[n]
            out[s, :, lanes] = held[s]
        return carry

    lax.fori_loop(0, TILES, one_tile, 0)


def scan_kernel(reverse, ends, rate, reaching):
    decay = jnp.exp(-float(ROWS) * rate[...])
    count = ends.shape[0]
    state = jnp.zeros(ends.shape[1:], f32)
    for place in range(count):
        at = count - 1 - place if reverse else place
        reaching[at] = state
        state = decay[None] * state + ends[at]


def mid_kernel(
    reaching, inner, query, rate, res, gain, weight,
    query_slope, conv_slope, edge, states,
    held, prod, conv, mixed, slope, prod_slope, sems,
):
    shards, _, width = weight.shape
    copies = [pltpu.make_async_copy(weight.at[p], held.at[p], sems.at[p]) for p in range(shards)]
    for copy in copies:
        copy.start()

    def conv_tile(tile, carry):
        lanes = tile_lanes(tile)
        decay = rate[:, lanes]
        scaled = res[:, lanes]
        ahead = sublane_index() + 1.0
        step8 = jnp.exp(-8.0 * decay)
        step8_rows = [row(step8, m) for m in range(M)]
        reach = [row(scaled, m) * jnp.exp(-row(decay, m) * ahead) for m in range(M)]
        for s in range(3):
            totals = [inner[s, 8 * i : 8 * i + 8, lanes] for i in range(8)]
            for m in range(M):
                state = reaching[m, tile // QUARTER, s, pl.ds(tile % QUARTER, 1), :]
                term = reach[m] * state
                for i in range(8):
                    totals[i] = totals[i] + term
                    if i < 7:
                        term = term * step8_rows[m]
            rounded = jnp.concatenate(totals, 0).astype(bf16)
            conv[s, :, lanes] = rounded
            product = query[s, :, lanes].astype(f32) * rounded.astype(f32)
            prod[pl.ds(s * ROWS, ROWS), lanes] = product.astype(bf16)
        return carry

    lax.fori_loop(0, TILES, conv_tile, 0)

    block = 256
    squares = jnp.zeros((3 * ROWS, 1), f32)
    for p in range(shards):
        copies[p].wait()

        def mix(t, total):
            columns = pl.ds(pl.multiple_of(t * block, block), block)
            y = jnp.dot(prod[...], held[p, :, columns], preferred_element_type=f32)
            mixed[p, :, columns] = y
            return total + jnp.sum(y * y, axis=1, keepdims=True)

        squares = lax.fori_loop(0, width // block, mix, squares)

    inv = lax.rsqrt(squares / D + eps)
    inv_clean, inv_pert, inv_teacher = inv[:ROWS], inv[ROWS : 2 * ROWS], inv[2 * ROWS :]

    def slopes(p, t):
        columns = pl.ds(pl.multiple_of(t * LANES, LANES), LANES)
        g = gain[p : p + 1, columns]
        y = mixed[p, :, columns]
        y_clean, y_pert, y_teacher = y[:ROWS], y[ROWS : 2 * ROWS], y[2 * ROWS :]
        clean = y_clean * inv_clean * g
        pert = y_pert * inv_pert * g
        teacher = y_teacher * inv_teacher * g
        change = pert - clean
        slope_clean = -2.0 * change
        slope_pert = 2.0 * change + 2.0 * teacher_weight * (pert - teacher)
        return columns, y_clean, y_pert, g * slope_clean, g * slope_pert

    zero = jnp.zeros((ROWS, LANES), f32)
    sums = (zero, zero)
    for p in range(shards):

        def inner_sums(t, sums):
            _, y_clean, y_pert, a, b = slopes(p, t)
            return sums[0] + a * y_clean, sums[1] + b * y_pert

        sums = lax.fori_loop(0, width // LANES, inner_sums, sums)
    scale_clean = inv_clean**3 * (jnp.sum(sums[0], axis=1, keepdims=True) / D)
    scale_pert = inv_pert**3 * (jnp.sum(sums[1], axis=1, keepdims=True) / D)

    for p in range(shards):

        def out_slopes(t, carry):
            columns, y_clean, y_pert, a, b = slopes(p, t)
            slope[p, 0:ROWS, columns] = (inv_clean * a - y_clean * scale_clean).astype(bf16)
            slope[p, ROWS : 2 * ROWS, columns] = (inv_pert * b - y_pert * scale_pert).astype(bf16)
            return carry

        lax.fori_loop(0, width // LANES, out_slopes, 0)

    def back(t, carry):
        rows = pl.ds(pl.multiple_of(t * block, block), block)
        total = jnp.zeros((2 * ROWS, block), f32)
        for p in range(shards):
            total = total + lax.dot_general(
                slope[p], held[p, rows, :], (((1,), (1,)), ((), ())), preferred_element_type=f32
            )
        prod_slope[:, rows] = total
        return carry

    lax.fori_loop(0, C // block, back, 0)

    def state_tile(tile, carry):
        lanes = tile_lanes(tile)
        decay = rate[:, lanes]
        ahead = sublane_index()
        step8 = jnp.exp(-8.0 * decay)
        step8_rows = [row(step8, m) for m in range(M)]
        weights = [jnp.exp(-row(decay, m) * ahead) for m in range(M)]
        for s in range(2):
            value = prod_slope[pl.ds(s * ROWS, ROWS), lanes]
            direct = value * conv[s, :, lanes].astype(f32)
            query_slope[s, :, lanes] = direct
            rounded = (value * query[s, :, lanes].astype(f32)).astype(bf16)
            conv_slope[s, :, lanes] = rounded
            x = rounded.astype(f32)
            edge[s, :, lanes] = jnp.concatenate([direct[0:8], x[0:8]], 0).astype(bf16)
            for m in range(M):
                state = x[56:64]
                for i in range(6, -1, -1):
                    state = state * step8_rows[m] + x[8 * i : 8 * i + 8]
                state = jnp.sum(state * weights[m], axis=0, keepdims=True)
                states[m, tile // QUARTER, s, pl.ds(tile % QUARTER, 1), :] = state
        return carry

    lax.fori_loop(0, TILES, state_tile, 0)


def final_kernel(
    reaching, inner, query_slope, next_edge, clean, pert, halo, next_rows, taps, rate, res,
    grad_clean, grad_pert,
    ext, unit,
):
    def one_tile(tile, carry):
        lanes = tile_lanes(tile)
        decay = rate[:, lanes]
        scaled = res[:, lanes]
        step8 = jnp.exp(-8.0 * decay)
        step8_rows = [row(step8, m) for m in range(M)]
        behind = 8.0 - sublane_index()
        first = sublane_index() == 0.0
        reach = [row(scaled, m) * jnp.exp(-row(decay, m) * behind) for m in range(M)]
        beyond = [row(scaled, m) * jnp.exp(row(decay, m) * sublane_index()) for m in range(M)]
        for s, (features, grad) in enumerate(((clean, grad_clean), (pert, grad_pert))):
            totals = [inner[s, 8 * i : 8 * i + 8, lanes] for i in range(8)]
            after = jnp.zeros((8, LANES), f32)
            edge = next_edge[s, :, lanes].astype(f32)
            passed = jnp.where(first, 0.0, row(edge, 8))
            for m in range(M):
                state = reaching[m, tile // QUARTER, s, pl.ds(tile % QUARTER, 1), :]
                after = after + beyond[m] * (state - passed)
                term = reach[m] * state
                for i in range(7, -1, -1):
                    totals[i] = totals[i] + term
                    if i > 0:
                        term = term * step8_rows[m]
            totals.append(after)
            gated_slope = jnp.concatenate(totals, 0).astype(bf16).astype(f32)
            parts = []
            for branch in (1, 2):
                columns = tile_lanes(tile, branch)
                tail = tile_lanes(tile, branch - 1)
                slot = s * 2 + branch - 1
                ext[slot, 8 : 8 + ROWS, :] = features[:, columns].astype(f32)
                ext[slot, 6:8, :] = halo[s, :, columns].astype(f32)
                ext[slot, 72:80, :] = jnp.zeros((8, LANES), f32)
                ext[slot, 72:74, :] = next_rows[s, :, tail].astype(f32)
                tap = taps[:, columns]
                parts.append(
                    tap[0:1] * ext[slot, 8:80, :]
                    + tap[1:2] * ext[slot, 7:79, :]
                    + tap[2:3] * ext[slot, 6:78, :]
                )
            unit[3 * s, 0:ROWS, :] = query_slope[s, :, lanes]
            unit[3 * s, ROWS : ROWS + 8, :] = edge[0:8]
            unit[3 * s + 1] = gated_slope * parts[1]
            unit[3 * s + 2] = gated_slope * parts[0]
            for branch in range(3):
                columns = tile_lanes(tile, branch)
                tap = taps[:, columns]
                slot = 3 * s + branch
                grad[:, columns] = (
                    tap[0:1] * unit[slot, 0:ROWS, :]
                    + tap[1:2] * unit[slot, 1 : 1 + ROWS, :]
                    + tap[2:3] * unit[slot, 2 : 2 + ROWS, :]
                ).astype(bf16)
        return carry

    lax.fori_loop(0, TILES, one_tile, 0)


def array(*shape, dtype=f32):
    return jax.ShapeDtypeStruct(shape, dtype)


def within(data, rate, res, reverse):
    streams = data.shape[0]
    return pl.pallas_call(
        functools.partial(within_kernel, streams, reverse),
        out_shape=array(streams, ROWS, C),
        in_specs=whole(3),
        out_specs=whole(1)[0],
        scratch_shapes=[pltpu.VMEM((streams, ROWS, LANES), f32), pltpu.VMEM((8 * M + 8, LANES), f32)],
        compiler_params=params(8),
        cost_estimate=pl.CostEstimate(
            flops=streams * 100_000_000, bytes_accessed=streams * 6 * ROWS * C, transcendentals=0
        ),
    )(data, rate, res)


def scan(ends, own_rate, reverse):
    return pl.pallas_call(
        functools.partial(scan_kernel, reverse),
        out_shape=array(*ends.shape),
        in_specs=whole(2),
        out_specs=whole(1)[0],
        compiler_params=params(4),
    )(ends, own_rate)


def exchanged(states):
    pieces = M * TILES // QUARTER
    shape = states.shape
    flat = states.reshape(pieces, *shape[-3:])
    return lax.all_to_all(flat, "ctx", split_axis=0, concat_axis=0, tiled=True)


def passed_along(value, steps):
    count = lax.axis_size("ctx")
    first, last = max(0, -steps), min(count, count - steps)
    return lax.ppermute(value, "ctx", [(source, source + steps) for source in range(first, last)])


def per_device(
    feat_clean, feat_pert, feat_teacher, short_taps, residues, decay_rate, out_weight, norm_gain
):
    clean, pert, teacher = feat_clean[0], feat_pert[0], feat_teacher[0]
    halo = passed_along(jnp.stack([clean[-2:], pert[-2:], teacher[-2:]]), 1)
    next_rows = passed_along(jnp.stack([clean[:2, C:], pert[:2, C:]]), -1)
    weight = lax.all_gather(out_weight, "dp", axis=0, tiled=False)
    gain = norm_gain.reshape(weight.shape[0], -1)
    rate, res = decay_rate.T, residues.T
    own = lax.axis_index("ctx")
    own_rate = lax.dynamic_slice(
        rate, (own // QUARTER, (own % QUARTER) * QUARTER * LANES), (1, QUARTER * LANES)
    ).reshape(QUARTER, LANES)
    state_shape = (M, TILES // QUARTER)

    query, gated, ends = pl.pallas_call(
        gate_kernel,
        out_shape=(
            array(3, ROWS, C, dtype=bf16),
            array(3, ROWS, C, dtype=bf16),
            array(*state_shape, 3, QUARTER, LANES),
        ),
        in_specs=whole(6),
        out_specs=tuple(whole(3)),
        scratch_shapes=[pltpu.VMEM((9, 8 + ROWS, LANES), f32)],
        compiler_params=params(12),
    )(clean, pert, teacher, halo, short_taps, rate)

    ends = exchanged(ends)
    inner = within(gated, rate, res, False)
    reaching = exchanged(scan(ends, own_rate, False)).reshape(*state_shape, 3, QUARTER, LANES)

    query_slope, conv_slope, edge, ends = pl.pallas_call(
        mid_kernel,
        out_shape=(
            array(2, ROWS, C),
            array(2, ROWS, C, dtype=bf16),
            array(2, 16, C, dtype=bf16),
            array(*state_shape, 2, QUARTER, LANES),
        ),
        in_specs=whole(6) + [pl.BlockSpec(memory_space=pl.ANY)],
        out_specs=tuple(whole(4)),
        scratch_shapes=[
            pltpu.VMEM(weight.shape, bf16),
            pltpu.VMEM((3 * ROWS, C), bf16),
            pltpu.VMEM((3, ROWS, C), bf16),
            pltpu.VMEM((weight.shape[0], 3 * ROWS, weight.shape[2]), f32),
            pltpu.VMEM((weight.shape[0], 2 * ROWS, weight.shape[2]), bf16),
            pltpu.VMEM((2 * ROWS, C), f32),
            pltpu.SemaphoreType.DMA((weight.shape[0],)),
        ],
        compiler_params=params(44),
    )(reaching, inner, query, rate, res, gain, weight)

    next_edge = passed_along(edge, -1)
    ends = exchanged(ends)
    inner = within(conv_slope, rate, res, True)
    reaching = exchanged(scan(ends, own_rate, True)).reshape(*state_shape, 2, QUARTER, LANES)

    grads = pl.pallas_call(
        final_kernel,
        out_shape=(array(ROWS, 3 * C, dtype=bf16), array(ROWS, 3 * C, dtype=bf16)),
        in_specs=whole(11),
        out_specs=tuple(whole(2)),
        scratch_shapes=[
            pltpu.VMEM((4, 16 + ROWS, LANES), f32),
            pltpu.VMEM((6, 8 + ROWS, LANES), f32),
        ],
        compiler_params=params(16),
    )(
        reaching, inner, query_slope, next_edge, clean, pert, halo, next_rows, short_taps, rate, res
    )
    return grads[0][None], grads[1][None]


def solution(mesh):
    rows = P("dp", "ctx", None)
    in_specs = (rows, rows, rows, P(), P(), P(), P(None, "dp"), P())
    return jax.shard_map(
        per_device, mesh=mesh, in_specs=in_specs, out_specs=(rows, rows), check_vma=False
    )
```

time: 374 us -> 217 us (0.58)
  the two profiles are of different devices: /device:TPU:6 before, /device:TPU:24 now
where the time goes in v1:
time: 217 us; the launch traced here: 216 us
  waiting for transfers between devices  92 us (42%)
  Pallas kernels  42.4 us (20%)
  starting transfers between devices  33.5 us (15%)
  blocking collectives  23.7 us (11%)
  between operations  14.3 us (7%)
  local copies, waits for them, and re-layouts  9.77 us (5%)
    all_gather x1, waiting for transfers between devices, per_device(): weight = lax.all_gather(out_weight, 'dp', axis=0, tiled=False)  63.8 us
    all_to_all x1, blocking collectives, exchanged(): return lax.all_to_all(flat, 'ctx', split_axis=0, concat_axis=0, tiled=True)  23.7 us
    pallas_call x1, Pallas kernels, per_device(): pl.pallas_call(mid_kernel, out_shape=(array(2, ROWS, C), array(2, ROWS, C...  22 us
    all_to_all x3, starting transfers between devices, exchanged(): return lax.all_to_all(flat, 'ctx', split_axis=0, concat_axis=0, tiled=True)  20.6 us
    all_to_all x3, waiting for transfers between devices, exchanged(): return lax.all_to_all(flat, 'ctx', split_axis=0, concat_axis=0, tiled=True)  18.4 us
    ppermute x3, starting transfers between devices, passed_along(): lax.ppermute(value, 'ctx', [(source, source + steps) for source in range(...  12.8 us
    pallas_call x2, Pallas kernels, within(): pl.pallas_call(functools.partial(within_kernel, streams, reverse), out_sh...  9.91 us
    unnamed x38, local copies, waits for them, and re-layouts  9.56 us
  transfers between devices with their start and end apart: 7, of which 4 were waited for; matrix products, arithmetic and copies ran while one was open for 0% of the time, Pallas kernels for 7%

profile of v1, /device:TPU:24, one launch (start us, length us, event | category | flops | bytes accessed | tf_op | source)
XLA Modules:
  0.0 215.9 jit_solution(4907329946950365915)
XLA Ops:
  7.3 0.7 all-gather.3.cloned.1.call-update
  8.0 0.3 copy-done
  8.3 0.2 copy-done.1
  8.6 0.2 copy-done.6
  8.8 0.1 pad_maximum_fusion
  8.9 3.4 %collective-permute-start = (bf16[3,2,6144]{2,1,0:T(2,128)(2,1)S(1)}, bf16[3,2,6144]{2,1,0:T(2,128)(2,1)S(1)}, u32[]{:S(2)}, u32[]{:S(2)}) collective-permute-start(bf16[3,2,6144]{2,1,0:T(2,128)(2,1)S(1)} %pad_maximum_fusion), channel_id=1, source_target_pairs={{0,1},{1,2},{2,3},{3,4},{4,5},{5,6},{6,7},{7,8},{8,9},{9,10},{10,1... | collective-permute-start | bytes 221192 | tf_op jit(solution)/shard_map/ppermute | solution.py:365
  12.3 9.1 %collective-permute-done.halo = bf16[3,2,6144]{2,1,0:T(2,128)(2,1)S(1)} collective-permute-done((bf16[3,2,6144]{2,1,0:T(2,128)(2,1)S(1)}, bf16[3,2,6144]{2,1,0:T(2,128)(2,1)S(1)}, u32[]{:S(2)}, u32[]{:S(2)}) %collective-permute-start) | collective-permute-done | bytes 73760 | tf_op jit(solution)/shard_map/ppermute | solution.py:365
  21.4 4.1 %shard_map.95 = (bf16[3,64,2048]{2,1,0:T(8,128)(2,1)S(1)}, bf16[3,64,2048]{2,1,0:T(8,128)(2,1)S(1)}, f32[16,4,3,4,128]{4,3,2,1,0:T(4,128)S(1)}) custom-call(bf16[64,6144]{1,0:T(8,128)(2,1)S(1)} %bitcast.17, bf16[64,6144]{1,0:T(8,128)(2,1)S(1)} %bitcast.20, bf16[64,6144]{1,0:T(8,128)(2,1)S(1)} %bitcast.33, bf16[3,2,6144]{2,1,0:T(2,128)(2,1)S(1)} %collective-permute-done.halo, ...), custom_call_target="tpu_custom_call" | custom-call | tf_op jit(solution)/shard_map/pallas_call | solution.py:383
  25.6 0.9 copy-done.9
  26.4 0.7 copy-done.13
  27.2 7.7 %all-to-all-start = ((f32[64,3,4,128]{3,2,1,0:T(4,128)}), f32[64,3,4,128]{3,2,1,0:T(4,128)S(1)}, u32[]{:S(2)}, u32[]{:S(2)}) async-start(f32[64,3,4,128]{3,2,1,0:T(4,128)} %bitcast.34), calls=%async_computation | async-start | bytes 786432 | tf_op jit(solution)/shard_map/all_to_all | solution.py:359
  35.0 12.9 %all-to-all-done.ends = f32[64,3,4,128]{3,2,1,0:T(4,128)S(1)} async-done(((f32[64,3,4,128]{3,2,1,0:T(4,128)}), f32[64,3,4,128]{3,2,1,0:T(4,128)S(1)}, u32[]{:S(2)}, u32[]{:S(2)}) %all-to-all-start) | async-done | bytes 393248 | tf_op jit(solution)/shard_map/all_to_all | solution.py:359
  47.9 0.9 shard_map.96
  48.8 6.9 %all-to-all-start.1 = ((f32[64,3,4,128]{3,2,1,0:T(4,128)}), f32[64,3,4,128]{3,2,1,0:T(4,128)}, u32[]{:S(2)}, u32[]{:S(2)}) async-start(f32[64,3,4,128]{3,2,1,0:T(4,128)} %shard_map.96), calls=%async_computation.1 | async-start | bytes 786432 | tf_op jit(solution)/shard_map/all_to_all | solution.py:359
  55.7 1.1 copy-done.10
  56.9 5.8 %shard_map.97.inner = f32[3,64,2048]{2,1,0:T(8,128)S(1)} custom-call(bf16[3,64,2048]{2,1,0:T(8,128)(2,1)S(1)} %copy-done.10, f32[16,2048]{1,0:T(8,128)S(1)} %bitcast.24, f32[16,2048]{1,0:T(8,128)S(1)} %bitcast.28), custom_call_target="tpu_custom_call" | custom-call | flops 300000000 | bytes 2359296 | tf_op jit(solution)/shard_map/pallas_call | solution.py:332
  62.7 5.5 %all-to-all-done.1 = f32[64,3,4,128]{3,2,1,0:T(4,128)} async-done(((f32[64,3,4,128]{3,2,1,0:T(4,128)}), f32[64,3,4,128]{3,2,1,0:T(4,128)}, u32[]{:S(2)}, u32[]{:S(2)}) %all-to-all-start.1) | async-done | bytes 393248 | tf_op jit(solution)/shard_map/all_to_all | solution.py:359
  68.1 63.8 %all-gather.3.cloned.1.call-done = bf16[8192,1024]{1,0:T(8,128)(2,1)} async-done(((bf16[2048,1024]{1,0:T(8,128)(2,1)}), bf16[8192,1024]{1,0:T(8,128)(2,1)}) %all-gather.3.cloned.1.call-update) | async-done | bytes 16777232 | tf_op jit(solution)/shard_map/all_gather | solution.py:374
  132.0 1.1 copy-done.8
  133.1 22.0 %shard_map.98 = (f32[2,64,2048]{2,1,0:T(8,128)S(1)}, bf16[2,64,2048]{2,1,0:T(8,128)(2,1)S(1)}, bf16[2,16,2048]{2,1,0:T(8,128)(2,1)S(1)}, f32[16,4,2,4,128]{4,3,2,1,0:T(4,128)S(1)}) custom-call(f32[16,4,3,4,128]{4,3,2,1,0:T(4,128)} %bitcast.6.reaching, f32[3,64,2048]{2,1,0:T(8,128)S(1)} %shard_map.97.inner, bf16[3,64,2048]{2,1,0:T(8,128)(2,1)S(1)} %copy-done.8, ...), custom_call_target="tpu_custom_call" | custom-call | tf_op jit(solution)/shard_map/pallas_call | solution.py:400
  155.2 1.0 copy-done.4
  156.1 0.8 copy-done.11
  156.9 23.7 %all_to_all.20.ends = f32[64,2,4,128]{3,2,1,0:T(4,128)S(1)} all-to-all(f32[64,2,4,128]{3,2,1,0:T(4,128)S(1)} %bitcast.35), channel_id=1, replica_groups=mesh['dp'=4,'ctx'=64] {'ctx'}, dimensions={0} | all-to-all | bytes 524288 | tf_op jit(solution)/shard_map/all_to_all | solution.py:359
  180.6 0.8 shard_map.99
  181.5 6.1 %all-to-all-start.3 = ((f32[64,2,4,128]{3,2,1,0:T(4,128)}), f32[64,2,4,128]{3,2,1,0:T(4,128)S(1)}, u32[]{:S(2)}, u32[]{:S(2)}) async-start(f32[64,2,4,128]{3,2,1,0:T(4,128)} %shard_map.99), calls=%async_computation.3 | async-start | bytes 524288 | tf_op jit(solution)/shard_map/all_to_all | solution.py:359
  187.6 6.7 %collective-permute-start.1 = (bf16[2,16,2048]{2,1,0:T(8,128)(2,1)}, bf16[2,16,2048]{2,1,0:T(8,128)(2,1)S(1)}, u32[]{:S(2)}, u32[]{:S(2)}) collective-permute-start(bf16[2,16,2048]{2,1,0:T(8,128)(2,1)} %copy-done.17), channel_id=1, source_target_pairs={{1,0},{2,1},{3,2},{4,3},{5,4},{6,5},{7,6},{8,7},{9,8},{10,9},{11,1... | collective-permute-start | bytes 393224 | tf_op jit(solution)/shard_map/ppermute | solution.py:365
  194.4 2.8 %collective-permute-start.2 = (bf16[2,2,4096]{2,1,0:T(2,128)(2,1)S(1)}, bf16[2,2,4096]{2,1,0:T(2,128)(2,1)S(1)}, u32[]{:S(2)}, u32[]{:S(2)}) collective-permute-start(bf16[2,2,4096]{2,1,0:T(2,128)(2,1)S(1)} %pad_maximum_fusion.1), channel_id=1, source_target_pairs={{1,0},{2,1},{3,2},{4,3},{5,4},{6,5},{7,6},{8,7},{9,8},{10,9},{11,1... | collective-permute-start | bytes 98312 | tf_op jit(solution)/shard_map/ppermute | solution.py:365
  197.1 1.0 copy-done.12
  198.2 4.1 %shard_map.100.inner = f32[2,64,2048]{2,1,0:T(8,128)S(1)} custom-call(bf16[2,64,2048]{2,1,0:T(8,128)(2,1)S(1)} %copy-done.12, f32[16,2048]{1,0:T(8,128)S(1)} %bitcast.26, f32[16,2048]{1,0:T(8,128)S(1)} %bitcast.30), custom_call_target="tpu_custom_call" | custom-call | flops 200000000 | bytes 1572864 | tf_op jit(solution)/shard_map/pallas_call | solution.py:332
  202.3 1.2 copy-done.5
  203.5 0.9 copy-done.16
  204.4 4.6 %shard_map.101 = (bf16[64,6144]{1,0:T(8,128)(2,1)}, bf16[64,6144]{1,0:T(8,128)(2,1)}) custom-call(f32[16,4,2,4,128]{4,3,2,1,0:T(4,128)S(1)} %bitcast.32, f32[2,64,2048]{2,1,0:T(8,128)S(1)} %shard_map.100.inner, f32[2,64,2048]{2,1,0:T(8,128)S(1)} %copy-done.5, bf16[2,16,2048]{2,1,0:T(8,128)(2,1)S(1)} %collective-permute-done.1.next_edge, ...), custom_call_target="tpu_custom_call" | custom-call | tf_op jit(solution)/shard_map/pallas_call | solution.py:427
  (37 shorter events, 0.4 us)
Async XLA Ops:
  7.2 1.1 copy-start
  7.2 1.4 copy-start.1
  7.2 1.6 copy-start.6
  7.2 14.2 %copy-start.2 = (f32[2048,16]{0,1:T(8,128)S(1)}, f32[2048,16]{0,1:T(8,128)}, u32[]{:S(2)}) copy-start(f32[2048,16]{0,1:T(8,128)} %param.13) | copy-start | bytes 393220
  7.2 14.2 %copy-start.14 = (f32[3,6144]{1,0:T(4,128)S(1)}, f32[3,6144]{1,0:T(4,128)}, u32[]{:S(2)}) copy-start(f32[3,6144]{1,0:T(4,128)} %taps.3) | copy-start | bytes 221188
  7.2 48.5 %copy-start.18 = (f32[4096]{0:T(1024)S(1)}, f32[4096]{0:T(1024)}, u32[]{:S(2)}) copy-start(f32[4096]{0:T(1024)} %param.15) | copy-start | bytes 49156
  7.2 48.5 %copy-start.3 = (f32[2048,16]{0,1:T(8,128)S(1)}, f32[2048,16]{0,1:T(8,128)}, u32[]{:S(2)}) copy-start(f32[2048,16]{0,1:T(8,128)} %param.12) | copy-start | bytes 393220
  7.2 124.7 %all-gather.3.cloned.1.call-start = ((), (), s32[]{:S(2)}) async-start(), calls=%async_computation.4 | async-start | bytes 20971520 | tf_op jit(solution)/shard_map/all_gather | solution.py:374
  8.9 12.5 %collective-permute-start = (bf16[3,2,6144]{2,1,0:T(2,128)(2,1)S(1)}, bf16[3,2,6144]{2,1,0:T(2,128)(2,1)S(1)}, u32[]{:S(2)}, u32[]{:S(2)}) collective-permute-start(bf16[3,2,6144]{2,1,0:T(2,128)(2,1)S(1)} %pad_maximum_fusion), channel_id=1, source_target_pairs={{0,1},{1,2},{2,3},{3,4},{4,5},{5,6},{6,7},{7,8},{8,9},{9,10},{10,1... | collective-permute-start | bytes 221192 | tf_op jit(solution)/shard_map/ppermute | solution.py:365
  21.4 4.1 %copy-start.15 = (bf16[3,2,6144]{2,1,0:T(2,128)(2,1)}, bf16[3,2,6144]{2,1,0:T(2,128)(2,1)S(1)}, u32[]{:S(2)}) copy-start(bf16[3,2,6144]{2,1,0:T(2,128)(2,1)S(1)} %collective-permute-done.halo) | copy-start | bytes 221188
  25.5 0.9 copy-start.9
  26.4 0.7 copy-start.13
  27.2 28.5 %copy-start.7 = (bf16[3,64,2048]{2,1,0:T(8,128)(2,1)}, bf16[3,64,2048]{2,1,0:T(8,128)(2,1)S(1)}, u32[]{:S(2)}) copy-start(bf16[3,64,2048]{2,1,0:T(8,128)(2,1)S(1)} %get-tuple-element.13.query) | copy-start | bytes 2359300
  27.2 20.7 %all-to-all-start = ((f32[64,3,4,128]{3,2,1,0:T(4,128)}), f32[64,3,4,128]{3,2,1,0:T(4,128)S(1)}, u32[]{:S(2)}, u32[]{:S(2)}) async-start(f32[64,3,4,128]{3,2,1,0:T(4,128)} %bitcast.34), calls=%async_computation | async-start | bytes 786432 | tf_op jit(solution)/shard_map/all_to_all | solution.py:359
  48.8 19.3 %all-to-all-start.1 = ((f32[64,3,4,128]{3,2,1,0:T(4,128)}), f32[64,3,4,128]{3,2,1,0:T(4,128)}, u32[]{:S(2)}, u32[]{:S(2)}) async-start(f32[64,3,4,128]{3,2,1,0:T(4,128)} %shard_map.96), calls=%async_computation.1 | async-start | bytes 786432 | tf_op jit(solution)/shard_map/all_to_all | solution.py:359
  55.7 1.1 copy-start.10
  132.0 1.1 copy-start.8
  155.1 1.0 copy-start.4
  156.1 0.8 copy-start.11
  156.9 23.7 %copy-start.17 = (bf16[2,16,2048]{2,1,0:T(8,128)(2,1)}, bf16[2,16,2048]{2,1,0:T(8,128)(2,1)S(1)}, u32[]{:S(2)}) copy-start(bf16[2,16,2048]{2,1,0:T(8,128)(2,1)S(1)} %get-tuple-element.17) | copy-start | bytes 393220
  181.5 20.8 %all-to-all-start.3 = ((f32[64,2,4,128]{3,2,1,0:T(4,128)}), f32[64,2,4,128]{3,2,1,0:T(4,128)S(1)}, u32[]{:S(2)}, u32[]{:S(2)}) async-start(f32[64,2,4,128]{3,2,1,0:T(4,128)} %shard_map.99), calls=%async_computation.3 | async-start | bytes 524288 | tf_op jit(solution)/shard_map/all_to_all | solution.py:359
  187.6 14.7 %collective-permute-start.1 = (bf16[2,16,2048]{2,1,0:T(8,128)(2,1)}, bf16[2,16,2048]{2,1,0:T(8,128)(2,1)S(1)}, u32[]{:S(2)}, u32[]{:S(2)}) collective-permute-start(bf16[2,16,2048]{2,1,0:T(8,128)(2,1)} %copy-done.17), channel_id=1, source_target_pairs={{1,0},{2,1},{3,2},{4,3},{5,4},{6,5},{7,6},{8,7},{9,8},{10,9},{11,1... | collective-permute-start | bytes 393224 | tf_op jit(solution)/shard_map/ppermute | solution.py:365
  194.4 7.9 %collective-permute-start.2 = (bf16[2,2,4096]{2,1,0:T(2,128)(2,1)S(1)}, bf16[2,2,4096]{2,1,0:T(2,128)(2,1)S(1)}, u32[]{:S(2)}, u32[]{:S(2)}) collective-permute-start(bf16[2,2,4096]{2,1,0:T(2,128)(2,1)S(1)} %pad_maximum_fusion.1), channel_id=1, source_target_pairs={{1,0},{2,1},{3,2},{4,3},{5,4},{6,5},{7,6},{8,7},{9,8},{10,9},{11,1... | collective-permute-start | bytes 98312 | tf_op jit(solution)/shard_map/ppermute | solution.py:365
  197.1 1.0 copy-start.12
  202.3 1.2 copy-start.5
  203.5 0.9 copy-start.16
Sparse Core Ops, SparseCore 0:
  9.9 122.0 all-gather.2

commit v2 on v1

--- a/solution.py
+++ b/solution.py
@@ -18,6 +18,9 @@
 D = 4096
 LANES = 128
 TILES = C // LANES
+WIDTH = D // 4
+BAND = C // 4
+BLOCK = 256
 QUARTER = 4
 
 
@@ -136,13 +139,13 @@
         state = decay[None] * state + ends[at]
 
 
-def mid_kernel(
-    reaching, inner, query, rate, res, gain, weight,
-    query_slope, conv_slope, edge, states,
-    held, prod, conv, mixed, slope, prod_slope, sems,
+def mix_kernel(
+    reaching, inner, query, rate, res, own_weight, core_weight, prod, conv, mixed, held, sems
 ):
-    shards, _, width = weight.shape
-    copies = [pltpu.make_async_copy(weight.at[p], held.at[p], sems.at[p]) for p in range(shards)]
+    copies = [
+        pltpu.make_async_copy(weight, held.at[p], sems.at[p])
+        for p, weight in enumerate((own_weight, core_weight))
+    ]
     for copy in copies:
         copy.start()
 
@@ -164,33 +167,79 @@
                     if i < 7:
                         term = term * step8_rows[m]
             rounded = jnp.concatenate(totals, 0).astype(bf16)
-            conv[s, :, lanes] = rounded
+            if s < 2:
+                conv[s, :, lanes] = rounded
             product = query[s, :, lanes].astype(f32) * rounded.astype(f32)
             prod[pl.ds(s * ROWS, ROWS), lanes] = product.astype(bf16)
         return carry
 
     lax.fori_loop(0, TILES, conv_tile, 0)
 
-    block = 256
-    squares = jnp.zeros((3 * ROWS, 1), f32)
+    for p in range(2):
+        copies[p].wait()
+        mix_shard(prod, held.at[p], mixed.at[p])
+
+
+def mix_shard(prod, weight, mixed):
+    def mix(t, carry):
+        columns = pl.ds(pl.multiple_of(t * BLOCK, BLOCK), BLOCK)
+        mixed[:, columns] = jnp.dot(prod[...], weight[:, columns], preferred_element_type=f32)
+        return carry
+
+    lax.fori_loop(0, WIDTH // BLOCK, mix, 0)
+
+
+def slope_kernel(
+    prod, conv, query, rate, near_mixed, gain, *refs,
+):
+    weights, refs = refs[:12], refs[12:]
+    query_slope, conv_slope, edge, states, held, far_mixed, slope, prod_slope, sems = refs
+    dp, ctx = lax.axis_index("dp"), lax.axis_index("ctx")
+    x, z = ctx % 4, (ctx // 4) % 8
+    colour = (x % 2) * 2 + z % 2
+    across_x = (1 - x % 2) * 2 + z % 2
+    across_z = (x % 2) * 2 + 1 - z % 2
+    starts = (colour * BAND, across_x * BAND, across_z * BAND, (3 - colour) * BAND)
+    places = []
+    for p in (2, 3):
+        for q in range(3):
+            places.append((p, starts[q], BAND))
+        for half in range(2):
+            places.append((p, starts[3] + half * (BAND // 2), BAND // 2))
+    places += [(0, 0, C), (1, 0, C)]
+    copies = [
+        pltpu.make_async_copy(
+            weight, held.at[p, pl.ds(pl.multiple_of(start, BAND // 2), size), :], sems.at[n]
+        )
+        for n, (weight, (p, start, size)) in enumerate(zip(weights, places))
+    ]
+    for copy in copies:
+        copy.start()
+    high, core = dp // 2, dp % 2
+    shard = (2 * high + core, 2 * high + 1 - core, 2 * (1 - high) + core, 2 * (1 - high) + 1 - core)
+    shards, width = 4, WIDTH
+    mixed = (near_mixed.at[0], near_mixed.at[1], far_mixed.at[0], far_mixed.at[1])
+    for p in range(2):
+        for copy in copies[5 * p : 5 * p + 5]:
+            copy.wait()
+        mix_shard(prod, held.at[2 + p], far_mixed.at[p])
+
+    squares = jnp.zeros((3 * ROWS, LANES), f32)
     for p in range(shards):
-        copies[p].wait()
-
-        def mix(t, total):
-            columns = pl.ds(pl.multiple_of(t * block, block), block)
-            y = jnp.dot(prod[...], held[p, :, columns], preferred_element_type=f32)
-            mixed[p, :, columns] = y
-            return total + jnp.sum(y * y, axis=1, keepdims=True)
-
-        squares = lax.fori_loop(0, width // block, mix, squares)
-
+
+        def square_sums(t, total):
+            y = mixed[p][:, pl.ds(pl.multiple_of(t * LANES, LANES), LANES)]
+            return total + y * y
+
+        squares = lax.fori_loop(0, width // LANES, square_sums, squares)
+    squares = jnp.sum(squares, axis=1, keepdims=True)
     inv = lax.rsqrt(squares / D + eps)
     inv_clean, inv_pert, inv_teacher = inv[:ROWS], inv[ROWS : 2 * ROWS], inv[2 * ROWS :]
 
     def slopes(p, t):
         columns = pl.ds(pl.multiple_of(t * LANES, LANES), LANES)
-        g = gain[p : p + 1, columns]
-        y = mixed[p, :, columns]
+        g = gain[shard[p], :, columns]
+        y = mixed[p][:, columns]
         y_clean, y_pert, y_teacher = y[:ROWS], y[ROWS : 2 * ROWS], y[2 * ROWS :]
         clean = y_clean * inv_clean * g
         pert = y_pert * inv_pert * g
@@ -222,9 +271,12 @@
 
         lax.fori_loop(0, width // LANES, out_slopes, 0)
 
+    for copy in copies[10:]:
+        copy.wait()
+
     def back(t, carry):
-        rows = pl.ds(pl.multiple_of(t * block, block), block)
-        total = jnp.zeros((2 * ROWS, block), f32)
+        rows = pl.ds(pl.multiple_of(t * BLOCK, BLOCK), BLOCK)
+        total = jnp.zeros((2 * ROWS, BLOCK), f32)
         for p in range(shards):
             total = total + lax.dot_general(
                 slope[p], held[p, rows, :], (((1,), (1,)), ((), ())), preferred_element_type=f32
@@ -232,7 +284,7 @@
         prod_slope[:, rows] = total
         return carry
 
-    lax.fori_loop(0, C // block, back, 0)
+    lax.fori_loop(0, C // BLOCK, back, 0)
 
     def state_tile(tile, carry):
         lanes = tile_lanes(tile)
@@ -365,20 +417,50 @@
     return lax.ppermute(value, "ctx", [(source, source + steps) for source in range(first, last)])
 
 
+def partner(device, kind):
+    x, z, low, core, high = device % 4, device // 4 % 8, device // 32 % 2, device // 64 % 2, device // 128
+    if kind == "core":
+        core = 1 - core
+    elif kind == "y":
+        high, low = divmod(3 - (high * 2 + low), 2)
+    else:
+        place, count = (x, 4) if kind == "x" else (z, 8)
+        ahead = place % 2 == core
+        place = (place + (1 if ahead else -1)) % count
+        x, z = (place, z) if kind == "x" else (x, place)
+    return (high * 2 + core) * 64 + low * 32 + z * 4 + x
+
+
+def swapped(value, kind):
+    return lax.ppermute(
+        value, ("dp", "ctx"), [(device, partner(device, kind)) for device in range(256)]
+    )
+
+
+def tied(*values):
+    return lax.optimization_barrier(values)
+
+
 def per_device(
     feat_clean, feat_pert, feat_teacher, short_taps, residues, decay_rate, out_weight, norm_gain
 ):
     clean, pert, teacher = feat_clean[0], feat_pert[0], feat_teacher[0]
-    halo = passed_along(jnp.stack([clean[-2:], pert[-2:], teacher[-2:]]), 1)
+    last_rows = jnp.stack([clean[-2:], pert[-2:], teacher[-2:]])
+    last_rows, out_weight = tied(last_rows, out_weight)
+    halo = passed_along(last_rows, 1)
     next_rows = passed_along(jnp.stack([clean[:2, C:], pert[:2, C:]]), -1)
-    weight = lax.all_gather(out_weight, "dp", axis=0, tiled=False)
-    gain = norm_gain.reshape(weight.shape[0], -1)
+    gain = norm_gain.reshape(4, 1, WIDTH)
     rate, res = decay_rate.T, residues.T
     own = lax.axis_index("ctx")
     own_rate = lax.dynamic_slice(
         rate, (own // QUARTER, (own % QUARTER) * QUARTER * LANES), (1, QUARTER * LANES)
     ).reshape(QUARTER, LANES)
     state_shape = (M, TILES // QUARTER)
+
+    x, z = own % 4, own // 4 % 8
+    colour = (x % 2) * 2 + z % 2
+    core_weight = swapped(out_weight, "core")
+    band = swapped(lax.dynamic_slice(out_weight, (colour * BAND, 0), (BAND, WIDTH)), "y")
 
     query, gated, ends = pl.pallas_call(
         gate_kernel,
@@ -390,34 +472,54 @@
         in_specs=whole(6),
         out_specs=tuple(whole(3)),
         scratch_shapes=[pltpu.VMEM((9, 8 + ROWS, LANES), f32)],
-        compiler_params=params(12),
+        compiler_params=params(4),
     )(clean, pert, teacher, halo, short_taps, rate)
 
     ends = exchanged(ends)
     inner = within(gated, rate, res, False)
+    inner, band = tied(inner, band)
+    band_x, band_z = swapped(band, "x"), swapped(band, "z")
+    ends, inner = tied(ends, inner)
     reaching = exchanged(scan(ends, own_rate, False)).reshape(*state_shape, 3, QUARTER, LANES)
-
+    reaching, band_x, band_z = tied(reaching, band_x, band_z)
+    half = BAND // 2
+    last_x, last_z = swapped(band_z[:half], "x"), swapped(band_x[half:], "z")
+
+    prod, conv, near_mixed = pl.pallas_call(
+        mix_kernel,
+        out_shape=(
+            array(3 * ROWS, C, dtype=bf16),
+            array(2, ROWS, C, dtype=bf16),
+            array(2, 3 * ROWS, WIDTH),
+        ),
+        in_specs=whole(5) + [pl.BlockSpec(memory_space=pltpu.HBM)] * 2,
+        out_specs=tuple(whole(3)),
+        scratch_shapes=[pltpu.VMEM((2, C, WIDTH), bf16), pltpu.SemaphoreType.DMA((2,))],
+        compiler_params=params(12),
+        cost_estimate=pl.CostEstimate(flops=5_000_000_000, bytes_accessed=14_000_000, transcendentals=0),
+    )(reaching, inner, query, rate, res, out_weight, core_weight)
+
+    far = [band, band_x, band_z, last_x, last_z]
+    pieces = far + [swapped(piece, "core") for piece in far] + [out_weight, core_weight]
     query_slope, conv_slope, edge, ends = pl.pallas_call(
-        mid_kernel,
+        slope_kernel,
         out_shape=(
             array(2, ROWS, C),
             array(2, ROWS, C, dtype=bf16),
             array(2, 16, C, dtype=bf16),
             array(*state_shape, 2, QUARTER, LANES),
         ),
-        in_specs=whole(6) + [pl.BlockSpec(memory_space=pl.ANY)],
+        in_specs=whole(6) + [pl.BlockSpec(memory_space=pltpu.HBM)] * 12,
         out_specs=tuple(whole(4)),
         scratch_shapes=[
-            pltpu.VMEM(weight.shape, bf16),
-            pltpu.VMEM((3 * ROWS, C), bf16),
-            pltpu.VMEM((3, ROWS, C), bf16),
-            pltpu.VMEM((weight.shape[0], 3 * ROWS, weight.shape[2]), f32),
-            pltpu.VMEM((weight.shape[0], 2 * ROWS, weight.shape[2]), bf16),
+            pltpu.VMEM((4, C, WIDTH), bf16),
+            pltpu.VMEM((2, 3 * ROWS, WIDTH), f32),
+            pltpu.VMEM((4, 2 * ROWS, WIDTH), bf16),
             pltpu.VMEM((2 * ROWS, C), f32),
-            pltpu.SemaphoreType.DMA((weight.shape[0],)),
+            pltpu.SemaphoreType.DMA((12,)),
         ],
-        compiler_params=params(44),
-    )(reaching, inner, query, rate, res, gain, weight)
+        compiler_params=params(24),
+    )(prod, conv, query, rate, near_mixed, gain, *pieces)
 
     next_edge = passed_along(edge, -1)
     ends = exchanged(ends)

time: 217 us -> 164 us (0.76)
  waiting for transfers between devices: 92 us -> 20.5 us
  blocking collectives: 23.7 us -> 42.1 us
  between operations: 14.3 us -> 1.05 us
  local copies, waits for them, and re-layouts: 9.77 us -> 21.6 us
    all_gather x1 -> x0, waiting for transfers between devices: 63.8 us -> none  [per_device(): weight = lax.all_gather(out_weight, 'dp', axis=0, tiled=False)]
    all_to_all x1 -> x2, blocking collectives: 23.7 us -> 42.1 us  [exchanged(): return lax.all_to_all(flat, 'ctx', split_axis=0, concat_axis=0, tiled=True)]
    all_to_all x3 -> x2, waiting for transfers between devices: 18.4 us -> 3.84 us  [exchanged(): return lax.all_to_all(flat, 'ctx', split_axis=0, concat_axis=0, tiled=True)]
    ppermute x0 -> x11, starting transfers between devices: none -> 8.47 us  [swapped(): lax.ppermute(value, ('dp', 'ctx'), [(device, partner(device, kind)) for d...]
    unnamed x38 -> x50, local copies, waits for them, and re-layouts: 9.56 us -> 17.3 us
    ppermute x0 -> x11, waiting for transfers between devices: none -> 7.34 us  [swapped(): lax.ppermute(value, ('dp', 'ctx'), [(device, partner(device, kind)) for d...]
    all_to_all x3 -> x2, starting transfers between devices: 20.6 us -> 13.3 us  [exchanged(): return lax.all_to_all(flat, 'ctx', split_axis=0, concat_axis=0, tiled=True)]
    slice x3 -> x5, local copies, waits for them, and re-layouts: 0.09 us -> 2.88 us  [the longest x3 2.81 us: per_device(): last_rows = jnp.stack([clean[-2:], pert[-2:], teacher[-2:]])]
  transfers between devices with their start and end apart: 7 -> 16, of which waited for: 4 -> 4; matrix products, arithmetic and copies ran while one was open for 0% -> 1% of each run, Pallas kernels for 7% -> 13%
where the time goes in v2:
time: 164 us; the launch traced here: 161 us
  Pallas kernels  42.7 us (26%)
  blocking collectives  42.1 us (26%)
  starting transfers between devices  33.2 us (20%)
  local copies, waits for them, and re-layouts  21.6 us (13%)
  waiting for transfers between devices  20.5 us (12%)
    all_to_all x2, blocking collectives, exchanged(): return lax.all_to_all(flat, 'ctx', split_axis=0, concat_axis=0, tiled=True)  42.1 us
    unnamed x50, local copies, waits for them, and re-layouts  17.3 us
    pallas_call x1, Pallas kernels, per_device(): pl.pallas_call(slope_kernel, out_shape=(array(2, ROWS, C), array(2, ROWS,...  16.5 us
    all_to_all x2, starting transfers between devices, exchanged(): return lax.all_to_all(flat, 'ctx', split_axis=0, concat_axis=0, tiled=True)  13.3 us
    ppermute x3, starting transfers between devices, passed_along(): lax.ppermute(value, 'ctx', [(source, source + steps) for source in range(...  11.4 us
    pallas_call x2, Pallas kernels, within(): pl.pallas_call(functools.partial(within_kernel, streams, reverse), out_sh...  9.91 us
    ppermute x3, waiting for transfers between devices, passed_along(): lax.ppermute(value, 'ctx', [(source, source + steps) for source in range(...  9.28 us
    ppermute x11, starting transfers between devices, swapped(): lax.ppermute(value, ('dp', 'ctx'), [(device, partner(device, kind)) for d...  8.47 us
  transfers between devices with their start and end apart: 16, of which 4 were waited for; matrix products, arithmetic and copies ran while one was open for 1% of the time, Pallas kernels for 13%

profile of v2, /device:TPU:24, one launch (start us, length us, event | category | flops | bytes accessed | tf_op | source)
XLA Modules:
  0.0 161.2 jit_solution(7665613673677998349)
XLA Ops:
  3.8 1.3 constant_dynamic-slice_fusion
  5.1 2.0 %collective-permute-start.1 = (bf16[512,1024]{1,0:T(8,128)(2,1)S(1)}, bf16[512,1024]{1,0:T(8,128)(2,1)}, u32[]{:S(2)}, u32[]{:S(2)}) collective-permute-start(bf16[512,1024]{1,0:T(8,128)(2,1)S(1)} %constant_dynamic-slice_fusion), channel_id=1, source_target_pairs={{0,160},{1,161},{2,162},{3,163},{4,164},{5,165},{6,166},{7,167},{8... | collective-permute-start | bytes 3145736 | tf_op jit(solution)/shard_map/ppermute | solution.py:435
  7.1 1.9 %collective-permute-start = (bf16[3,2,6144]{2,1,0:T(2,128)(2,1)S(1)}, bf16[3,2,6144]{2,1,0:T(2,128)(2,1)S(1)}, u32[]{:S(2)}, u32[]{:S(2)}) collective-permute-start(bf16[3,2,6144]{2,1,0:T(2,128)(2,1)S(1)} %pad_maximum_fusion), channel_id=1, source_target_pairs={{0,1},{1,2},{2,3},{3,4},{4,5},{5,6},{6,7},{7,8},{8,9},{9,10},{10,1... | collective-permute-start | bytes 221192 | tf_op jit(solution)/shard_map/ppermute | solution.py:417
  9.0 9.3 %collective-permute-done.halo = bf16[3,2,6144]{2,1,0:T(2,128)(2,1)S(1)} collective-permute-done((bf16[3,2,6144]{2,1,0:T(2,128)(2,1)S(1)}, bf16[3,2,6144]{2,1,0:T(2,128)(2,1)S(1)}, u32[]{:S(2)}, u32[]{:S(2)}) %collective-permute-start) | collective-permute-done | bytes 73760 | tf_op jit(solution)/shard_map/ppermute | solution.py:417
  18.3 1.1 copy-done.2
  19.5 1.1 copy-done.4
  21.5 1.1 copy-done.15
  23.5 4.9 %shard_map.95 = (bf16[3,64,2048]{2,1,0:T(8,128)(2,1)S(1)}, bf16[3,64,2048]{2,1,0:T(8,128)(2,1)S(1)}, f32[16,4,3,4,128]{4,3,2,1,0:T(4,128)}) custom-call(bf16[64,6144]{1,0:T(8,128)(2,1)S(1)} %bitcast.17, bf16[64,6144]{1,0:T(8,128)(2,1)S(1)} %bitcast.20, bf16[64,6144]{1,0:T(8,128)(2,1)S(1)} %bitcast.34, bf16[3,2,6144]{2,1,0:T(2,128)(2,1)S(1)} %collective-permute-done.halo, ...), custom_call_target="tpu_custom_call" | custom-call | tf_op jit(solution)/shard_map/pallas_call | solution.py:465
  29.3 7.2 %all-to-all-start = ((f32[64,3,4,128]{3,2,1,0:T(4,128)}), f32[64,3,4,128]{3,2,1,0:T(4,128)S(1)}, u32[]{:S(2)}, u32[]{:S(2)}) async-start(f32[64,3,4,128]{3,2,1,0:T(4,128)} %bitcast.4), calls=%async_computation | async-start | bytes 786432 | tf_op jit(solution)/shard_map/all_to_all | solution.py:411
  36.5 5.8 %shard_map.96.inner = f32[3,64,2048]{2,1,0:T(8,128)S(1)} custom-call(bf16[3,64,2048]{2,1,0:T(8,128)(2,1)S(1)} %get-tuple-element.25.data, f32[16,2048]{1,0:T(8,128)S(1)} %bitcast.24, f32[16,2048]{1,0:T(8,128)S(1)} %bitcast.29), custom_call_target="tpu_custom_call" | custom-call | flops 300000000 | bytes 2359296 | tf_op jit(solution)/shard_map/pallas_call | solution.py:384
  42.3 1.2 copy-done.10
  43.5 1.5 collective-permute-start.2
  45.0 1.5 collective-permute-start.3
  46.6 3.8 %all-to-all-done.ends = f32[64,3,4,128]{3,2,1,0:T(4,128)S(1)} async-done(((f32[64,3,4,128]{3,2,1,0:T(4,128)}), f32[64,3,4,128]{3,2,1,0:T(4,128)S(1)}, u32[]{:S(2)}, u32[]{:S(2)}) %all-to-all-start) | async-done | bytes 393248 | tf_op jit(solution)/shard_map/all_to_all | solution.py:411
  50.5 21.9 %all_to_all.20 = f32[64,3,4,128]{3,2,1,0:T(4,128)S(1)} all-to-all(f32[64,3,4,128]{3,2,1,0:T(4,128)S(1)} %shard_map.97), channel_id=1, replica_groups=mesh['dp'=4,'ctx'=64] {'ctx'}, dimensions={0} | all-to-all | bytes 786432 | tf_op jit(solution)/shard_map/all_to_all | solution.py:411
  73.6 1.9 %collective-permute-start.6 = (bf16[256,1024]{1,0:T(8,128)(2,1)S(1)}, bf16[256,1024]{1,0:T(8,128)(2,1)S(1)}, u32[]{:S(2)}, u32[]{:S(2)}) collective-permute-start(bf16[256,1024]{1,0:T(8,128)(2,1)S(1)} %slice.28), channel_id=1, source_target_pairs={{0,4},{1,5},{2,6},{3,7},{4,0},{5,1},{6,2},{7,3},{8,12},{9,13},{10,... | collective-permute-start | bytes 1572872 | tf_op jit(solution)/shard_map/ppermute | solution.py:435
  75.4 6.4 %collective-permute-done.5.refs_3_ = bf16[256,1024]{1,0:T(8,128)(2,1)S(1)} collective-permute-done((bf16[256,1024]{1,0:T(8,128)(2,1)S(1)}, bf16[256,1024]{1,0:T(8,128)(2,1)S(1)}, u32[]{:S(2)}, u32[]{:S(2)}) %collective-permute-start.5) | collective-permute-done | bytes 524320 | tf_op jit(solution)/shard_map/ppermute | solution.py:435
  83.3 2.2 %copy-done = bf16[2048,1024]{1,0:T(8,128)(2,1)S(1)} copy-done((bf16[2048,1024]{1,0:T(8,128)(2,1)S(1)}, bf16[2048,1024]{1,0:T(8,128)(2,1)}, u32[]{:S(2)}) %copy-start) | copy-done | bytes 4194328
  85.4 1.4 copy-done.11
  86.9 1.1 copy-done.17
  88.0 5.9 %shard_map.98 = (bf16[192,2048]{1,0:T(8,128)(2,1)S(1)}, bf16[2,64,2048]{2,1,0:T(8,128)(2,1)S(1)}, f32[2,192,1024]{2,1,0:T(8,128)S(1)}) custom-call(f32[16,4,3,4,128]{4,3,2,1,0:T(4,128)S(1)} %bitcast.35, f32[3,64,2048]{2,1,0:T(8,128)S(1)} %copy-done.11, bf16[3,64,2048]{2,1,0:T(8,128)(2,1)S(1)} %copy-done.17, f32[16,2048]{1,0:T(8,128)S(1)} %bitcast.25, ...), custom_call_target="tpu_custom_call" | custom-call | flops 5000000000 | bytes 14000000 | tf_op jit(solution)/shard_map/pallas_call | solution.py:488
  94.0 1.2 copy-done.9
  95.2 16.5 %shard_map.99 = (f32[2,64,2048]{2,1,0:T(8,128)S(1)}, bf16[2,64,2048]{2,1,0:T(8,128)(2,1)S(1)}, bf16[2,16,2048]{2,1,0:T(8,128)(2,1)S(1)}, f32[16,4,2,4,128]{4,3,2,1,0:T(4,128)S(1)}) custom-call(bf16[192,2048]{1,0:T(8,128)(2,1)S(1)} %get-tuple-element.33.prod, bf16[2,64,2048]{2,1,0:T(8,128)(2,1)S(1)} %get-tuple-element.34.conv, ...), custom_call_target="tpu_custom_call" | custom-call | tf_op jit(solution)/shard_map/pallas_call | solution.py:504
  111.7 1.0 copy-done.13
  113.5 20.2 %all_to_all.21.ends = f32[64,2,4,128]{3,2,1,0:T(4,128)S(1)} all-to-all(f32[64,2,4,128]{3,2,1,0:T(4,128)S(1)} %bitcast.36), channel_id=1, replica_groups=mesh['dp'=4,'ctx'=64] {'ctx'}, dimensions={0} | all-to-all | bytes 524288 | tf_op jit(solution)/shard_map/all_to_all | solution.py:411
  134.5 6.1 %all-to-all-start.3 = ((f32[64,2,4,128]{3,2,1,0:T(4,128)}), f32[64,2,4,128]{3,2,1,0:T(4,128)S(1)}, u32[]{:S(2)}, u32[]{:S(2)}) async-start(f32[64,2,4,128]{3,2,1,0:T(4,128)} %shard_map.100), calls=%async_computation.3 | async-start | bytes 524288 | tf_op jit(solution)/shard_map/all_to_all | solution.py:411
  140.6 6.7 %collective-permute-start.12 = (bf16[2,16,2048]{2,1,0:T(8,128)(2,1)}, bf16[2,16,2048]{2,1,0:T(8,128)(2,1)S(1)}, u32[]{:S(2)}, u32[]{:S(2)}) collective-permute-start(bf16[2,16,2048]{2,1,0:T(8,128)(2,1)} %copy-done.24), channel_id=1, source_target_pairs={{1,0},{2,1},{3,2},{4,3},{5,4},{6,5},{7,6},{8,7},{9,8},{10,9},{11,1... | collective-permute-start | bytes 393224 | tf_op jit(solution)/shard_map/ppermute | solution.py:417
  147.4 2.8 %collective-permute-start.13 = (bf16[2,2,4096]{2,1,0:T(2,128)(2,1)S(1)}, bf16[2,2,4096]{2,1,0:T(2,128)(2,1)S(1)}, u32[]{:S(2)}, u32[]{:S(2)}) collective-permute-start(bf16[2,2,4096]{2,1,0:T(2,128)(2,1)S(1)} %pad_maximum_fusion.1), channel_id=1, source_target_pairs={{1,0},{2,1},{3,2},{4,3},{5,4},{6,5},{7,6},{8,7},{9,8},{10,9},{11,1... | collective-permute-start | bytes 98312 | tf_op jit(solution)/shard_map/ppermute | solution.py:417
  150.2 1.0 copy-done.20
  151.2 4.1 %shard_map.101.inner = f32[2,64,2048]{2,1,0:T(8,128)S(1)} custom-call(bf16[2,64,2048]{2,1,0:T(8,128)(2,1)S(1)} %copy-done.20, f32[16,2048]{1,0:T(8,128)S(1)} %bitcast.27, f32[16,2048]{1,0:T(8,128)S(1)} %bitcast.31), custom_call_target="tpu_custom_call" | custom-call | flops 200000000 | bytes 1572864 | tf_op jit(solution)/shard_map/pallas_call | solution.py:384
  155.4 1.2 copy-done.14
  156.6 4.6 %shard_map.102 = (bf16[64,6144]{1,0:T(8,128)(2,1)}, bf16[64,6144]{1,0:T(8,128)(2,1)}) custom-call(f32[16,4,2,4,128]{4,3,2,1,0:T(4,128)S(1)} %bitcast.33, f32[2,64,2048]{2,1,0:T(8,128)S(1)} %shard_map.101.inner, f32[2,64,2048]{2,1,0:T(8,128)S(1)} %copy-done.14, bf16[2,16,2048]{2,1,0:T(8,128)(2,1)S(1)} %collective-permute-done.12.next_edge, ...), custom_call_target="tpu_custom_call" | custom-call | tf_op jit(solution)/shard_map/pallas_call | solution.py:529
  (70 shorter events, 10.2 us)
Async XLA Ops:
  0.6 35.9 %copy-start.7 = (f32[2048,16]{0,1:T(8,128)S(1)}, f32[2048,16]{0,1:T(8,128)}, u32[]{:S(2)}) copy-start(f32[2048,16]{0,1:T(8,128)} %param.13) | copy-start | bytes 393220
  0.6 35.9 %copy-start.12 = (f32[2048,16]{0,1:T(8,128)S(1)}, f32[2048,16]{0,1:T(8,128)}, u32[]{:S(2)}) copy-start(f32[2048,16]{0,1:T(8,128)} %param.12) | copy-start | bytes 393220
  3.6 79.3 %collective-permute-start.4 = (bf16[2048,1024]{1,0:T(8,128)(2,1)}, bf16[2048,1024]{1,0:T(8,128)(2,1)}, u32[]{:S(2)}, u32[]{:S(2)}) collective-permute-start(bf16[2048,1024]{1,0:T(8,128)(2,1)} %refs_10_), channel_id=1, source_target_pairs={{0,64},{1,65},{2,66},{3,67},{4,68},{5,69},{6,70},{7,71},{8,72},{9,... | collective-permute-start | bytes 12582920 | tf_op jit(solution)/shard_map/ppermute | solution.py:435
  5.1 38.4 %collective-permute-start.1 = (bf16[512,1024]{1,0:T(8,128)(2,1)S(1)}, bf16[512,1024]{1,0:T(8,128)(2,1)}, u32[]{:S(2)}, u32[]{:S(2)}) collective-permute-start(bf16[512,1024]{1,0:T(8,128)(2,1)S(1)} %constant_dynamic-slice_fusion), channel_id=1, source_target_pairs={{0,160},{1,161},{2,162},{3,163},{4,164},{5,165},{6,166},{7,167},{8... | collective-permute-start | bytes 3145736 | tf_op jit(solution)/shard_map/ppermute | solution.py:435
  7.1 11.2 %collective-permute-start = (bf16[3,2,6144]{2,1,0:T(2,128)(2,1)S(1)}, bf16[3,2,6144]{2,1,0:T(2,128)(2,1)S(1)}, u32[]{:S(2)}, u32[]{:S(2)}) collective-permute-start(bf16[3,2,6144]{2,1,0:T(2,128)(2,1)S(1)} %pad_maximum_fusion), channel_id=1, source_target_pairs={{0,1},{1,2},{2,3},{3,4},{4,5},{5,6},{6,7},{7,8},{8,9},{9,10},{10,1... | collective-permute-start | bytes 221192 | tf_op jit(solution)/shard_map/ppermute | solution.py:417
  18.3 1.1 copy-start.2
  29.3 21.1 %all-to-all-start = ((f32[64,3,4,128]{3,2,1,0:T(4,128)}), f32[64,3,4,128]{3,2,1,0:T(4,128)S(1)}, u32[]{:S(2)}, u32[]{:S(2)}) async-start(f32[64,3,4,128]{3,2,1,0:T(4,128)} %bitcast.4), calls=%async_computation | async-start | bytes 786432 | tf_op jit(solution)/shard_map/all_to_all | solution.py:411
  42.3 1.2 copy-start.10
  43.5 28.9 %collective-permute-start.2 = (bf16[512,1024]{1,0:T(8,128)(2,1)}, bf16[512,1024]{1,0:T(8,128)(2,1)S(1)}, u32[]{:S(2)}, u32[]{:S(2)}) collective-permute-start(bf16[512,1024]{1,0:T(8,128)(2,1)} %collective-permute-done.1.refs_0_), channel_id=1, source_target_pairs={{0,1},{1,0},{2,3},{3,2},{4,5},{5,4},{6,7},{7,6},{8,9},{9,8},{10,11... | collective-permute-start | bytes 3145736 | tf_op jit(solution)/shard_map/ppermute | solution.py:435
  45.0 27.5 %collective-permute-start.3 = (bf16[512,1024]{1,0:T(8,128)(2,1)}, bf16[512,1024]{1,0:T(8,128)(2,1)S(1)}, u32[]{:S(2)}, u32[]{:S(2)}) collective-permute-start(bf16[512,1024]{1,0:T(8,128)(2,1)} %collective-permute-done.1.refs_0_), channel_id=1, source_target_pairs={{0,4},{1,5},{2,6},{3,7},{4,0},{5,1},{6,2},{7,3},{8,12},{9,13},{10,... | collective-permute-start | bytes 3145736 | tf_op jit(solution)/shard_map/ppermute | solution.py:435
  72.5 21.4 %copy-start.8 = (bf16[512,1024]{1,0:T(8,128)(2,1)}, bf16[512,1024]{1,0:T(8,128)(2,1)S(1)}, u32[]{:S(2)}) copy-start(bf16[512,1024]{1,0:T(8,128)(2,1)S(1)} %collective-permute-done.3.refs_2_) | copy-start | bytes 3145732
  72.5 9.3 %collective-permute-start.5 = (bf16[256,1024]{1,0:T(8,128)(2,1)S(1)}, bf16[256,1024]{1,0:T(8,128)(2,1)S(1)}, u32[]{:S(2)}, u32[]{:S(2)}) collective-permute-start(bf16[256,1024]{1,0:T(8,128)(2,1)S(1)} %slice.27), channel_id=1, source_target_pairs={{0,1},{1,0},{2,3},{3,2},{4,5},{5,4},{6,7},{7,6},{8,9},{9,8},{10,11... | collective-permute-start | bytes 1572872 | tf_op jit(solution)/shard_map/ppermute | solution.py:435
  72.9 21.0 %collective-permute-start.7 = (bf16[512,1024]{1,0:T(8,128)(2,1)}, bf16[512,1024]{1,0:T(8,128)(2,1)S(1)}, u32[]{:S(2)}, u32[]{:S(2)}) collective-permute-start(bf16[512,1024]{1,0:T(8,128)(2,1)} %collective-permute-done.1.refs_0_), channel_id=1, source_target_pairs={{0,64},{1,65},{2,66},{3,67},{4,68},{5,69},{6,70},{7,71},{8,72},{9,... | collective-permute-start | bytes 3145736 | tf_op jit(solution)/shard_map/ppermute | solution.py:435
  73.0 20.9 %collective-permute-start.8 = (bf16[512,1024]{1,0:T(8,128)(2,1)S(1)}, bf16[512,1024]{1,0:T(8,128)(2,1)S(1)}, u32[]{:S(2)}, u32[]{:S(2)}) collective-permute-start(bf16[512,1024]{1,0:T(8,128)(2,1)S(1)} %collective-permute-done.2.refs_1_), channel_id=1, source_target_pairs={{0,64},{1,65},{2,66},{3,67},{4,68},{5,69},{6,70},{7,71},{8,72},{9,... | collective-permute-start | bytes 3145736 | tf_op jit(solution)/shard_map/ppermute | solution.py:435
  73.6 9.2 %collective-permute-start.6 = (bf16[256,1024]{1,0:T(8,128)(2,1)S(1)}, bf16[256,1024]{1,0:T(8,128)(2,1)S(1)}, u32[]{:S(2)}, u32[]{:S(2)}) collective-permute-start(bf16[256,1024]{1,0:T(8,128)(2,1)S(1)} %slice.28), channel_id=1, source_target_pairs={{0,4},{1,5},{2,6},{3,7},{4,0},{5,1},{6,2},{7,3},{8,12},{9,13},{10,... | collective-permute-start | bytes 1572872 | tf_op jit(solution)/shard_map/ppermute | solution.py:435
  81.8 12.1 %collective-permute-start.9 = (bf16[512,1024]{1,0:T(8,128)(2,1)S(1)}, bf16[512,1024]{1,0:T(8,128)(2,1)S(1)}, u32[]{:S(2)}, u32[]{:S(2)}) collective-permute-start(bf16[512,1024]{1,0:T(8,128)(2,1)S(1)} %collective-permute-done.3.refs_2_), channel_id=1, source_target_pairs={{0,64},{1,65},{2,66},{3,67},{4,68},{5,69},{6,70},{7,71},{8,72},{9,... | collective-permute-start | bytes 3145736 | tf_op jit(solution)/shard_map/ppermute | solution.py:435
  82.7 11.2 %collective-permute-start.10 = (bf16[256,1024]{1,0:T(8,128)(2,1)S(1)}, bf16[256,1024]{1,0:T(8,128)(2,1)S(1)}, u32[]{:S(2)}, u32[]{:S(2)}) collective-permute-start(bf16[256,1024]{1,0:T(8,128)(2,1)S(1)} %collective-permute-done.5.refs_3_), channel_id=1, source_target_pairs={{0,64},{1,65},{2,66},{3,67},{4,68},{5,69},{6,70},{7,71},{8,72},{9,... | collective-permute-start | bytes 1572872 | tf_op jit(solution)/shard_map/ppermute | solution.py:435
  82.9 11.0 %collective-permute-start.11 = (bf16[256,1024]{1,0:T(8,128)(2,1)S(1)}, bf16[256,1024]{1,0:T(8,128)(2,1)S(1)}, u32[]{:S(2)}, u32[]{:S(2)}) collective-permute-start(bf16[256,1024]{1,0:T(8,128)(2,1)S(1)} %collective-permute-done.6.refs_4_), channel_id=1, source_target_pairs={{0,64},{1,65},{2,66},{3,67},{4,68},{5,69},{6,70},{7,71},{8,72},{9,... | collective-permute-start | bytes 1572872 | tf_op jit(solution)/shard_map/ppermute | solution.py:435
  83.3 2.2 %copy-start = (bf16[2048,1024]{1,0:T(8,128)(2,1)S(1)}, bf16[2048,1024]{1,0:T(8,128)(2,1)}, u32[]{:S(2)}) copy-start(bf16[2048,1024]{1,0:T(8,128)(2,1)} %refs_10_) | copy-start | bytes 12582916
  85.4 1.4 copy-start.11
  88.0 6.0 %copy-start.1 = (bf16[2048,1024]{1,0:T(8,128)(2,1)S(1)}, bf16[2048,1024]{1,0:T(8,128)(2,1)}, u32[]{:S(2)}) copy-start(bf16[2048,1024]{1,0:T(8,128)(2,1)} %refs_10_) | copy-start | bytes 12582916
  88.0 6.0 %copy-start.18 = (bf16[3,64,2048]{2,1,0:T(8,128)(2,1)S(1)}, bf16[3,64,2048]{2,1,0:T(8,128)(2,1)}, u32[]{:S(2)}) copy-start(bf16[3,64,2048]{2,1,0:T(8,128)(2,1)} %copy-done.16) | copy-start | bytes 2359300
  88.0 6.0 %copy-start.23 = (f32[4096]{0:T(1024)S(1)}, f32[4096]{0:T(1024)}, u32[]{:S(2)}) copy-start(f32[4096]{0:T(1024)} %param.15) | copy-start | bytes 49156
  94.0 1.2 copy-start.9
  95.2 45.4 %copy-start.3 = (bf16[1,64,6144]{2,1,0:T(8,128)(2,1)S(1)}, bf16[1,64,6144]{2,1,0:T(8,128)(2,1)}, u32[]{:S(2)}) copy-start(bf16[1,64,6144]{2,1,0:T(8,128)(2,1)} %param.8) | copy-start | bytes 2359300
  95.2 45.4 %copy-start.5 = (bf16[1,64,6144]{2,1,0:T(8,128)(2,1)S(1)}, bf16[1,64,6144]{2,1,0:T(8,128)(2,1)}, u32[]{:S(2)}) copy-start(bf16[1,64,6144]{2,1,0:T(8,128)(2,1)} %param.9) | copy-start | bytes 2359300
  95.2 60.2 %copy-start.22 = (f32[3,6144]{1,0:T(4,128)S(1)}, f32[3,6144]{1,0:T(4,128)}, u32[]{:S(2)}) copy-start(f32[3,6144]{1,0:T(4,128)} %taps.3) | copy-start | bytes 221188
  113.5 20.2 %copy-start.24 = (bf16[2,16,2048]{2,1,0:T(8,128)(2,1)}, bf16[2,16,2048]{2,1,0:T(8,128)(2,1)S(1)}, u32[]{:S(2)}) copy-start(bf16[2,16,2048]{2,1,0:T(8,128)(2,1)S(1)} %get-tuple-element.41) | copy-start | bytes 393220
  134.5 20.9 %all-to-all-start.3 = ((f32[64,2,4,128]{3,2,1,0:T(4,128)}), f32[64,2,4,128]{3,2,1,0:T(4,128)S(1)}, u32[]{:S(2)}, u32[]{:S(2)}) async-start(f32[64,2,4,128]{3,2,1,0:T(4,128)} %shard_map.100), calls=%async_computation.3 | async-start | bytes 524288 | tf_op jit(solution)/shard_map/all_to_all | solution.py:411
  140.6 14.7 %collective-permute-start.12 = (bf16[2,16,2048]{2,1,0:T(8,128)(2,1)}, bf16[2,16,2048]{2,1,0:T(8,128)(2,1)S(1)}, u32[]{:S(2)}, u32[]{:S(2)}) collective-permute-start(bf16[2,16,2048]{2,1,0:T(8,128)(2,1)} %copy-done.24), channel_id=1, source_target_pairs={{1,0},{2,1},{3,2},{4,3},{5,4},{6,5},{7,6},{8,7},{9,8},{10,9},{11,1... | collective-permute-start | bytes 393224 | tf_op jit(solution)/shard_map/ppermute | solution.py:417
  147.4 7.9 %collective-permute-start.13 = (bf16[2,2,4096]{2,1,0:T(2,128)(2,1)S(1)}, bf16[2,2,4096]{2,1,0:T(2,128)(2,1)S(1)}, u32[]{:S(2)}, u32[]{:S(2)}) collective-permute-start(bf16[2,2,4096]{2,1,0:T(2,128)(2,1)S(1)} %pad_maximum_fusion.1), channel_id=1, source_target_pairs={{1,0},{2,1},{3,2},{4,3},{5,4},{6,5},{7,6},{8,7},{9,8},{10,9},{11,1... | collective-permute-start | bytes 98312 | tf_op jit(solution)/shard_map/ppermute | solution.py:417
  155.4 1.2 copy-start.14
  (9 other events, 8.9 us)

commit v3 on v2

--- a/solution.py
+++ b/solution.py
@@ -21,7 +21,8 @@
 WIDTH = D // 4
 BAND = C // 4
 BLOCK = 256
-QUARTER = 4
+QUARTERS = 4
+QUARTER = TILES // QUARTERS
 
 
 def tile_lanes(tile, branch=0):
@@ -36,15 +37,41 @@
     return jnp.broadcast_to(value[index : index + 1], (8, LANES))
 
 
-def whole(count):
-    return [pl.BlockSpec(memory_space=pltpu.VMEM)] * count
+def far():
+    return pl.BlockSpec(memory_space=pltpu.HBM)
 
 
 def params(mib):
     return pltpu.CompilerParams(vmem_limit_bytes=mib * 2**20)
 
 
-def gate_kernel(clean, pert, teacher, halo, taps, rate, query, gated, states, ext):
+def edge_kernel(*refs):
+    features, (weight, last_rows, first_rows, band, sem) = refs[:5], refs[5:]
+    copy = pltpu.make_async_copy(
+        weight.at[pl.ds(pl.multiple_of(bands(lax.axis_index("ctx"))[0], BAND), BAND), :], band, sem
+    )
+    copy.start()
+    for s in range(3):
+        last_rows[s] = features[s][6:8, :]
+    for s in range(2):
+        first_rows[s] = features[3 + s][0:2, C:]
+    copy.wait()
+
+
+def bands(ctx):
+    x, z = ctx % 2, (ctx // 4) % 2
+    return (
+        (2 * x + z) * BAND,
+        (2 * (1 - x) + z) * BAND,
+        (2 * x + 1 - z) * BAND,
+        (2 * (1 - x) + 1 - z) * BAND,
+    )
+
+
+def gate_kernel(*refs):
+    features, halos, taps = refs[:9], refs[9:12], refs[12:15]
+    rate, query, gated, states, ext = refs[15:]
+
     def one_tile(tile, carry):
         lanes = tile_lanes(tile)
         decay = rate[:, lanes]
@@ -52,14 +79,13 @@
         back = 7.0 - sublane_index()
         step8_rows = [row(step8, m) for m in range(M)]
         weights = [jnp.exp(-row(decay, m) * back) for m in range(M)]
-        for s, features in enumerate((clean, pert, teacher)):
+        for s in range(3):
             parts = []
             for branch in range(3):
-                columns = tile_lanes(tile, branch)
                 slot = s * 3 + branch
-                ext[slot, 8 : 8 + ROWS, :] = features[:, columns].astype(f32)
-                ext[slot, 6:8, :] = halo[s, :, columns].astype(f32)
-                tap = taps[:, columns]
+                ext[slot, 8 : 8 + ROWS, :] = features[slot][:, lanes].astype(f32)
+                ext[slot, 6:8, :] = halos[branch][s, :, lanes].astype(f32)
+                tap = taps[branch][:, lanes]
                 parts.append(
                     tap[0:1] * ext[slot, 8 : 8 + ROWS, :]
                     + tap[1:2] * ext[slot, 7 : 7 + ROWS, :]
@@ -74,10 +100,10 @@
                 for i in range(1, 8):
                     state = state * step8_rows[m] + x[8 * i : 8 * i + 8]
                 state = jnp.sum(state * weights[m], axis=0, keepdims=True)
-                states[m, tile // QUARTER, s, pl.ds(tile % QUARTER, 1), :] = state
+                states[m, 0, s, pl.ds(tile, 1), :] = state
         return carry
 
-    lax.fori_loop(0, TILES, one_tile, 0)
+    lax.fori_loop(0, QUARTER, one_tile, 0)
 
 
 def within_kernel(streams, reverse, data, rate, res, out, held, near):
@@ -126,7 +152,7 @@
             out[s, :, lanes] = held[s]
         return carry
 
-    lax.fori_loop(0, TILES, one_tile, 0)
+    lax.fori_loop(0, QUARTER, one_tile, 0)
 
 
 def scan_kernel(reverse, ends, rate, reaching):
@@ -140,12 +166,20 @@
 
 
 def mix_kernel(
-    reaching, inner, query, rate, res, own_weight, core_weight, prod, conv, mixed, held, sems
+    reaching_far, inner_far, query_far, rate, res, own_weight, core_weight,
+    prod, conv, mixed,
+    reaching, inner, query, held, sems,
 ):
-    copies = [
-        pltpu.make_async_copy(weight, held.at[p], sems.at[p])
-        for p, weight in enumerate((own_weight, core_weight))
-    ]
+    copies = []
+    for q in range(QUARTERS):
+        lanes = pl.ds(q * QUARTER * LANES, QUARTER * LANES)
+        copies += [
+            pltpu.make_async_copy(reaching_far.at[:, q], reaching.at[:, q], sems.at[3 * q]),
+            pltpu.make_async_copy(inner_far.at[:, :, lanes], inner.at[:, :, lanes], sems.at[3 * q + 1]),
+            pltpu.make_async_copy(query_far.at[:, :, lanes], query.at[:, :, lanes], sems.at[3 * q + 2]),
+        ]
+    for p, weight in enumerate((own_weight, core_weight)):
+        copies.append(pltpu.make_async_copy(weight, held.at[p], sems.at[3 * QUARTERS + p]))
     for copy in copies:
         copy.start()
 
@@ -173,10 +207,13 @@
             prod[pl.ds(s * ROWS, ROWS), lanes] = product.astype(bf16)
         return carry
 
-    lax.fori_loop(0, TILES, conv_tile, 0)
+    for q in range(QUARTERS):
+        for copy in copies[3 * q : 3 * q + 3]:
+            copy.wait()
+        lax.fori_loop(QUARTER * q, QUARTER * q + QUARTER, conv_tile, 0)
 
     for p in range(2):
-        copies[p].wait()
+        copies[3 * QUARTERS + p].wait()
         mix_shard(prod, held.at[p], mixed.at[p])
 
 
@@ -189,17 +226,12 @@
     lax.fori_loop(0, WIDTH // BLOCK, mix, 0)
 
 
-def slope_kernel(
-    prod, conv, query, rate, near_mixed, gain, *refs,
-):
+def slope_kernel(prod, near_far, conv_far, query_far, rate, gain, *refs):
     weights, refs = refs[:12], refs[12:]
-    query_slope, conv_slope, edge, states, held, far_mixed, slope, prod_slope, sems = refs
+    query_slope, conv_slope, edge, states = refs[:4]
+    held, near_mixed, conv, query, far_mixed, slope, prod_slope, sems = refs[4:]
     dp, ctx = lax.axis_index("dp"), lax.axis_index("ctx")
-    x, z = ctx % 4, (ctx // 4) % 8
-    colour = (x % 2) * 2 + z % 2
-    across_x = (1 - x % 2) * 2 + z % 2
-    across_z = (x % 2) * 2 + 1 - z % 2
-    starts = (colour * BAND, across_x * BAND, across_z * BAND, (3 - colour) * BAND)
+    starts = bands(ctx)
     places = []
     for p in (2, 3):
         for q in range(3):
@@ -213,6 +245,12 @@
         )
         for n, (weight, (p, start, size)) in enumerate(zip(weights, places))
     ]
+    late = [
+        pltpu.make_async_copy(near_far, near_mixed, sems.at[12]),
+        pltpu.make_async_copy(conv_far, conv, sems.at[13]),
+        pltpu.make_async_copy(query_far.at[0:2], query, sems.at[14]),
+    ]
+    copies += late
     for copy in copies:
         copy.start()
     high, core = dp // 2, dp % 2
@@ -224,6 +262,8 @@
             copy.wait()
         mix_shard(prod, held.at[2 + p], far_mixed.at[p])
 
+    for copy in late:
+        copy.wait()
     squares = jnp.zeros((3 * ROWS, LANES), f32)
     for p in range(shards):
 
@@ -271,7 +311,7 @@
 
         lax.fori_loop(0, width // LANES, out_slopes, 0)
 
-    for copy in copies[10:]:
+    for copy in copies[10:12]:
         copy.wait()
 
     def back(t, carry):
@@ -312,11 +352,12 @@
     lax.fori_loop(0, TILES, state_tile, 0)
 
 
-def final_kernel(
-    reaching, inner, query_slope, next_edge, clean, pert, halo, next_rows, taps, rate, res,
-    grad_clean, grad_pert,
-    ext, unit,
-):
+def final_kernel(*refs):
+    reaching, inner, query_slope, next_edge = refs[:4]
+    features, halos, next_rows, taps = refs[4:8], refs[8:10], refs[10:12], refs[12:15]
+    rate, res, grad_clean, grad_pert, ext, unit, grads, sems = refs[15:]
+    quarter_at = pl.program_id(0)
+
     def one_tile(tile, carry):
         lanes = tile_lanes(tile)
         decay = rate[:, lanes]
@@ -327,13 +368,13 @@
         first = sublane_index() == 0.0
         reach = [row(scaled, m) * jnp.exp(-row(decay, m) * behind) for m in range(M)]
         beyond = [row(scaled, m) * jnp.exp(row(decay, m) * sublane_index()) for m in range(M)]
-        for s, (features, grad) in enumerate(((clean, grad_clean), (pert, grad_pert))):
+        for s in range(2):
             totals = [inner[s, 8 * i : 8 * i + 8, lanes] for i in range(8)]
             after = jnp.zeros((8, LANES), f32)
             edge = next_edge[s, :, lanes].astype(f32)
             passed = jnp.where(first, 0.0, row(edge, 8))
             for m in range(M):
-                state = reaching[m, tile // QUARTER, s, pl.ds(tile % QUARTER, 1), :]
+                state = reaching[m, 0, s, pl.ds(tile, 1), :]
                 after = after + beyond[m] * (state - passed)
                 term = reach[m] * state
                 for i in range(7, -1, -1):
@@ -343,15 +384,13 @@
             totals.append(after)
             gated_slope = jnp.concatenate(totals, 0).astype(bf16).astype(f32)
             parts = []
-            for branch in (1, 2):
-                columns = tile_lanes(tile, branch)
-                tail = tile_lanes(tile, branch - 1)
-                slot = s * 2 + branch - 1
-                ext[slot, 8 : 8 + ROWS, :] = features[:, columns].astype(f32)
-                ext[slot, 6:8, :] = halo[s, :, columns].astype(f32)
+            for branch in range(2):
+                slot = s * 2 + branch
+                ext[slot, 8 : 8 + ROWS, :] = features[slot][:, lanes].astype(f32)
+                ext[slot, 6:8, :] = halos[branch][s, :, lanes].astype(f32)
                 ext[slot, 72:80, :] = jnp.zeros((8, LANES), f32)
-                ext[slot, 72:74, :] = next_rows[s, :, tail].astype(f32)
-                tap = taps[:, columns]
+                ext[slot, 72:74, :] = next_rows[branch][s, :, lanes].astype(f32)
+                tap = taps[branch + 1][:, lanes]
                 parts.append(
                     tap[0:1] * ext[slot, 8:80, :]
                     + tap[1:2] * ext[slot, 7:79, :]
@@ -362,17 +401,47 @@
             unit[3 * s + 1] = gated_slope * parts[1]
             unit[3 * s + 2] = gated_slope * parts[0]
             for branch in range(3):
-                columns = tile_lanes(tile, branch)
-                tap = taps[:, columns]
+                tap = taps[branch][:, lanes]
                 slot = 3 * s + branch
-                grad[:, columns] = (
+                grads[quarter_at, slot, :, lanes] = (
                     tap[0:1] * unit[slot, 0:ROWS, :]
                     + tap[1:2] * unit[slot, 1 : 1 + ROWS, :]
                     + tap[2:3] * unit[slot, 2 : 2 + ROWS, :]
                 ).astype(bf16)
         return carry
 
-    lax.fori_loop(0, TILES, one_tile, 0)
+    lax.fori_loop(0, QUARTER, one_tile, 0)
+
+    def copies(at):
+        width = QUARTER * LANES
+        return [
+            pltpu.make_async_copy(
+                grads.at[at, 3 * s + branch],
+                grad.at[:, pl.ds(pl.multiple_of(branch * C + at * width, width), width)],
+                sems.at[at, 3 * s + branch],
+            )
+            for s, grad in enumerate((grad_clean, grad_pert))
+            for branch in range(3)
+        ]
+
+    for copy in copies(quarter_at):
+        copy.start()
+
+    @pl.when(quarter_at == QUARTERS - 1)
+    def _():
+        for at in range(QUARTERS):
+            for copy in copies(at):
+                copy.wait()
+
+
+def quarter(*lead, branch=0):
+    return pl.BlockSpec(
+        (*lead, QUARTER * LANES), lambda q: (*(0 for _ in lead), branch * QUARTERS + q)
+    )
+
+
+def quarter_states(streams):
+    return pl.BlockSpec((M, 1, streams, QUARTER, LANES), lambda q: (0, q, 0, 0, 0))
 
 
 def array(*shape, dtype=f32):
@@ -384,10 +453,11 @@
     return pl.pallas_call(
         functools.partial(within_kernel, streams, reverse),
         out_shape=array(streams, ROWS, C),
-        in_specs=whole(3),
-        out_specs=whole(1)[0],
+        grid=(QUARTERS,),
+        in_specs=[quarter(streams, ROWS), quarter(M), quarter(M)],
+        out_specs=quarter(streams, ROWS),
         scratch_shapes=[pltpu.VMEM((streams, ROWS, LANES), f32), pltpu.VMEM((8 * M + 8, LANES), f32)],
-        compiler_params=params(8),
+        compiler_params=params(60),
         cost_estimate=pl.CostEstimate(
             flops=streams * 100_000_000, bytes_accessed=streams * 6 * ROWS * C, transcendentals=0
         ),
@@ -398,8 +468,6 @@
     return pl.pallas_call(
         functools.partial(scan_kernel, reverse),
         out_shape=array(*ends.shape),
-        in_specs=whole(2),
-        out_specs=whole(1)[0],
         compiler_params=params(4),
     )(ends, own_rate)
 
@@ -445,22 +513,36 @@
     feat_clean, feat_pert, feat_teacher, short_taps, residues, decay_rate, out_weight, norm_gain
 ):
     clean, pert, teacher = feat_clean[0], feat_pert[0], feat_teacher[0]
-    last_rows = jnp.stack([clean[-2:], pert[-2:], teacher[-2:]])
-    last_rows, out_weight = tied(last_rows, out_weight)
-    halo = passed_along(last_rows, 1)
-    next_rows = passed_along(jnp.stack([clean[:2, C:], pert[:2, C:]]), -1)
     gain = norm_gain.reshape(4, 1, WIDTH)
     rate, res = decay_rate.T, residues.T
     own = lax.axis_index("ctx")
     own_rate = lax.dynamic_slice(
         rate, (own // QUARTER, (own % QUARTER) * QUARTER * LANES), (1, QUARTER * LANES)
     ).reshape(QUARTER, LANES)
-    state_shape = (M, TILES // QUARTER)
-
-    x, z = own % 4, own // 4 % 8
-    colour = (x % 2) * 2 + z % 2
-    core_weight = swapped(out_weight, "core")
-    band = swapped(lax.dynamic_slice(out_weight, (colour * BAND, 0), (BAND, WIDTH)), "y")
+    state_shape = (M, QUARTERS)
+
+    eight = [pl.BlockSpec((8, 3 * C), lambda i: (7, 0))] * 3 + [pl.BlockSpec((8, 3 * C), lambda i: (0, 0))] * 2
+    last_rows, first_rows, band = pl.pallas_call(
+        edge_kernel,
+        out_shape=(
+            array(3, 2, 3 * C, dtype=bf16),
+            array(2, 2, 2 * C, dtype=bf16),
+            array(BAND, WIDTH, dtype=bf16),
+        ),
+        grid=(1,),
+        in_specs=eight + [far()],
+        out_specs=(
+            pl.BlockSpec((3, 2, 3 * C), lambda i: (0, 0, 0)),
+            pl.BlockSpec((2, 2, 2 * C), lambda i: (0, 0, 0)),
+            far(),
+        ),
+        scratch_shapes=[pltpu.SemaphoreType.DMA],
+        compiler_params=params(60),
+    )(clean, pert, teacher, clean, pert, out_weight)
+    halo = passed_along(last_rows, 1)
+    halo, to_core, band = tied(halo, out_weight, band)
+    core_weight = swapped(to_core, "core")
+    band = swapped(band, "y")
 
     query, gated, ends = pl.pallas_call(
         gate_kernel,
@@ -469,11 +551,17 @@
             array(3, ROWS, C, dtype=bf16),
             array(*state_shape, 3, QUARTER, LANES),
         ),
-        in_specs=whole(6),
-        out_specs=tuple(whole(3)),
+        grid=(QUARTERS,),
+        in_specs=[quarter(ROWS, branch=b) for _ in range(3) for b in range(3)]
+        + [quarter(3, 2, branch=b) for b in range(3)]
+        + [quarter(3, branch=b) for b in range(3)]
+        + [quarter(M)],
+        out_specs=(quarter(3, ROWS), quarter(3, ROWS), quarter_states(3)),
         scratch_shapes=[pltpu.VMEM((9, 8 + ROWS, LANES), f32)],
-        compiler_params=params(4),
-    )(clean, pert, teacher, halo, short_taps, rate)
+        compiler_params=params(60),
+    )(
+        *(clean,) * 3, *(pert,) * 3, *(teacher,) * 3, *(halo,) * 3, *(short_taps,) * 3, rate
+    )
 
     ends = exchanged(ends)
     inner = within(gated, rate, res, False)
@@ -484,6 +572,8 @@
     reaching, band_x, band_z = tied(reaching, band_x, band_z)
     half = BAND // 2
     last_x, last_z = swapped(band_z[:half], "x"), swapped(band_x[half:], "z")
+    near = [band, band_x, band_z]
+    near_core = [swapped(piece, "core") for piece in near]
 
     prod, conv, near_mixed = pl.pallas_call(
         mix_kernel,
@@ -492,15 +582,24 @@
             array(2, ROWS, C, dtype=bf16),
             array(2, 3 * ROWS, WIDTH),
         ),
-        in_specs=whole(5) + [pl.BlockSpec(memory_space=pltpu.HBM)] * 2,
-        out_specs=tuple(whole(3)),
-        scratch_shapes=[pltpu.VMEM((2, C, WIDTH), bf16), pltpu.SemaphoreType.DMA((2,))],
-        compiler_params=params(12),
-        cost_estimate=pl.CostEstimate(flops=5_000_000_000, bytes_accessed=14_000_000, transcendentals=0),
+        in_specs=[far()] * 3 + [pl.BlockSpec()] * 2 + [far()] * 2,
+        scratch_shapes=[
+            pltpu.VMEM((M, QUARTERS, 3, QUARTER, LANES), f32),
+            pltpu.VMEM((3, ROWS, C), f32),
+            pltpu.VMEM((3, ROWS, C), bf16),
+            pltpu.VMEM((2, C, WIDTH), bf16),
+            pltpu.SemaphoreType.DMA((3 * QUARTERS + 2,)),
+        ],
+        compiler_params=params(60),
+        cost_estimate=pl.CostEstimate(
+            flops=5_000_000_000, bytes_accessed=14_000_000, transcendentals=0
+        ),
     )(reaching, inner, query, rate, res, out_weight, core_weight)
 
-    far = [band, band_x, band_z, last_x, last_z]
-    pieces = far + [swapped(piece, "core") for piece in far] + [out_weight, core_weight]
+    prod, last_x, last_z = tied(prod, last_x, last_z)
+    last = [last_x, last_z]
+    last_core = [swapped(piece, "core") for piece in last]
+    pieces = near + last + near_core + last_core + [out_weight, core_weight]
     query_slope, conv_slope, edge, ends = pl.pallas_call(
         slope_kernel,
         out_shape=(
@@ -509,35 +608,47 @@
             array(2, 16, C, dtype=bf16),
             array(*state_shape, 2, QUARTER, LANES),
         ),
-        in_specs=whole(6) + [pl.BlockSpec(memory_space=pltpu.HBM)] * 12,
-        out_specs=tuple(whole(4)),
+        in_specs=[pl.BlockSpec()] + [far()] * 3 + [pl.BlockSpec()] * 2 + [far()] * 12,
         scratch_shapes=[
             pltpu.VMEM((4, C, WIDTH), bf16),
             pltpu.VMEM((2, 3 * ROWS, WIDTH), f32),
+            pltpu.VMEM((2, ROWS, C), bf16),
+            pltpu.VMEM((2, ROWS, C), bf16),
+            pltpu.VMEM((2, 3 * ROWS, WIDTH), f32),
             pltpu.VMEM((4, 2 * ROWS, WIDTH), bf16),
             pltpu.VMEM((2 * ROWS, C), f32),
-            pltpu.SemaphoreType.DMA((12,)),
+            pltpu.SemaphoreType.DMA((15,)),
         ],
-        compiler_params=params(24),
-    )(prod, conv, query, rate, near_mixed, gain, *pieces)
+        compiler_params=params(60),
+    )(prod, near_mixed, conv, query, rate, gain, *pieces)
 
     next_edge = passed_along(edge, -1)
     ends = exchanged(ends)
     inner = within(conv_slope, rate, res, True)
     reaching = exchanged(scan(ends, own_rate, True)).reshape(*state_shape, 2, QUARTER, LANES)
 
+    first_rows = passed_along(first_rows, -1)
     grads = pl.pallas_call(
         final_kernel,
         out_shape=(array(ROWS, 3 * C, dtype=bf16), array(ROWS, 3 * C, dtype=bf16)),
-        in_specs=whole(11),
-        out_specs=tuple(whole(2)),
+        grid=(QUARTERS,),
+        in_specs=[quarter_states(2), quarter(2, ROWS), quarter(2, ROWS), quarter(2, 16)]
+        + [quarter(ROWS, branch=b) for _ in range(2) for b in (1, 2)]
+        + [quarter(3, 2, branch=b) for b in (1, 2)]
+        + [quarter(2, 2, branch=b) for b in (0, 1)]
+        + [quarter(3, branch=b) for b in range(3)]
+        + [quarter(M), quarter(M)],
+        out_specs=(far(), far()),
         scratch_shapes=[
             pltpu.VMEM((4, 16 + ROWS, LANES), f32),
             pltpu.VMEM((6, 8 + ROWS, LANES), f32),
+            pltpu.VMEM((QUARTERS, 6, ROWS, QUARTER * LANES), bf16),
+            pltpu.SemaphoreType.DMA((QUARTERS, 6)),
         ],
-        compiler_params=params(16),
+        compiler_params=params(60),
     )(
-        reaching, inner, query_slope, next_edge, clean, pert, halo, next_rows, short_taps, rate, res
+        reaching, inner, query_slope, next_edge, *(clean,) * 2, *(pert,) * 2, *(halo,) * 2,
+        *(first_rows,) * 2, *(short_taps,) * 3, rate, res,
     )
     return grads[0][None], grads[1][None]
 

time: 164 us -> 190 us (1.16); the launches traced: 161 us -> 189 us
  Pallas kernels: 42.7 us -> 91.6 us
  local copies, waits for them, and re-layouts: 21.6 us -> 4.95 us
  waiting for transfers between devices: 20.5 us -> 17 us
  starting transfers between devices: 33.2 us -> 31.2 us
    pallas_call x0 -> x1, Pallas kernels: none -> 34.6 us  [per_device(): pl.pallas_call(edge_kernel, out_shape=(array(3, 2, 3 * C, dtype=bf16), ar...]
    unnamed x50 -> x22, local copies, waits for them, and re-layouts: 17.3 us -> 2.43 us
    pallas_call x1, Pallas kernels: 16.5 us -> 20.8 us  [per_device(): pl.pallas_call(slope_kernel, out_shape=(array(2, ROWS, C), array(2, ROWS,...]
    ppermute x11, starting transfers between devices: 8.47 us -> 4.43 us  [swapped(): lax.ppermute(value, ('dp', 'ctx'), [(device, partner(device, kind)) for d...]
    pallas_call x2, Pallas kernels: 9.91 us -> 13.5 us  [within(): pl.pallas_call(functools.partial(within_kernel, streams, reverse), out_sh...]
    pallas_call x1, Pallas kernels: 5.87 us -> 8.99 us  [per_device(): pl.pallas_call(mix_kernel, out_shape=(array(3 * ROWS, C, dtype=bf16), arr...]
    slice x3 -> x0, local copies, waits for them, and re-layouts: 2.81 us -> none  [per_device(): last_rows = jnp.stack([clean[-2:], pert[-2:], teacher[-2:]])]
    all_to_all x2, waiting for transfers between devices: 3.84 us -> 1.04 us  [exchanged(): return lax.all_to_all(flat, 'ctx', split_axis=0, concat_axis=0, tiled=True)]
  transfers between devices with their start and end apart: 16 -> 16, of which waited for: 4 -> 5; matrix products, arithmetic and copies ran while one was open for 1% -> 1% of each run, Pallas kernels for 13% -> 15%
where the time goes in v3:
time: 190 us; the launch traced here: 189 us
  Pallas kernels  91.6 us (48%)
  blocking collectives  43.7 us (23%)
  starting transfers between devices  31.2 us (16%)
  waiting for transfers between devices  17 us (9%)
  local copies, waits for them, and re-layouts  4.95 us (3%)
    all_to_all x2, blocking collectives, exchanged(): return lax.all_to_all(flat, 'ctx', split_axis=0, concat_axis=0, tiled=True)  43.7 us
    pallas_call x1, Pallas kernels, per_device(): pl.pallas_call(edge_kernel, out_shape=(array(3, 2, 3 * C, dtype=bf16), ar...  34.6 us
    pallas_call x1, Pallas kernels, per_device(): pl.pallas_call(slope_kernel, out_shape=(array(2, ROWS, C), array(2, ROWS,...  20.8 us
    all_to_all x2, starting transfers between devices, exchanged(): return lax.all_to_all(flat, 'ctx', split_axis=0, concat_axis=0, tiled=True)  13.9 us
    pallas_call x2, Pallas kernels, within(): pl.pallas_call(functools.partial(within_kernel, streams, reverse), out_sh...  13.5 us
    ppermute x3, starting transfers between devices, passed_along(): lax.ppermute(value, 'ctx', [(source, source + steps) for source in range(...  12.8 us
    ppermute x3, waiting for transfers between devices, passed_along(): lax.ppermute(value, 'ctx', [(source, source + steps) for source in range(...  9.27 us
    pallas_call x1, Pallas kernels, per_device(): pl.pallas_call(mix_kernel, out_shape=(array(3 * ROWS, C, dtype=bf16), arr...  8.99 us
  transfers between devices with their start and end apart: 16, of which 5 were waited for; matrix products, arithmetic and copies ran while one was open for 1% of the time, Pallas kernels for 15%

profile of v3, /device:TPU:24, one launch (start us, length us, event | category | flops | bytes accessed | tf_op | source)
XLA Modules:
  0.0 189.5 jit_solution(3974601175346386682)
XLA Ops:
  0.6 34.6 %shard_map.95 = (bf16[3,2,6144]{2,1,0:T(2,128)(2,1)}, bf16[2,2,4096]{2,1,0:T(2,128)(2,1)}, bf16[512,1024]{1,0:T(8,128)(2,1)}) custom-call(bf16[64,6144]{1,0:T(8,128)(2,1)} %bitcast.15, bf16[64,6144]{1,0:T(8,128)(2,1)} %bitcast.22, bf16[64,6144]{1,0:T(8,128)(2,1)} %bitcast.29, bf16[64,6144]{1,0:T(8,128)(2,1)} %bitcast.16, bf16[64,6144]{1,0:T(8,128)(2,1)} %bitcast.23, ...), custom_call_target="tpu_custom_call" | custom-call | tf_op jit(solution)/shard_map/pallas_call | solution.py:525
  35.2 3.4 %collective-permute-start = (bf16[3,2,6144]{2,1,0:T(2,128)(2,1)}, bf16[3,2,6144]{2,1,0:T(2,128)(2,1)S(1)}, u32[]{:S(2)}, u32[]{:S(2)}) collective-permute-start(bf16[3,2,6144]{2,1,0:T(2,128)(2,1)} %get-tuple-element.30), channel_id=1, source_target_pairs={{0,1},{1,2},{2,3},{3,4},{4,5},{5,6},{6,7},{7,8},{8,9},{9,10},{10,1... | collective-permute-start | bytes 221192 | tf_op jit(solution)/shard_map/ppermute | solution.py:485
  38.6 9.3 %collective-permute-done.refs_9_.refs_10_.refs_11_.refs_8_ = bf16[3,2,6144]{2,1,0:T(2,128)(2,1)S(1)} collective-permute-done((bf16[3,2,6144]{2,1,0:T(2,128)(2,1)}, bf16[3,2,6144]{2,1,0:T(2,128)(2,1)S(1)}, u32[]{:S(2)}, u32[]{:S(2)}) %collective-permute-start) | collective-permute-done | bytes 73760 | tf_op jit(solution)/shard_map/ppermute | solution.py:485
  47.9 0.6 copy-done.2
  48.5 6.4 %shard_map.96 = (bf16[3,64,2048]{2,1,0:T(8,128)(2,1)}, bf16[3,64,2048]{2,1,0:T(8,128)(2,1)}, f32[16,4,3,4,128]{4,3,2,1,0:T(4,128)}) custom-call(bf16[64,6144]{1,0:T(8,128)(2,1)} %bitcast.17, bf16[64,6144]{1,0:T(8,128)(2,1)} %bitcast.18, bf16[64,6144]{1,0:T(8,128)(2,1)} %bitcast.19, bf16[64,6144]{1,0:T(8,128)(2,1)} %bitcast.24, bf16[64,6144]{1,0:T(8,128)(2,1)} %bitcast.25, ...), custom_call_target="tpu_custom_call" | custom-call | tf_op jit(solution)/shard_map/pallas_call | solution.py:547
  55.0 7.7 %all-to-all-start = ((f32[64,3,4,128]{3,2,1,0:T(4,128)}), f32[64,3,4,128]{3,2,1,0:T(4,128)S(1)}, u32[]{:S(2)}, u32[]{:S(2)}) async-start(f32[64,3,4,128]{3,2,1,0:T(4,128)} %bitcast.44), calls=%async_computation | async-start | bytes 786432 | tf_op jit(solution)/shard_map/all_to_all | solution.py:479
  62.7 7.6 %shard_map.97.inner_far = f32[3,64,2048]{2,1,0:T(8,128)} custom-call(bf16[3,64,2048]{2,1,0:T(8,128)(2,1)} %get-tuple-element.34.data, f32[16,2048]{1,0:T(8,128)} %bitcast.34, f32[16,2048]{1,0:T(8,128)} %bitcast.39), custom_call_target="tpu_custom_call" | custom-call | flops 300000000 | bytes 2359296 | tf_op jit(solution)/shard_map/pallas_call | solution.py:453
  70.3 4.7 %collective-permute-done.1.refs_0_ = bf16[512,1024]{1,0:T(8,128)(2,1)} collective-permute-done((bf16[512,1024]{1,0:T(8,128)(2,1)}, bf16[512,1024]{1,0:T(8,128)(2,1)}, u32[]{:S(2)}, u32[]{:S(2)}) %collective-permute-start.1) | collective-permute-done | bytes 1048608 | tf_op jit(solution)/shard_map/ppermute | solution.py:503
  75.0 0.8 dynamic-slice.3
  75.8 1.0 all-to-all-done.ends
  77.0 22.8 %all_to_all.20 = f32[64,3,4,128]{3,2,1,0:T(4,128)} all-to-all(f32[64,3,4,128]{3,2,1,0:T(4,128)S(1)} %shard_map.98), channel_id=1, replica_groups=mesh['dp'=4,'ctx'=64] {'ctx'}, dimensions={0} | all-to-all | bytes 786432 | tf_op jit(solution)/shard_map/all_to_all | solution.py:479
  99.8 0.9 slice.6
  100.8 0.8 slice.7
  101.6 2.3 %collective-permute-start.6 = (bf16[256,1024]{1,0:T(8,128)(2,1)}, bf16[256,1024]{1,0:T(8,128)(2,1)S(1)}, u32[]{:S(2)}, u32[]{:S(2)}) collective-permute-start(bf16[256,1024]{1,0:T(8,128)(2,1)} %slice.7), channel_id=1, source_target_pairs={{0,4},{1,5},{2,6},{3,7},{4,0},{5,1},{6,2},{7,3},{8,12},{9,13},{10,... | collective-permute-start | bytes 1572872 | tf_op jit(solution)/shard_map/ppermute | solution.py:503
  103.9 0.7 collective-permute-start.5
  104.6 0.5 collective-permute-start.9
  105.1 9.0 %shard_map.99 = (bf16[192,2048]{1,0:T(8,128)(2,1)}, bf16[2,64,2048]{2,1,0:T(8,128)(2,1)}, f32[2,192,1024]{2,1,0:T(8,128)}) custom-call(f32[16,4,3,4,128]{4,3,2,1,0:T(4,128)} %bitcast.45, f32[3,64,2048]{2,1,0:T(8,128)} %shard_map.97.inner_far, bf16[3,64,2048]{2,1,0:T(8,128)(2,1)} %get-tuple-element.41.query_far, f32[16,2048]{1,0:T(8,128)} %bitcast.35, ...), custom_call_target="tpu_custom_call" | custom-call | flops 5000000000 | bytes 14000000 | tf_op jit(solution)/shard_map/pallas_call | solution.py:578
  114.2 0.6 collective-permute-start.10
  114.8 0.3 collective-permute-start.11
  115.1 1.4 collective-permute-done.10.refs_8_
  116.5 0.5 collective-permute-done.11.refs_9_
  117.1 0.2 copy-done.6
  117.3 0.8 copy-done.7
  118.1 20.8 %shard_map.100 = (f32[2,64,2048]{2,1,0:T(8,128)}, bf16[2,64,2048]{2,1,0:T(8,128)(2,1)}, bf16[2,16,2048]{2,1,0:T(8,128)(2,1)}, f32[16,4,2,4,128]{4,3,2,1,0:T(4,128)}) custom-call(bf16[192,2048]{1,0:T(8,128)(2,1)} %get-tuple-element.46.prod, f32[2,192,1024]{2,1,0:T(8,128)} %get-tuple-element.47.near_far, bf16[2,64,2048]{2,1,0:T(8,128)(2,1)} %get-tuple-element.48.conv_far, ...), custom_call_target="tpu_custom_call" | custom-call | tf_op jit(solution)/shard_map/pallas_call | solution.py:603
  138.9 20.9 %all_to_all.21.ends = f32[64,2,4,128]{3,2,1,0:T(4,128)S(1)} all-to-all(f32[64,2,4,128]{3,2,1,0:T(4,128)} %bitcast.46), channel_id=1, replica_groups=mesh['dp'=4,'ctx'=64] {'ctx'}, dimensions={0} | all-to-all | bytes 524288 | tf_op jit(solution)/shard_map/all_to_all | solution.py:479
  159.8 0.8 shard_map.101
  160.7 6.2 %all-to-all-start.3 = ((f32[64,2,4,128]{3,2,1,0:T(4,128)}), f32[64,2,4,128]{3,2,1,0:T(4,128)S(1)}, u32[]{:S(2)}, u32[]{:S(2)}) async-start(f32[64,2,4,128]{3,2,1,0:T(4,128)} %shard_map.101), calls=%async_computation.3 | async-start | bytes 524288 | tf_op jit(solution)/shard_map/all_to_all | solution.py:479
  166.9 6.7 %collective-permute-start.12 = (bf16[2,16,2048]{2,1,0:T(8,128)(2,1)}, bf16[2,16,2048]{2,1,0:T(8,128)(2,1)S(1)}, u32[]{:S(2)}, u32[]{:S(2)}) collective-permute-start(bf16[2,16,2048]{2,1,0:T(8,128)(2,1)} %get-tuple-element.54), channel_id=1, source_target_pairs={{1,0},{2,1},{3,2},{4,3},{5,4},{6,5},{7,6},{8,7},{9,8},{10,9},{11,1... | collective-permute-start | bytes 393224 | tf_op jit(solution)/shard_map/ppermute | solution.py:485
  173.6 2.8 %collective-permute-start.13 = (bf16[2,2,4096]{2,1,0:T(2,128)(2,1)S(1)}, bf16[2,2,4096]{2,1,0:T(2,128)(2,1)S(1)}, u32[]{:S(2)}, u32[]{:S(2)}) collective-permute-start(bf16[2,2,4096]{2,1,0:T(2,128)(2,1)S(1)} %copy-done.10), channel_id=1, source_target_pairs={{1,0},{2,1},{3,2},{4,3},{5,4},{6,5},{7,6},{8,7},{9,8},{10,9},{11,1... | collective-permute-start | bytes 98312 | tf_op jit(solution)/shard_map/ppermute | solution.py:485
  176.4 5.8 %shard_map.102.refs_1_ = f32[2,64,2048]{2,1,0:T(8,128)} custom-call(bf16[2,64,2048]{2,1,0:T(8,128)(2,1)} %get-tuple-element.52.data, f32[16,2048]{1,0:T(8,128)} %bitcast.37, f32[16,2048]{1,0:T(8,128)} %bitcast.41), custom_call_target="tpu_custom_call" | custom-call | flops 200000000 | bytes 1572864 | tf_op jit(solution)/shard_map/pallas_call | solution.py:453
  182.3 0.6 copy-done.8
  183.0 6.3 %shard_map.103 = (bf16[64,6144]{1,0:T(8,128)(2,1)}, bf16[64,6144]{1,0:T(8,128)(2,1)}) custom-call(f32[16,4,2,4,128]{4,3,2,1,0:T(4,128)} %bitcast.43, f32[2,64,2048]{2,1,0:T(8,128)} %shard_map.102.refs_1_, f32[2,64,2048]{2,1,0:T(8,128)} %get-tuple-element.53.refs_2_, bf16[2,16,2048]{2,1,0:T(8,128)(2,1)} %copy-done.9, bf16[64,6144]{1,0:T(8,128)(2,1)} %bitcast.20, ...), custom_call_target="tpu_custom_call" | custom-call | tf_op jit(solution)/shard_map/pallas_call | solution.py:631
  (36 shorter events, 0.4 us)
Async XLA Ops:
  35.2 12.7 %collective-permute-start = (bf16[3,2,6144]{2,1,0:T(2,128)(2,1)}, bf16[3,2,6144]{2,1,0:T(2,128)(2,1)S(1)}, u32[]{:S(2)}, u32[]{:S(2)}) collective-permute-start(bf16[3,2,6144]{2,1,0:T(2,128)(2,1)} %get-tuple-element.30), channel_id=1, source_target_pairs={{0,1},{1,2},{2,3},{3,4},{4,5},{5,6},{6,7},{7,8},{8,9},{9,10},{10,1... | collective-permute-start | bytes 221192 | tf_op jit(solution)/shard_map/ppermute | solution.py:485
  47.9 0.6 copy-start.2
  47.9 57.2 %collective-permute-start.4 = (bf16[2048,1024]{1,0:T(8,128)(2,1)}, bf16[2048,1024]{1,0:T(8,128)(2,1)}, u32[]{:S(2)}, u32[]{:S(2)}) collective-permute-start(bf16[2048,1024]{1,0:T(8,128)(2,1)} %refs_10_.1), channel_id=1, source_target_pairs={{0,64},{1,65},{2,66},{3,67},{4,68},{5,69},{6,70},{7,71},{8,72},{9,... | collective-permute-start | bytes 12582920 | tf_op jit(solution)/shard_map/ppermute | solution.py:503
  47.9 27.1 %collective-permute-start.1 = (bf16[512,1024]{1,0:T(8,128)(2,1)}, bf16[512,1024]{1,0:T(8,128)(2,1)}, u32[]{:S(2)}, u32[]{:S(2)}) collective-permute-start(bf16[512,1024]{1,0:T(8,128)(2,1)} %get-tuple-element.35), channel_id=1, source_target_pairs={{0,160},{1,161},{2,162},{3,163},{4,164},{5,165},{6,166},{7,167},{8... | collective-permute-start | bytes 3145736 | tf_op jit(solution)/shard_map/ppermute | solution.py:503
  55.0 21.9 %all-to-all-start = ((f32[64,3,4,128]{3,2,1,0:T(4,128)}), f32[64,3,4,128]{3,2,1,0:T(4,128)S(1)}, u32[]{:S(2)}, u32[]{:S(2)}) async-start(f32[64,3,4,128]{3,2,1,0:T(4,128)} %bitcast.44), calls=%async_computation | async-start | bytes 786432 | tf_op jit(solution)/shard_map/all_to_all | solution.py:479
  75.0 24.8 %collective-permute-start.3 = (bf16[512,1024]{1,0:T(8,128)(2,1)}, bf16[512,1024]{1,0:T(8,128)(2,1)S(1)}, u32[]{:S(2)}, u32[]{:S(2)}) collective-permute-start(bf16[512,1024]{1,0:T(8,128)(2,1)} %collective-permute-done.1.refs_0_), channel_id=1, source_target_pairs={{0,4},{1,5},{2,6},{3,7},{4,0},{5,1},{6,2},{7,3},{8,12},{9,13},{10,... | collective-permute-start | bytes 3145736 | tf_op jit(solution)/shard_map/ppermute | solution.py:503
  75.0 24.8 %collective-permute-start.2 = (bf16[512,1024]{1,0:T(8,128)(2,1)}, bf16[512,1024]{1,0:T(8,128)(2,1)S(1)}, u32[]{:S(2)}, u32[]{:S(2)}) collective-permute-start(bf16[512,1024]{1,0:T(8,128)(2,1)} %collective-permute-done.1.refs_0_), channel_id=1, source_target_pairs={{0,1},{1,0},{2,3},{3,2},{4,5},{5,4},{6,7},{7,6},{8,9},{9,8},{10,11... | collective-permute-start | bytes 3145736 | tf_op jit(solution)/shard_map/ppermute | solution.py:503
  99.8 14.3 %copy-start = (bf16[512,1024]{1,0:T(8,128)(2,1)}, bf16[512,1024]{1,0:T(8,128)(2,1)S(1)}, u32[]{:S(2)}) copy-start(bf16[512,1024]{1,0:T(8,128)(2,1)S(1)} %collective-permute-done.3.refs_2_) | copy-start | bytes 3145732
  99.8 14.3 %copy-start.1 = (bf16[512,1024]{1,0:T(8,128)(2,1)}, bf16[512,1024]{1,0:T(8,128)(2,1)S(1)}, u32[]{:S(2)}) copy-start(bf16[512,1024]{1,0:T(8,128)(2,1)S(1)} %collective-permute-done.2.refs_1_) | copy-start | bytes 3145732
  101.6 12.6 %collective-permute-start.6 = (bf16[256,1024]{1,0:T(8,128)(2,1)}, bf16[256,1024]{1,0:T(8,128)(2,1)S(1)}, u32[]{:S(2)}, u32[]{:S(2)}) collective-permute-start(bf16[256,1024]{1,0:T(8,128)(2,1)} %slice.7), channel_id=1, source_target_pairs={{0,4},{1,5},{2,6},{3,7},{4,0},{5,1},{6,2},{7,3},{8,12},{9,13},{10,... | collective-permute-start | bytes 1572872 | tf_op jit(solution)/shard_map/ppermute | solution.py:503
  103.9 10.3 %collective-permute-start.5 = (bf16[256,1024]{1,0:T(8,128)(2,1)}, bf16[256,1024]{1,0:T(8,128)(2,1)}, u32[]{:S(2)}, u32[]{:S(2)}) collective-permute-start(bf16[256,1024]{1,0:T(8,128)(2,1)} %slice.6), channel_id=1, source_target_pairs={{0,1},{1,0},{2,3},{3,2},{4,5},{5,4},{6,7},{7,6},{8,9},{9,8},{10,11... | collective-permute-start | bytes 1572872 | tf_op jit(solution)/shard_map/ppermute | solution.py:503
  104.6 10.4 %collective-permute-start.7 = (bf16[512,1024]{1,0:T(8,128)(2,1)}, bf16[512,1024]{1,0:T(8,128)(2,1)S(1)}, u32[]{:S(2)}, u32[]{:S(2)}) collective-permute-start(bf16[512,1024]{1,0:T(8,128)(2,1)} %collective-permute-done.1.refs_0_), channel_id=1, source_target_pairs={{0,64},{1,65},{2,66},{3,67},{4,68},{5,69},{6,70},{7,71},{8,72},{9,... | collective-permute-start | bytes 3145736 | tf_op jit(solution)/shard_map/ppermute | solution.py:503
  104.6 10.4 %collective-permute-start.9 = (bf16[512,1024]{1,0:T(8,128)(2,1)S(1)}, bf16[512,1024]{1,0:T(8,128)(2,1)}, u32[]{:S(2)}, u32[]{:S(2)}) collective-permute-start(bf16[512,1024]{1,0:T(8,128)(2,1)S(1)} %collective-permute-done.3.refs_2_), channel_id=1, source_target_pairs={{0,64},{1,65},{2,66},{3,67},{4,68},{5,69},{6,70},{7,71},{8,72},{9,... | collective-permute-start | bytes 3145736 | tf_op jit(solution)/shard_map/ppermute | solution.py:503
  105.1 9.9 %collective-permute-start.8 = (bf16[512,1024]{1,0:T(8,128)(2,1)S(1)}, bf16[512,1024]{1,0:T(8,128)(2,1)}, u32[]{:S(2)}, u32[]{:S(2)}) collective-permute-start(bf16[512,1024]{1,0:T(8,128)(2,1)S(1)} %collective-permute-done.2.refs_1_), channel_id=1, source_target_pairs={{0,64},{1,65},{2,66},{3,67},{4,68},{5,69},{6,70},{7,71},{8,72},{9,... | collective-permute-start | bytes 3145736 | tf_op jit(solution)/shard_map/ppermute | solution.py:503
  114.2 4.0 %copy-start.5 = (bf16[256,1024]{1,0:T(8,128)(2,1)}, bf16[256,1024]{1,0:T(8,128)(2,1)S(1)}, u32[]{:S(2)}) copy-start(bf16[256,1024]{1,0:T(8,128)(2,1)S(1)} %collective-permute-done.6.refs_4_) | copy-start | bytes 1572868
  114.2 2.3 %collective-permute-start.10 = (bf16[256,1024]{1,0:T(8,128)(2,1)}, bf16[256,1024]{1,0:T(8,128)(2,1)S(1)}, u32[]{:S(2)}, u32[]{:S(2)}) collective-permute-start(bf16[256,1024]{1,0:T(8,128)(2,1)} %collective-permute-done.5.refs_3_), channel_id=1, source_target_pairs={{0,64},{1,65},{2,66},{3,67},{4,68},{5,69},{6,70},{7,71},{8,72},{9,... | collective-permute-start | bytes 1572872 | tf_op jit(solution)/shard_map/ppermute | solution.py:503
  114.8 2.3 %collective-permute-start.11 = (bf16[256,1024]{1,0:T(8,128)(2,1)S(1)}, bf16[256,1024]{1,0:T(8,128)(2,1)S(1)}, u32[]{:S(2)}, u32[]{:S(2)}) collective-permute-start(bf16[256,1024]{1,0:T(8,128)(2,1)S(1)} %collective-permute-done.6.refs_4_), channel_id=1, source_target_pairs={{0,64},{1,65},{2,66},{3,67},{4,68},{5,69},{6,70},{7,71},{8,72},{9,... | collective-permute-start | bytes 1572872 | tf_op jit(solution)/shard_map/ppermute | solution.py:503
  115.1 3.1 %copy-start.3 = (bf16[512,1024]{1,0:T(8,128)(2,1)}, bf16[512,1024]{1,0:T(8,128)(2,1)S(1)}, u32[]{:S(2)}) copy-start(bf16[512,1024]{1,0:T(8,128)(2,1)S(1)} %collective-permute-done.7.refs_5_) | copy-start | bytes 3145732
  116.5 0.8 copy-start.6
  117.3 0.8 copy-start.7
  118.1 55.5 %copy-start.10 = (bf16[2,2,4096]{2,1,0:T(2,128)(2,1)S(1)}, bf16[2,2,4096]{2,1,0:T(2,128)(2,1)}, u32[]{:S(2)}) copy-start(bf16[2,2,4096]{2,1,0:T(2,128)(2,1)} %get-tuple-element.55) | copy-start | bytes 98308
  160.7 21.6 %all-to-all-start.3 = ((f32[64,2,4,128]{3,2,1,0:T(4,128)}), f32[64,2,4,128]{3,2,1,0:T(4,128)S(1)}, u32[]{:S(2)}, u32[]{:S(2)}) async-start(f32[64,2,4,128]{3,2,1,0:T(4,128)} %shard_map.101), calls=%async_computation.3 | async-start | bytes 524288 | tf_op jit(solution)/shard_map/all_to_all | solution.py:479
  166.9 15.3 %collective-permute-start.12 = (bf16[2,16,2048]{2,1,0:T(8,128)(2,1)}, bf16[2,16,2048]{2,1,0:T(8,128)(2,1)S(1)}, u32[]{:S(2)}, u32[]{:S(2)}) collective-permute-start(bf16[2,16,2048]{2,1,0:T(8,128)(2,1)} %get-tuple-element.54), channel_id=1, source_target_pairs={{1,0},{2,1},{3,2},{4,3},{5,4},{6,5},{7,6},{8,7},{9,8},{10,9},{11,1... | collective-permute-start | bytes 393224 | tf_op jit(solution)/shard_map/ppermute | solution.py:485
  173.6 8.6 %collective-permute-start.13 = (bf16[2,2,4096]{2,1,0:T(2,128)(2,1)S(1)}, bf16[2,2,4096]{2,1,0:T(2,128)(2,1)S(1)}, u32[]{:S(2)}, u32[]{:S(2)}) collective-permute-start(bf16[2,2,4096]{2,1,0:T(2,128)(2,1)S(1)} %copy-done.10), channel_id=1, source_target_pairs={{1,0},{2,1},{3,2},{4,3},{5,4},{6,5},{7,6},{8,7},{9,8},{10,9},{11,1... | collective-permute-start | bytes 98312 | tf_op jit(solution)/shard_map/ppermute | solution.py:485
  182.2 0.6 copy-start.8
  182.2 0.7 copy-start.9
  182.3 0.7 copy-start.4

commit v4 on v3

--- a/solution.py
+++ b/solution.py
@@ -21,6 +21,7 @@
 WIDTH = D // 4
 BAND = C // 4
 BLOCK = 256
+PIECES = 7
 QUARTERS = 4
 QUARTER = TILES // QUARTERS
 
@@ -47,9 +48,8 @@
 
 def edge_kernel(*refs):
     features, (weight, last_rows, first_rows, band, sem) = refs[:5], refs[5:]
-    copy = pltpu.make_async_copy(
-        weight.at[pl.ds(pl.multiple_of(bands(lax.axis_index("ctx"))[0], BAND), BAND), :], band, sem
-    )
+    start = pl.multiple_of(bands(lax.axis_index("ctx"))[0], BAND)
+    copy = pltpu.make_async_copy(weight.at[pl.ds(start, BAND), :], band, sem)
     copy.start()
     for s in range(3):
         last_rows[s] = features[s][6:8, :]
@@ -167,8 +167,8 @@
 
 def mix_kernel(
     reaching_far, inner_far, query_far, rate, res, own_weight, core_weight,
-    prod, conv, mixed,
-    reaching, inner, query, held, sems,
+    prod, conv, mixed, held,
+    reaching, inner, query, sems,
 ):
     copies = []
     for q in range(QUARTERS):
@@ -226,44 +226,51 @@
     lax.fori_loop(0, WIDTH // BLOCK, mix, 0)
 
 
-def slope_kernel(prod, near_far, conv_far, query_far, rate, gain, *refs):
-    weights, refs = refs[:12], refs[12:]
-    query_slope, conv_slope, edge, states = refs[:4]
-    held, near_mixed, conv, query, far_mixed, slope, prod_slope, sems = refs[4:]
+def backward(slope, weights):
+    total = jnp.zeros((2 * ROWS, BLOCK), f32)
+    for p, weight in enumerate(weights):
+        total = total + lax.dot_general(
+            slope[p], weight[...], (((1,), (1,)), ((), ())), preferred_element_type=f32
+        )
+    return total
+
+
+def slope_kernel(prod, near_mixed, conv_far, query_far, rate, gain, held, *refs):
+    pieces, refs = (refs[0:PIECES], refs[PIECES : 2 * PIECES]), refs[2 * PIECES :]
+    query_slope, conv_slope, edge, states, conv, query, far_mixed, slope, prod_slope, sems = refs
     dp, ctx = lax.axis_index("dp"), lax.axis_index("ctx")
-    starts = bands(ctx)
-    places = []
-    for p in (2, 3):
-        for q in range(3):
-            places.append((p, starts[q], BAND))
-        for half in range(2):
-            places.append((p, starts[3] + half * (BAND // 2), BAND // 2))
-    places += [(0, 0, C), (1, 0, C)]
-    copies = [
-        pltpu.make_async_copy(
-            weight, held.at[p, pl.ds(pl.multiple_of(start, BAND // 2), size), :], sems.at[n]
-        )
-        for n, (weight, (p, start, size)) in enumerate(zip(weights, places))
+    late = [
+        pltpu.make_async_copy(conv_far, conv, sems.at[0]),
+        pltpu.make_async_copy(query_far.at[0:2], query, sems.at[1]),
     ]
-    late = [
-        pltpu.make_async_copy(near_far, near_mixed, sems.at[12]),
-        pltpu.make_async_copy(conv_far, conv, sems.at[13]),
-        pltpu.make_async_copy(query_far.at[0:2], query, sems.at[14]),
-    ]
-    copies += late
-    for copy in copies:
+    for copy in late:
         copy.start()
     high, core = dp // 2, dp % 2
     shard = (2 * high + core, 2 * high + 1 - core, 2 * (1 - high) + core, 2 * (1 - high) + 1 - core)
     shards, width = 4, WIDTH
     mixed = (near_mixed.at[0], near_mixed.at[1], far_mixed.at[0], far_mixed.at[1])
+    first, along_x, along_z, last = bands(ctx)
+    half = BAND // 2
+    begins = (first, along_x, along_x + half, along_z, along_z + half, last, last + half)
+
+    def rows_of(piece, at=0, count=None):
+        count = pieces[0][piece].shape[0] if count is None else count
+        return pl.ds(pl.multiple_of(begins[piece] + at, half), count)
+
     for p in range(2):
-        for copy in copies[5 * p : 5 * p + 5]:
-            copy.wait()
-        mix_shard(prod, held.at[2 + p], far_mixed.at[p])
-
-    for copy in late:
-        copy.wait()
+
+        def mix(t, carry):
+            columns = pl.ds(pl.multiple_of(t * BLOCK, BLOCK), BLOCK)
+            total = jnp.zeros((3 * ROWS, BLOCK), f32)
+            for n, piece in enumerate(pieces[p]):
+                total = total + jnp.dot(
+                    prod[:, rows_of(n)], piece[:, columns], preferred_element_type=f32
+                )
+            far_mixed[p, :, columns] = total
+            return carry
+
+        lax.fori_loop(0, width // BLOCK, mix, 0)
+
     squares = jnp.zeros((3 * ROWS, LANES), f32)
     for p in range(shards):
 
@@ -311,20 +318,15 @@
 
         lax.fori_loop(0, width // LANES, out_slopes, 0)
 
-    for copy in copies[10:12]:
+    for n in range(PIECES):
+        for at in range(0, pieces[0][n].shape[0], BLOCK):
+            rows = rows_of(n, at, BLOCK)
+            prod_slope[:, rows] = backward(
+                slope, [held.at[0, rows], held.at[1, rows]] + [pieces[p][n].at[at : at + BLOCK] for p in range(2)]
+            )
+
+    for copy in late:
         copy.wait()
-
-    def back(t, carry):
-        rows = pl.ds(pl.multiple_of(t * BLOCK, BLOCK), BLOCK)
-        total = jnp.zeros((2 * ROWS, BLOCK), f32)
-        for p in range(shards):
-            total = total + lax.dot_general(
-                slope[p], held[p, rows, :], (((1,), (1,)), ((), ())), preferred_element_type=f32
-            )
-        prod_slope[:, rows] = total
-        return carry
-
-    lax.fori_loop(0, C // BLOCK, back, 0)
 
     def state_tile(tile, carry):
         lanes = tile_lanes(tile)
@@ -464,6 +466,66 @@
     )(data, rate, res)
 
 
+def in_hbm(value):
+    return pltpu.with_memory_space_constraint(value, pltpu.HBM)
+
+
+def in_vmem(value):
+    return pltpu.with_memory_space_constraint(value, pltpu.VMEM)
+
+
+def mix_call(reaching, inner, query, rate, res, own_weight, core_weight):
+    near = pl.BlockSpec(memory_space=pltpu.VMEM)
+    return pl.pallas_call(
+        mix_kernel,
+        out_shape=(
+            pltpu.VMEM((3 * ROWS, C), bf16),
+            pltpu.HBM((2, ROWS, C), bf16),
+            pltpu.VMEM((2, 3 * ROWS, WIDTH), f32),
+            pltpu.VMEM((2, C, WIDTH), bf16),
+        ),
+        in_specs=[far()] * 3 + [pl.BlockSpec()] * 2 + [far()] * 2,
+        out_specs=(near, pl.BlockSpec(), near, near),
+        scratch_shapes=[
+            pltpu.VMEM((M, QUARTERS, 3, QUARTER, LANES), f32),
+            pltpu.VMEM((3, ROWS, C), f32),
+            pltpu.VMEM((3, ROWS, C), bf16),
+            pltpu.SemaphoreType.DMA((3 * QUARTERS + 2,)),
+        ],
+        compiler_params=params(8),
+        cost_estimate=pl.CostEstimate(
+            flops=5_000_000_000, bytes_accessed=14_000_000, transcendentals=0
+        ),
+    )(*map(in_hbm, (reaching, inner, query)), rate, res, *map(in_hbm, (own_weight, core_weight)))
+
+
+def slope_call(prod, near_mixed, conv, query, rate, gain, held, *pieces):
+    near = pl.BlockSpec(memory_space=pltpu.VMEM)
+    return pl.pallas_call(
+        slope_kernel,
+        out_shape=(
+            pltpu.HBM((2, ROWS, C), f32),
+            pltpu.HBM((2, ROWS, C), bf16),
+            array(2, 16, C, dtype=bf16),
+            array(M, QUARTERS, 2, QUARTER, LANES),
+        ),
+        in_specs=[near] * 2 + [far()] * 2 + [pl.BlockSpec()] * 2 + [near] * (1 + 2 * PIECES),
+        out_specs=(pl.BlockSpec(),) * 4,
+        scratch_shapes=[
+            pltpu.VMEM((2, ROWS, C), bf16),
+            pltpu.VMEM((2, ROWS, C), bf16),
+            pltpu.VMEM((2, 3 * ROWS, WIDTH), f32),
+            pltpu.VMEM((4, 2 * ROWS, WIDTH), bf16),
+            pltpu.VMEM((2 * ROWS, C), f32),
+            pltpu.SemaphoreType.DMA((2,)),
+        ],
+        compiler_params=params(10),
+    )(
+        in_vmem(prod), in_vmem(near_mixed), in_hbm(conv), in_hbm(query), rate, gain,
+        in_vmem(held), *map(in_vmem, pieces),
+    )
+
+
 def scan(ends, own_rate, reverse):
     return pl.pallas_call(
         functools.partial(scan_kernel, reverse),
@@ -534,7 +596,7 @@
         out_specs=(
             pl.BlockSpec((3, 2, 3 * C), lambda i: (0, 0, 0)),
             pl.BlockSpec((2, 2, 2 * C), lambda i: (0, 0, 0)),
-            far(),
+            pl.BlockSpec((BAND, WIDTH), lambda i: (0, 0)),
         ),
         scratch_shapes=[pltpu.SemaphoreType.DMA],
         compiler_params=params(60),
@@ -566,61 +628,29 @@
     ends = exchanged(ends)
     inner = within(gated, rate, res, False)
     inner, band = tied(inner, band)
-    band_x, band_z = swapped(band, "x"), swapped(band, "z")
+    half = BAND // 2
+    upper, lower = band[:half], band[half:]
+    upper_x, lower_x = swapped(upper, "x"), swapped(lower, "x")
+    upper_z, lower_z = swapped(upper, "z"), swapped(lower, "z")
     ends, inner = tied(ends, inner)
     reaching = exchanged(scan(ends, own_rate, False)).reshape(*state_shape, 3, QUARTER, LANES)
-    reaching, band_x, band_z = tied(reaching, band_x, band_z)
-    half = BAND // 2
-    last_x, last_z = swapped(band_z[:half], "x"), swapped(band_x[half:], "z")
-    near = [band, band_x, band_z]
+    reaching, upper_x, lower_x, upper_z, lower_z = tied(
+        reaching, upper_x, lower_x, upper_z, lower_z
+    )
+    last_x, last_z = swapped(upper_z, "x"), swapped(lower_x, "z")
+    near = [band, upper_x, lower_x, upper_z, lower_z]
     near_core = [swapped(piece, "core") for piece in near]
 
-    prod, conv, near_mixed = pl.pallas_call(
-        mix_kernel,
-        out_shape=(
-            array(3 * ROWS, C, dtype=bf16),
-            array(2, ROWS, C, dtype=bf16),
-            array(2, 3 * ROWS, WIDTH),
-        ),
-        in_specs=[far()] * 3 + [pl.BlockSpec()] * 2 + [far()] * 2,
-        scratch_shapes=[
-            pltpu.VMEM((M, QUARTERS, 3, QUARTER, LANES), f32),
-            pltpu.VMEM((3, ROWS, C), f32),
-            pltpu.VMEM((3, ROWS, C), bf16),
-            pltpu.VMEM((2, C, WIDTH), bf16),
-            pltpu.SemaphoreType.DMA((3 * QUARTERS + 2,)),
-        ],
-        compiler_params=params(60),
-        cost_estimate=pl.CostEstimate(
-            flops=5_000_000_000, bytes_accessed=14_000_000, transcendentals=0
-        ),
-    )(reaching, inner, query, rate, res, out_weight, core_weight)
+    prod, conv, near_mixed, held = mix_call(
+        reaching, inner, query, rate, res, out_weight, core_weight
+    )
 
     prod, last_x, last_z = tied(prod, last_x, last_z)
     last = [last_x, last_z]
     last_core = [swapped(piece, "core") for piece in last]
-    pieces = near + last + near_core + last_core + [out_weight, core_weight]
-    query_slope, conv_slope, edge, ends = pl.pallas_call(
-        slope_kernel,
-        out_shape=(
-            array(2, ROWS, C),
-            array(2, ROWS, C, dtype=bf16),
-            array(2, 16, C, dtype=bf16),
-            array(*state_shape, 2, QUARTER, LANES),
-        ),
-        in_specs=[pl.BlockSpec()] + [far()] * 3 + [pl.BlockSpec()] * 2 + [far()] * 12,
-        scratch_shapes=[
-            pltpu.VMEM((4, C, WIDTH), bf16),
-            pltpu.VMEM((2, 3 * ROWS, WIDTH), f32),
-            pltpu.VMEM((2, ROWS, C), bf16),
-            pltpu.VMEM((2, ROWS, C), bf16),
-            pltpu.VMEM((2, 3 * ROWS, WIDTH), f32),
-            pltpu.VMEM((4, 2 * ROWS, WIDTH), bf16),
-            pltpu.VMEM((2 * ROWS, C), f32),
-            pltpu.SemaphoreType.DMA((15,)),
-        ],
-        compiler_params=params(60),
-    )(prod, near_mixed, conv, query, rate, gain, *pieces)
+    query_slope, conv_slope, edge, ends = slope_call(
+        prod, near_mixed, conv, query, rate, gain, held, *near, *last, *near_core, *last_core
+    )
 
     next_edge = passed_along(edge, -1)
     ends = exchanged(ends)

time: 190 us -> 161 us (0.85)
  Pallas kernels: 91.6 us -> 55.3 us
  blocking collectives: 43.7 us -> 21.1 us
  waiting for transfers between devices: 17 us -> 34.1 us
  starting transfers between devices: 31.2 us -> 46.3 us
  local copies, waits for them, and re-layouts: 4.95 us -> 2.32 us
    pallas_call x1, Pallas kernels: 34.6 us -> 3.37 us  [per_device(): pl.pallas_call(edge_kernel, out_shape=(array(3, 2, 3 * C, dtype=bf16), ar...]
    all_to_all x2 -> x1, blocking collectives: 43.7 us -> 21.1 us  [exchanged(): return lax.all_to_all(flat, 'ctx', split_axis=0, concat_axis=0, tiled=True)]
    ppermute x11 -> x15, waiting for transfers between devices: 6.72 us -> 23.6 us  [swapped(): lax.ppermute(value, ('dp', 'ctx'), [(device, partner(device, kind)) for d...]
    all_to_all x2 -> x3, starting transfers between devices: 13.9 us -> 22.1 us  [exchanged(): return lax.all_to_all(flat, 'ctx', split_axis=0, concat_axis=0, tiled=True)]
    ppermute x11 -> x15, starting transfers between devices: 4.43 us -> 11.4 us  [swapped(): lax.ppermute(value, ('dp', 'ctx'), [(device, partner(device, kind)) for d...]
    pallas_call x2, Pallas kernels: 29.8 us -> 24 us  [the longest x1 16.5 us: slope_call(): pl.pallas_call(slope_kernel, out_shape=(pltpu.HBM((2, ROWS, C), f32), plt...]
  transfers between devices with their start and end apart: 16 -> 21, of which waited for: 5 -> 8; matrix products, arithmetic and copies ran while one was open for 1% -> 1% of each run, Pallas kernels for 15% -> 18%
where the time goes in v4:
time: 161 us; the launch traced here: 160 us
  Pallas kernels  55.3 us (34%)
  starting transfers between devices  46.3 us (29%)
  waiting for transfers between devices  34.1 us (21%)
  blocking collectives  21.1 us (13%)
  local copies, waits for them, and re-layouts  2.32 us (1%)
    ppermute x15, waiting for transfers between devices, swapped(): lax.ppermute(value, ('dp', 'ctx'), [(device, partner(device, kind)) for d...  23.6 us
    all_to_all x3, starting transfers between devices, exchanged(): return lax.all_to_all(flat, 'ctx', split_axis=0, concat_axis=0, tiled=True)  22.1 us
    all_to_all x1, blocking collectives, exchanged(): return lax.all_to_all(flat, 'ctx', split_axis=0, concat_axis=0, tiled=True)  21.1 us
    pallas_call x1, Pallas kernels, slope_call(): pl.pallas_call(slope_kernel, out_shape=(pltpu.HBM((2, ROWS, C), f32), plt...  16.5 us
    pallas_call x2, Pallas kernels, within(): pl.pallas_call(functools.partial(within_kernel, streams, reverse), out_sh...  13.4 us
    ppermute x3, starting transfers between devices, passed_along(): lax.ppermute(value, 'ctx', [(source, source + steps) for source in range(...  12.8 us
    ppermute x15, starting transfers between devices, swapped(): lax.ppermute(value, ('dp', 'ctx'), [(device, partner(device, kind)) for d...  11.4 us
    ppermute x3, waiting for transfers between devices, passed_along(): lax.ppermute(value, 'ctx', [(source, source + steps) for source in range(...  9.27 us
  transfers between devices with their start and end apart: 21, of which 8 were waited for; matrix products, arithmetic and copies ran while one was open for 1% of the time, Pallas kernels for 18%

profile of v4, /device:TPU:24, one launch (start us, length us, event | category | flops | bytes accessed | tf_op | source)
XLA Modules:
  0.0 160.1 jit_solution(2047365997939231836)
XLA Ops:
  0.6 3.4 %shard_map.95 = (bf16[3,2,6144]{2,1,0:T(2,128)(2,1)}, bf16[2,2,4096]{2,1,0:T(2,128)(2,1)}, bf16[512,1024]{1,0:T(8,128)(2,1)}) custom-call(bf16[64,6144]{1,0:T(8,128)(2,1)} %bitcast.27, bf16[64,6144]{1,0:T(8,128)(2,1)} %bitcast.34, bf16[64,6144]{1,0:T(8,128)(2,1)} %bitcast.41, bf16[64,6144]{1,0:T(8,128)(2,1)} %bitcast.28, bf16[64,6144]{1,0:T(8,128)(2,1)} %bitcast.35, ...), custom_call_target="tpu_custom_call" | custom-call | tf_op jit(solution)/shard_map/pallas_call | solution.py:587
  4.0 3.4 %collective-permute-start = (bf16[3,2,6144]{2,1,0:T(2,128)(2,1)}, bf16[3,2,6144]{2,1,0:T(2,128)(2,1)S(1)}, u32[]{:S(2)}, u32[]{:S(2)}) collective-permute-start(bf16[3,2,6144]{2,1,0:T(2,128)(2,1)} %get-tuple-element.33), channel_id=1, source_target_pairs={{0,1},{1,2},{2,3},{3,4},{4,5},{5,6},{6,7},{7,8},{8,9},{9,10},{10,1... | collective-permute-start | bytes 221192 | tf_op jit(solution)/shard_map/ppermute | solution.py:547
  7.4 9.3 %collective-permute-done.refs_9_.refs_10_.refs_11_.refs_8_ = bf16[3,2,6144]{2,1,0:T(2,128)(2,1)S(1)} collective-permute-done((bf16[3,2,6144]{2,1,0:T(2,128)(2,1)}, bf16[3,2,6144]{2,1,0:T(2,128)(2,1)S(1)}, u32[]{:S(2)}, u32[]{:S(2)}) %collective-permute-start) | collective-permute-done | bytes 73760 | tf_op jit(solution)/shard_map/ppermute | solution.py:547
  16.7 0.6 copy-done.3
  17.3 6.4 %shard_map.96 = (bf16[3,64,2048]{2,1,0:T(8,128)(2,1)}, bf16[3,64,2048]{2,1,0:T(8,128)(2,1)}, f32[16,4,3,4,128]{4,3,2,1,0:T(4,128)}) custom-call(bf16[64,6144]{1,0:T(8,128)(2,1)} %bitcast.29, bf16[64,6144]{1,0:T(8,128)(2,1)} %bitcast.30, bf16[64,6144]{1,0:T(8,128)(2,1)} %bitcast.31, bf16[64,6144]{1,0:T(8,128)(2,1)} %bitcast.36, bf16[64,6144]{1,0:T(8,128)(2,1)} %bitcast.37, ...), custom_call_target="tpu_custom_call" | custom-call | tf_op jit(solution)/shard_map/pallas_call | solution.py:609
  23.8 7.8 %all-to-all-start = ((f32[64,3,4,128]{3,2,1,0:T(4,128)}), f32[64,3,4,128]{3,2,1,0:T(4,128)S(1)}, u32[]{:S(2)}, u32[]{:S(2)}) async-start(f32[64,3,4,128]{3,2,1,0:T(4,128)} %bitcast.46), calls=%async_computation | async-start | bytes 786432 | tf_op jit(solution)/shard_map/all_to_all | solution.py:541
  31.6 7.6 %shard_map.97.inner_far = f32[3,64,2048]{2,1,0:T(8,128)} custom-call(bf16[3,64,2048]{2,1,0:T(8,128)(2,1)} %get-tuple-element.37.data, f32[16,2048]{1,0:T(8,128)} %bitcast.14, f32[16,2048]{1,0:T(8,128)} %bitcast.19), custom_call_target="tpu_custom_call" | custom-call | flops 300000000 | bytes 2359296 | tf_op jit(solution)/shard_map/pallas_call | solution.py:455
  39.2 4.5 %collective-permute-done.1.refs_0_ = bf16[512,1024]{1,0:T(8,128)(2,1)S(1)} collective-permute-done((bf16[512,1024]{1,0:T(8,128)(2,1)}, bf16[512,1024]{1,0:T(8,128)(2,1)S(1)}, u32[]{:S(2)}, u32[]{:S(2)}) %collective-permute-start.1) | collective-permute-done | bytes 1048608 | tf_op jit(solution)/shard_map/ppermute | solution.py:565
  43.7 0.9 fusion
  44.6 1.2 all-to-all-done.ends
  45.8 0.9 shard_map.98
  46.7 8.2 %all-to-all-start.1 = ((f32[64,3,4,128]{3,2,1,0:T(4,128)}), f32[64,3,4,128]{3,2,1,0:T(4,128)}, u32[]{:S(2)}, u32[]{:S(2)}) async-start(f32[64,3,4,128]{3,2,1,0:T(4,128)} %shard_map.98), calls=%async_computation.1 | async-start | bytes 786432 | tf_op jit(solution)/shard_map/all_to_all | solution.py:541
  54.9 1.6 collective-permute-start.3
  56.4 1.5 collective-permute-start.4
  58.5 1.7 %collective-permute-start.9 = (bf16[512,1024]{1,0:T(8,128)(2,1)S(1)}, bf16[512,1024]{1,0:T(8,128)(2,1)S(1)}, u32[]{:S(2)}, u32[]{:S(2)}) collective-permute-start(bf16[512,1024]{1,0:T(8,128)(2,1)S(1)} %collective-permute-done.1.refs_0_), channel_id=1, source_target_pairs={{0,64},{1,65},{2,66},{3,67},{4,68},{5,69},{6,70},{7,71},{8,72},{9,... | collective-permute-start | bytes 3145736 | tf_op jit(solution)/shard_map/ppermute | solution.py:565
  60.2 7.5 %collective-permute-done.3.refs_2_ = bf16[256,1024]{1,0:T(8,128)(2,1)} collective-permute-done((bf16[256,1024]{1,0:T(8,128)(2,1)S(1)}, bf16[256,1024]{1,0:T(8,128)(2,1)}, u32[]{:S(2)}, u32[]{:S(2)}) %collective-permute-start.3) | collective-permute-done | bytes 524320 | tf_op jit(solution)/shard_map/ppermute | solution.py:565
  67.6 3.5 %collective-permute-done.4.refs_3_ = bf16[256,1024]{1,0:T(8,128)(2,1)} collective-permute-done((bf16[256,1024]{1,0:T(8,128)(2,1)}, bf16[256,1024]{1,0:T(8,128)(2,1)}, u32[]{:S(2)}, u32[]{:S(2)}) %collective-permute-start.4) | collective-permute-done | bytes 524320 | tf_op jit(solution)/shard_map/ppermute | solution.py:565
  71.1 5.6 %collective-permute-done.5.refs_4_ = bf16[256,1024]{1,0:T(8,128)(2,1)} collective-permute-done((bf16[256,1024]{1,0:T(8,128)(2,1)S(1)}, bf16[256,1024]{1,0:T(8,128)(2,1)}, u32[]{:S(2)}, u32[]{:S(2)}) %collective-permute-start.5) | collective-permute-done | bytes 524320 | tf_op jit(solution)/shard_map/ppermute | solution.py:565
  76.8 1.5 collective-permute-start.7
  78.8 1.7 %collective-permute-start.10 = (bf16[256,1024]{1,0:T(8,128)(2,1)S(1)}, bf16[256,1024]{1,0:T(8,128)(2,1)S(1)}, u32[]{:S(2)}, u32[]{:S(2)}) collective-permute-start(bf16[256,1024]{1,0:T(8,128)(2,1)S(1)} %collective-permute-done.2.refs_1_), channel_id=1, source_target_pairs={{0,64},{1,65},{2,66},{3,67},{4,68},{5,69},{6,70},{7,71},{8,72},{9,... | collective-permute-start | bytes 1572872 | tf_op jit(solution)/shard_map/ppermute | solution.py:565
  80.5 7.4 %shard_map.99 = (bf16[192,2048]{1,0:T(8,128)(2,1)S(1)}, bf16[2,64,2048]{2,1,0:T(8,128)(2,1)}, f32[2,192,1024]{2,1,0:T(8,128)S(1)}, bf16[2,2048,1024]{2,1,0:T(8,128)(2,1)S(1)}) custom-call(f32[16,4,3,4,128]{4,3,2,1,0:T(4,128)} %bitcast.7.reaching_far, f32[3,64,2048]{2,1,0:T(8,128)} %shard_map.97.inner_far, bf16[3,64,2048]{2,1,0:T(8,128)(2,1)} %get-tuple-element.44.query_far, ...), custom_call_target="tpu_custom_call" | custom-call | flops 5000000000 | bytes 14000000 | tf_op jit(solution)/shard_map/pallas_call | solution.py:479
  88.5 1.3 collective-permute-start.13
  90.3 1.9 %collective-permute-done.13.refs_11_ = bf16[256,1024]{1,0:T(8,128)(2,1)S(1)} collective-permute-done((bf16[256,1024]{1,0:T(8,128)(2,1)}, bf16[256,1024]{1,0:T(8,128)(2,1)S(1)}, u32[]{:S(2)}, u32[]{:S(2)}) %collective-permute-start.13) | collective-permute-done | bytes 524320 | tf_op jit(solution)/shard_map/ppermute | solution.py:565
  92.2 0.6 collective-permute-done.15.refs_13_
  92.9 16.5 %shard_map.100 = (f32[2,64,2048]{2,1,0:T(8,128)}, bf16[2,64,2048]{2,1,0:T(8,128)(2,1)}, bf16[2,16,2048]{2,1,0:T(8,128)(2,1)S(1)}, f32[16,4,2,4,128]{4,3,2,1,0:T(4,128)S(1)}) custom-call(bf16[192,2048]{1,0:T(8,128)(2,1)S(1)} %get-tuple-element.49.prod, f32[2,192,1024]{2,1,0:T(8,128)S(1)} %get-tuple-element.50.near_mixed, ...), custom_call_target="tpu_custom_call" | custom-call | tf_op jit(solution)/shard_map/pallas_call | solution.py:504
  109.4 21.1 %all_to_all.20.ends = f32[64,2,4,128]{3,2,1,0:T(4,128)S(1)} all-to-all(f32[64,2,4,128]{3,2,1,0:T(4,128)S(1)} %bitcast.23), channel_id=1, replica_groups=mesh['dp'=4,'ctx'=64] {'ctx'}, dimensions={0} | all-to-all | bytes 524288 | tf_op jit(solution)/shard_map/all_to_all | solution.py:541
  130.5 0.8 shard_map.101
  131.4 6.1 %all-to-all-start.3 = ((f32[64,2,4,128]{3,2,1,0:T(4,128)}), f32[64,2,4,128]{3,2,1,0:T(4,128)S(1)}, u32[]{:S(2)}, u32[]{:S(2)}) async-start(f32[64,2,4,128]{3,2,1,0:T(4,128)} %shard_map.101), calls=%async_computation.3 | async-start | bytes 524288 | tf_op jit(solution)/shard_map/all_to_all | solution.py:541
  137.5 6.7 %collective-permute-start.16 = (bf16[2,16,2048]{2,1,0:T(8,128)(2,1)S(1)}, bf16[2,16,2048]{2,1,0:T(8,128)(2,1)S(1)}, u32[]{:S(2)}, u32[]{:S(2)}) collective-permute-start(bf16[2,16,2048]{2,1,0:T(8,128)(2,1)S(1)} %get-tuple-element.60), channel_id=1, source_target_pairs={{1,0},{2,1},{3,2},{4,3},{5,4},{6,5},{7,6},{8,7},{9,8},{10,9},{11,1... | collective-permute-start | bytes 393224 | tf_op jit(solution)/shard_map/ppermute | solution.py:547
  144.2 2.8 %collective-permute-start.17 = (bf16[2,2,4096]{2,1,0:T(2,128)(2,1)S(1)}, bf16[2,2,4096]{2,1,0:T(2,128)(2,1)S(1)}, u32[]{:S(2)}, u32[]{:S(2)}) collective-permute-start(bf16[2,2,4096]{2,1,0:T(2,128)(2,1)S(1)} %copy-done.7), channel_id=1, source_target_pairs={{1,0},{2,1},{3,2},{4,3},{5,4},{6,5},{7,6},{8,7},{9,8},{10,9},{11,1... | collective-permute-start | bytes 98312 | tf_op jit(solution)/shard_map/ppermute | solution.py:547
  147.0 5.8 %shard_map.102.refs_1_ = f32[2,64,2048]{2,1,0:T(8,128)} custom-call(bf16[2,64,2048]{2,1,0:T(8,128)(2,1)} %get-tuple-element.58.data, f32[16,2048]{1,0:T(8,128)} %bitcast.15, f32[16,2048]{1,0:T(8,128)} %bitcast.20), custom_call_target="tpu_custom_call" | custom-call | flops 200000000 | bytes 1572864 | tf_op jit(solution)/shard_map/pallas_call | solution.py:455
  153.6 6.3 %shard_map.103 = (bf16[64,6144]{1,0:T(8,128)(2,1)}, bf16[64,6144]{1,0:T(8,128)(2,1)}) custom-call(f32[16,4,2,4,128]{4,3,2,1,0:T(4,128)} %bitcast.45, f32[2,64,2048]{2,1,0:T(8,128)} %shard_map.102.refs_1_, f32[2,64,2048]{2,1,0:T(8,128)} %get-tuple-element.59.refs_2_, bf16[2,16,2048]{2,1,0:T(8,128)(2,1)} %copy-done.6, bf16[64,6144]{1,0:T(8,128)(2,1)} %bitcast.32, ...), custom_call_target="tpu_custom_call" | custom-call | tf_op jit(solution)/shard_map/pallas_call | solution.py:661
  (38 shorter events, 3.1 us)
Async XLA Ops:
  4.0 12.7 %collective-permute-start = (bf16[3,2,6144]{2,1,0:T(2,128)(2,1)}, bf16[3,2,6144]{2,1,0:T(2,128)(2,1)S(1)}, u32[]{:S(2)}, u32[]{:S(2)}) collective-permute-start(bf16[3,2,6144]{2,1,0:T(2,128)(2,1)} %get-tuple-element.33), channel_id=1, source_target_pairs={{0,1},{1,2},{2,3},{3,4},{4,5},{5,6},{6,7},{7,8},{8,9},{9,10},{10,1... | collective-permute-start | bytes 221192 | tf_op jit(solution)/shard_map/ppermute | solution.py:547
  16.7 0.6 copy-start.3
  16.7 63.8 %collective-permute-start.6 = (bf16[2048,1024]{1,0:T(8,128)(2,1)}, bf16[2048,1024]{1,0:T(8,128)(2,1)}, u32[]{:S(2)}, u32[]{:S(2)}) collective-permute-start(bf16[2048,1024]{1,0:T(8,128)(2,1)} %own_weight.1), channel_id=1, source_target_pairs={{0,64},{1,65},{2,66},{3,67},{4,68},{5,69},{6,70},{7,71},{8,72},{9,... | collective-permute-start | bytes 12582920 | tf_op jit(solution)/shard_map/ppermute | solution.py:565
  16.7 27.0 %collective-permute-start.1 = (bf16[512,1024]{1,0:T(8,128)(2,1)}, bf16[512,1024]{1,0:T(8,128)(2,1)S(1)}, u32[]{:S(2)}, u32[]{:S(2)}) collective-permute-start(bf16[512,1024]{1,0:T(8,128)(2,1)} %get-tuple-element.38), channel_id=1, source_target_pairs={{0,160},{1,161},{2,162},{3,163},{4,164},{5,165},{6,166},{7,167},{8... | collective-permute-start | bytes 3145736 | tf_op jit(solution)/shard_map/ppermute | solution.py:565
  23.7 20.8 %copy-start = (f32[2048,16]{0,1:T(8,128)S(1)}, f32[2048,16]{0,1:T(8,128)}, u32[]{:S(2)}) copy-start(f32[2048,16]{0,1:T(8,128)} %param.13) | copy-start | bytes 393220
  23.7 56.7 %copy-start.1 = (f32[2048,16]{0,1:T(8,128)S(1)}, f32[2048,16]{0,1:T(8,128)}, u32[]{:S(2)}) copy-start(f32[2048,16]{0,1:T(8,128)} %param.12) | copy-start | bytes 393220
  23.8 22.0 %all-to-all-start = ((f32[64,3,4,128]{3,2,1,0:T(4,128)}), f32[64,3,4,128]{3,2,1,0:T(4,128)S(1)}, u32[]{:S(2)}, u32[]{:S(2)}) async-start(f32[64,3,4,128]{3,2,1,0:T(4,128)} %bitcast.46), calls=%async_computation | async-start | bytes 786432 | tf_op jit(solution)/shard_map/all_to_all | solution.py:541
  44.5 13.9 %collective-permute-start.2 = (bf16[256,1024]{1,0:T(8,128)(2,1)}, bf16[256,1024]{1,0:T(8,128)(2,1)S(1)}, u32[]{:S(2)}, u32[]{:S(2)}) collective-permute-start(bf16[256,1024]{1,0:T(8,128)(2,1)} %get-tuple-element.65), channel_id=1, source_target_pairs={{0,1},{1,0},{2,3},{3,2},{4,5},{5,4},{6,7},{7,6},{8,9},{9,8},{10,11... | collective-permute-start | bytes 1572872 | tf_op jit(solution)/shard_map/ppermute | solution.py:565
  46.7 30.0 %all-to-all-start.1 = ((f32[64,3,4,128]{3,2,1,0:T(4,128)}), f32[64,3,4,128]{3,2,1,0:T(4,128)}, u32[]{:S(2)}, u32[]{:S(2)}) async-start(f32[64,3,4,128]{3,2,1,0:T(4,128)} %shard_map.98), calls=%async_computation.1 | async-start | bytes 786432 | tf_op jit(solution)/shard_map/all_to_all | solution.py:541
  54.9 12.7 %collective-permute-start.3 = (bf16[256,1024]{1,0:T(8,128)(2,1)S(1)}, bf16[256,1024]{1,0:T(8,128)(2,1)}, u32[]{:S(2)}, u32[]{:S(2)}) collective-permute-start(bf16[256,1024]{1,0:T(8,128)(2,1)S(1)} %get-tuple-element.64), channel_id=1, source_target_pairs={{0,1},{1,0},{2,3},{3,2},{4,5},{5,4},{6,7},{7,6},{8,9},{9,8},{10,11... | collective-permute-start | bytes 1572872 | tf_op jit(solution)/shard_map/ppermute | solution.py:565
  56.4 14.7 %collective-permute-start.4 = (bf16[256,1024]{1,0:T(8,128)(2,1)}, bf16[256,1024]{1,0:T(8,128)(2,1)}, u32[]{:S(2)}, u32[]{:S(2)}) collective-permute-start(bf16[256,1024]{1,0:T(8,128)(2,1)} %get-tuple-element.65), channel_id=1, source_target_pairs={{0,4},{1,5},{2,6},{3,7},{4,0},{5,1},{6,2},{7,3},{8,12},{9,13},{10,... | collective-permute-start | bytes 1572872 | tf_op jit(solution)/shard_map/ppermute | solution.py:565
  57.9 18.8 %collective-permute-start.5 = (bf16[256,1024]{1,0:T(8,128)(2,1)S(1)}, bf16[256,1024]{1,0:T(8,128)(2,1)}, u32[]{:S(2)}, u32[]{:S(2)}) collective-permute-start(bf16[256,1024]{1,0:T(8,128)(2,1)S(1)} %get-tuple-element.64), channel_id=1, source_target_pairs={{0,4},{1,5},{2,6},{3,7},{4,0},{5,1},{6,2},{7,3},{8,12},{9,13},{10,... | collective-permute-start | bytes 1572872 | tf_op jit(solution)/shard_map/ppermute | solution.py:565
  58.5 31.3 %collective-permute-start.9 = (bf16[512,1024]{1,0:T(8,128)(2,1)S(1)}, bf16[512,1024]{1,0:T(8,128)(2,1)S(1)}, u32[]{:S(2)}, u32[]{:S(2)}) collective-permute-start(bf16[512,1024]{1,0:T(8,128)(2,1)S(1)} %collective-permute-done.1.refs_0_), channel_id=1, source_target_pairs={{0,64},{1,65},{2,66},{3,67},{4,68},{5,69},{6,70},{7,71},{8,72},{9,... | collective-permute-start | bytes 3145736 | tf_op jit(solution)/shard_map/ppermute | solution.py:565
  76.8 11.2 %collective-permute-start.7 = (bf16[256,1024]{1,0:T(8,128)(2,1)}, bf16[256,1024]{1,0:T(8,128)(2,1)S(1)}, u32[]{:S(2)}, u32[]{:S(2)}) collective-permute-start(bf16[256,1024]{1,0:T(8,128)(2,1)} %collective-permute-done.4.refs_3_), channel_id=1, source_target_pairs={{0,1},{1,0},{2,3},{3,2},{4,5},{5,4},{6,7},{7,6},{8,9},{9,8},{10,11... | collective-permute-start | bytes 1572872 | tf_op jit(solution)/shard_map/ppermute | solution.py:565
  78.2 10.3 %collective-permute-start.8 = (bf16[256,1024]{1,0:T(8,128)(2,1)}, bf16[256,1024]{1,0:T(8,128)(2,1)S(1)}, u32[]{:S(2)}, u32[]{:S(2)}) collective-permute-start(bf16[256,1024]{1,0:T(8,128)(2,1)} %collective-permute-done.3.refs_2_), channel_id=1, source_target_pairs={{0,4},{1,5},{2,6},{3,7},{4,0},{5,1},{6,2},{7,3},{8,12},{9,13},{10,... | collective-permute-start | bytes 1572872 | tf_op jit(solution)/shard_map/ppermute | solution.py:565
  78.8 11.1 %collective-permute-start.10 = (bf16[256,1024]{1,0:T(8,128)(2,1)S(1)}, bf16[256,1024]{1,0:T(8,128)(2,1)S(1)}, u32[]{:S(2)}, u32[]{:S(2)}) collective-permute-start(bf16[256,1024]{1,0:T(8,128)(2,1)S(1)} %collective-permute-done.2.refs_1_), channel_id=1, source_target_pairs={{0,64},{1,65},{2,66},{3,67},{4,68},{5,69},{6,70},{7,71},{8,72},{9,... | collective-permute-start | bytes 1572872 | tf_op jit(solution)/shard_map/ppermute | solution.py:565
  80.5 9.9 %collective-permute-start.11 = (bf16[256,1024]{1,0:T(8,128)(2,1)}, bf16[256,1024]{1,0:T(8,128)(2,1)S(1)}, u32[]{:S(2)}, u32[]{:S(2)}) collective-permute-start(bf16[256,1024]{1,0:T(8,128)(2,1)} %collective-permute-done.3.refs_2_), channel_id=1, source_target_pairs={{0,64},{1,65},{2,66},{3,67},{4,68},{5,69},{6,70},{7,71},{8,72},{9,... | collective-permute-start | bytes 1572872 | tf_op jit(solution)/shard_map/ppermute | solution.py:565
  80.5 12.4 %copy-start.2 = (f32[4096]{0:T(1024)S(1)}, f32[4096]{0:T(1024)}, u32[]{:S(2)}) copy-start(f32[4096]{0:T(1024)} %param.15) | copy-start | bytes 49156
  87.9 2.4 %collective-permute-start.12 = (bf16[256,1024]{1,0:T(8,128)(2,1)}, bf16[256,1024]{1,0:T(8,128)(2,1)S(1)}, u32[]{:S(2)}, u32[]{:S(2)}) collective-permute-start(bf16[256,1024]{1,0:T(8,128)(2,1)} %collective-permute-done.4.refs_3_), channel_id=1, source_target_pairs={{0,64},{1,65},{2,66},{3,67},{4,68},{5,69},{6,70},{7,71},{8,72},{9,... | collective-permute-start | bytes 1572872 | tf_op jit(solution)/shard_map/ppermute | solution.py:565
  88.5 3.7 %collective-permute-start.13 = (bf16[256,1024]{1,0:T(8,128)(2,1)}, bf16[256,1024]{1,0:T(8,128)(2,1)S(1)}, u32[]{:S(2)}, u32[]{:S(2)}) collective-permute-start(bf16[256,1024]{1,0:T(8,128)(2,1)} %collective-permute-done.5.refs_4_), channel_id=1, source_target_pairs={{0,64},{1,65},{2,66},{3,67},{4,68},{5,69},{6,70},{7,71},{8,72},{9,... | collective-permute-start | bytes 1572872 | tf_op jit(solution)/shard_map/ppermute | solution.py:565
  89.8 2.4 %collective-permute-start.14 = (bf16[256,1024]{1,0:T(8,128)(2,1)S(1)}, bf16[256,1024]{1,0:T(8,128)(2,1)S(1)}, u32[]{:S(2)}, u32[]{:S(2)}) collective-permute-start(bf16[256,1024]{1,0:T(8,128)(2,1)S(1)} %collective-permute-done.7.refs_5_), channel_id=1, source_target_pairs={{0,64},{1,65},{2,66},{3,67},{4,68},{5,69},{6,70},{7,71},{8,72},{9,... | collective-permute-start | bytes 1572872 | tf_op jit(solution)/shard_map/ppermute | solution.py:565
  89.8 3.0 %collective-permute-start.15 = (bf16[256,1024]{1,0:T(8,128)(2,1)S(1)}, bf16[256,1024]{1,0:T(8,128)(2,1)S(1)}, u32[]{:S(2)}, u32[]{:S(2)}) collective-permute-start(bf16[256,1024]{1,0:T(8,128)(2,1)S(1)} %collective-permute-done.8.refs_6_), channel_id=1, source_target_pairs={{0,64},{1,65},{2,66},{3,67},{4,68},{5,69},{6,70},{7,71},{8,72},{9,... | collective-permute-start | bytes 1572872 | tf_op jit(solution)/shard_map/ppermute | solution.py:565
  92.9 51.3 %copy-start.7 = (bf16[2,2,4096]{2,1,0:T(2,128)(2,1)S(1)}, bf16[2,2,4096]{2,1,0:T(2,128)(2,1)}, u32[]{:S(2)}) copy-start(bf16[2,2,4096]{2,1,0:T(2,128)(2,1)} %get-tuple-element.61) | copy-start | bytes 98308
  131.4 21.4 %all-to-all-start.3 = ((f32[64,2,4,128]{3,2,1,0:T(4,128)}), f32[64,2,4,128]{3,2,1,0:T(4,128)S(1)}, u32[]{:S(2)}, u32[]{:S(2)}) async-start(f32[64,2,4,128]{3,2,1,0:T(4,128)} %shard_map.101), calls=%async_computation.3 | async-start | bytes 524288 | tf_op jit(solution)/shard_map/all_to_all | solution.py:541
  137.5 15.3 %collective-permute-start.16 = (bf16[2,16,2048]{2,1,0:T(8,128)(2,1)S(1)}, bf16[2,16,2048]{2,1,0:T(8,128)(2,1)S(1)}, u32[]{:S(2)}, u32[]{:S(2)}) collective-permute-start(bf16[2,16,2048]{2,1,0:T(8,128)(2,1)S(1)} %get-tuple-element.60), channel_id=1, source_target_pairs={{1,0},{2,1},{3,2},{4,3},{5,4},{6,5},{7,6},{8,7},{9,8},{10,9},{11,1... | collective-permute-start | bytes 393224 | tf_op jit(solution)/shard_map/ppermute | solution.py:547
  144.2 8.6 %collective-permute-start.17 = (bf16[2,2,4096]{2,1,0:T(2,128)(2,1)S(1)}, bf16[2,2,4096]{2,1,0:T(2,128)(2,1)S(1)}, u32[]{:S(2)}, u32[]{:S(2)}) collective-permute-start(bf16[2,2,4096]{2,1,0:T(2,128)(2,1)S(1)} %copy-done.7), channel_id=1, source_target_pairs={{1,0},{2,1},{3,2},{4,3},{5,4},{6,5},{7,6},{8,7},{9,8},{10,9},{11,1... | collective-permute-start | bytes 98312 | tf_op jit(solution)/shard_map/ppermute | solution.py:547
  152.8 0.6 copy-start.5
  152.8 0.7 copy-start.6
  152.8 0.8 copy-start.4

commit v5 on v4

--- a/solution.py
+++ b/solution.py
@@ -20,8 +20,8 @@
 TILES = C // LANES
 WIDTH = D // 4
 BAND = C // 4
-BLOCK = 256
-PIECES = 7
+BLOCK = 512
+PIECES = 8
 QUARTERS = 4
 QUARTER = TILES // QUARTERS
 
@@ -47,15 +47,27 @@
 
 
 def edge_kernel(*refs):
-    features, (weight, last_rows, first_rows, band, sem) = refs[:5], refs[5:]
-    start = pl.multiple_of(bands(lax.axis_index("ctx"))[0], BAND)
-    copy = pltpu.make_async_copy(weight.at[pl.ds(start, BAND), :], band, sem)
-    copy.start()
+    features, (last_rows, first_rows) = refs[:5], refs[5:]
     for s in range(3):
         last_rows[s] = features[s][6:8, :]
     for s in range(2):
         first_rows[s] = features[3 + s][0:2, C:]
-    copy.wait()
+
+
+def band_kernel(weight, band, sems):
+    start = bands(lax.axis_index("ctx"))[0]
+    copies = [
+        pltpu.make_async_copy(
+            weight.at[pl.ds(pl.multiple_of(start + n * (BAND // 2), BAND // 2), BAND // 2), :],
+            band.at[n],
+            sems.at[n],
+        )
+        for n in range(2)
+    ]
+    for copy in copies:
+        copy.start()
+    for copy in copies:
+        copy.wait()
 
 
 def bands(ctx):
@@ -166,20 +178,19 @@
 
 
 def mix_kernel(
-    reaching_far, inner_far, query_far, rate, res, own_weight, core_weight,
+    reaching, inner_far, query_far, rate, res, own_weight, core_weight,
     prod, conv, mixed, held,
-    reaching, inner, query, sems,
+    inner, query, sems,
 ):
     copies = []
     for q in range(QUARTERS):
         lanes = pl.ds(q * QUARTER * LANES, QUARTER * LANES)
         copies += [
-            pltpu.make_async_copy(reaching_far.at[:, q], reaching.at[:, q], sems.at[3 * q]),
-            pltpu.make_async_copy(inner_far.at[:, :, lanes], inner.at[:, :, lanes], sems.at[3 * q + 1]),
-            pltpu.make_async_copy(query_far.at[:, :, lanes], query.at[:, :, lanes], sems.at[3 * q + 2]),
+            pltpu.make_async_copy(inner_far.at[:, :, lanes], inner.at[:, :, lanes], sems.at[2 * q]),
+            pltpu.make_async_copy(query_far.at[:, :, lanes], query.at[:, :, lanes], sems.at[2 * q + 1]),
         ]
     for p, weight in enumerate((own_weight, core_weight)):
-        copies.append(pltpu.make_async_copy(weight, held.at[p], sems.at[3 * QUARTERS + p]))
+        copies.append(pltpu.make_async_copy(weight, held.at[p], sems.at[2 * QUARTERS + p]))
     for copy in copies:
         copy.start()
 
@@ -208,12 +219,12 @@
         return carry
 
     for q in range(QUARTERS):
-        for copy in copies[3 * q : 3 * q + 3]:
+        for copy in copies[2 * q : 2 * q + 2]:
             copy.wait()
         lax.fori_loop(QUARTER * q, QUARTER * q + QUARTER, conv_tile, 0)
 
     for p in range(2):
-        copies[3 * QUARTERS + p].wait()
+        copies[2 * QUARTERS + p].wait()
         mix_shard(prod, held.at[p], mixed.at[p])
 
 
@@ -226,13 +237,13 @@
     lax.fori_loop(0, WIDTH // BLOCK, mix, 0)
 
 
-def backward(slope, weights):
-    total = jnp.zeros((2 * ROWS, BLOCK), f32)
+def backward(slope, first, weights):
+    total = 0.0
     for p, weight in enumerate(weights):
         total = total + lax.dot_general(
-            slope[p], weight[...], (((1,), (1,)), ((), ())), preferred_element_type=f32
+            weight[...], slope[first + p], (((1,), (1,)), ((), ())), preferred_element_type=f32
         )
-    return total
+    return total.T
 
 
 def slope_kernel(prod, near_mixed, conv_far, query_far, rate, gain, held, *refs):
@@ -251,11 +262,10 @@
     mixed = (near_mixed.at[0], near_mixed.at[1], far_mixed.at[0], far_mixed.at[1])
     first, along_x, along_z, last = bands(ctx)
     half = BAND // 2
-    begins = (first, along_x, along_x + half, along_z, along_z + half, last, last + half)
-
-    def rows_of(piece, at=0, count=None):
-        count = pieces[0][piece].shape[0] if count is None else count
-        return pl.ds(pl.multiple_of(begins[piece] + at, half), count)
+    begins = [start + at for start in (first, along_x, along_z, last) for at in (0, half)]
+
+    def rows_of(piece):
+        return pl.ds(pl.multiple_of(begins[piece], half), half)
 
     for p in range(2):
 
@@ -318,12 +328,15 @@
 
         lax.fori_loop(0, width // LANES, out_slopes, 0)
 
+    def near_back(t, carry):
+        rows = pl.ds(pl.multiple_of(t * 2 * BLOCK, 2 * BLOCK), 2 * BLOCK)
+        prod_slope[:, rows] = backward(slope, 0, [held.at[0, rows], held.at[1, rows]])
+        return carry
+
+    lax.fori_loop(0, C // (2 * BLOCK), near_back, 0)
     for n in range(PIECES):
-        for at in range(0, pieces[0][n].shape[0], BLOCK):
-            rows = rows_of(n, at, BLOCK)
-            prod_slope[:, rows] = backward(
-                slope, [held.at[0, rows], held.at[1, rows]] + [pieces[p][n].at[at : at + BLOCK] for p in range(2)]
-            )
+        rows = rows_of(n)
+        prod_slope[:, rows] += backward(slope, 2, [pieces[0][n], pieces[1][n]])
 
     for copy in late:
         copy.wait()
@@ -450,20 +463,38 @@
     return jax.ShapeDtypeStruct(shape, dtype)
 
 
-def within(data, rate, res, reverse):
+def within(data, rate, res, reverse, start, count):
     streams = data.shape[0]
+    width = QUARTER * LANES
     return pl.pallas_call(
         functools.partial(within_kernel, streams, reverse),
-        out_shape=array(streams, ROWS, C),
-        grid=(QUARTERS,),
-        in_specs=[quarter(streams, ROWS), quarter(M), quarter(M)],
-        out_specs=quarter(streams, ROWS),
+        out_shape=array(streams, ROWS, count * width),
+        grid=(count,),
+        in_specs=[
+            pl.BlockSpec((streams, ROWS, width), lambda q: (0, 0, start + q)),
+            pl.BlockSpec((M, width), lambda q: (0, start + q)),
+            pl.BlockSpec((M, width), lambda q: (0, start + q)),
+        ],
+        out_specs=pl.BlockSpec((streams, ROWS, width), lambda q: (0, 0, q)),
         scratch_shapes=[pltpu.VMEM((streams, ROWS, LANES), f32), pltpu.VMEM((8 * M + 8, LANES), f32)],
         compiler_params=params(60),
         cost_estimate=pl.CostEstimate(
-            flops=streams * 100_000_000, bytes_accessed=streams * 6 * ROWS * C, transcendentals=0
+            flops=streams * count * 25_000_000,
+            bytes_accessed=streams * count * 6 * ROWS * width,
+            transcendentals=0,
         ),
     )(data, rate, res)
+
+
+def band_call(weight):
+    return pl.pallas_call(
+        band_kernel,
+        out_shape=pltpu.VMEM((2, BAND // 2, WIDTH), bf16),
+        in_specs=[far()],
+        out_specs=pl.BlockSpec(memory_space=pltpu.VMEM),
+        scratch_shapes=[pltpu.SemaphoreType.DMA((2,))],
+        compiler_params=params(4),
+    )(in_hbm(weight))
 
 
 def in_hbm(value):
@@ -484,19 +515,21 @@
             pltpu.VMEM((2, 3 * ROWS, WIDTH), f32),
             pltpu.VMEM((2, C, WIDTH), bf16),
         ),
-        in_specs=[far()] * 3 + [pl.BlockSpec()] * 2 + [far()] * 2,
+        in_specs=[near] + [far()] * 2 + [pl.BlockSpec()] * 2 + [far()] * 2,
         out_specs=(near, pl.BlockSpec(), near, near),
         scratch_shapes=[
-            pltpu.VMEM((M, QUARTERS, 3, QUARTER, LANES), f32),
             pltpu.VMEM((3, ROWS, C), f32),
             pltpu.VMEM((3, ROWS, C), bf16),
-            pltpu.SemaphoreType.DMA((3 * QUARTERS + 2,)),
+            pltpu.SemaphoreType.DMA((2 * QUARTERS + 2,)),
         ],
         compiler_params=params(8),
         cost_estimate=pl.CostEstimate(
             flops=5_000_000_000, bytes_accessed=14_000_000, transcendentals=0
         ),
-    )(*map(in_hbm, (reaching, inner, query)), rate, res, *map(in_hbm, (own_weight, core_weight)))
+    )(
+        in_vmem(reaching), *map(in_hbm, (inner, query)), rate, res,
+        *map(in_hbm, (own_weight, core_weight)),
+    )
 
 
 def slope_call(prod, near_mixed, conv, query, rate, gain, held, *pieces):
@@ -584,34 +617,30 @@
     state_shape = (M, QUARTERS)
 
     eight = [pl.BlockSpec((8, 3 * C), lambda i: (7, 0))] * 3 + [pl.BlockSpec((8, 3 * C), lambda i: (0, 0))] * 2
-    last_rows, first_rows, band = pl.pallas_call(
+    last_rows, first_rows = pl.pallas_call(
         edge_kernel,
-        out_shape=(
-            array(3, 2, 3 * C, dtype=bf16),
-            array(2, 2, 2 * C, dtype=bf16),
-            array(BAND, WIDTH, dtype=bf16),
-        ),
+        out_shape=(pltpu.VMEM((3, 2, 3 * C), bf16), pltpu.HBM((2, 2, 2 * C), bf16)),
         grid=(1,),
-        in_specs=eight + [far()],
+        in_specs=eight,
         out_specs=(
             pl.BlockSpec((3, 2, 3 * C), lambda i: (0, 0, 0)),
             pl.BlockSpec((2, 2, 2 * C), lambda i: (0, 0, 0)),
-            pl.BlockSpec((BAND, WIDTH), lambda i: (0, 0)),
         ),
-        scratch_shapes=[pltpu.SemaphoreType.DMA],
-        compiler_params=params(60),
-    )(clean, pert, teacher, clean, pert, out_weight)
+        compiler_params=params(4),
+    )(*map(in_hbm, (clean, pert, teacher, clean, pert)))
     halo = passed_along(last_rows, 1)
-    halo, to_core, band = tied(halo, out_weight, band)
+    _, to_band = tied(last_rows, out_weight)
+    band = band_call(to_band)
+    halo, band, to_core = tied(halo, band, out_weight)
+    band = swapped(band, "y")
     core_weight = swapped(to_core, "core")
-    band = swapped(band, "y")
 
     query, gated, ends = pl.pallas_call(
         gate_kernel,
         out_shape=(
-            array(3, ROWS, C, dtype=bf16),
-            array(3, ROWS, C, dtype=bf16),
-            array(*state_shape, 3, QUARTER, LANES),
+            pltpu.HBM((3, ROWS, C), bf16),
+            pltpu.HBM((3, ROWS, C), bf16),
+            pltpu.HBM((*state_shape, 3, QUARTER, LANES), f32),
         ),
         grid=(QUARTERS,),
         in_specs=[quarter(ROWS, branch=b) for _ in range(3) for b in range(3)]
@@ -620,44 +649,39 @@
         + [quarter(M)],
         out_specs=(quarter(3, ROWS), quarter(3, ROWS), quarter_states(3)),
         scratch_shapes=[pltpu.VMEM((9, 8 + ROWS, LANES), f32)],
-        compiler_params=params(60),
+        compiler_params=params(16),
     )(
-        *(clean,) * 3, *(pert,) * 3, *(teacher,) * 3, *(halo,) * 3, *(short_taps,) * 3, rate
+        *map(in_hbm, (clean,) * 3 + (pert,) * 3 + (teacher,) * 3), *(halo,) * 3,
+        *map(in_hbm, (short_taps,) * 3 + (rate,)),
     )
 
     ends = exchanged(ends)
-    inner = within(gated, rate, res, False)
+    inner = within(gated, rate, res, False, 0, QUARTERS)
     inner, band = tied(inner, band)
-    half = BAND // 2
-    upper, lower = band[:half], band[half:]
-    upper_x, lower_x = swapped(upper, "x"), swapped(lower, "x")
-    upper_z, lower_z = swapped(upper, "z"), swapped(lower, "z")
-    ends, inner = tied(ends, inner)
+    upper, lower = band[0], band[1]
+    upper_x, upper_z = swapped(upper, "x"), swapped(upper, "z")
+    lower_x, lower_z = swapped(lower, "x"), swapped(lower, "z")
+    ends, inner, lower_x, upper_z = tied(ends, inner, lower_x, upper_z)
     reaching = exchanged(scan(ends, own_rate, False)).reshape(*state_shape, 3, QUARTER, LANES)
-    reaching, upper_x, lower_x, upper_z, lower_z = tied(
-        reaching, upper_x, lower_x, upper_z, lower_z
-    )
     last_x, last_z = swapped(upper_z, "x"), swapped(lower_x, "z")
-    near = [band, upper_x, lower_x, upper_z, lower_z]
-    near_core = [swapped(piece, "core") for piece in near]
+    reaching, last_x, last_z = tied(reaching, last_x, last_z)
+    far_pieces = [upper, lower, upper_x, lower_x, upper_z, lower_z, last_x, last_z]
+    core_pieces = [swapped(piece, "core") for piece in far_pieces]
 
     prod, conv, near_mixed, held = mix_call(
         reaching, inner, query, rate, res, out_weight, core_weight
     )
-
-    prod, last_x, last_z = tied(prod, last_x, last_z)
-    last = [last_x, last_z]
-    last_core = [swapped(piece, "core") for piece in last]
     query_slope, conv_slope, edge, ends = slope_call(
-        prod, near_mixed, conv, query, rate, gain, held, *near, *last, *near_core, *last_core
-    )
-
-    next_edge = passed_along(edge, -1)
+        prod, near_mixed, conv, query, rate, gain, held, *far_pieces, *core_pieces
+    )
+
     ends = exchanged(ends)
-    inner = within(conv_slope, rate, res, True)
+    first_rows, edge = tied(first_rows, edge)
+    next_edge, first_rows = passed_along(edge, -1), passed_along(first_rows, -1)
+    inner = within(conv_slope, rate, res, True, 0, QUARTERS)
+    ends, inner, next_edge, first_rows = tied(ends, inner, next_edge, first_rows)
     reaching = exchanged(scan(ends, own_rate, True)).reshape(*state_shape, 2, QUARTER, LANES)
 
-    first_rows = passed_along(first_rows, -1)
     grads = pl.pallas_call(
         final_kernel,
         out_shape=(array(ROWS, 3 * C, dtype=bf16), array(ROWS, 3 * C, dtype=bf16)),
@@ -675,10 +699,11 @@
             pltpu.VMEM((QUARTERS, 6, ROWS, QUARTER * LANES), bf16),
             pltpu.SemaphoreType.DMA((QUARTERS, 6)),
         ],
-        compiler_params=params(60),
+        compiler_params=params(16),
     )(
-        reaching, inner, query_slope, next_edge, *(clean,) * 2, *(pert,) * 2, *(halo,) * 2,
-        *(first_rows,) * 2, *(short_taps,) * 3, rate, res,
+        reaching, *map(in_hbm, (inner, query_slope)), next_edge,
+        *map(in_hbm, (clean,) * 2 + (pert,) * 2), *(halo,) * 2, *(first_rows,) * 2,
+        *map(in_hbm, (short_taps,) * 3 + (rate, res)),
     )
     return grads[0][None], grads[1][None]
 

time: 161 us -> 154 us (0.957)
  Pallas kernels: 55.3 us -> 51.5 us
  blocking collectives: 21.1 us -> 18.5 us
  local copies, waits for them, and re-layouts: 2.32 us -> 0.17 us
    all_to_all x3, waiting for transfers between devices: 1.16 us -> 13 us  [exchanged(): return lax.all_to_all(flat, 'ctx', split_axis=0, concat_axis=0, tiled=True)]
    ppermute x15 -> x16, waiting for transfers between devices: 23.6 us -> 12.2 us  [swapped(): lax.ppermute(value, ('dp', 'ctx'), [(device, partner(device, kind)) for d...]
    all_to_all x3, starting transfers between devices: 22.1 us -> 25.8 us  [exchanged(): return lax.all_to_all(flat, 'ctx', split_axis=0, concat_axis=0, tiled=True)]
    all_to_all x1, blocking collectives: 21.1 us -> 18.5 us  [exchanged(): return lax.all_to_all(flat, 'ctx', split_axis=0, concat_axis=0, tiled=True)]
    ppermute x15 -> x16, starting transfers between devices: 11.4 us -> 9.03 us  [swapped(): lax.ppermute(value, ('dp', 'ctx'), [(device, partner(device, kind)) for d...]
    pallas_call x2 -> x3, Pallas kernels: 9.79 us -> 9.27 us  [the longest x1 6.31 us: per_device(): pl.pallas_call(gate_kernel, out_shape=(pltpu.HBM((3, ROWS, C), bf16), plt...]
  transfers between devices with their start and end apart: 21 -> 22, of which waited for: 8 -> 6; matrix products, arithmetic and copies ran while one was open for 1% -> 0% of each run, Pallas kernels for 18% -> 18%
where the time goes in v5:
time: 154 us; the launch traced here: 152 us
  Pallas kernels  51.5 us (33%)
  starting transfers between devices  47.6 us (31%)
  waiting for transfers between devices  33 us (21%)
  blocking collectives  18.5 us (12%)
    all_to_all x3, starting transfers between devices, exchanged(): return lax.all_to_all(flat, 'ctx', split_axis=0, concat_axis=0, tiled=True)  25.8 us
    all_to_all x1, blocking collectives, exchanged(): return lax.all_to_all(flat, 'ctx', split_axis=0, concat_axis=0, tiled=True)  18.5 us
    pallas_call x1, Pallas kernels, slope_call(): pl.pallas_call(slope_kernel, out_shape=(pltpu.HBM((2, ROWS, C), f32), plt...  15.6 us
    pallas_call x2, Pallas kernels, within(): pl.pallas_call(functools.partial(within_kernel, streams, reverse), out_sh...  13.5 us
    all_to_all x3, waiting for transfers between devices, exchanged(): return lax.all_to_all(flat, 'ctx', split_axis=0, concat_axis=0, tiled=True)  13 us
    ppermute x3, starting transfers between devices, passed_along(): lax.ppermute(value, 'ctx', [(source, source + steps) for source in range(...  12.8 us
    ppermute x16, waiting for transfers between devices, swapped(): lax.ppermute(value, ('dp', 'ctx'), [(device, partner(device, kind)) for d...  12.2 us
    ppermute x16, starting transfers between devices, swapped(): lax.ppermute(value, ('dp', 'ctx'), [(device, partner(device, kind)) for d...  9.03 us
  transfers between devices with their start and end apart: 22, of which 6 were waited for; matrix products, arithmetic and copies ran while one was open for 0% of the time, Pallas kernels for 18%

profile of v5, /device:TPU:24, one launch (start us, length us, event | category | flops | bytes accessed | tf_op | source)
XLA Modules:
  0.0 151.8 jit_solution(8108549164401452409)
XLA Ops:
  0.6 1.7 %shard_map.95 = (bf16[3,2,6144]{2,1,0:T(2,128)(2,1)S(1)}, bf16[2,2,4096]{2,1,0:T(2,128)(2,1)}) custom-call(bf16[64,6144]{1,0:T(8,128)(2,1)} %bitcast.32, bf16[64,6144]{1,0:T(8,128)(2,1)} %bitcast.39, bf16[64,6144]{1,0:T(8,128)(2,1)} %bitcast.46, bf16[64,6144]{1,0:T(8,128)(2,1)} %bitcast.33, bf16[64,6144]{1,0:T(8,128)(2,1)} %bitcast.40), custom_call_target="tpu_custom_call" | custom-call | tf_op jit(solution)/shard_map/pallas_call | solution.py:620
  2.4 3.4 %collective-permute-start = (bf16[3,2,6144]{2,1,0:T(2,128)(2,1)S(1)}, bf16[3,2,6144]{2,1,0:T(2,128)(2,1)S(1)}, u32[]{:S(2)}, u32[]{:S(2)}) collective-permute-start(bf16[3,2,6144]{2,1,0:T(2,128)(2,1)S(1)} %get-tuple-element.36), channel_id=1, source_target_pairs={{0,1},{1,2},{2,3},{3,4},{4,5},{5,6},{6,7},{7,8},{8,9},{9,10},{10,1... | collective-permute-start | bytes 221192 | tf_op jit(solution)/shard_map/ppermute | solution.py:580
  5.7 1.2 shard_map.96
  7.0 7.8 %collective-permute-done.refs_9_.refs_10_.refs_11_.refs_8_ = bf16[3,2,6144]{2,1,0:T(2,128)(2,1)S(1)} collective-permute-done((bf16[3,2,6144]{2,1,0:T(2,128)(2,1)S(1)}, bf16[3,2,6144]{2,1,0:T(2,128)(2,1)S(1)}, u32[]{:S(2)}, u32[]{:S(2)}) %collective-permute-start) | collective-permute-done | bytes 73760 | tf_op jit(solution)/shard_map/ppermute | solution.py:580
  14.8 6.3 %shard_map.97 = (bf16[3,64,2048]{2,1,0:T(8,128)(2,1)}, bf16[3,64,2048]{2,1,0:T(8,128)(2,1)}, f32[16,4,3,4,128]{4,3,2,1,0:T(4,128)}) custom-call(bf16[64,6144]{1,0:T(8,128)(2,1)} %bitcast.34, bf16[64,6144]{1,0:T(8,128)(2,1)} %bitcast.35, bf16[64,6144]{1,0:T(8,128)(2,1)} %bitcast.36, bf16[64,6144]{1,0:T(8,128)(2,1)} %bitcast.41, bf16[64,6144]{1,0:T(8,128)(2,1)} %bitcast.42, ...), custom_call_target="tpu_custom_call" | custom-call | tf_op jit(solution)/shard_map/pallas_call | solution.py:638
  21.2 8.0 %all-to-all-start = ((f32[64,3,4,128]{3,2,1,0:T(4,128)}), f32[64,3,4,128]{3,2,1,0:T(4,128)S(1)}, u32[]{:S(2)}, u32[]{:S(2)}) async-start(f32[64,3,4,128]{3,2,1,0:T(4,128)} %bitcast.50), calls=%async_computation | async-start | bytes 786432 | tf_op jit(solution)/shard_map/all_to_all | solution.py:574
  29.2 7.6 %shard_map.98.inner_far = f32[3,64,2048]{2,1,0:T(8,128)} custom-call(bf16[3,64,2048]{2,1,0:T(8,128)(2,1)} %get-tuple-element.40.data, f32[16,2048]{1,0:T(8,128)} %bitcast.18, f32[16,2048]{1,0:T(8,128)} %bitcast.23), custom_call_target="tpu_custom_call" | custom-call | flops 300000000 | bytes 2359296 | tf_op jit(solution)/shard_map/pallas_call | solution.py:469
  36.8 4.8 %collective-permute-done.1 = bf16[2,256,1024]{2,1,0:T(8,128)(2,1)S(1)} collective-permute-done((bf16[2,256,1024]{2,1,0:T(8,128)(2,1)S(1)}, bf16[2,256,1024]{2,1,0:T(8,128)(2,1)S(1)}, u32[]{:S(2)}, u32[]{:S(2)}) %collective-permute-start.1) | collective-permute-done | bytes 1048608 | tf_op jit(solution)/shard_map/ppermute | solution.py:598
  41.8 0.1 collective-permute-start.3
  41.9 1.9 %collective-permute-start.7 = (bf16[256,1024]{1,0:T(8,128)(2,1)S(1)}, bf16[256,1024]{1,0:T(8,128)(2,1)S(1)}, u32[]{:S(2)}, u32[]{:S(2)}) collective-permute-start(bf16[256,1024]{1,0:T(8,128)(2,1)S(1)} %get-tuple-element.70.refs_0_), channel_id=1, source_target_pairs={{0,1},{1,0},{2,3},{3,2},{4,5},{5,4},{6,7},{7,6},{8,9},{9,8},{10,11... | collective-permute-start | bytes 1572872 | tf_op jit(solution)/shard_map/ppermute | solution.py:598
  43.8 7.1 %collective-permute-done.2.refs_3_ = bf16[256,1024]{1,0:T(8,128)(2,1)S(1)} collective-permute-done((bf16[256,1024]{1,0:T(8,128)(2,1)S(1)}, bf16[256,1024]{1,0:T(8,128)(2,1)S(1)}, u32[]{:S(2)}, u32[]{:S(2)}) %collective-permute-start.2) | collective-permute-done | bytes 524320 | tf_op jit(solution)/shard_map/ppermute | solution.py:598
  50.9 0.1 collective-permute-done.3.refs_4_
  51.0 1.9 %collective-permute-start.4 = (bf16[256,1024]{1,0:T(8,128)(2,1)S(1)}, bf16[256,1024]{1,0:T(8,128)(2,1)}, u32[]{:S(2)}, u32[]{:S(2)}) collective-permute-start(bf16[256,1024]{1,0:T(8,128)(2,1)S(1)} %collective-permute-done.3.refs_4_), channel_id=1, source_target_pairs={{0,1},{1,0},{2,3},{3,2},{4,5},{5,4},{6,7},{7,6},{8,9},{9,8},{10,11... | collective-permute-start | bytes 1572872 | tf_op jit(solution)/shard_map/ppermute | solution.py:598
  53.0 0.9 shard_map.99
  53.9 8.2 %all-to-all-start.1 = ((f32[64,3,4,128]{3,2,1,0:T(4,128)}), f32[64,3,4,128]{3,2,1,0:T(4,128)S(1)}, u32[]{:S(2)}, u32[]{:S(2)}) async-start(f32[64,3,4,128]{3,2,1,0:T(4,128)} %shard_map.99), calls=%async_computation.1 | async-start | bytes 786432 | tf_op jit(solution)/shard_map/all_to_all | solution.py:574
  62.2 1.6 %collective-permute-start.8 = (bf16[256,1024]{1,0:T(8,128)(2,1)S(1)}, bf16[256,1024]{1,0:T(8,128)(2,1)}, u32[]{:S(2)}, u32[]{:S(2)}) collective-permute-start(bf16[256,1024]{1,0:T(8,128)(2,1)S(1)} %get-tuple-element.71.refs_1_), channel_id=1, source_target_pairs={{0,4},{1,5},{2,6},{3,7},{4,0},{5,1},{6,2},{7,3},{8,12},{9,13},{10,... | collective-permute-start | bytes 1572872 | tf_op jit(solution)/shard_map/ppermute | solution.py:598
  63.8 0.7 collective-permute-start.10
  64.6 0.4 collective-permute-start.12
  65.0 13.0 %all-to-all-done.1 = f32[64,3,4,128]{3,2,1,0:T(4,128)S(1)} async-done(((f32[64,3,4,128]{3,2,1,0:T(4,128)}), f32[64,3,4,128]{3,2,1,0:T(4,128)S(1)}, u32[]{:S(2)}, u32[]{:S(2)}) %all-to-all-start.1) | async-done | bytes 393248 | tf_op jit(solution)/shard_map/all_to_all | solution.py:574
  78.0 0.1 collective-permute-done.8.refs_5_
  78.1 1.2 collective-permute-start.13
  79.3 0.5 collective-permute-start.14
  79.9 0.4 collective-permute-start.16
  80.4 6.1 %shard_map.100 = (bf16[192,2048]{1,0:T(8,128)(2,1)S(1)}, bf16[2,64,2048]{2,1,0:T(8,128)(2,1)}, f32[2,192,1024]{2,1,0:T(8,128)S(1)}, bf16[2,2048,1024]{2,1,0:T(8,128)(2,1)S(1)}) custom-call(f32[16,4,3,4,128]{4,3,2,1,0:T(4,128)S(1)} %bitcast.28, f32[3,64,2048]{2,1,0:T(8,128)} %shard_map.98.inner_far, bf16[3,64,2048]{2,1,0:T(8,128)(2,1)} %get-tuple-element.49.query_far, ...), custom_call_target="tpu_custom_call" | custom-call | flops 5000000000 | bytes 14000000 | tf_op jit(solution)/shard_map/pallas_call | solution.py:510
  86.5 15.6 %shard_map.101 = (f32[2,64,2048]{2,1,0:T(8,128)}, bf16[2,64,2048]{2,1,0:T(8,128)(2,1)}, bf16[2,16,2048]{2,1,0:T(8,128)(2,1)S(1)}, f32[16,4,2,4,128]{4,3,2,1,0:T(4,128)}) custom-call(bf16[192,2048]{1,0:T(8,128)(2,1)S(1)} %get-tuple-element.51.prod, f32[2,192,1024]{2,1,0:T(8,128)S(1)} %get-tuple-element.52.near_mixed, ...), custom_call_target="tpu_custom_call" | custom-call | tf_op jit(solution)/shard_map/pallas_call | solution.py:537
  102.2 9.5 %all-to-all-start.2 = ((f32[64,2,4,128]{3,2,1,0:T(4,128)}), f32[64,2,4,128]{3,2,1,0:T(4,128)S(1)}, u32[]{:S(2)}, u32[]{:S(2)}) async-start(f32[64,2,4,128]{3,2,1,0:T(4,128)} %bitcast.11), calls=%async_computation.2 | async-start | bytes 524288 | tf_op jit(solution)/shard_map/all_to_all | solution.py:574
  111.6 6.7 %collective-permute-start.17 = (bf16[2,16,2048]{2,1,0:T(8,128)(2,1)S(1)}, bf16[2,16,2048]{2,1,0:T(8,128)(2,1)S(1)}, u32[]{:S(2)}, u32[]{:S(2)}) collective-permute-start(bf16[2,16,2048]{2,1,0:T(8,128)(2,1)S(1)} %get-tuple-element.61), channel_id=1, source_target_pairs={{1,0},{2,1},{3,2},{4,3},{5,4},{6,5},{7,6},{8,7},{9,8},{10,9},{11,1... | collective-permute-start | bytes 393224 | tf_op jit(solution)/shard_map/ppermute | solution.py:580
  118.3 2.8 %collective-permute-start.18 = (bf16[2,2,4096]{2,1,0:T(2,128)(2,1)S(1)}, bf16[2,2,4096]{2,1,0:T(2,128)(2,1)S(1)}, u32[]{:S(2)}, u32[]{:S(2)}) collective-permute-start(bf16[2,2,4096]{2,1,0:T(2,128)(2,1)S(1)} %copy-done.3), channel_id=1, source_target_pairs={{1,0},{2,1},{3,2},{4,3},{5,4},{6,5},{7,6},{8,7},{9,8},{10,9},{11,1... | collective-permute-start | bytes 98312 | tf_op jit(solution)/shard_map/ppermute | solution.py:580
  121.1 5.9 %shard_map.102.refs_1_ = f32[2,64,2048]{2,1,0:T(8,128)} custom-call(bf16[2,64,2048]{2,1,0:T(8,128)(2,1)} %get-tuple-element.58.data, f32[16,2048]{1,0:T(8,128)} %bitcast.19, f32[16,2048]{1,0:T(8,128)} %bitcast.24), custom_call_target="tpu_custom_call" | custom-call | flops 200000000 | bytes 1572864 | tf_op jit(solution)/shard_map/pallas_call | solution.py:469
  127.0 0.1 shard_map.103
  127.1 18.5 %all_to_all.20 = f32[64,2,4,128]{3,2,1,0:T(4,128)S(1)} all-to-all(f32[64,2,4,128]{3,2,1,0:T(4,128)S(1)} %shard_map.103), channel_id=1, replica_groups=mesh['dp'=4,'ctx'=64] {'ctx'}, dimensions={0} | all-to-all | bytes 524288 | tf_op jit(solution)/shard_map/all_to_all | solution.py:574
  145.6 6.0 %shard_map.104 = (bf16[64,6144]{1,0:T(8,128)(2,1)}, bf16[64,6144]{1,0:T(8,128)(2,1)}) custom-call(f32[16,4,2,4,128]{4,3,2,1,0:T(4,128)S(1)} %bitcast.27, f32[2,64,2048]{2,1,0:T(8,128)} %shard_map.102.refs_1_, f32[2,64,2048]{2,1,0:T(8,128)} %get-tuple-element.65.refs_2_, bf16[2,16,2048]{2,1,0:T(8,128)(2,1)S(1)} %collective-permute-done.17.refs_3_, ...), custom_call_target="tpu_custom_call" | custom-call | tf_op jit(solution)/shard_map/pallas_call | solution.py:685
  (33 shorter events, 0.5 us)
Async XLA Ops:
  2.4 12.5 %collective-permute-start = (bf16[3,2,6144]{2,1,0:T(2,128)(2,1)S(1)}, bf16[3,2,6144]{2,1,0:T(2,128)(2,1)S(1)}, u32[]{:S(2)}, u32[]{:S(2)}) collective-permute-start(bf16[3,2,6144]{2,1,0:T(2,128)(2,1)S(1)} %get-tuple-element.36), channel_id=1, source_target_pairs={{0,1},{1,2},{2,3},{3,4},{4,5},{5,6},{6,7},{7,8},{8,9},{9,10},{10,1... | collective-permute-start | bytes 221192 | tf_op jit(solution)/shard_map/ppermute | solution.py:580
  14.8 65.1 %collective-permute-start.6 = (bf16[2048,1024]{1,0:T(8,128)(2,1)}, bf16[2048,1024]{1,0:T(8,128)(2,1)}, u32[]{:S(2)}, u32[]{:S(2)}) collective-permute-start(bf16[2048,1024]{1,0:T(8,128)(2,1)} %own_weight.1), channel_id=1, source_target_pairs={{0,64},{1,65},{2,66},{3,67},{4,68},{5,69},{6,70},{7,71},{8,72},{9,... | collective-permute-start | bytes 12582920 | tf_op jit(solution)/shard_map/ppermute | solution.py:598
  14.8 26.8 %collective-permute-start.1 = (bf16[2,256,1024]{2,1,0:T(8,128)(2,1)S(1)}, bf16[2,256,1024]{2,1,0:T(8,128)(2,1)S(1)}, u32[]{:S(2)}, u32[]{:S(2)}) collective-permute-start(bf16[2,256,1024]{2,1,0:T(8,128)(2,1)S(1)} %shard_map.96), channel_id=1, source_target_pairs={{0,160},{1,161},{2,162},{3,163},{4,164},{5,165},{6,166},{7,167},{8... | collective-permute-start | bytes 3145736 | tf_op jit(solution)/shard_map/ppermute | solution.py:598
  21.1 31.8 %copy-start = (f32[2048,16]{0,1:T(8,128)S(1)}, f32[2048,16]{0,1:T(8,128)}, u32[]{:S(2)}) copy-start(f32[2048,16]{0,1:T(8,128)} %param.13) | copy-start | bytes 393220
  21.1 59.2 %copy-start.1 = (f32[2048,16]{0,1:T(8,128)S(1)}, f32[2048,16]{0,1:T(8,128)}, u32[]{:S(2)}) copy-start(f32[2048,16]{0,1:T(8,128)} %param.12) | copy-start | bytes 393220
  21.2 22.6 %all-to-all-start = ((f32[64,3,4,128]{3,2,1,0:T(4,128)}), f32[64,3,4,128]{3,2,1,0:T(4,128)S(1)}, u32[]{:S(2)}, u32[]{:S(2)}) async-start(f32[64,3,4,128]{3,2,1,0:T(4,128)} %bitcast.50), calls=%async_computation | async-start | bytes 786432 | tf_op jit(solution)/shard_map/all_to_all | solution.py:574
  41.7 9.3 %collective-permute-start.2 = (bf16[256,1024]{1,0:T(8,128)(2,1)S(1)}, bf16[256,1024]{1,0:T(8,128)(2,1)S(1)}, u32[]{:S(2)}, u32[]{:S(2)}) collective-permute-start(bf16[256,1024]{1,0:T(8,128)(2,1)S(1)} %get-tuple-element.71.refs_1_), channel_id=1, source_target_pairs={{0,1},{1,0},{2,3},{3,2},{4,5},{5,4},{6,7},{7,6},{8,9},{9,8},{10,11... | collective-permute-start | bytes 1572872 | tf_op jit(solution)/shard_map/ppermute | solution.py:598
  41.8 9.3 %collective-permute-start.3 = (bf16[256,1024]{1,0:T(8,128)(2,1)S(1)}, bf16[256,1024]{1,0:T(8,128)(2,1)S(1)}, u32[]{:S(2)}, u32[]{:S(2)}) collective-permute-start(bf16[256,1024]{1,0:T(8,128)(2,1)S(1)} %get-tuple-element.70.refs_0_), channel_id=1, source_target_pairs={{0,4},{1,5},{2,6},{3,7},{4,0},{5,1},{6,2},{7,3},{8,12},{9,13},{10,... | collective-permute-start | bytes 1572872 | tf_op jit(solution)/shard_map/ppermute | solution.py:598
  41.9 21.9 %collective-permute-start.7 = (bf16[256,1024]{1,0:T(8,128)(2,1)S(1)}, bf16[256,1024]{1,0:T(8,128)(2,1)S(1)}, u32[]{:S(2)}, u32[]{:S(2)}) collective-permute-start(bf16[256,1024]{1,0:T(8,128)(2,1)S(1)} %get-tuple-element.70.refs_0_), channel_id=1, source_target_pairs={{0,1},{1,0},{2,3},{3,2},{4,5},{5,4},{6,7},{7,6},{8,9},{9,8},{10,11... | collective-permute-start | bytes 1572872 | tf_op jit(solution)/shard_map/ppermute | solution.py:598
  51.0 13.4 %collective-permute-start.4 = (bf16[256,1024]{1,0:T(8,128)(2,1)S(1)}, bf16[256,1024]{1,0:T(8,128)(2,1)}, u32[]{:S(2)}, u32[]{:S(2)}) collective-permute-start(bf16[256,1024]{1,0:T(8,128)(2,1)S(1)} %collective-permute-done.3.refs_4_), channel_id=1, source_target_pairs={{0,1},{1,0},{2,3},{3,2},{4,5},{5,4},{6,7},{7,6},{8,9},{9,8},{10,11... | collective-permute-start | bytes 1572872 | tf_op jit(solution)/shard_map/ppermute | solution.py:598
  53.0 11.6 %collective-permute-start.5 = (bf16[256,1024]{1,0:T(8,128)(2,1)S(1)}, bf16[256,1024]{1,0:T(8,128)(2,1)}, u32[]{:S(2)}, u32[]{:S(2)}) collective-permute-start(bf16[256,1024]{1,0:T(8,128)(2,1)S(1)} %collective-permute-done.2.refs_3_), channel_id=1, source_target_pairs={{0,4},{1,5},{2,6},{3,7},{4,0},{5,1},{6,2},{7,3},{8,12},{9,13},{10,... | collective-permute-start | bytes 1572872 | tf_op jit(solution)/shard_map/ppermute | solution.py:598
  53.9 24.0 %all-to-all-start.1 = ((f32[64,3,4,128]{3,2,1,0:T(4,128)}), f32[64,3,4,128]{3,2,1,0:T(4,128)S(1)}, u32[]{:S(2)}, u32[]{:S(2)}) async-start(f32[64,3,4,128]{3,2,1,0:T(4,128)} %shard_map.99), calls=%async_computation.1 | async-start | bytes 786432 | tf_op jit(solution)/shard_map/all_to_all | solution.py:574
  62.2 15.9 %collective-permute-start.8 = (bf16[256,1024]{1,0:T(8,128)(2,1)S(1)}, bf16[256,1024]{1,0:T(8,128)(2,1)}, u32[]{:S(2)}, u32[]{:S(2)}) collective-permute-start(bf16[256,1024]{1,0:T(8,128)(2,1)S(1)} %get-tuple-element.71.refs_1_), channel_id=1, source_target_pairs={{0,4},{1,5},{2,6},{3,7},{4,0},{5,1},{6,2},{7,3},{8,12},{9,13},{10,... | collective-permute-start | bytes 1572872 | tf_op jit(solution)/shard_map/ppermute | solution.py:598
  63.8 15.5 %collective-permute-start.10 = (bf16[256,1024]{1,0:T(8,128)(2,1)S(1)}, bf16[256,1024]{1,0:T(8,128)(2,1)}, u32[]{:S(2)}, u32[]{:S(2)}) collective-permute-start(bf16[256,1024]{1,0:T(8,128)(2,1)S(1)} %get-tuple-element.71.refs_1_), channel_id=1, source_target_pairs={{0,64},{1,65},{2,66},{3,67},{4,68},{5,69},{6,70},{7,71},{8,72},{9,... | collective-permute-start | bytes 1572872 | tf_op jit(solution)/shard_map/ppermute | solution.py:598
  64.5 14.9 %collective-permute-start.9 = (bf16[256,1024]{1,0:T(8,128)(2,1)S(1)}, bf16[256,1024]{1,0:T(8,128)(2,1)}, u32[]{:S(2)}, u32[]{:S(2)}) collective-permute-start(bf16[256,1024]{1,0:T(8,128)(2,1)S(1)} %get-tuple-element.70.refs_0_), channel_id=1, source_target_pairs={{0,64},{1,65},{2,66},{3,67},{4,68},{5,69},{6,70},{7,71},{8,72},{9,... | collective-permute-start | bytes 1572872 | tf_op jit(solution)/shard_map/ppermute | solution.py:598
  64.6 15.3 %collective-permute-start.12 = (bf16[256,1024]{1,0:T(8,128)(2,1)S(1)}, bf16[256,1024]{1,0:T(8,128)(2,1)}, u32[]{:S(2)}, u32[]{:S(2)}) collective-permute-start(bf16[256,1024]{1,0:T(8,128)(2,1)S(1)} %collective-permute-done.2.refs_3_), channel_id=1, source_target_pairs={{0,64},{1,65},{2,66},{3,67},{4,68},{5,69},{6,70},{7,71},{8,72},{9,... | collective-permute-start | bytes 1572872 | tf_op jit(solution)/shard_map/ppermute | solution.py:598
  78.1 8.3 %collective-permute-start.13 = (bf16[256,1024]{1,0:T(8,128)(2,1)S(1)}, bf16[256,1024]{1,0:T(8,128)(2,1)S(1)}, u32[]{:S(2)}, u32[]{:S(2)}) collective-permute-start(bf16[256,1024]{1,0:T(8,128)(2,1)S(1)} %collective-permute-done.3.refs_4_), channel_id=1, source_target_pairs={{0,64},{1,65},{2,66},{3,67},{4,68},{5,69},{6,70},{7,71},{8,72},{9,... | collective-permute-start | bytes 1572872 | tf_op jit(solution)/shard_map/ppermute | solution.py:598
  79.3 7.1 %collective-permute-start.11 = (bf16[256,1024]{1,0:T(8,128)(2,1)S(1)}, bf16[256,1024]{1,0:T(8,128)(2,1)S(1)}, u32[]{:S(2)}, u32[]{:S(2)}) collective-permute-start(bf16[256,1024]{1,0:T(8,128)(2,1)S(1)} %collective-permute-done.7.refs_2_), channel_id=1, source_target_pairs={{0,64},{1,65},{2,66},{3,67},{4,68},{5,69},{6,70},{7,71},{8,72},{9,... | collective-permute-start | bytes 1572872 | tf_op jit(solution)/shard_map/ppermute | solution.py:598
  79.3 7.2 %collective-permute-start.14 = (bf16[256,1024]{1,0:T(8,128)(2,1)}, bf16[256,1024]{1,0:T(8,128)(2,1)S(1)}, u32[]{:S(2)}, u32[]{:S(2)}) collective-permute-start(bf16[256,1024]{1,0:T(8,128)(2,1)} %collective-permute-done.8.refs_5_), channel_id=1, source_target_pairs={{0,64},{1,65},{2,66},{3,67},{4,68},{5,69},{6,70},{7,71},{8,72},{9,... | collective-permute-start | bytes 1572872 | tf_op jit(solution)/shard_map/ppermute | solution.py:598
  79.8 6.7 %collective-permute-start.15 = (bf16[256,1024]{1,0:T(8,128)(2,1)}, bf16[256,1024]{1,0:T(8,128)(2,1)S(1)}, u32[]{:S(2)}, u32[]{:S(2)}) collective-permute-start(bf16[256,1024]{1,0:T(8,128)(2,1)} %collective-permute-done.4.refs_6_), channel_id=1, source_target_pairs={{0,64},{1,65},{2,66},{3,67},{4,68},{5,69},{6,70},{7,71},{8,72},{9,... | collective-permute-start | bytes 1572872 | tf_op jit(solution)/shard_map/ppermute | solution.py:598
  79.9 6.6 %collective-permute-start.16 = (bf16[256,1024]{1,0:T(8,128)(2,1)}, bf16[256,1024]{1,0:T(8,128)(2,1)S(1)}, u32[]{:S(2)}, u32[]{:S(2)}) collective-permute-start(bf16[256,1024]{1,0:T(8,128)(2,1)} %collective-permute-done.5.refs_7_), channel_id=1, source_target_pairs={{0,64},{1,65},{2,66},{3,67},{4,68},{5,69},{6,70},{7,71},{8,72},{9,... | collective-permute-start | bytes 1572872 | tf_op jit(solution)/shard_map/ppermute | solution.py:598
  80.4 6.2 %copy-start.2 = (f32[4096]{0:T(1024)S(1)}, f32[4096]{0:T(1024)}, u32[]{:S(2)}) copy-start(f32[4096]{0:T(1024)} %param.15) | copy-start | bytes 49156
  86.5 31.8 %copy-start.3 = (bf16[2,2,4096]{2,1,0:T(2,128)(2,1)S(1)}, bf16[2,2,4096]{2,1,0:T(2,128)(2,1)}, u32[]{:S(2)}) copy-start(bf16[2,2,4096]{2,1,0:T(2,128)(2,1)} %get-tuple-element.62) | copy-start | bytes 98308
  102.2 24.8 %all-to-all-start.2 = ((f32[64,2,4,128]{3,2,1,0:T(4,128)}), f32[64,2,4,128]{3,2,1,0:T(4,128)S(1)}, u32[]{:S(2)}, u32[]{:S(2)}) async-start(f32[64,2,4,128]{3,2,1,0:T(4,128)} %bitcast.11), calls=%async_computation.2 | async-start | bytes 524288 | tf_op jit(solution)/shard_map/all_to_all | solution.py:574
  111.6 15.3 %collective-permute-start.17 = (bf16[2,16,2048]{2,1,0:T(8,128)(2,1)S(1)}, bf16[2,16,2048]{2,1,0:T(8,128)(2,1)S(1)}, u32[]{:S(2)}, u32[]{:S(2)}) collective-permute-start(bf16[2,16,2048]{2,1,0:T(8,128)(2,1)S(1)} %get-tuple-element.61), channel_id=1, source_target_pairs={{1,0},{2,1},{3,2},{4,3},{5,4},{6,5},{7,6},{8,7},{9,8},{10,9},{11,1... | collective-permute-start | bytes 393224 | tf_op jit(solution)/shard_map/ppermute | solution.py:580
  118.3 8.6 %collective-permute-start.18 = (bf16[2,2,4096]{2,1,0:T(2,128)(2,1)S(1)}, bf16[2,2,4096]{2,1,0:T(2,128)(2,1)S(1)}, u32[]{:S(2)}, u32[]{:S(2)}) collective-permute-start(bf16[2,2,4096]{2,1,0:T(2,128)(2,1)S(1)} %copy-done.3), channel_id=1, source_target_pairs={{1,0},{2,1},{3,2},{4,3},{5,4},{6,5},{7,6},{8,7},{9,8},{10,9},{11,1... | collective-permute-start | bytes 98312 | tf_op jit(solution)/shard_map/ppermute | solution.py:580

commit v6 on v5

--- a/solution.py
+++ b/solution.py
@@ -173,14 +173,14 @@
     state = jnp.zeros(ends.shape[1:], f32)
     for place in range(count):
         at = count - 1 - place if reverse else place
-        reaching[at] = state
-        state = decay[None] * state + ends[at]
+        reaching[at] = state.astype(bf16)
+        state = decay[None] * state + ends[at].astype(f32)
 
 
 def mix_kernel(
-    reaching, inner_far, query_far, rate, res, own_weight, core_weight,
+    arriving, inner_far, query_far, rate, res, own_weight, core_weight,
     prod, conv, mixed, held,
-    inner, query, sems,
+    reaching, inner, query, sems,
 ):
     copies = []
     for q in range(QUARTERS):
@@ -193,6 +193,7 @@
         copies.append(pltpu.make_async_copy(weight, held.at[p], sems.at[2 * QUARTERS + p]))
     for copy in copies:
         copy.start()
+    reaching[...] = arriving[...].astype(f32)
 
     def conv_tile(tile, carry):
         lanes = tile_lanes(tile)
@@ -248,7 +249,7 @@
 
 def slope_kernel(prod, near_mixed, conv_far, query_far, rate, gain, held, *refs):
     pieces, refs = (refs[0:PIECES], refs[PIECES : 2 * PIECES]), refs[2 * PIECES :]
-    query_slope, conv_slope, edge, states, conv, query, far_mixed, slope, prod_slope, sems = refs
+    query_slope, conv_slope, edge, states, conv, query, far_mixed, slope, prod_slope, ends, sems = refs
     dp, ctx = lax.axis_index("dp"), lax.axis_index("ctx")
     late = [
         pltpu.make_async_copy(conv_far, conv, sems.at[0]),
@@ -291,6 +292,7 @@
         squares = lax.fori_loop(0, width // LANES, square_sums, squares)
     squares = jnp.sum(squares, axis=1, keepdims=True)
     inv = lax.rsqrt(squares / D + eps)
+    inv = jnp.broadcast_to(inv, (3 * ROWS, LANES))
     inv_clean, inv_pert, inv_teacher = inv[:ROWS], inv[ROWS : 2 * ROWS], inv[2 * ROWS :]
 
     def slopes(p, t):
@@ -361,17 +363,19 @@
                 for i in range(6, -1, -1):
                     state = state * step8_rows[m] + x[8 * i : 8 * i + 8]
                 state = jnp.sum(state * weights[m], axis=0, keepdims=True)
-                states[m, tile // QUARTER, s, pl.ds(tile % QUARTER, 1), :] = state
+                ends[m, tile // QUARTER, s, pl.ds(tile % QUARTER, 1), :] = state
         return carry
 
     lax.fori_loop(0, TILES, state_tile, 0)
+    states[...] = ends[...].astype(bf16)
 
 
 def final_kernel(*refs):
-    reaching, inner, query_slope, next_edge = refs[:4]
+    arriving, inner, query_slope, next_edge = refs[:4]
     features, halos, next_rows, taps = refs[4:8], refs[8:10], refs[10:12], refs[12:15]
-    rate, res, grad_clean, grad_pert, ext, unit, grads, sems = refs[15:]
+    rate, res, grad_clean, grad_pert, reaching, ext, unit, grads, sems = refs[15:]
     quarter_at = pl.program_id(0)
+    reaching[...] = arriving[...].astype(f32)
 
     def one_tile(tile, carry):
         lanes = tile_lanes(tile)
@@ -518,6 +522,7 @@
         in_specs=[near] + [far()] * 2 + [pl.BlockSpec()] * 2 + [far()] * 2,
         out_specs=(near, pl.BlockSpec(), near, near),
         scratch_shapes=[
+            pltpu.VMEM((M, QUARTERS, 3, QUARTER, LANES), f32),
             pltpu.VMEM((3, ROWS, C), f32),
             pltpu.VMEM((3, ROWS, C), bf16),
             pltpu.SemaphoreType.DMA((2 * QUARTERS + 2,)),
@@ -540,7 +545,7 @@
             pltpu.HBM((2, ROWS, C), f32),
             pltpu.HBM((2, ROWS, C), bf16),
             array(2, 16, C, dtype=bf16),
-            array(M, QUARTERS, 2, QUARTER, LANES),
+            array(M, QUARTERS, 2, QUARTER, LANES, dtype=bf16),
         ),
         in_specs=[near] * 2 + [far()] * 2 + [pl.BlockSpec()] * 2 + [near] * (1 + 2 * PIECES),
         out_specs=(pl.BlockSpec(),) * 4,
@@ -550,6 +555,7 @@
             pltpu.VMEM((2, 3 * ROWS, WIDTH), f32),
             pltpu.VMEM((4, 2 * ROWS, WIDTH), bf16),
             pltpu.VMEM((2 * ROWS, C), f32),
+            pltpu.VMEM((M, QUARTERS, 2, QUARTER, LANES), f32),
             pltpu.SemaphoreType.DMA((2,)),
         ],
         compiler_params=params(10),
@@ -562,7 +568,7 @@
 def scan(ends, own_rate, reverse):
     return pl.pallas_call(
         functools.partial(scan_kernel, reverse),
-        out_shape=array(*ends.shape),
+        out_shape=array(*ends.shape, dtype=bf16),
         compiler_params=params(4),
     )(ends, own_rate)
 
@@ -661,25 +667,29 @@
     upper, lower = band[0], band[1]
     upper_x, upper_z = swapped(upper, "x"), swapped(upper, "z")
     lower_x, lower_z = swapped(lower, "x"), swapped(lower, "z")
-    ends, inner, lower_x, upper_z = tied(ends, inner, lower_x, upper_z)
+    ends, inner = tied(ends, inner)
     reaching = exchanged(scan(ends, own_rate, False)).reshape(*state_shape, 3, QUARTER, LANES)
+    reaching, upper_x, upper_z, lower_x, lower_z = tied(
+        reaching, upper_x, upper_z, lower_x, lower_z
+    )
     last_x, last_z = swapped(upper_z, "x"), swapped(lower_x, "z")
-    reaching, last_x, last_z = tied(reaching, last_x, last_z)
-    far_pieces = [upper, lower, upper_x, lower_x, upper_z, lower_z, last_x, last_z]
+    far_pieces = [upper, lower, upper_x, lower_x, upper_z, lower_z]
     core_pieces = [swapped(piece, "core") for piece in far_pieces]
 
     prod, conv, near_mixed, held = mix_call(
         reaching, inner, query, rate, res, out_weight, core_weight
     )
+    prod, last_x, last_z = tied(prod, last_x, last_z)
+    far_pieces += [last_x, last_z]
+    core_pieces += [swapped(last_x, "core"), swapped(last_z, "core")]
     query_slope, conv_slope, edge, ends = slope_call(
         prod, near_mixed, conv, query, rate, gain, held, *far_pieces, *core_pieces
     )
 
     ends = exchanged(ends)
-    first_rows, edge = tied(first_rows, edge)
+    inner = within(conv_slope, rate, res, True, 0, QUARTERS)
+    ends, inner, edge, first_rows = tied(ends, inner, edge, first_rows)
     next_edge, first_rows = passed_along(edge, -1), passed_along(first_rows, -1)
-    inner = within(conv_slope, rate, res, True, 0, QUARTERS)
-    ends, inner, next_edge, first_rows = tied(ends, inner, next_edge, first_rows)
     reaching = exchanged(scan(ends, own_rate, True)).reshape(*state_shape, 2, QUARTER, LANES)
 
     grads = pl.pallas_call(
@@ -694,6 +704,7 @@
         + [quarter(M), quarter(M)],
         out_specs=(far(), far()),
         scratch_shapes=[
+            pltpu.VMEM((M, 1, 2, QUARTER, LANES), f32),
             pltpu.VMEM((4, 16 + ROWS, LANES), f32),
             pltpu.VMEM((6, 8 + ROWS, LANES), f32),
             pltpu.VMEM((QUARTERS, 6, ROWS, QUARTER * LANES), bf16),

time: 154 us -> 139 us (0.903); the launches traced: 152 us -> 139 us
  waiting for transfers between devices: 33 us -> 23.1 us
  starting transfers between devices: 47.6 us -> 44.8 us
    all_to_all x3, waiting for transfers between devices: 13 us -> 4.2 us  [exchanged(): return lax.all_to_all(flat, 'ctx', split_axis=0, concat_axis=0, tiled=True)]
    ppermute x16, waiting for transfers between devices: 12.2 us -> 8.07 us  [swapped(): lax.ppermute(value, ('dp', 'ctx'), [(device, partner(device, kind)) for d...]
    all_to_all x3, starting transfers between devices: 25.8 us -> 22.5 us  [exchanged(): return lax.all_to_all(flat, 'ctx', split_axis=0, concat_axis=0, tiled=True)]
    ppermute x3, waiting for transfers between devices: 7.82 us -> 10.9 us  [passed_along(): lax.ppermute(value, 'ctx', [(source, source + steps) for source in range(...]
  transfers between devices with their start and end apart: 22 -> 22, of which waited for: 6 -> 8; matrix products, arithmetic and copies ran while one was open for 0% -> 0% of each run, Pallas kernels for 18% -> 20%
where the time goes in v6:
time: 139 us
  Pallas kernels  50.7 us (36%)
  starting transfers between devices  44.8 us (32%)
  waiting for transfers between devices  23.1 us (17%)
  blocking collectives  18.8 us (14%)
    all_to_all x3, starting transfers between devices, exchanged(): return lax.all_to_all(flat, 'ctx', split_axis=0, concat_axis=0, tiled=True)  22.5 us
    all_to_all x1, blocking collectives, exchanged(): return lax.all_to_all(flat, 'ctx', split_axis=0, concat_axis=0, tiled=True)  18.8 us
    pallas_call x1, Pallas kernels, slope_call(): pl.pallas_call(slope_kernel, out_shape=(pltpu.HBM((2, ROWS, C), f32), plt...  14.8 us
    pallas_call x2, Pallas kernels, within(): pl.pallas_call(functools.partial(within_kernel, streams, reverse), out_sh...  13.5 us
    ppermute x3, starting transfers between devices, passed_along(): lax.ppermute(value, 'ctx', [(source, source + steps) for source in range(...  12.8 us
    ppermute x3, waiting for transfers between devices, passed_along(): lax.ppermute(value, 'ctx', [(source, source + steps) for source in range(...  10.9 us
    ppermute x16, starting transfers between devices, swapped(): lax.ppermute(value, ('dp', 'ctx'), [(device, partner(device, kind)) for d...  9.5 us
    ppermute x16, waiting for transfers between devices, swapped(): lax.ppermute(value, ('dp', 'ctx'), [(device, partner(device, kind)) for d...  8.07 us
  transfers between devices with their start and end apart: 22, of which 8 were waited for; matrix products, arithmetic and copies ran while one was open for 0% of the time, Pallas kernels for 20%

profile of v6, /device:TPU:24, one launch (start us, length us, event | category | flops | bytes accessed | tf_op | source)
XLA Modules:
  0.0 138.6 jit_solution(5125679397746062286)
XLA Ops:
  0.6 1.7 %shard_map.95 = (bf16[3,2,6144]{2,1,0:T(2,128)(2,1)S(1)}, bf16[2,2,4096]{2,1,0:T(2,128)(2,1)}) custom-call(bf16[64,6144]{1,0:T(8,128)(2,1)} %bitcast.32, bf16[64,6144]{1,0:T(8,128)(2,1)} %bitcast.39, bf16[64,6144]{1,0:T(8,128)(2,1)} %bitcast.46, bf16[64,6144]{1,0:T(8,128)(2,1)} %bitcast.33, bf16[64,6144]{1,0:T(8,128)(2,1)} %bitcast.40), custom_call_target="tpu_custom_call" | custom-call | tf_op jit(solution)/shard_map/pallas_call | solution.py:626
  2.4 3.4 %collective-permute-start = (bf16[3,2,6144]{2,1,0:T(2,128)(2,1)S(1)}, bf16[3,2,6144]{2,1,0:T(2,128)(2,1)S(1)}, u32[]{:S(2)}, u32[]{:S(2)}) collective-permute-start(bf16[3,2,6144]{2,1,0:T(2,128)(2,1)S(1)} %get-tuple-element.37), channel_id=1, source_target_pairs={{0,1},{1,2},{2,3},{3,4},{4,5},{5,6},{6,7},{7,8},{8,9},{9,10},{10,1... | collective-permute-start | bytes 221192 | tf_op jit(solution)/shard_map/ppermute | solution.py:586
  5.7 1.2 shard_map.96
  7.0 7.8 %collective-permute-done.refs_9_.refs_10_.refs_11_.refs_8_ = bf16[3,2,6144]{2,1,0:T(2,128)(2,1)S(1)} collective-permute-done((bf16[3,2,6144]{2,1,0:T(2,128)(2,1)S(1)}, bf16[3,2,6144]{2,1,0:T(2,128)(2,1)S(1)}, u32[]{:S(2)}, u32[]{:S(2)}) %collective-permute-start) | collective-permute-done | bytes 73760 | tf_op jit(solution)/shard_map/ppermute | solution.py:586
  14.8 6.3 %shard_map.97 = (bf16[3,64,2048]{2,1,0:T(8,128)(2,1)}, bf16[3,64,2048]{2,1,0:T(8,128)(2,1)}, f32[16,4,3,4,128]{4,3,2,1,0:T(4,128)}) custom-call(bf16[64,6144]{1,0:T(8,128)(2,1)} %bitcast.34, bf16[64,6144]{1,0:T(8,128)(2,1)} %bitcast.35, bf16[64,6144]{1,0:T(8,128)(2,1)} %bitcast.36, bf16[64,6144]{1,0:T(8,128)(2,1)} %bitcast.41, bf16[64,6144]{1,0:T(8,128)(2,1)} %bitcast.42, ...), custom_call_target="tpu_custom_call" | custom-call | tf_op jit(solution)/shard_map/pallas_call | solution.py:644
  21.2 8.0 %all-to-all-start = ((f32[64,3,4,128]{3,2,1,0:T(4,128)}), f32[64,3,4,128]{3,2,1,0:T(4,128)S(1)}, u32[]{:S(2)}, u32[]{:S(2)}) async-start(f32[64,3,4,128]{3,2,1,0:T(4,128)} %bitcast.50), calls=%async_computation | async-start | bytes 786432 | tf_op jit(solution)/shard_map/all_to_all | solution.py:580
  29.2 7.6 %shard_map.98.inner_far = f32[3,64,2048]{2,1,0:T(8,128)} custom-call(bf16[3,64,2048]{2,1,0:T(8,128)(2,1)} %get-tuple-element.41.data, f32[16,2048]{1,0:T(8,128)} %bitcast.18, f32[16,2048]{1,0:T(8,128)} %bitcast.23), custom_call_target="tpu_custom_call" | custom-call | flops 300000000 | bytes 2359296 | tf_op jit(solution)/shard_map/pallas_call | solution.py:473
  36.8 4.8 %collective-permute-done.1 = bf16[2,256,1024]{2,1,0:T(8,128)(2,1)S(1)} collective-permute-done((bf16[2,256,1024]{2,1,0:T(8,128)(2,1)S(1)}, bf16[2,256,1024]{2,1,0:T(8,128)(2,1)S(1)}, u32[]{:S(2)}, u32[]{:S(2)}) %collective-permute-start.1) | collective-permute-done | bytes 1048608 | tf_op jit(solution)/shard_map/ppermute | solution.py:604
  41.9 1.9 %collective-permute-start.4 = (bf16[256,1024]{1,0:T(8,128)(2,1)S(1)}, bf16[256,1024]{1,0:T(8,128)(2,1)S(1)}, u32[]{:S(2)}, u32[]{:S(2)}) collective-permute-start(bf16[256,1024]{1,0:T(8,128)(2,1)S(1)} %get-tuple-element.72.refs_1_), channel_id=1, source_target_pairs={{0,1},{1,0},{2,3},{3,2},{4,5},{5,4},{6,7},{7,6},{8,9},{9,8},{10,11... | collective-permute-start | bytes 1572872 | tf_op jit(solution)/shard_map/ppermute | solution.py:604
  43.8 2.0 %collective-permute-start.5 = (bf16[256,1024]{1,0:T(8,128)(2,1)S(1)}, bf16[256,1024]{1,0:T(8,128)(2,1)}, u32[]{:S(2)}, u32[]{:S(2)}) collective-permute-start(bf16[256,1024]{1,0:T(8,128)(2,1)S(1)} %get-tuple-element.72.refs_1_), channel_id=1, source_target_pairs={{0,4},{1,5},{2,6},{3,7},{4,0},{5,1},{6,2},{7,3},{8,12},{9,13},{10,... | collective-permute-start | bytes 1572872 | tf_op jit(solution)/shard_map/ppermute | solution.py:604
  45.9 0.1 shard_map.99
  46.0 18.8 %all_to_all.20 = bf16[64,3,4,128]{3,2,1,0:T(4,128)(2,1)S(1)} all-to-all(bf16[64,3,4,128]{3,2,1,0:T(4,128)(2,1)S(1)} %shard_map.99), channel_id=1, replica_groups=mesh['dp'=4,'ctx'=64] {'ctx'}, dimensions={0} | all-to-all | bytes 393216 | tf_op jit(solution)/shard_map/all_to_all | solution.py:580
  64.9 0.8 collective-permute-start.7
  65.7 1.8 %collective-permute-start.8 = (bf16[256,1024]{1,0:T(8,128)(2,1)S(1)}, bf16[256,1024]{1,0:T(8,128)(2,1)S(1)}, u32[]{:S(2)}, u32[]{:S(2)}) collective-permute-start(bf16[256,1024]{1,0:T(8,128)(2,1)S(1)} %collective-permute-done.4.refs_3_), channel_id=1, source_target_pairs={{0,4},{1,5},{2,6},{3,7},{4,0},{5,1},{6,2},{7,3},{8,12},{9,13},{10,... | collective-permute-start | bytes 1572872 | tf_op jit(solution)/shard_map/ppermute | solution.py:604
  67.6 0.5 collective-permute-start.9
  68.1 6.1 %shard_map.100 = (bf16[192,2048]{1,0:T(8,128)(2,1)S(1)}, bf16[2,64,2048]{2,1,0:T(8,128)(2,1)}, f32[2,192,1024]{2,1,0:T(8,128)S(1)}, bf16[2,2048,1024]{2,1,0:T(8,128)(2,1)S(1)}) custom-call(bf16[16,4,3,4,128]{4,3,2,1,0:T(4,128)(2,1)S(1)} %bitcast.28, f32[3,64,2048]{2,1,0:T(8,128)} %shard_map.98.inner_far, bf16[3,64,2048]{2,1,0:T(8,128)(2,1)} %get-tuple-element.48.query_far, ...), custom_call_target="tpu_custom_call" | custom-call | flops 5000000000 | bytes 14000000 | tf_op jit(solution)/shard_map/pallas_call | solution.py:514
  74.2 0.6 collective-permute-start.12
  74.9 1.0 collective-permute-start.13
  75.9 0.5 collective-permute-start.15
  76.5 1.6 %collective-permute-done.13.refs_12_ = bf16[256,1024]{1,0:T(8,128)(2,1)S(1)} collective-permute-done((bf16[256,1024]{1,0:T(8,128)(2,1)S(1)}, bf16[256,1024]{1,0:T(8,128)(2,1)S(1)}, u32[]{:S(2)}, u32[]{:S(2)}) %collective-permute-start.13) | collective-permute-done | bytes 524320 | tf_op jit(solution)/shard_map/ppermute | solution.py:604
  78.1 0.9 collective-permute-done.14.refs_13_
  79.0 0.7 collective-permute-done.16.refs_15_
  79.7 14.8 %shard_map.101 = (f32[2,64,2048]{2,1,0:T(8,128)}, bf16[2,64,2048]{2,1,0:T(8,128)(2,1)}, bf16[2,16,2048]{2,1,0:T(8,128)(2,1)S(1)}, bf16[16,4,2,4,128]{4,3,2,1,0:T(4,128)(2,1)}) custom-call(bf16[192,2048]{1,0:T(8,128)(2,1)S(1)} %get-tuple-element.53.prod, f32[2,192,1024]{2,1,0:T(8,128)S(1)} %get-tuple-element.54.near_mixed, ...), custom_call_target="tpu_custom_call" | custom-call | tf_op jit(solution)/shard_map/pallas_call | solution.py:542
  94.5 7.4 %all-to-all-start.2 = ((bf16[64,2,4,128]{3,2,1,0:T(4,128)(2,1)}), bf16[64,2,4,128]{3,2,1,0:T(4,128)(2,1)S(1)}, u32[]{:S(2)}, u32[]{:S(2)}) async-start(bf16[64,2,4,128]{3,2,1,0:T(4,128)(2,1)} %bitcast.11), calls=%async_computation.2 | async-start | bytes 262144 | tf_op jit(solution)/shard_map/all_to_all | solution.py:580
  101.9 5.9 %shard_map.102.refs_1_ = f32[2,64,2048]{2,1,0:T(8,128)} custom-call(bf16[2,64,2048]{2,1,0:T(8,128)(2,1)} %get-tuple-element.62.data, f32[16,2048]{1,0:T(8,128)} %bitcast.19, f32[16,2048]{1,0:T(8,128)} %bitcast.24), custom_call_target="tpu_custom_call" | custom-call | flops 200000000 | bytes 1572864 | tf_op jit(solution)/shard_map/pallas_call | solution.py:473
  107.7 4.2 %all-to-all-done.2.ends = bf16[64,2,4,128]{3,2,1,0:T(4,128)(2,1)S(1)} async-done(((bf16[64,2,4,128]{3,2,1,0:T(4,128)(2,1)}), bf16[64,2,4,128]{3,2,1,0:T(4,128)(2,1)S(1)}, u32[]{:S(2)}, u32[]{:S(2)}) %all-to-all-start.2) | async-done | bytes 131104 | tf_op jit(solution)/shard_map/all_to_all | solution.py:580
  111.9 0.8 shard_map.103
  112.7 7.1 %all-to-all-start.3 = ((bf16[64,2,4,128]{3,2,1,0:T(4,128)(2,1)}), bf16[64,2,4,128]{3,2,1,0:T(4,128)(2,1)S(1)}, u32[]{:S(2)}, u32[]{:S(2)}) async-start(bf16[64,2,4,128]{3,2,1,0:T(4,128)(2,1)} %shard_map.103), calls=%async_computation.3 | async-start | bytes 262144 | tf_op jit(solution)/shard_map/all_to_all | solution.py:580
  119.8 6.7 %collective-permute-start.17 = (bf16[2,16,2048]{2,1,0:T(8,128)(2,1)S(1)}, bf16[2,16,2048]{2,1,0:T(8,128)(2,1)S(1)}, u32[]{:S(2)}, u32[]{:S(2)}) collective-permute-start(bf16[2,16,2048]{2,1,0:T(8,128)(2,1)S(1)} %get-tuple-element.68), channel_id=1, source_target_pairs={{1,0},{2,1},{3,2},{4,3},{5,4},{6,5},{7,6},{8,7},{9,8},{10,9},{11,1... | collective-permute-start | bytes 393224 | tf_op jit(solution)/shard_map/ppermute | solution.py:586
  126.5 2.8 %collective-permute-start.18 = (bf16[2,2,4096]{2,1,0:T(2,128)(2,1)S(1)}, bf16[2,2,4096]{2,1,0:T(2,128)(2,1)S(1)}, u32[]{:S(2)}, u32[]{:S(2)}) collective-permute-start(bf16[2,2,4096]{2,1,0:T(2,128)(2,1)S(1)} %copy-done.3), channel_id=1, source_target_pairs={{1,0},{2,1},{3,2},{4,3},{5,4},{6,5},{7,6},{8,7},{9,8},{10,9},{11,1... | collective-permute-start | bytes 98312 | tf_op jit(solution)/shard_map/ppermute | solution.py:586
  129.3 3.0 %collective-permute-done.18.refs_10_.refs_11_ = bf16[2,2,4096]{2,1,0:T(2,128)(2,1)S(1)} collective-permute-done((bf16[2,2,4096]{2,1,0:T(2,128)(2,1)S(1)}, bf16[2,2,4096]{2,1,0:T(2,128)(2,1)S(1)}, u32[]{:S(2)}, u32[]{:S(2)}) %collective-permute-start.18) | collective-permute-done | bytes 32800 | tf_op jit(solution)/shard_map/ppermute | solution.py:586
  132.3 6.1 %shard_map.104 = (bf16[64,6144]{1,0:T(8,128)(2,1)}, bf16[64,6144]{1,0:T(8,128)(2,1)}) custom-call(bf16[16,4,2,4,128]{4,3,2,1,0:T(4,128)(2,1)S(1)} %bitcast.27, f32[2,64,2048]{2,1,0:T(8,128)} %shard_map.102.refs_1_, f32[2,64,2048]{2,1,0:T(8,128)} %get-tuple-element.67.refs_2_, bf16[2,16,2048]{2,1,0:T(8,128)(2,1)S(1)} %collective-permute-done.17.refs_3_, ...), custom_call_target="tpu_custom_call" | custom-call | tf_op jit(solution)/shard_map/pallas_call | solution.py:695
  (33 shorter events, 0.6 us)
Async XLA Ops:
  2.4 12.5 %collective-permute-start = (bf16[3,2,6144]{2,1,0:T(2,128)(2,1)S(1)}, bf16[3,2,6144]{2,1,0:T(2,128)(2,1)S(1)}, u32[]{:S(2)}, u32[]{:S(2)}) collective-permute-start(bf16[3,2,6144]{2,1,0:T(2,128)(2,1)S(1)} %get-tuple-element.37), channel_id=1, source_target_pairs={{0,1},{1,2},{2,3},{3,4},{4,5},{5,6},{6,7},{7,8},{8,9},{9,10},{10,1... | collective-permute-start | bytes 221192 | tf_op jit(solution)/shard_map/ppermute | solution.py:586
  14.8 53.3 %collective-permute-start.6 = (bf16[2048,1024]{1,0:T(8,128)(2,1)}, bf16[2048,1024]{1,0:T(8,128)(2,1)}, u32[]{:S(2)}, u32[]{:S(2)}) collective-permute-start(bf16[2048,1024]{1,0:T(8,128)(2,1)} %own_weight.1), channel_id=1, source_target_pairs={{0,64},{1,65},{2,66},{3,67},{4,68},{5,69},{6,70},{7,71},{8,72},{9,... | collective-permute-start | bytes 12582920 | tf_op jit(solution)/shard_map/ppermute | solution.py:604
  14.8 26.8 %collective-permute-start.1 = (bf16[2,256,1024]{2,1,0:T(8,128)(2,1)S(1)}, bf16[2,256,1024]{2,1,0:T(8,128)(2,1)S(1)}, u32[]{:S(2)}, u32[]{:S(2)}) collective-permute-start(bf16[2,256,1024]{2,1,0:T(8,128)(2,1)S(1)} %shard_map.96), channel_id=1, source_target_pairs={{0,160},{1,161},{2,162},{3,163},{4,164},{5,165},{6,166},{7,167},{8... | collective-permute-start | bytes 3145736 | tf_op jit(solution)/shard_map/ppermute | solution.py:604
  21.1 24.7 %copy-start = (f32[2048,16]{0,1:T(8,128)S(1)}, f32[2048,16]{0,1:T(8,128)}, u32[]{:S(2)}) copy-start(f32[2048,16]{0,1:T(8,128)} %param.13) | copy-start | bytes 393220
  21.2 46.9 %copy-start.1 = (f32[2048,16]{0,1:T(8,128)S(1)}, f32[2048,16]{0,1:T(8,128)}, u32[]{:S(2)}) copy-start(f32[2048,16]{0,1:T(8,128)} %param.12) | copy-start | bytes 393220
  21.2 24.7 %all-to-all-start = ((f32[64,3,4,128]{3,2,1,0:T(4,128)}), f32[64,3,4,128]{3,2,1,0:T(4,128)S(1)}, u32[]{:S(2)}, u32[]{:S(2)}) async-start(f32[64,3,4,128]{3,2,1,0:T(4,128)} %bitcast.50), calls=%async_computation | async-start | bytes 786432 | tf_op jit(solution)/shard_map/all_to_all | solution.py:580
  41.7 23.2 %collective-permute-start.2 = (bf16[256,1024]{1,0:T(8,128)(2,1)S(1)}, bf16[256,1024]{1,0:T(8,128)(2,1)S(1)}, u32[]{:S(2)}, u32[]{:S(2)}) collective-permute-start(bf16[256,1024]{1,0:T(8,128)(2,1)S(1)} %get-tuple-element.73.refs_0_), channel_id=1, source_target_pairs={{0,1},{1,0},{2,3},{3,2},{4,5},{5,4},{6,7},{7,6},{8,9},{9,8},{10,11... | collective-permute-start | bytes 1572872 | tf_op jit(solution)/shard_map/ppermute | solution.py:604
  41.8 23.1 %collective-permute-start.3 = (bf16[256,1024]{1,0:T(8,128)(2,1)S(1)}, bf16[256,1024]{1,0:T(8,128)(2,1)S(1)}, u32[]{:S(2)}, u32[]{:S(2)}) collective-permute-start(bf16[256,1024]{1,0:T(8,128)(2,1)S(1)} %get-tuple-element.73.refs_0_), channel_id=1, source_target_pairs={{0,4},{1,5},{2,6},{3,7},{4,0},{5,1},{6,2},{7,3},{8,12},{9,13},{10,... | collective-permute-start | bytes 1572872 | tf_op jit(solution)/shard_map/ppermute | solution.py:604
  41.9 23.0 %collective-permute-start.4 = (bf16[256,1024]{1,0:T(8,128)(2,1)S(1)}, bf16[256,1024]{1,0:T(8,128)(2,1)S(1)}, u32[]{:S(2)}, u32[]{:S(2)}) collective-permute-start(bf16[256,1024]{1,0:T(8,128)(2,1)S(1)} %get-tuple-element.72.refs_1_), channel_id=1, source_target_pairs={{0,1},{1,0},{2,3},{3,2},{4,5},{5,4},{6,7},{7,6},{8,9},{9,8},{10,11... | collective-permute-start | bytes 1572872 | tf_op jit(solution)/shard_map/ppermute | solution.py:604
  43.8 21.1 %collective-permute-start.5 = (bf16[256,1024]{1,0:T(8,128)(2,1)S(1)}, bf16[256,1024]{1,0:T(8,128)(2,1)}, u32[]{:S(2)}, u32[]{:S(2)}) collective-permute-start(bf16[256,1024]{1,0:T(8,128)(2,1)S(1)} %get-tuple-element.72.refs_1_), channel_id=1, source_target_pairs={{0,4},{1,5},{2,6},{3,7},{4,0},{5,1},{6,2},{7,3},{8,12},{9,13},{10,... | collective-permute-start | bytes 1572872 | tf_op jit(solution)/shard_map/ppermute | solution.py:604
  64.9 9.3 %collective-permute-start.7 = (bf16[256,1024]{1,0:T(8,128)(2,1)S(1)}, bf16[256,1024]{1,0:T(8,128)(2,1)S(1)}, u32[]{:S(2)}, u32[]{:S(2)}) collective-permute-start(bf16[256,1024]{1,0:T(8,128)(2,1)S(1)} %collective-permute-done.3.refs_4_), channel_id=1, source_target_pairs={{0,1},{1,0},{2,3},{3,2},{4,5},{5,4},{6,7},{7,6},{8,9},{9,8},{10,11... | collective-permute-start | bytes 1572872 | tf_op jit(solution)/shard_map/ppermute | solution.py:604
  65.7 9.2 %collective-permute-start.8 = (bf16[256,1024]{1,0:T(8,128)(2,1)S(1)}, bf16[256,1024]{1,0:T(8,128)(2,1)S(1)}, u32[]{:S(2)}, u32[]{:S(2)}) collective-permute-start(bf16[256,1024]{1,0:T(8,128)(2,1)S(1)} %collective-permute-done.4.refs_3_), channel_id=1, source_target_pairs={{0,4},{1,5},{2,6},{3,7},{4,0},{5,1},{6,2},{7,3},{8,12},{9,13},{10,... | collective-permute-start | bytes 1572872 | tf_op jit(solution)/shard_map/ppermute | solution.py:604
  67.6 8.3 %collective-permute-start.10 = (bf16[256,1024]{1,0:T(8,128)(2,1)S(1)}, bf16[256,1024]{1,0:T(8,128)(2,1)S(1)}, u32[]{:S(2)}, u32[]{:S(2)}) collective-permute-start(bf16[256,1024]{1,0:T(8,128)(2,1)S(1)} %get-tuple-element.72.refs_1_), channel_id=1, source_target_pairs={{0,64},{1,65},{2,66},{3,67},{4,68},{5,69},{6,70},{7,71},{8,72},{9,... | collective-permute-start | bytes 1572872 | tf_op jit(solution)/shard_map/ppermute | solution.py:604
  67.6 8.3 %collective-permute-start.9 = (bf16[256,1024]{1,0:T(8,128)(2,1)S(1)}, bf16[256,1024]{1,0:T(8,128)(2,1)S(1)}, u32[]{:S(2)}, u32[]{:S(2)}) collective-permute-start(bf16[256,1024]{1,0:T(8,128)(2,1)S(1)} %get-tuple-element.73.refs_0_), channel_id=1, source_target_pairs={{0,64},{1,65},{2,66},{3,67},{4,68},{5,69},{6,70},{7,71},{8,72},{9,... | collective-permute-start | bytes 1572872 | tf_op jit(solution)/shard_map/ppermute | solution.py:604
  68.1 8.3 %collective-permute-start.11 = (bf16[256,1024]{1,0:T(8,128)(2,1)S(1)}, bf16[256,1024]{1,0:T(8,128)(2,1)S(1)}, u32[]{:S(2)}, u32[]{:S(2)}) collective-permute-start(bf16[256,1024]{1,0:T(8,128)(2,1)S(1)} %collective-permute-done.2.refs_2_), channel_id=1, source_target_pairs={{0,64},{1,65},{2,66},{3,67},{4,68},{5,69},{6,70},{7,71},{8,72},{9,... | collective-permute-start | bytes 1572872 | tf_op jit(solution)/shard_map/ppermute | solution.py:604
  68.1 11.6 %copy-start.2 = (f32[4096]{0:T(1024)S(1)}, f32[4096]{0:T(1024)}, u32[]{:S(2)}) copy-start(f32[4096]{0:T(1024)} %param.15) | copy-start | bytes 49156
  74.2 2.3 %collective-permute-start.12 = (bf16[256,1024]{1,0:T(8,128)(2,1)S(1)}, bf16[256,1024]{1,0:T(8,128)(2,1)S(1)}, u32[]{:S(2)}, u32[]{:S(2)}) collective-permute-start(bf16[256,1024]{1,0:T(8,128)(2,1)S(1)} %collective-permute-done.4.refs_3_), channel_id=1, source_target_pairs={{0,64},{1,65},{2,66},{3,67},{4,68},{5,69},{6,70},{7,71},{8,72},{9,... | collective-permute-start | bytes 1572872 | tf_op jit(solution)/shard_map/ppermute | solution.py:604
  74.9 3.2 %collective-permute-start.13 = (bf16[256,1024]{1,0:T(8,128)(2,1)S(1)}, bf16[256,1024]{1,0:T(8,128)(2,1)S(1)}, u32[]{:S(2)}, u32[]{:S(2)}) collective-permute-start(bf16[256,1024]{1,0:T(8,128)(2,1)S(1)} %collective-permute-done.3.refs_4_), channel_id=1, source_target_pairs={{0,64},{1,65},{2,66},{3,67},{4,68},{5,69},{6,70},{7,71},{8,72},{9,... | collective-permute-start | bytes 1572872 | tf_op jit(solution)/shard_map/ppermute | solution.py:604
  75.9 3.1 %collective-permute-start.14 = (bf16[256,1024]{1,0:T(8,128)(2,1)}, bf16[256,1024]{1,0:T(8,128)(2,1)S(1)}, u32[]{:S(2)}, u32[]{:S(2)}) collective-permute-start(bf16[256,1024]{1,0:T(8,128)(2,1)} %collective-permute-done.5.refs_5_), channel_id=1, source_target_pairs={{0,64},{1,65},{2,66},{3,67},{4,68},{5,69},{6,70},{7,71},{8,72},{9,... | collective-permute-start | bytes 1572872 | tf_op jit(solution)/shard_map/ppermute | solution.py:604
  75.9 3.1 %collective-permute-start.15 = (bf16[256,1024]{1,0:T(8,128)(2,1)S(1)}, bf16[256,1024]{1,0:T(8,128)(2,1)S(1)}, u32[]{:S(2)}, u32[]{:S(2)}) collective-permute-start(bf16[256,1024]{1,0:T(8,128)(2,1)S(1)} %collective-permute-done.7.refs_6_), channel_id=1, source_target_pairs={{0,64},{1,65},{2,66},{3,67},{4,68},{5,69},{6,70},{7,71},{8,72},{9,... | collective-permute-start | bytes 1572872 | tf_op jit(solution)/shard_map/ppermute | solution.py:604
  76.4 3.3 %collective-permute-start.16 = (bf16[256,1024]{1,0:T(8,128)(2,1)S(1)}, bf16[256,1024]{1,0:T(8,128)(2,1)S(1)}, u32[]{:S(2)}, u32[]{:S(2)}) collective-permute-start(bf16[256,1024]{1,0:T(8,128)(2,1)S(1)} %collective-permute-done.8.refs_7_), channel_id=1, source_target_pairs={{0,64},{1,65},{2,66},{3,67},{4,68},{5,69},{6,70},{7,71},{8,72},{9,... | collective-permute-start | bytes 1572872 | tf_op jit(solution)/shard_map/ppermute | solution.py:604
  79.7 46.8 %copy-start.3 = (bf16[2,2,4096]{2,1,0:T(2,128)(2,1)S(1)}, bf16[2,2,4096]{2,1,0:T(2,128)(2,1)}, u32[]{:S(2)}) copy-start(bf16[2,2,4096]{2,1,0:T(2,128)(2,1)} %get-tuple-element.69) | copy-start | bytes 98308
  94.5 17.4 %all-to-all-start.2 = ((bf16[64,2,4,128]{3,2,1,0:T(4,128)(2,1)}), bf16[64,2,4,128]{3,2,1,0:T(4,128)(2,1)S(1)}, u32[]{:S(2)}, u32[]{:S(2)}) async-start(bf16[64,2,4,128]{3,2,1,0:T(4,128)(2,1)} %bitcast.11), calls=%async_computation.2 | async-start | bytes 262144 | tf_op jit(solution)/shard_map/all_to_all | solution.py:580
  112.7 19.6 %all-to-all-start.3 = ((bf16[64,2,4,128]{3,2,1,0:T(4,128)(2,1)}), bf16[64,2,4,128]{3,2,1,0:T(4,128)(2,1)S(1)}, u32[]{:S(2)}, u32[]{:S(2)}) async-start(bf16[64,2,4,128]{3,2,1,0:T(4,128)(2,1)} %shard_map.103), calls=%async_computation.3 | async-start | bytes 262144 | tf_op jit(solution)/shard_map/all_to_all | solution.py:580
  119.8 12.5 %collective-permute-start.17 = (bf16[2,16,2048]{2,1,0:T(8,128)(2,1)S(1)}, bf16[2,16,2048]{2,1,0:T(8,128)(2,1)S(1)}, u32[]{:S(2)}, u32[]{:S(2)}) collective-permute-start(bf16[2,16,2048]{2,1,0:T(8,128)(2,1)S(1)} %get-tuple-element.68), channel_id=1, source_target_pairs={{1,0},{2,1},{3,2},{4,3},{5,4},{6,5},{7,6},{8,7},{9,8},{10,9},{11,1... | collective-permute-start | bytes 393224 | tf_op jit(solution)/shard_map/ppermute | solution.py:586
  126.5 5.8 %collective-permute-start.18 = (bf16[2,2,4096]{2,1,0:T(2,128)(2,1)S(1)}, bf16[2,2,4096]{2,1,0:T(2,128)(2,1)S(1)}, u32[]{:S(2)}, u32[]{:S(2)}) collective-permute-start(bf16[2,2,4096]{2,1,0:T(2,128)(2,1)S(1)} %copy-done.3), channel_id=1, source_target_pairs={{1,0},{2,1},{3,2},{4,3},{5,4},{6,5},{7,6},{8,7},{9,8},{10,9},{11,1... | collective-permute-start | bytes 98312 | tf_op jit(solution)/shard_map/ppermute | solution.py:586

commit v7 on v6

--- a/solution.py
+++ b/solution.py
@@ -21,7 +21,7 @@
 WIDTH = D // 4
 BAND = C // 4
 BLOCK = 512
-PIECES = 8
+PIECES = 5
 QUARTERS = 4
 QUARTER = TILES // QUARTERS
 
@@ -59,7 +59,7 @@
     copies = [
         pltpu.make_async_copy(
             weight.at[pl.ds(pl.multiple_of(start + n * (BAND // 2), BAND // 2), BAND // 2), :],
-            band.at[n],
+            band.at[pl.ds(n * (BAND // 2), BAND // 2), :],
             sems.at[n],
         )
         for n in range(2)
@@ -247,7 +247,7 @@
     return total.T
 
 
-def slope_kernel(prod, near_mixed, conv_far, query_far, rate, gain, held, *refs):
+def slope_kernel(prod, near_mixed, conv_far, query_far, rate, gain, first_rows, held, *refs):
     pieces, refs = (refs[0:PIECES], refs[PIECES : 2 * PIECES]), refs[2 * PIECES :]
     query_slope, conv_slope, edge, states, conv, query, far_mixed, slope, prod_slope, ends, sems = refs
     dp, ctx = lax.axis_index("dp"), lax.axis_index("ctx")
@@ -263,10 +263,10 @@
     mixed = (near_mixed.at[0], near_mixed.at[1], far_mixed.at[0], far_mixed.at[1])
     first, along_x, along_z, last = bands(ctx)
     half = BAND // 2
-    begins = [start + at for start in (first, along_x, along_z, last) for at in (0, half)]
+    begins = (first, along_x, along_z, last, last + half)
 
     def rows_of(piece):
-        return pl.ds(pl.multiple_of(begins[piece], half), half)
+        return pl.ds(pl.multiple_of(begins[piece], half), pieces[0][piece].shape[0])
 
     for p in range(2):
 
@@ -357,7 +357,8 @@
             rounded = (value * query[s, :, lanes].astype(f32)).astype(bf16)
             conv_slope[s, :, lanes] = rounded
             x = rounded.astype(f32)
-            edge[s, :, lanes] = jnp.concatenate([direct[0:8], x[0:8]], 0).astype(bf16)
+            rows = [first_rows[s, :, tile_lanes(tile, branch)].astype(f32) for branch in range(2)]
+            edge[s, :, lanes] = jnp.concatenate([direct[0:2], x[0:2], *rows], 0).astype(bf16)
             for m in range(M):
                 state = x[56:64]
                 for i in range(6, -1, -1):
@@ -372,8 +373,8 @@
 
 def final_kernel(*refs):
     arriving, inner, query_slope, next_edge = refs[:4]
-    features, halos, next_rows, taps = refs[4:8], refs[8:10], refs[10:12], refs[12:15]
-    rate, res, grad_clean, grad_pert, reaching, ext, unit, grads, sems = refs[15:]
+    features, halos, taps = refs[4:8], refs[8:10], refs[10:13]
+    rate, res, grad_clean, grad_pert, reaching, ext, unit, grads, sems = refs[13:]
     quarter_at = pl.program_id(0)
     reaching[...] = arriving[...].astype(f32)
 
@@ -391,7 +392,7 @@
             totals = [inner[s, 8 * i : 8 * i + 8, lanes] for i in range(8)]
             after = jnp.zeros((8, LANES), f32)
             edge = next_edge[s, :, lanes].astype(f32)
-            passed = jnp.where(first, 0.0, row(edge, 8))
+            passed = jnp.where(first, 0.0, row(edge, 2))
             for m in range(M):
                 state = reaching[m, 0, s, pl.ds(tile, 1), :]
                 after = after + beyond[m] * (state - passed)
@@ -408,7 +409,7 @@
                 ext[slot, 8 : 8 + ROWS, :] = features[slot][:, lanes].astype(f32)
                 ext[slot, 6:8, :] = halos[branch][s, :, lanes].astype(f32)
                 ext[slot, 72:80, :] = jnp.zeros((8, LANES), f32)
-                ext[slot, 72:74, :] = next_rows[branch][s, :, lanes].astype(f32)
+                ext[slot, 72:74, :] = edge[4 + 2 * branch : 6 + 2 * branch]
                 tap = taps[branch + 1][:, lanes]
                 parts.append(
                     tap[0:1] * ext[slot, 8:80, :]
@@ -493,7 +494,7 @@
 def band_call(weight):
     return pl.pallas_call(
         band_kernel,
-        out_shape=pltpu.VMEM((2, BAND // 2, WIDTH), bf16),
+        out_shape=pltpu.VMEM((BAND, WIDTH), bf16),
         in_specs=[far()],
         out_specs=pl.BlockSpec(memory_space=pltpu.VMEM),
         scratch_shapes=[pltpu.SemaphoreType.DMA((2,))],
@@ -537,17 +538,17 @@
     )
 
 
-def slope_call(prod, near_mixed, conv, query, rate, gain, held, *pieces):
+def slope_call(prod, near_mixed, conv, query, rate, gain, first_rows, held, *pieces):
     near = pl.BlockSpec(memory_space=pltpu.VMEM)
     return pl.pallas_call(
         slope_kernel,
         out_shape=(
             pltpu.HBM((2, ROWS, C), f32),
             pltpu.HBM((2, ROWS, C), bf16),
-            array(2, 16, C, dtype=bf16),
+            array(2, 8, C, dtype=bf16),
             array(M, QUARTERS, 2, QUARTER, LANES, dtype=bf16),
         ),
-        in_specs=[near] * 2 + [far()] * 2 + [pl.BlockSpec()] * 2 + [near] * (1 + 2 * PIECES),
+        in_specs=[near] * 2 + [far()] * 2 + [pl.BlockSpec()] * 3 + [near] * (1 + 2 * PIECES),
         out_specs=(pl.BlockSpec(),) * 4,
         scratch_shapes=[
             pltpu.VMEM((2, ROWS, C), bf16),
@@ -560,7 +561,7 @@
         ],
         compiler_params=params(10),
     )(
-        in_vmem(prod), in_vmem(near_mixed), in_hbm(conv), in_hbm(query), rate, gain,
+        in_vmem(prod), in_vmem(near_mixed), in_hbm(conv), in_hbm(query), rate, gain, first_rows,
         in_vmem(held), *map(in_vmem, pieces),
     )
 
@@ -664,16 +665,13 @@
     ends = exchanged(ends)
     inner = within(gated, rate, res, False, 0, QUARTERS)
     inner, band = tied(inner, band)
-    upper, lower = band[0], band[1]
-    upper_x, upper_z = swapped(upper, "x"), swapped(upper, "z")
-    lower_x, lower_z = swapped(lower, "x"), swapped(lower, "z")
+    band_x, band_z = swapped(band, "x"), swapped(band, "z")
     ends, inner = tied(ends, inner)
     reaching = exchanged(scan(ends, own_rate, False)).reshape(*state_shape, 3, QUARTER, LANES)
-    reaching, upper_x, upper_z, lower_x, lower_z = tied(
-        reaching, upper_x, upper_z, lower_x, lower_z
-    )
-    last_x, last_z = swapped(upper_z, "x"), swapped(lower_x, "z")
-    far_pieces = [upper, lower, upper_x, lower_x, upper_z, lower_z]
+    reaching, band_x, band_z = tied(reaching, band_x, band_z)
+    half = BAND // 2
+    last_x, last_z = swapped(band_z[:half], "x"), swapped(band_x[half:], "z")
+    far_pieces = [band, band_x, band_z]
     core_pieces = [swapped(piece, "core") for piece in far_pieces]
 
     prod, conv, near_mixed, held = mix_call(
@@ -683,23 +681,22 @@
     far_pieces += [last_x, last_z]
     core_pieces += [swapped(last_x, "core"), swapped(last_z, "core")]
     query_slope, conv_slope, edge, ends = slope_call(
-        prod, near_mixed, conv, query, rate, gain, held, *far_pieces, *core_pieces
+        prod, near_mixed, conv, query, rate, gain, first_rows, held, *far_pieces, *core_pieces
     )
 
     ends = exchanged(ends)
     inner = within(conv_slope, rate, res, True, 0, QUARTERS)
-    ends, inner, edge, first_rows = tied(ends, inner, edge, first_rows)
-    next_edge, first_rows = passed_along(edge, -1), passed_along(first_rows, -1)
+    ends, inner, edge = tied(ends, inner, edge)
+    next_edge = passed_along(edge, -1)
     reaching = exchanged(scan(ends, own_rate, True)).reshape(*state_shape, 2, QUARTER, LANES)
 
     grads = pl.pallas_call(
         final_kernel,
         out_shape=(array(ROWS, 3 * C, dtype=bf16), array(ROWS, 3 * C, dtype=bf16)),
         grid=(QUARTERS,),
-        in_specs=[quarter_states(2), quarter(2, ROWS), quarter(2, ROWS), quarter(2, 16)]
+        in_specs=[quarter_states(2), quarter(2, ROWS), quarter(2, ROWS), quarter(2, 8)]
         + [quarter(ROWS, branch=b) for _ in range(2) for b in (1, 2)]
         + [quarter(3, 2, branch=b) for b in (1, 2)]
-        + [quarter(2, 2, branch=b) for b in (0, 1)]
         + [quarter(3, branch=b) for b in range(3)]
         + [quarter(M), quarter(M)],
         out_specs=(far(), far()),
@@ -713,7 +710,7 @@
         compiler_params=params(16),
     )(
         reaching, *map(in_hbm, (inner, query_slope)), next_edge,
-        *map(in_hbm, (clean,) * 2 + (pert,) * 2), *(halo,) * 2, *(first_rows,) * 2,
+        *map(in_hbm, (clean,) * 2 + (pert,) * 2), *(halo,) * 2,
         *map(in_hbm, (short_taps,) * 3 + (rate, res)),
     )
     return grads[0][None], grads[1][None]

time: 139 us -> 137 us (0.986); the launches traced: 139 us -> 135 us
  starting transfers between devices: 44.8 us -> 38.5 us
    ppermute x16 -> x11, starting transfers between devices: 9.5 us -> 3.96 us  [swapped(): lax.ppermute(value, ('dp', 'ctx'), [(device, partner(device, kind)) for d...]
    all_to_all x3, waiting for transfers between devices: 4.2 us -> 6.96 us  [exchanged(): return lax.all_to_all(flat, 'ctx', split_axis=0, concat_axis=0, tiled=True)]
    ppermute x3 -> x2, starting transfers between devices: 12.8 us -> 10.1 us  [passed_along(): lax.ppermute(value, 'ctx', [(source, source + steps) for source in range(...]
    all_to_all x3, starting transfers between devices: 22.5 us -> 24.5 us  [exchanged(): return lax.all_to_all(flat, 'ctx', split_axis=0, concat_axis=0, tiled=True)]
    ppermute x3 -> x2, waiting for transfers between devices: 10.9 us -> 9.7 us  [passed_along(): lax.ppermute(value, 'ctx', [(source, source + steps) for source in range(...]
    ppermute x16 -> x11, waiting for transfers between devices: 8.07 us -> 7.59 us  [swapped(): lax.ppermute(value, ('dp', 'ctx'), [(device, partner(device, kind)) for d...]
  transfers between devices with their start and end apart: 22 -> 16, of which waited for: 8 -> 9; matrix products, arithmetic and copies ran while one was open for 0% -> 0% of each run, Pallas kernels for 20% -> 20%
where the time goes in v7:
time: 137 us; the launch traced here: 135 us
  Pallas kernels  50.9 us (37%)
  starting transfers between devices  38.5 us (28%)
  waiting for transfers between devices  24.2 us (18%)
  blocking collectives  20.1 us (15%)
    all_to_all x3, starting transfers between devices, exchanged(): return lax.all_to_all(flat, 'ctx', split_axis=0, concat_axis=0, tiled=True)  24.5 us
    all_to_all x1, blocking collectives, exchanged(): return lax.all_to_all(flat, 'ctx', split_axis=0, concat_axis=0, tiled=True)  20.1 us
    pallas_call x1, Pallas kernels, slope_call(): pl.pallas_call(slope_kernel, out_shape=(pltpu.HBM((2, ROWS, C), f32), plt...  15.1 us
    pallas_call x2, Pallas kernels, within(): pl.pallas_call(functools.partial(within_kernel, streams, reverse), out_sh...  13.4 us
    ppermute x2, starting transfers between devices, passed_along(): lax.ppermute(value, 'ctx', [(source, source + steps) for source in range(...  10.1 us
    ppermute x2, waiting for transfers between devices, passed_along(): lax.ppermute(value, 'ctx', [(source, source + steps) for source in range(...  9.7 us
    ppermute x11, waiting for transfers between devices, swapped(): lax.ppermute(value, ('dp', 'ctx'), [(device, partner(device, kind)) for d...  7.59 us
    all_to_all x3, waiting for transfers between devices, exchanged(): return lax.all_to_all(flat, 'ctx', split_axis=0, concat_axis=0, tiled=True)  6.96 us
  transfers between devices with their start and end apart: 16, of which 9 were waited for; matrix products, arithmetic and copies ran while one was open for 0% of the time, Pallas kernels for 20%

profile of v7, /device:TPU:24, one launch (start us, length us, event | category | flops | bytes accessed | tf_op | source)
XLA Modules:
  0.0 134.9 jit_solution(8450801982810794900)
XLA Ops:
  0.6 1.7 %shard_map.95 = (bf16[3,2,6144]{2,1,0:T(2,128)(2,1)S(1)}, bf16[2,2,4096]{2,1,0:T(2,128)(2,1)}) custom-call(bf16[64,6144]{1,0:T(8,128)(2,1)} %bitcast.28, bf16[64,6144]{1,0:T(8,128)(2,1)} %bitcast.35, bf16[64,6144]{1,0:T(8,128)(2,1)} %bitcast.42, bf16[64,6144]{1,0:T(8,128)(2,1)} %bitcast.29, bf16[64,6144]{1,0:T(8,128)(2,1)} %bitcast.36), custom_call_target="tpu_custom_call" | custom-call | tf_op jit(solution)/shard_map/pallas_call | solution.py:627
  2.3 3.4 %collective-permute-start = (bf16[3,2,6144]{2,1,0:T(2,128)(2,1)S(1)}, bf16[3,2,6144]{2,1,0:T(2,128)(2,1)S(1)}, u32[]{:S(2)}, u32[]{:S(2)}) collective-permute-start(bf16[3,2,6144]{2,1,0:T(2,128)(2,1)S(1)} %get-tuple-element.34), channel_id=1, source_target_pairs={{0,1},{1,2},{2,3},{3,4},{4,5},{5,6},{6,7},{7,8},{8,9},{9,10},{10,1... | collective-permute-start | bytes 221192 | tf_op jit(solution)/shard_map/ppermute | solution.py:587
  5.7 1.2 shard_map.96
  7.0 7.8 %collective-permute-done.refs_9_.refs_10_.refs_11_.refs_8_ = bf16[3,2,6144]{2,1,0:T(2,128)(2,1)S(1)} collective-permute-done((bf16[3,2,6144]{2,1,0:T(2,128)(2,1)S(1)}, bf16[3,2,6144]{2,1,0:T(2,128)(2,1)S(1)}, u32[]{:S(2)}, u32[]{:S(2)}) %collective-permute-start) | collective-permute-done | bytes 73760 | tf_op jit(solution)/shard_map/ppermute | solution.py:587
  14.8 6.4 %shard_map.97 = (bf16[3,64,2048]{2,1,0:T(8,128)(2,1)}, bf16[3,64,2048]{2,1,0:T(8,128)(2,1)}, f32[16,4,3,4,128]{4,3,2,1,0:T(4,128)}) custom-call(bf16[64,6144]{1,0:T(8,128)(2,1)} %bitcast.30, bf16[64,6144]{1,0:T(8,128)(2,1)} %bitcast.31, bf16[64,6144]{1,0:T(8,128)(2,1)} %bitcast.32, bf16[64,6144]{1,0:T(8,128)(2,1)} %bitcast.37, bf16[64,6144]{1,0:T(8,128)(2,1)} %bitcast.38, ...), custom_call_target="tpu_custom_call" | custom-call | tf_op jit(solution)/shard_map/pallas_call | solution.py:645
  21.2 0.0 copy-start.1
  21.2 8.0 %all-to-all-start = ((f32[64,3,4,128]{3,2,1,0:T(4,128)}), f32[64,3,4,128]{3,2,1,0:T(4,128)S(1)}, u32[]{:S(2)}, u32[]{:S(2)}) async-start(f32[64,3,4,128]{3,2,1,0:T(4,128)} %bitcast.46), calls=%async_computation | async-start | bytes 786432 | tf_op jit(solution)/shard_map/all_to_all | solution.py:581
  29.2 7.6 %shard_map.98.inner_far = f32[3,64,2048]{2,1,0:T(8,128)} custom-call(bf16[3,64,2048]{2,1,0:T(8,128)(2,1)} %get-tuple-element.38.data, f32[16,2048]{1,0:T(8,128)} %bitcast.14, f32[16,2048]{1,0:T(8,128)} %bitcast.19), custom_call_target="tpu_custom_call" | custom-call | flops 300000000 | bytes 2359296 | tf_op jit(solution)/shard_map/pallas_call | solution.py:474
  36.8 4.9 %collective-permute-done.1.refs_0_ = bf16[512,1024]{1,0:T(8,128)(2,1)} collective-permute-done((bf16[512,1024]{1,0:T(8,128)(2,1)S(1)}, bf16[512,1024]{1,0:T(8,128)(2,1)}, u32[]{:S(2)}, u32[]{:S(2)}) %collective-permute-start.1) | collective-permute-done | bytes 1048608 | tf_op jit(solution)/shard_map/ppermute | solution.py:605
  41.7 0.1 dynamic-slice.3
  41.8 1.6 %all-to-all-done.ends = f32[64,3,4,128]{3,2,1,0:T(4,128)S(1)} async-done(((f32[64,3,4,128]{3,2,1,0:T(4,128)}), f32[64,3,4,128]{3,2,1,0:T(4,128)S(1)}, u32[]{:S(2)}, u32[]{:S(2)}) %all-to-all-start) | async-done | bytes 393248 | tf_op jit(solution)/shard_map/all_to_all | solution.py:581
  43.4 0.1 shard_map.99
  43.5 20.1 %all_to_all.20 = bf16[64,3,4,128]{3,2,1,0:T(4,128)(2,1)S(1)} all-to-all(bf16[64,3,4,128]{3,2,1,0:T(4,128)(2,1)S(1)} %shard_map.99), channel_id=1, replica_groups=mesh['dp'=4,'ctx'=64] {'ctx'}, dimensions={0} | all-to-all | bytes 393216 | tf_op jit(solution)/shard_map/all_to_all | solution.py:581
  63.7 0.9 collective-permute-start.5
  64.6 2.0 %collective-permute-start.6 = (bf16[256,1024]{1,0:T(8,128)(2,1)S(1)}, bf16[256,1024]{1,0:T(8,128)(2,1)S(1)}, u32[]{:S(2)}, u32[]{:S(2)}) collective-permute-start(bf16[256,1024]{1,0:T(8,128)(2,1)S(1)} %slice.7), channel_id=1, source_target_pairs={{0,4},{1,5},{2,6},{3,7},{4,0},{5,1},{6,2},{7,3},{8,12},{9,13},{10,... | collective-permute-start | bytes 1572872 | tf_op jit(solution)/shard_map/ppermute | solution.py:605
  66.7 0.5 collective-permute-start.8
  67.2 6.1 %shard_map.100 = (bf16[192,2048]{1,0:T(8,128)(2,1)S(1)}, bf16[2,64,2048]{2,1,0:T(8,128)(2,1)}, f32[2,192,1024]{2,1,0:T(8,128)S(1)}, bf16[2,2048,1024]{2,1,0:T(8,128)(2,1)S(1)}) custom-call(bf16[16,4,3,4,128]{4,3,2,1,0:T(4,128)(2,1)S(1)} %bitcast.24, f32[3,64,2048]{2,1,0:T(8,128)} %shard_map.98.inner_far, bf16[3,64,2048]{2,1,0:T(8,128)(2,1)} %get-tuple-element.45.query_far, ...), custom_call_target="tpu_custom_call" | custom-call | flops 5000000000 | bytes 14000000 | tf_op jit(solution)/shard_map/pallas_call | solution.py:515
  73.4 0.6 collective-permute-done.6.refs_4_
  73.9 0.0 collective-permute-start.10
  73.9 0.5 collective-permute-start.11
  74.4 1.4 %collective-permute-done.10.refs_8_ = bf16[256,1024]{1,0:T(8,128)(2,1)S(1)} collective-permute-done((bf16[256,1024]{1,0:T(8,128)(2,1)S(1)}, bf16[256,1024]{1,0:T(8,128)(2,1)S(1)}, u32[]{:S(2)}, u32[]{:S(2)}) %collective-permute-start.10) | collective-permute-done | bytes 524320 | tf_op jit(solution)/shard_map/ppermute | solution.py:605
  75.8 0.7 collective-permute-done.11.refs_9_
  76.6 15.1 %shard_map.101 = (f32[2,64,2048]{2,1,0:T(8,128)}, bf16[2,64,2048]{2,1,0:T(8,128)(2,1)}, bf16[2,8,2048]{2,1,0:T(8,128)(2,1)S(1)}, bf16[16,4,2,4,128]{4,3,2,1,0:T(4,128)(2,1)}) custom-call(bf16[192,2048]{1,0:T(8,128)(2,1)S(1)} %get-tuple-element.50.prod, f32[2,192,1024]{2,1,0:T(8,128)S(1)} %get-tuple-element.51.near_mixed, ...), custom_call_target="tpu_custom_call" | custom-call | tf_op jit(solution)/shard_map/pallas_call | solution.py:543
  91.7 9.2 %all-to-all-start.2 = ((bf16[64,2,4,128]{3,2,1,0:T(4,128)(2,1)}), bf16[64,2,4,128]{3,2,1,0:T(4,128)(2,1)S(1)}, u32[]{:S(2)}, u32[]{:S(2)}) async-start(bf16[64,2,4,128]{3,2,1,0:T(4,128)(2,1)} %bitcast.9), calls=%async_computation.2 | async-start | bytes 262144 | tf_op jit(solution)/shard_map/all_to_all | solution.py:581
  100.9 5.8 %shard_map.102.refs_1_ = f32[2,64,2048]{2,1,0:T(8,128)} custom-call(bf16[2,64,2048]{2,1,0:T(8,128)(2,1)} %get-tuple-element.58.data, f32[16,2048]{1,0:T(8,128)} %bitcast.15, f32[16,2048]{1,0:T(8,128)} %bitcast.20), custom_call_target="tpu_custom_call" | custom-call | flops 200000000 | bytes 1572864 | tf_op jit(solution)/shard_map/pallas_call | solution.py:474
  106.7 4.1 %all-to-all-done.2.ends = bf16[64,2,4,128]{3,2,1,0:T(4,128)(2,1)S(1)} async-done(((bf16[64,2,4,128]{3,2,1,0:T(4,128)(2,1)}), bf16[64,2,4,128]{3,2,1,0:T(4,128)(2,1)S(1)}, u32[]{:S(2)}, u32[]{:S(2)}) %all-to-all-start.2) | async-done | bytes 131104 | tf_op jit(solution)/shard_map/all_to_all | solution.py:581
  110.8 0.8 shard_map.103
  111.6 7.2 %all-to-all-start.3 = ((bf16[64,2,4,128]{3,2,1,0:T(4,128)(2,1)}), bf16[64,2,4,128]{3,2,1,0:T(4,128)(2,1)S(1)}, u32[]{:S(2)}, u32[]{:S(2)}) async-start(bf16[64,2,4,128]{3,2,1,0:T(4,128)(2,1)} %shard_map.103), calls=%async_computation.3 | async-start | bytes 262144 | tf_op jit(solution)/shard_map/all_to_all | solution.py:581
  118.8 6.7 %collective-permute-start.12 = (bf16[2,8,2048]{2,1,0:T(8,128)(2,1)S(1)}, bf16[2,8,2048]{2,1,0:T(8,128)(2,1)S(1)}, u32[]{:S(2)}, u32[]{:S(2)}) collective-permute-start(bf16[2,8,2048]{2,1,0:T(8,128)(2,1)S(1)} %get-tuple-element.63), channel_id=1, source_target_pairs={{1,0},{2,1},{3,2},{4,3},{5,4},{6,5},{7,6},{8,7},{9,8},{10,9},{11,1... | collective-permute-start | bytes 196616 | tf_op jit(solution)/shard_map/ppermute | solution.py:587
  125.5 1.9 %collective-permute-done.12.refs_3_ = bf16[2,8,2048]{2,1,0:T(8,128)(2,1)S(1)} collective-permute-done((bf16[2,8,2048]{2,1,0:T(8,128)(2,1)S(1)}, bf16[2,8,2048]{2,1,0:T(8,128)(2,1)S(1)}, u32[]{:S(2)}, u32[]{:S(2)}) %collective-permute-start.12) | collective-permute-done | bytes 65568 | tf_op jit(solution)/shard_map/ppermute | solution.py:587
  127.4 1.3 all-to-all-done.3
  128.7 6.0 %shard_map.104 = (bf16[64,6144]{1,0:T(8,128)(2,1)}, bf16[64,6144]{1,0:T(8,128)(2,1)}) custom-call(bf16[16,4,2,4,128]{4,3,2,1,0:T(4,128)(2,1)S(1)} %bitcast.23, f32[2,64,2048]{2,1,0:T(8,128)} %shard_map.102.refs_1_, f32[2,64,2048]{2,1,0:T(8,128)} %get-tuple-element.62.refs_2_, bf16[2,8,2048]{2,1,0:T(8,128)(2,1)S(1)} %collective-permute-done.12.refs_3_, ...), custom_call_target="tpu_custom_call" | custom-call | tf_op jit(solution)/shard_map/pallas_call | solution.py:693
  (22 shorter events, 0.1 us)
Async XLA Ops:
  2.3 12.5 %collective-permute-start = (bf16[3,2,6144]{2,1,0:T(2,128)(2,1)S(1)}, bf16[3,2,6144]{2,1,0:T(2,128)(2,1)S(1)}, u32[]{:S(2)}, u32[]{:S(2)}) collective-permute-start(bf16[3,2,6144]{2,1,0:T(2,128)(2,1)S(1)} %get-tuple-element.34), channel_id=1, source_target_pairs={{0,1},{1,2},{2,3},{3,4},{4,5},{5,6},{6,7},{7,8},{8,9},{9,10},{10,1... | collective-permute-start | bytes 221192 | tf_op jit(solution)/shard_map/ppermute | solution.py:587
  14.8 52.4 %collective-permute-start.4 = (bf16[2048,1024]{1,0:T(8,128)(2,1)}, bf16[2048,1024]{1,0:T(8,128)(2,1)}, u32[]{:S(2)}, u32[]{:S(2)}) collective-permute-start(bf16[2048,1024]{1,0:T(8,128)(2,1)} %own_weight.1), channel_id=1, source_target_pairs={{0,64},{1,65},{2,66},{3,67},{4,68},{5,69},{6,70},{7,71},{8,72},{9,... | collective-permute-start | bytes 12582920 | tf_op jit(solution)/shard_map/ppermute | solution.py:605
  14.8 26.9 %collective-permute-start.1 = (bf16[512,1024]{1,0:T(8,128)(2,1)S(1)}, bf16[512,1024]{1,0:T(8,128)(2,1)}, u32[]{:S(2)}, u32[]{:S(2)}) collective-permute-start(bf16[512,1024]{1,0:T(8,128)(2,1)S(1)} %shard_map.96), channel_id=1, source_target_pairs={{0,160},{1,161},{2,162},{3,163},{4,164},{5,165},{6,166},{7,167},{8... | collective-permute-start | bytes 3145736 | tf_op jit(solution)/shard_map/ppermute | solution.py:605
  14.8 26.9 %copy-start = (f32[2048,16]{0,1:T(8,128)S(1)}, f32[2048,16]{0,1:T(8,128)}, u32[]{:S(2)}) copy-start(f32[2048,16]{0,1:T(8,128)} %param.13) | copy-start | bytes 393220
  21.2 46.1 %copy-start.1 = (f32[2048,16]{0,1:T(8,128)S(1)}, f32[2048,16]{0,1:T(8,128)}, u32[]{:S(2)}) copy-start(f32[2048,16]{0,1:T(8,128)} %param.12) | copy-start | bytes 393220
  21.2 22.2 %all-to-all-start = ((f32[64,3,4,128]{3,2,1,0:T(4,128)}), f32[64,3,4,128]{3,2,1,0:T(4,128)S(1)}, u32[]{:S(2)}, u32[]{:S(2)}) async-start(f32[64,3,4,128]{3,2,1,0:T(4,128)} %bitcast.46), calls=%async_computation | async-start | bytes 786432 | tf_op jit(solution)/shard_map/all_to_all | solution.py:581
  41.7 22.0 %collective-permute-start.2 = (bf16[512,1024]{1,0:T(8,128)(2,1)}, bf16[512,1024]{1,0:T(8,128)(2,1)S(1)}, u32[]{:S(2)}, u32[]{:S(2)}) collective-permute-start(bf16[512,1024]{1,0:T(8,128)(2,1)} %collective-permute-done.1.refs_0_), channel_id=1, source_target_pairs={{0,1},{1,0},{2,3},{3,2},{4,5},{5,4},{6,7},{7,6},{8,9},{9,8},{10,11... | collective-permute-start | bytes 3145736 | tf_op jit(solution)/shard_map/ppermute | solution.py:605
  41.7 22.0 %collective-permute-start.3 = (bf16[512,1024]{1,0:T(8,128)(2,1)}, bf16[512,1024]{1,0:T(8,128)(2,1)S(1)}, u32[]{:S(2)}, u32[]{:S(2)}) collective-permute-start(bf16[512,1024]{1,0:T(8,128)(2,1)} %collective-permute-done.1.refs_0_), channel_id=1, source_target_pairs={{0,4},{1,5},{2,6},{3,7},{4,0},{5,1},{6,2},{7,3},{8,12},{9,13},{10,... | collective-permute-start | bytes 3145736 | tf_op jit(solution)/shard_map/ppermute | solution.py:605
  63.7 9.6 %collective-permute-start.5 = (bf16[256,1024]{1,0:T(8,128)(2,1)S(1)}, bf16[256,1024]{1,0:T(8,128)(2,1)S(1)}, u32[]{:S(2)}, u32[]{:S(2)}) collective-permute-start(bf16[256,1024]{1,0:T(8,128)(2,1)S(1)} %slice.6), channel_id=1, source_target_pairs={{0,1},{1,0},{2,3},{3,2},{4,5},{5,4},{6,7},{7,6},{8,9},{9,8},{10,11... | collective-permute-start | bytes 1572872 | tf_op jit(solution)/shard_map/ppermute | solution.py:605
  64.6 9.3 %collective-permute-start.6 = (bf16[256,1024]{1,0:T(8,128)(2,1)S(1)}, bf16[256,1024]{1,0:T(8,128)(2,1)S(1)}, u32[]{:S(2)}, u32[]{:S(2)}) collective-permute-start(bf16[256,1024]{1,0:T(8,128)(2,1)S(1)} %slice.7), channel_id=1, source_target_pairs={{0,4},{1,5},{2,6},{3,7},{4,0},{5,1},{6,2},{7,3},{8,12},{9,13},{10,... | collective-permute-start | bytes 1572872 | tf_op jit(solution)/shard_map/ppermute | solution.py:605
  66.7 7.7 %collective-permute-start.7 = (bf16[512,1024]{1,0:T(8,128)(2,1)}, bf16[512,1024]{1,0:T(8,128)(2,1)S(1)}, u32[]{:S(2)}, u32[]{:S(2)}) collective-permute-start(bf16[512,1024]{1,0:T(8,128)(2,1)} %collective-permute-done.1.refs_0_), channel_id=1, source_target_pairs={{0,64},{1,65},{2,66},{3,67},{4,68},{5,69},{6,70},{7,71},{8,72},{9,... | collective-permute-start | bytes 3145736 | tf_op jit(solution)/shard_map/ppermute | solution.py:605
  66.7 7.7 %collective-permute-start.8 = (bf16[512,1024]{1,0:T(8,128)(2,1)S(1)}, bf16[512,1024]{1,0:T(8,128)(2,1)S(1)}, u32[]{:S(2)}, u32[]{:S(2)}) collective-permute-start(bf16[512,1024]{1,0:T(8,128)(2,1)S(1)} %collective-permute-done.2.refs_1_), channel_id=1, source_target_pairs={{0,64},{1,65},{2,66},{3,67},{4,68},{5,69},{6,70},{7,71},{8,72},{9,... | collective-permute-start | bytes 3145736 | tf_op jit(solution)/shard_map/ppermute | solution.py:605
  67.2 7.2 %collective-permute-start.9 = (bf16[512,1024]{1,0:T(8,128)(2,1)S(1)}, bf16[512,1024]{1,0:T(8,128)(2,1)S(1)}, u32[]{:S(2)}, u32[]{:S(2)}) collective-permute-start(bf16[512,1024]{1,0:T(8,128)(2,1)S(1)} %collective-permute-done.3.refs_2_), channel_id=1, source_target_pairs={{0,64},{1,65},{2,66},{3,67},{4,68},{5,69},{6,70},{7,71},{8,72},{9,... | collective-permute-start | bytes 3145736 | tf_op jit(solution)/shard_map/ppermute | solution.py:605
  67.2 9.4 %copy-start.2 = (bf16[2,2,4096]{2,1,0:T(2,128)(2,1)S(1)}, bf16[2,2,4096]{2,1,0:T(2,128)(2,1)}, u32[]{:S(2)}) copy-start(bf16[2,2,4096]{2,1,0:T(2,128)(2,1)} %get-tuple-element.53.first_rows) | copy-start | bytes 98308
  67.2 9.4 %copy-start.3 = (f32[4096]{0:T(1024)S(1)}, f32[4096]{0:T(1024)}, u32[]{:S(2)}) copy-start(f32[4096]{0:T(1024)} %param.15) | copy-start | bytes 49156
  73.9 1.9 %collective-permute-start.10 = (bf16[256,1024]{1,0:T(8,128)(2,1)S(1)}, bf16[256,1024]{1,0:T(8,128)(2,1)S(1)}, u32[]{:S(2)}, u32[]{:S(2)}) collective-permute-start(bf16[256,1024]{1,0:T(8,128)(2,1)S(1)} %collective-permute-done.5.refs_3_), channel_id=1, source_target_pairs={{0,64},{1,65},{2,66},{3,67},{4,68},{5,69},{6,70},{7,71},{8,72},{9,... | collective-permute-start | bytes 1572872 | tf_op jit(solution)/shard_map/ppermute | solution.py:605
  73.9 2.7 %collective-permute-start.11 = (bf16[256,1024]{1,0:T(8,128)(2,1)S(1)}, bf16[256,1024]{1,0:T(8,128)(2,1)S(1)}, u32[]{:S(2)}, u32[]{:S(2)}) collective-permute-start(bf16[256,1024]{1,0:T(8,128)(2,1)S(1)} %collective-permute-done.6.refs_4_), channel_id=1, source_target_pairs={{0,64},{1,65},{2,66},{3,67},{4,68},{5,69},{6,70},{7,71},{8,72},{9,... | collective-permute-start | bytes 1572872 | tf_op jit(solution)/shard_map/ppermute | solution.py:605
  91.7 19.2 %all-to-all-start.2 = ((bf16[64,2,4,128]{3,2,1,0:T(4,128)(2,1)}), bf16[64,2,4,128]{3,2,1,0:T(4,128)(2,1)S(1)}, u32[]{:S(2)}, u32[]{:S(2)}) async-start(bf16[64,2,4,128]{3,2,1,0:T(4,128)(2,1)} %bitcast.9), calls=%async_computation.2 | async-start | bytes 262144 | tf_op jit(solution)/shard_map/all_to_all | solution.py:581
  111.6 17.1 %all-to-all-start.3 = ((bf16[64,2,4,128]{3,2,1,0:T(4,128)(2,1)}), bf16[64,2,4,128]{3,2,1,0:T(4,128)(2,1)S(1)}, u32[]{:S(2)}, u32[]{:S(2)}) async-start(bf16[64,2,4,128]{3,2,1,0:T(4,128)(2,1)} %shard_map.103), calls=%async_computation.3 | async-start | bytes 262144 | tf_op jit(solution)/shard_map/all_to_all | solution.py:581
  118.8 8.6 %collective-permute-start.12 = (bf16[2,8,2048]{2,1,0:T(8,128)(2,1)S(1)}, bf16[2,8,2048]{2,1,0:T(8,128)(2,1)S(1)}, u32[]{:S(2)}, u32[]{:S(2)}) collective-permute-start(bf16[2,8,2048]{2,1,0:T(8,128)(2,1)S(1)} %get-tuple-element.63), channel_id=1, source_target_pairs={{1,0},{2,1},{3,2},{4,3},{5,4},{6,5},{7,6},{8,7},{9,8},{10,9},{11,1... | collective-permute-start | bytes 196616 | tf_op jit(solution)/shard_map/ppermute | solution.py:587

commit v8 on v7

--- a/solution.py
+++ b/solution.py
@@ -247,7 +247,34 @@
     return total.T
 
 
-def slope_kernel(prod, near_mixed, conv_far, query_far, rate, gain, first_rows, held, *refs):
+def piece_starts(ctx):
+    first, along_x, along_z, last = bands(ctx)
+    return first, along_x, along_z, last, last + BAND // 2
+
+
+def mix_pieces(prod, pieces, starts, begun, mixed):
+    def mix(t, carry):
+        columns = pl.ds(pl.multiple_of(t * BLOCK, BLOCK), BLOCK)
+        total = 0.0 if begun is None else begun[:, columns]
+        for piece, start in zip(pieces, starts):
+            rows = pl.ds(pl.multiple_of(start, BAND // 2), piece.shape[0])
+            total = total + jnp.dot(prod[:, rows], piece[:, columns], preferred_element_type=f32)
+        mixed[:, columns] = total
+        return carry
+
+    lax.fori_loop(0, WIDTH // BLOCK, mix, 0)
+
+
+def far_kernel(prod, *refs):
+    pieces, mixed = (refs[:3], refs[3:6]), refs[6]
+    starts = piece_starts(lax.axis_index("ctx"))
+    for p in range(2):
+        mix_pieces(prod, pieces[p], starts, None, mixed.at[p])
+
+
+def slope_kernel(
+    prod, near_mixed, begun, conv_far, query_far, rate, gain, first_rows, held, *refs
+):
     pieces, refs = (refs[0:PIECES], refs[PIECES : 2 * PIECES]), refs[2 * PIECES :]
     query_slope, conv_slope, edge, states, conv, query, far_mixed, slope, prod_slope, ends, sems = refs
     dp, ctx = lax.axis_index("dp"), lax.axis_index("ctx")
@@ -261,26 +288,13 @@
     shard = (2 * high + core, 2 * high + 1 - core, 2 * (1 - high) + core, 2 * (1 - high) + 1 - core)
     shards, width = 4, WIDTH
     mixed = (near_mixed.at[0], near_mixed.at[1], far_mixed.at[0], far_mixed.at[1])
-    first, along_x, along_z, last = bands(ctx)
-    half = BAND // 2
-    begins = (first, along_x, along_z, last, last + half)
+    starts = piece_starts(ctx)
 
     def rows_of(piece):
-        return pl.ds(pl.multiple_of(begins[piece], half), pieces[0][piece].shape[0])
+        return pl.ds(pl.multiple_of(starts[piece], BAND // 2), pieces[0][piece].shape[0])
 
     for p in range(2):
-
-        def mix(t, carry):
-            columns = pl.ds(pl.multiple_of(t * BLOCK, BLOCK), BLOCK)
-            total = jnp.zeros((3 * ROWS, BLOCK), f32)
-            for n, piece in enumerate(pieces[p]):
-                total = total + jnp.dot(
-                    prod[:, rows_of(n)], piece[:, columns], preferred_element_type=f32
-                )
-            far_mixed[p, :, columns] = total
-            return carry
-
-        lax.fori_loop(0, width // BLOCK, mix, 0)
+        mix_pieces(prod, pieces[p][3:], starts[3:], begun.at[p], far_mixed.at[p])
 
     squares = jnp.zeros((3 * ROWS, LANES), f32)
     for p in range(shards):
@@ -538,7 +552,21 @@
     )
 
 
-def slope_call(prod, near_mixed, conv, query, rate, gain, first_rows, held, *pieces):
+def far_call(prod, *pieces):
+    near = pl.BlockSpec(memory_space=pltpu.VMEM)
+    return pl.pallas_call(
+        far_kernel,
+        out_shape=pltpu.VMEM((2, 3 * ROWS, WIDTH), f32),
+        in_specs=[near] * 7,
+        out_specs=near,
+        compiler_params=params(4),
+        cost_estimate=pl.CostEstimate(
+            flops=2_400_000_000, bytes_accessed=10_000_000, transcendentals=0
+        ),
+    )(*map(in_vmem, (prod, *pieces)))
+
+
+def slope_call(prod, near_mixed, begun, conv, query, rate, gain, first_rows, held, *pieces):
     near = pl.BlockSpec(memory_space=pltpu.VMEM)
     return pl.pallas_call(
         slope_kernel,
@@ -548,7 +576,7 @@
             array(2, 8, C, dtype=bf16),
             array(M, QUARTERS, 2, QUARTER, LANES, dtype=bf16),
         ),
-        in_specs=[near] * 2 + [far()] * 2 + [pl.BlockSpec()] * 3 + [near] * (1 + 2 * PIECES),
+        in_specs=[near] * 3 + [far()] * 2 + [pl.BlockSpec()] * 3 + [near] * (1 + 2 * PIECES),
         out_specs=(pl.BlockSpec(),) * 4,
         scratch_shapes=[
             pltpu.VMEM((2, ROWS, C), bf16),
@@ -561,8 +589,8 @@
         ],
         compiler_params=params(10),
     )(
-        in_vmem(prod), in_vmem(near_mixed), in_hbm(conv), in_hbm(query), rate, gain, first_rows,
-        in_vmem(held), *map(in_vmem, pieces),
+        in_vmem(prod), in_vmem(near_mixed), in_vmem(begun), in_hbm(conv), in_hbm(query), rate, gain,
+        first_rows, in_vmem(held), *map(in_vmem, pieces),
     )
 
 
@@ -678,10 +706,12 @@
         reaching, inner, query, rate, res, out_weight, core_weight
     )
     prod, last_x, last_z = tied(prod, last_x, last_z)
+    begun = far_call(prod, *far_pieces, *core_pieces)
     far_pieces += [last_x, last_z]
     core_pieces += [swapped(last_x, "core"), swapped(last_z, "core")]
     query_slope, conv_slope, edge, ends = slope_call(
-        prod, near_mixed, conv, query, rate, gain, first_rows, held, *far_pieces, *core_pieces
+        prod, near_mixed, begun, conv, query, rate, gain, first_rows, held, *far_pieces,
+        *core_pieces,
     )
 
     ends = exchanged(ends)

time: 137 us -> 137 us (level)
  blocking collectives: 20.1 us -> 0 us
  waiting for transfers between devices: 24.2 us -> 34.1 us
  starting transfers between devices: 38.5 us -> 46.5 us
  Pallas kernels: 50.9 us -> 54 us
    all_to_all x1 -> x0, blocking collectives: 20.1 us -> none  [exchanged(): return lax.all_to_all(flat, 'ctx', split_axis=0, concat_axis=0, tiled=True)]
    all_to_all x3 -> x4, waiting for transfers between devices: 6.96 us -> 18.4 us  [exchanged(): return lax.all_to_all(flat, 'ctx', split_axis=0, concat_axis=0, tiled=True)]
    all_to_all x3 -> x4, starting transfers between devices: 24.5 us -> 30.5 us  [exchanged(): return lax.all_to_all(flat, 'ctx', split_axis=0, concat_axis=0, tiled=True)]
    pallas_call x0 -> x1, Pallas kernels: none -> 3.48 us  [far_call(): pl.pallas_call(far_kernel, out_shape=pltpu.VMEM((2, 3 * ROWS, WIDTH), f32...]
    ppermute x11, starting transfers between devices: 3.96 us -> 5.9 us  [swapped(): lax.ppermute(value, ('dp', 'ctx'), [(device, partner(device, kind)) for d...]
    ppermute x11, waiting for transfers between devices: 7.59 us -> 6.04 us  [swapped(): lax.ppermute(value, ('dp', 'ctx'), [(device, partner(device, kind)) for d...]
  transfers between devices with their start and end apart: 16 -> 17, of which waited for: 9 -> 9; matrix products, arithmetic and copies ran while one was open for 0% -> 0% of each run, Pallas kernels for 20% -> 23%
where the time goes in v8:
time: 137 us; the launch traced here: 136 us
  Pallas kernels  54 us (39%)
  starting transfers between devices  46.5 us (34%)
  waiting for transfers between devices  34.1 us (25%)
    all_to_all x4, starting transfers between devices, exchanged(): return lax.all_to_all(flat, 'ctx', split_axis=0, concat_axis=0, tiled=True)  30.5 us
    all_to_all x4, waiting for transfers between devices, exchanged(): return lax.all_to_all(flat, 'ctx', split_axis=0, concat_axis=0, tiled=True)  18.4 us
    pallas_call x1, Pallas kernels, slope_call(): pl.pallas_call(slope_kernel, out_shape=(pltpu.HBM((2, ROWS, C), f32), plt...  14 us
    pallas_call x2, Pallas kernels, within(): pl.pallas_call(functools.partial(within_kernel, streams, reverse), out_sh...  13.4 us
    ppermute x2, starting transfers between devices, passed_along(): lax.ppermute(value, 'ctx', [(source, source + steps) for source in range(...  10.1 us
    ppermute x2, waiting for transfers between devices, passed_along(): lax.ppermute(value, 'ctx', [(source, source + steps) for source in range(...  9.7 us
    pallas_call x1, Pallas kernels, per_device(): pl.pallas_call(gate_kernel, out_shape=(pltpu.HBM((3, ROWS, C), bf16), plt...  6.34 us
    pallas_call x1, Pallas kernels, mix_call(): pl.pallas_call(mix_kernel, out_shape=(pltpu.VMEM((3 * ROWS, C), bf16), pl...  6.11 us
  transfers between devices with their start and end apart: 17, of which 9 were waited for; matrix products, arithmetic and copies ran while one was open for 0% of the time, Pallas kernels for 23%

profile of v8, /device:TPU:24, one launch (start us, length us, event | category | flops | bytes accessed | tf_op | source)
XLA Modules:
  0.0 135.7 jit_solution(15821371840577188144)
XLA Ops:
  0.6 1.7 %shard_map.95 = (bf16[3,2,6144]{2,1,0:T(2,128)(2,1)S(1)}, bf16[2,2,4096]{2,1,0:T(2,128)(2,1)}) custom-call(bf16[64,6144]{1,0:T(8,128)(2,1)} %bitcast.28, bf16[64,6144]{1,0:T(8,128)(2,1)} %bitcast.35, bf16[64,6144]{1,0:T(8,128)(2,1)} %bitcast.42, bf16[64,6144]{1,0:T(8,128)(2,1)} %bitcast.29, bf16[64,6144]{1,0:T(8,128)(2,1)} %bitcast.36), custom_call_target="tpu_custom_call" | custom-call | tf_op jit(solution)/shard_map/pallas_call | solution.py:655
  2.3 3.4 %collective-permute-start = (bf16[3,2,6144]{2,1,0:T(2,128)(2,1)S(1)}, bf16[3,2,6144]{2,1,0:T(2,128)(2,1)S(1)}, u32[]{:S(2)}, u32[]{:S(2)}) collective-permute-start(bf16[3,2,6144]{2,1,0:T(2,128)(2,1)S(1)} %get-tuple-element.34), channel_id=1, source_target_pairs={{0,1},{1,2},{2,3},{3,4},{4,5},{5,6},{6,7},{7,8},{8,9},{9,10},{10,1... | collective-permute-start | bytes 221192 | tf_op jit(solution)/shard_map/ppermute | solution.py:615
  5.7 1.2 shard_map.96
  7.0 7.8 %collective-permute-done.refs_9_.refs_10_.refs_11_.refs_8_ = bf16[3,2,6144]{2,1,0:T(2,128)(2,1)S(1)} collective-permute-done((bf16[3,2,6144]{2,1,0:T(2,128)(2,1)S(1)}, bf16[3,2,6144]{2,1,0:T(2,128)(2,1)S(1)}, u32[]{:S(2)}, u32[]{:S(2)}) %collective-permute-start) | collective-permute-done | bytes 73760 | tf_op jit(solution)/shard_map/ppermute | solution.py:615
  14.8 6.3 %shard_map.97 = (bf16[3,64,2048]{2,1,0:T(8,128)(2,1)}, bf16[3,64,2048]{2,1,0:T(8,128)(2,1)}, f32[16,4,3,4,128]{4,3,2,1,0:T(4,128)}) custom-call(bf16[64,6144]{1,0:T(8,128)(2,1)} %bitcast.30, bf16[64,6144]{1,0:T(8,128)(2,1)} %bitcast.31, bf16[64,6144]{1,0:T(8,128)(2,1)} %bitcast.32, bf16[64,6144]{1,0:T(8,128)(2,1)} %bitcast.37, bf16[64,6144]{1,0:T(8,128)(2,1)} %bitcast.38, ...), custom_call_target="tpu_custom_call" | custom-call | tf_op jit(solution)/shard_map/pallas_call | solution.py:673
  21.2 8.0 %all-to-all-start = ((f32[64,3,4,128]{3,2,1,0:T(4,128)}), f32[64,3,4,128]{3,2,1,0:T(4,128)S(1)}, u32[]{:S(2)}, u32[]{:S(2)}) async-start(f32[64,3,4,128]{3,2,1,0:T(4,128)} %bitcast.46), calls=%async_computation | async-start | bytes 786432 | tf_op jit(solution)/shard_map/all_to_all | solution.py:609
  29.2 7.6 %shard_map.98.inner_far = f32[3,64,2048]{2,1,0:T(8,128)} custom-call(bf16[3,64,2048]{2,1,0:T(8,128)(2,1)} %get-tuple-element.38.data, f32[16,2048]{1,0:T(8,128)} %bitcast.14, f32[16,2048]{1,0:T(8,128)} %bitcast.19), custom_call_target="tpu_custom_call" | custom-call | flops 300000000 | bytes 2359296 | tf_op jit(solution)/shard_map/pallas_call | solution.py:488
  36.8 4.9 %collective-permute-done.1.refs_0_ = bf16[512,1024]{1,0:T(8,128)(2,1)} collective-permute-done((bf16[512,1024]{1,0:T(8,128)(2,1)S(1)}, bf16[512,1024]{1,0:T(8,128)(2,1)}, u32[]{:S(2)}, u32[]{:S(2)}) %collective-permute-start.1) | collective-permute-done | bytes 1048608 | tf_op jit(solution)/shard_map/ppermute | solution.py:633
  41.8 1.6 %all-to-all-done.ends = f32[64,3,4,128]{3,2,1,0:T(4,128)S(1)} async-done(((f32[64,3,4,128]{3,2,1,0:T(4,128)}), f32[64,3,4,128]{3,2,1,0:T(4,128)S(1)}, u32[]{:S(2)}, u32[]{:S(2)}) %all-to-all-start) | async-done | bytes 393248 | tf_op jit(solution)/shard_map/all_to_all | solution.py:609
  43.4 0.8 shard_map.99
  44.2 8.1 %all-to-all-start.1 = ((bf16[64,3,4,128]{3,2,1,0:T(4,128)(2,1)}), bf16[64,3,4,128]{3,2,1,0:T(4,128)(2,1)S(1)}, u32[]{:S(2)}, u32[]{:S(2)}) async-start(bf16[64,3,4,128]{3,2,1,0:T(4,128)(2,1)} %shard_map.99), calls=%async_computation.1 | async-start | bytes 393216 | tf_op jit(solution)/shard_map/all_to_all | solution.py:609
  52.3 0.1 collective-permute-start.7
  52.4 11.3 %all-to-all-done.1 = bf16[64,3,4,128]{3,2,1,0:T(4,128)(2,1)S(1)} async-done(((bf16[64,3,4,128]{3,2,1,0:T(4,128)(2,1)}), bf16[64,3,4,128]{3,2,1,0:T(4,128)(2,1)S(1)}, u32[]{:S(2)}, u32[]{:S(2)}) %all-to-all-start.1) | async-done | bytes 196640 | tf_op jit(solution)/shard_map/all_to_all | solution.py:609
  63.7 0.5 collective-permute-start.9
  64.3 0.9 collective-permute-start.5
  65.2 2.0 %collective-permute-start.6 = (bf16[256,1024]{1,0:T(8,128)(2,1)S(1)}, bf16[256,1024]{1,0:T(8,128)(2,1)S(1)}, u32[]{:S(2)}, u32[]{:S(2)}) collective-permute-start(bf16[256,1024]{1,0:T(8,128)(2,1)S(1)} %slice.7), channel_id=1, source_target_pairs={{0,4},{1,5},{2,6},{3,7},{4,0},{5,1},{6,2},{7,3},{8,12},{9,13},{10,... | collective-permute-start | bytes 1572872 | tf_op jit(solution)/shard_map/ppermute | solution.py:633
  67.1 6.1 %shard_map.100 = (bf16[192,2048]{1,0:T(8,128)(2,1)S(1)}, bf16[2,64,2048]{2,1,0:T(8,128)(2,1)}, f32[2,192,1024]{2,1,0:T(8,128)S(1)}, bf16[2,2048,1024]{2,1,0:T(8,128)(2,1)S(1)}) custom-call(bf16[16,4,3,4,128]{4,3,2,1,0:T(4,128)(2,1)S(1)} %bitcast.24, f32[3,64,2048]{2,1,0:T(8,128)} %shard_map.98.inner_far, bf16[3,64,2048]{2,1,0:T(8,128)(2,1)} %get-tuple-element.45.query_far, ...), custom_call_target="tpu_custom_call" | custom-call | flops 5000000000 | bytes 14000000 | tf_op jit(solution)/shard_map/pallas_call | solution.py:529
  73.3 0.3 collective-permute-done.5.refs_3_
  73.6 0.8 collective-permute-done.6.refs_4_
  74.4 2.2 %collective-permute-start.10 = (bf16[256,1024]{1,0:T(8,128)(2,1)S(1)}, bf16[256,1024]{1,0:T(8,128)(2,1)S(1)}, u32[]{:S(2)}, u32[]{:S(2)}) collective-permute-start(bf16[256,1024]{1,0:T(8,128)(2,1)S(1)} %collective-permute-done.5.refs_3_), channel_id=1, source_target_pairs={{0,64},{1,65},{2,66},{3,67},{4,68},{5,69},{6,70},{7,71},{8,72},{9,... | collective-permute-start | bytes 1572872 | tf_op jit(solution)/shard_map/ppermute | solution.py:633
  76.5 0.3 collective-permute-start.11
  76.8 3.5 %shard_map.101.begun = f32[2,192,1024]{2,1,0:T(8,128)S(1)} custom-call(bf16[192,2048]{1,0:T(8,128)(2,1)S(1)} %get-tuple-element.50.prod, bf16[512,1024]{1,0:T(8,128)(2,1)} %collective-permute-done.1.refs_0_, bf16[512,1024]{1,0:T(8,128)(2,1)S(1)} %collective-permute-done.2.refs_1_, bf16[512,1024]{1,0:T(8,128)(2,1)S(1)} %collective-permute-done.3.refs_2_, ...), custom_call_target="tpu_custom_call" | custom-call | flops 2400000000 | bytes 10000000 | tf_op jit(solution)/shard_map/pallas_call | solution.py:557
  80.4 14.0 %shard_map.102 = (f32[2,64,2048]{2,1,0:T(8,128)}, bf16[2,64,2048]{2,1,0:T(8,128)(2,1)}, bf16[2,8,2048]{2,1,0:T(8,128)(2,1)S(1)}, bf16[16,4,2,4,128]{4,3,2,1,0:T(4,128)(2,1)}) custom-call(bf16[192,2048]{1,0:T(8,128)(2,1)S(1)} %get-tuple-element.50.prod, f32[2,192,1024]{2,1,0:T(8,128)S(1)} %get-tuple-element.51.near_mixed, ...), custom_call_target="tpu_custom_call" | custom-call | tf_op jit(solution)/shard_map/pallas_call | solution.py:571
  94.4 7.3 %all-to-all-start.2 = ((bf16[64,2,4,128]{3,2,1,0:T(4,128)(2,1)}), bf16[64,2,4,128]{3,2,1,0:T(4,128)(2,1)S(1)}, u32[]{:S(2)}, u32[]{:S(2)}) async-start(bf16[64,2,4,128]{3,2,1,0:T(4,128)(2,1)} %bitcast.9), calls=%async_computation.2 | async-start | bytes 262144 | tf_op jit(solution)/shard_map/all_to_all | solution.py:609
  101.7 5.8 %shard_map.103.refs_1_ = f32[2,64,2048]{2,1,0:T(8,128)} custom-call(bf16[2,64,2048]{2,1,0:T(8,128)(2,1)} %get-tuple-element.58.data, f32[16,2048]{1,0:T(8,128)} %bitcast.15, f32[16,2048]{1,0:T(8,128)} %bitcast.20), custom_call_target="tpu_custom_call" | custom-call | flops 200000000 | bytes 1572864 | tf_op jit(solution)/shard_map/pallas_call | solution.py:488
  107.6 4.2 %all-to-all-done.2.ends = bf16[64,2,4,128]{3,2,1,0:T(4,128)(2,1)S(1)} async-done(((bf16[64,2,4,128]{3,2,1,0:T(4,128)(2,1)}), bf16[64,2,4,128]{3,2,1,0:T(4,128)(2,1)S(1)}, u32[]{:S(2)}, u32[]{:S(2)}) %all-to-all-start.2) | async-done | bytes 131104 | tf_op jit(solution)/shard_map/all_to_all | solution.py:609
  111.8 0.8 shard_map.104
  112.6 7.1 %all-to-all-start.3 = ((bf16[64,2,4,128]{3,2,1,0:T(4,128)(2,1)}), bf16[64,2,4,128]{3,2,1,0:T(4,128)(2,1)S(1)}, u32[]{:S(2)}, u32[]{:S(2)}) async-start(bf16[64,2,4,128]{3,2,1,0:T(4,128)(2,1)} %shard_map.104), calls=%async_computation.3 | async-start | bytes 262144 | tf_op jit(solution)/shard_map/all_to_all | solution.py:609
  119.7 6.7 %collective-permute-start.12 = (bf16[2,8,2048]{2,1,0:T(8,128)(2,1)S(1)}, bf16[2,8,2048]{2,1,0:T(8,128)(2,1)S(1)}, u32[]{:S(2)}, u32[]{:S(2)}) collective-permute-start(bf16[2,8,2048]{2,1,0:T(8,128)(2,1)S(1)} %get-tuple-element.63), channel_id=1, source_target_pairs={{1,0},{2,1},{3,2},{4,3},{5,4},{6,5},{7,6},{8,7},{9,8},{10,9},{11,1... | collective-permute-start | bytes 196616 | tf_op jit(solution)/shard_map/ppermute | solution.py:615
  126.3 1.9 %collective-permute-done.12.refs_3_ = bf16[2,8,2048]{2,1,0:T(8,128)(2,1)S(1)} collective-permute-done((bf16[2,8,2048]{2,1,0:T(8,128)(2,1)S(1)}, bf16[2,8,2048]{2,1,0:T(8,128)(2,1)S(1)}, u32[]{:S(2)}, u32[]{:S(2)}) %collective-permute-start.12) | collective-permute-done | bytes 65568 | tf_op jit(solution)/shard_map/ppermute | solution.py:615
  128.2 1.3 all-to-all-done.3
  129.5 6.0 %shard_map.105 = (bf16[64,6144]{1,0:T(8,128)(2,1)}, bf16[64,6144]{1,0:T(8,128)(2,1)}) custom-call(bf16[16,4,2,4,128]{4,3,2,1,0:T(4,128)(2,1)S(1)} %bitcast.23, f32[2,64,2048]{2,1,0:T(8,128)} %shard_map.103.refs_1_, f32[2,64,2048]{2,1,0:T(8,128)} %get-tuple-element.62.refs_2_, bf16[2,8,2048]{2,1,0:T(8,128)(2,1)S(1)} %collective-permute-done.12.refs_3_, ...), custom_call_target="tpu_custom_call" | custom-call | tf_op jit(solution)/shard_map/pallas_call | solution.py:723
  (24 shorter events, 0.2 us)
Async XLA Ops:
  2.3 12.5 %collective-permute-start = (bf16[3,2,6144]{2,1,0:T(2,128)(2,1)S(1)}, bf16[3,2,6144]{2,1,0:T(2,128)(2,1)S(1)}, u32[]{:S(2)}, u32[]{:S(2)}) collective-permute-start(bf16[3,2,6144]{2,1,0:T(2,128)(2,1)S(1)} %get-tuple-element.34), channel_id=1, source_target_pairs={{0,1},{1,2},{2,3},{3,4},{4,5},{5,6},{6,7},{7,8},{8,9},{9,10},{10,1... | collective-permute-start | bytes 221192 | tf_op jit(solution)/shard_map/ppermute | solution.py:615
  14.8 50.4 %collective-permute-start.4 = (bf16[2048,1024]{1,0:T(8,128)(2,1)}, bf16[2048,1024]{1,0:T(8,128)(2,1)}, u32[]{:S(2)}, u32[]{:S(2)}) collective-permute-start(bf16[2048,1024]{1,0:T(8,128)(2,1)} %own_weight.1), channel_id=1, source_target_pairs={{0,64},{1,65},{2,66},{3,67},{4,68},{5,69},{6,70},{7,71},{8,72},{9,... | collective-permute-start | bytes 12582920 | tf_op jit(solution)/shard_map/ppermute | solution.py:633
  14.8 26.9 %collective-permute-start.1 = (bf16[512,1024]{1,0:T(8,128)(2,1)S(1)}, bf16[512,1024]{1,0:T(8,128)(2,1)}, u32[]{:S(2)}, u32[]{:S(2)}) collective-permute-start(bf16[512,1024]{1,0:T(8,128)(2,1)S(1)} %shard_map.96), channel_id=1, source_target_pairs={{0,160},{1,161},{2,162},{3,163},{4,164},{5,165},{6,166},{7,167},{8... | collective-permute-start | bytes 3145736 | tf_op jit(solution)/shard_map/ppermute | solution.py:633
  14.8 26.9 %copy-start = (f32[2048,16]{0,1:T(8,128)S(1)}, f32[2048,16]{0,1:T(8,128)}, u32[]{:S(2)}) copy-start(f32[2048,16]{0,1:T(8,128)} %param.13) | copy-start | bytes 393220
  21.1 46.0 %copy-start.1 = (f32[2048,16]{0,1:T(8,128)S(1)}, f32[2048,16]{0,1:T(8,128)}, u32[]{:S(2)}) copy-start(f32[2048,16]{0,1:T(8,128)} %param.12) | copy-start | bytes 393220
  21.2 22.2 %all-to-all-start = ((f32[64,3,4,128]{3,2,1,0:T(4,128)}), f32[64,3,4,128]{3,2,1,0:T(4,128)S(1)}, u32[]{:S(2)}, u32[]{:S(2)}) async-start(f32[64,3,4,128]{3,2,1,0:T(4,128)} %bitcast.46), calls=%async_computation | async-start | bytes 786432 | tf_op jit(solution)/shard_map/all_to_all | solution.py:609
  41.7 22.0 %collective-permute-start.2 = (bf16[512,1024]{1,0:T(8,128)(2,1)}, bf16[512,1024]{1,0:T(8,128)(2,1)S(1)}, u32[]{:S(2)}, u32[]{:S(2)}) collective-permute-start(bf16[512,1024]{1,0:T(8,128)(2,1)} %collective-permute-done.1.refs_0_), channel_id=1, source_target_pairs={{0,1},{1,0},{2,3},{3,2},{4,5},{5,4},{6,7},{7,6},{8,9},{9,8},{10,11... | collective-permute-start | bytes 3145736 | tf_op jit(solution)/shard_map/ppermute | solution.py:633
  41.7 22.0 %collective-permute-start.3 = (bf16[512,1024]{1,0:T(8,128)(2,1)}, bf16[512,1024]{1,0:T(8,128)(2,1)S(1)}, u32[]{:S(2)}, u32[]{:S(2)}) collective-permute-start(bf16[512,1024]{1,0:T(8,128)(2,1)} %collective-permute-done.1.refs_0_), channel_id=1, source_target_pairs={{0,4},{1,5},{2,6},{3,7},{4,0},{5,1},{6,2},{7,3},{8,12},{9,13},{10,... | collective-permute-start | bytes 3145736 | tf_op jit(solution)/shard_map/ppermute | solution.py:633
  44.2 19.5 %all-to-all-start.1 = ((bf16[64,3,4,128]{3,2,1,0:T(4,128)(2,1)}), bf16[64,3,4,128]{3,2,1,0:T(4,128)(2,1)S(1)}, u32[]{:S(2)}, u32[]{:S(2)}) async-start(bf16[64,3,4,128]{3,2,1,0:T(4,128)(2,1)} %shard_map.99), calls=%async_computation.1 | async-start | bytes 393216 | tf_op jit(solution)/shard_map/all_to_all | solution.py:609
  52.3 24.5 %collective-permute-start.7 = (bf16[512,1024]{1,0:T(8,128)(2,1)}, bf16[512,1024]{1,0:T(8,128)(2,1)}, u32[]{:S(2)}, u32[]{:S(2)}) collective-permute-start(bf16[512,1024]{1,0:T(8,128)(2,1)} %collective-permute-done.1.refs_0_), channel_id=1, source_target_pairs={{0,64},{1,65},{2,66},{3,67},{4,68},{5,69},{6,70},{7,71},{8,72},{9,... | collective-permute-start | bytes 3145736 | tf_op jit(solution)/shard_map/ppermute | solution.py:633
  63.7 13.1 %collective-permute-start.8 = (bf16[512,1024]{1,0:T(8,128)(2,1)S(1)}, bf16[512,1024]{1,0:T(8,128)(2,1)S(1)}, u32[]{:S(2)}, u32[]{:S(2)}) collective-permute-start(bf16[512,1024]{1,0:T(8,128)(2,1)S(1)} %collective-permute-done.2.refs_1_), channel_id=1, source_target_pairs={{0,64},{1,65},{2,66},{3,67},{4,68},{5,69},{6,70},{7,71},{8,72},{9,... | collective-permute-start | bytes 3145736 | tf_op jit(solution)/shard_map/ppermute | solution.py:633
  63.7 13.1 %collective-permute-start.9 = (bf16[512,1024]{1,0:T(8,128)(2,1)S(1)}, bf16[512,1024]{1,0:T(8,128)(2,1)S(1)}, u32[]{:S(2)}, u32[]{:S(2)}) collective-permute-start(bf16[512,1024]{1,0:T(8,128)(2,1)S(1)} %collective-permute-done.3.refs_2_), channel_id=1, source_target_pairs={{0,64},{1,65},{2,66},{3,67},{4,68},{5,69},{6,70},{7,71},{8,72},{9,... | collective-permute-start | bytes 3145736 | tf_op jit(solution)/shard_map/ppermute | solution.py:633
  64.3 9.3 %collective-permute-start.5 = (bf16[256,1024]{1,0:T(8,128)(2,1)S(1)}, bf16[256,1024]{1,0:T(8,128)(2,1)S(1)}, u32[]{:S(2)}, u32[]{:S(2)}) collective-permute-start(bf16[256,1024]{1,0:T(8,128)(2,1)S(1)} %slice.6), channel_id=1, source_target_pairs={{0,1},{1,0},{2,3},{3,2},{4,5},{5,4},{6,7},{7,6},{8,9},{9,8},{10,11... | collective-permute-start | bytes 1572872 | tf_op jit(solution)/shard_map/ppermute | solution.py:633
  65.2 9.2 %collective-permute-start.6 = (bf16[256,1024]{1,0:T(8,128)(2,1)S(1)}, bf16[256,1024]{1,0:T(8,128)(2,1)S(1)}, u32[]{:S(2)}, u32[]{:S(2)}) collective-permute-start(bf16[256,1024]{1,0:T(8,128)(2,1)S(1)} %slice.7), channel_id=1, source_target_pairs={{0,4},{1,5},{2,6},{3,7},{4,0},{5,1},{6,2},{7,3},{8,12},{9,13},{10,... | collective-permute-start | bytes 1572872 | tf_op jit(solution)/shard_map/ppermute | solution.py:633
  74.4 6.0 %copy-start.2 = (bf16[2,2,4096]{2,1,0:T(2,128)(2,1)S(1)}, bf16[2,2,4096]{2,1,0:T(2,128)(2,1)}, u32[]{:S(2)}) copy-start(bf16[2,2,4096]{2,1,0:T(2,128)(2,1)} %get-tuple-element.53.first_rows) | copy-start | bytes 98308
  74.4 6.0 %copy-start.3 = (f32[4096]{0:T(1024)S(1)}, f32[4096]{0:T(1024)}, u32[]{:S(2)}) copy-start(f32[4096]{0:T(1024)} %param.15) | copy-start | bytes 49156
  74.4 6.0 %collective-permute-start.10 = (bf16[256,1024]{1,0:T(8,128)(2,1)S(1)}, bf16[256,1024]{1,0:T(8,128)(2,1)S(1)}, u32[]{:S(2)}, u32[]{:S(2)}) collective-permute-start(bf16[256,1024]{1,0:T(8,128)(2,1)S(1)} %collective-permute-done.5.refs_3_), channel_id=1, source_target_pairs={{0,64},{1,65},{2,66},{3,67},{4,68},{5,69},{6,70},{7,71},{8,72},{9,... | collective-permute-start | bytes 1572872 | tf_op jit(solution)/shard_map/ppermute | solution.py:633
  76.5 3.8 %collective-permute-start.11 = (bf16[256,1024]{1,0:T(8,128)(2,1)S(1)}, bf16[256,1024]{1,0:T(8,128)(2,1)S(1)}, u32[]{:S(2)}, u32[]{:S(2)}) collective-permute-start(bf16[256,1024]{1,0:T(8,128)(2,1)S(1)} %collective-permute-done.6.refs_4_), channel_id=1, source_target_pairs={{0,64},{1,65},{2,66},{3,67},{4,68},{5,69},{6,70},{7,71},{8,72},{9,... | collective-permute-start | bytes 1572872 | tf_op jit(solution)/shard_map/ppermute | solution.py:633
  94.4 17.4 %all-to-all-start.2 = ((bf16[64,2,4,128]{3,2,1,0:T(4,128)(2,1)}), bf16[64,2,4,128]{3,2,1,0:T(4,128)(2,1)S(1)}, u32[]{:S(2)}, u32[]{:S(2)}) async-start(bf16[64,2,4,128]{3,2,1,0:T(4,128)(2,1)} %bitcast.9), calls=%async_computation.2 | async-start | bytes 262144 | tf_op jit(solution)/shard_map/all_to_all | solution.py:609
  112.6 16.9 %all-to-all-start.3 = ((bf16[64,2,4,128]{3,2,1,0:T(4,128)(2,1)}), bf16[64,2,4,128]{3,2,1,0:T(4,128)(2,1)S(1)}, u32[]{:S(2)}, u32[]{:S(2)}) async-start(bf16[64,2,4,128]{3,2,1,0:T(4,128)(2,1)} %shard_map.104), calls=%async_computation.3 | async-start | bytes 262144 | tf_op jit(solution)/shard_map/all_to_all | solution.py:609
  119.7 8.6 %collective-permute-start.12 = (bf16[2,8,2048]{2,1,0:T(8,128)(2,1)S(1)}, bf16[2,8,2048]{2,1,0:T(8,128)(2,1)S(1)}, u32[]{:S(2)}, u32[]{:S(2)}) collective-permute-start(bf16[2,8,2048]{2,1,0:T(8,128)(2,1)S(1)} %get-tuple-element.63), channel_id=1, source_target_pairs={{1,0},{2,1},{3,2},{4,3},{5,4},{6,5},{7,6},{8,7},{9,8},{10,9},{11,1... | collective-permute-start | bytes 196616 | tf_op jit(solution)/shard_map/ppermute | solution.py:615

commit v9 on v8

--- a/solution.py
+++ b/solution.py
@@ -238,28 +238,25 @@
     lax.fori_loop(0, WIDTH // BLOCK, mix, 0)
 
 
-def backward(slope, first, weights):
-    total = 0.0
-    for p, weight in enumerate(weights):
-        total = total + lax.dot_general(
-            weight[...], slope[first + p], (((1,), (1,)), ((), ())), preferred_element_type=f32
-        )
-    return total.T
-
-
 def piece_starts(ctx):
     first, along_x, along_z, last = bands(ctx)
     return first, along_x, along_z, last, last + BAND // 2
 
 
 def mix_pieces(prod, pieces, starts, begun, mixed):
+    left = jnp.concatenate(
+        [
+            prod[:, pl.ds(pl.multiple_of(start, BAND // 2), piece.shape[0])]
+            for piece, start in zip(pieces, starts)
+        ],
+        axis=1,
+    )
+
     def mix(t, carry):
         columns = pl.ds(pl.multiple_of(t * BLOCK, BLOCK), BLOCK)
-        total = 0.0 if begun is None else begun[:, columns]
-        for piece, start in zip(pieces, starts):
-            rows = pl.ds(pl.multiple_of(start, BAND // 2), piece.shape[0])
-            total = total + jnp.dot(prod[:, rows], piece[:, columns], preferred_element_type=f32)
-        mixed[:, columns] = total
+        right = jnp.concatenate([piece[:, columns] for piece in pieces], axis=0)
+        total = jnp.dot(left, right, preferred_element_type=f32)
+        mixed[:, columns] = total if begun is None else total + begun[:, columns]
         return carry
 
     lax.fori_loop(0, WIDTH // BLOCK, mix, 0)
@@ -337,22 +334,23 @@
     for p in range(shards):
 
         def out_slopes(t, carry):
-            columns, y_clean, y_pert, a, b = slopes(p, t)
-            slope[p, 0:ROWS, columns] = (inv_clean * a - y_clean * scale_clean).astype(bf16)
-            slope[p, ROWS : 2 * ROWS, columns] = (inv_pert * b - y_pert * scale_pert).astype(bf16)
+            _, y_clean, y_pert, a, b = slopes(p, t)
+            whole = pl.ds(pl.multiple_of(p * width + t * LANES, LANES), LANES)
+            slope[0:ROWS, whole] = (inv_clean * a - y_clean * scale_clean).astype(bf16)
+            slope[ROWS : 2 * ROWS, whole] = (inv_pert * b - y_pert * scale_pert).astype(bf16)
             return carry
 
         lax.fori_loop(0, width // LANES, out_slopes, 0)
 
-    def near_back(t, carry):
-        rows = pl.ds(pl.multiple_of(t * 2 * BLOCK, 2 * BLOCK), 2 * BLOCK)
-        prod_slope[:, rows] = backward(slope, 0, [held.at[0, rows], held.at[1, rows]])
-        return carry
-
-    lax.fori_loop(0, C // (2 * BLOCK), near_back, 0)
     for n in range(PIECES):
         rows = rows_of(n)
-        prod_slope[:, rows] += backward(slope, 2, [pieces[0][n], pieces[1][n]])
+        weight = jnp.concatenate(
+            [held[0, rows, :], held[1, rows, :], pieces[0][n][...], pieces[1][n][...]], axis=1
+        )
+        total = lax.dot_general(
+            weight, slope[...], (((1,), (1,)), ((), ())), preferred_element_type=f32
+        )
+        prod_slope[:, rows] = total.T
 
     for copy in late:
         copy.wait()
@@ -582,7 +580,7 @@
             pltpu.VMEM((2, ROWS, C), bf16),
             pltpu.VMEM((2, ROWS, C), bf16),
             pltpu.VMEM((2, 3 * ROWS, WIDTH), f32),
-            pltpu.VMEM((4, 2 * ROWS, WIDTH), bf16),
+            pltpu.VMEM((2 * ROWS, D), bf16),
             pltpu.VMEM((2 * ROWS, C), f32),
             pltpu.VMEM((M, QUARTERS, 2, QUARTER, LANES), f32),
             pltpu.SemaphoreType.DMA((2,)),

time: 137 us -> 137 us (level)
  no operation moved by 1% of the time
where the time goes in v9:
time: 137 us; the launch traced here: 135 us
  Pallas kernels  53.6 us (39%)
  starting transfers between devices  46.4 us (34%)
  waiting for transfers between devices  34.1 us (25%)
    all_to_all x4, starting transfers between devices, exchanged(): return lax.all_to_all(flat, 'ctx', split_axis=0, concat_axis=0, tiled=True)  30.5 us
    all_to_all x4, waiting for transfers between devices, exchanged(): return lax.all_to_all(flat, 'ctx', split_axis=0, concat_axis=0, tiled=True)  18.4 us
    pallas_call x1, Pallas kernels, slope_call(): pl.pallas_call(slope_kernel, out_shape=(pltpu.HBM((2, ROWS, C), f32), plt...  13.6 us
    pallas_call x2, Pallas kernels, within(): pl.pallas_call(functools.partial(within_kernel, streams, reverse), out_sh...  13.4 us
    ppermute x2, starting transfers between devices, passed_along(): lax.ppermute(value, 'ctx', [(source, source + steps) for source in range(...  10.1 us
    ppermute x2, waiting for transfers between devices, passed_along(): lax.ppermute(value, 'ctx', [(source, source + steps) for source in range(...  9.7 us
    pallas_call x1, Pallas kernels, per_device(): pl.pallas_call(gate_kernel, out_shape=(pltpu.HBM((3, ROWS, C), bf16), plt...  6.34 us
    pallas_call x1, Pallas kernels, mix_call(): pl.pallas_call(mix_kernel, out_shape=(pltpu.VMEM((3 * ROWS, C), bf16), pl...  6.11 us
  transfers between devices with their start and end apart: 17, of which 9 were waited for; matrix products, arithmetic and copies ran while one was open for 0% of the time, Pallas kernels for 23%

profile of v9, /device:TPU:24, one launch (start us, length us, event | category | flops | bytes accessed | tf_op | source)
XLA Modules:
  0.0 135.3 jit_solution(6986247812049571638)
XLA Ops:
  0.6 1.7 %shard_map.95 = (bf16[3,2,6144]{2,1,0:T(2,128)(2,1)S(1)}, bf16[2,2,4096]{2,1,0:T(2,128)(2,1)}) custom-call(bf16[64,6144]{1,0:T(8,128)(2,1)} %bitcast.28, bf16[64,6144]{1,0:T(8,128)(2,1)} %bitcast.35, bf16[64,6144]{1,0:T(8,128)(2,1)} %bitcast.42, bf16[64,6144]{1,0:T(8,128)(2,1)} %bitcast.29, bf16[64,6144]{1,0:T(8,128)(2,1)} %bitcast.36), custom_call_target="tpu_custom_call" | custom-call | tf_op jit(solution)/shard_map/pallas_call | solution.py:653
  2.3 3.4 %collective-permute-start = (bf16[3,2,6144]{2,1,0:T(2,128)(2,1)S(1)}, bf16[3,2,6144]{2,1,0:T(2,128)(2,1)S(1)}, u32[]{:S(2)}, u32[]{:S(2)}) collective-permute-start(bf16[3,2,6144]{2,1,0:T(2,128)(2,1)S(1)} %get-tuple-element.34), channel_id=1, source_target_pairs={{0,1},{1,2},{2,3},{3,4},{4,5},{5,6},{6,7},{7,8},{8,9},{9,10},{10,1... | collective-permute-start | bytes 221192 | tf_op jit(solution)/shard_map/ppermute | solution.py:613
  5.7 1.2 shard_map.96
  7.0 7.8 %collective-permute-done.refs_9_.refs_10_.refs_11_.refs_8_ = bf16[3,2,6144]{2,1,0:T(2,128)(2,1)S(1)} collective-permute-done((bf16[3,2,6144]{2,1,0:T(2,128)(2,1)S(1)}, bf16[3,2,6144]{2,1,0:T(2,128)(2,1)S(1)}, u32[]{:S(2)}, u32[]{:S(2)}) %collective-permute-start) | collective-permute-done | bytes 73760 | tf_op jit(solution)/shard_map/ppermute | solution.py:613
  14.8 6.3 %shard_map.97 = (bf16[3,64,2048]{2,1,0:T(8,128)(2,1)}, bf16[3,64,2048]{2,1,0:T(8,128)(2,1)}, f32[16,4,3,4,128]{4,3,2,1,0:T(4,128)}) custom-call(bf16[64,6144]{1,0:T(8,128)(2,1)} %bitcast.30, bf16[64,6144]{1,0:T(8,128)(2,1)} %bitcast.31, bf16[64,6144]{1,0:T(8,128)(2,1)} %bitcast.32, bf16[64,6144]{1,0:T(8,128)(2,1)} %bitcast.37, bf16[64,6144]{1,0:T(8,128)(2,1)} %bitcast.38, ...), custom_call_target="tpu_custom_call" | custom-call | tf_op jit(solution)/shard_map/pallas_call | solution.py:671
  21.2 8.0 %all-to-all-start = ((f32[64,3,4,128]{3,2,1,0:T(4,128)}), f32[64,3,4,128]{3,2,1,0:T(4,128)S(1)}, u32[]{:S(2)}, u32[]{:S(2)}) async-start(f32[64,3,4,128]{3,2,1,0:T(4,128)} %bitcast.46), calls=%async_computation | async-start | bytes 786432 | tf_op jit(solution)/shard_map/all_to_all | solution.py:607
  29.2 7.6 %shard_map.98.inner_far = f32[3,64,2048]{2,1,0:T(8,128)} custom-call(bf16[3,64,2048]{2,1,0:T(8,128)(2,1)} %get-tuple-element.38.data, f32[16,2048]{1,0:T(8,128)} %bitcast.14, f32[16,2048]{1,0:T(8,128)} %bitcast.19), custom_call_target="tpu_custom_call" | custom-call | flops 300000000 | bytes 2359296 | tf_op jit(solution)/shard_map/pallas_call | solution.py:486
  36.8 4.9 %collective-permute-done.1.refs_0_ = bf16[512,1024]{1,0:T(8,128)(2,1)} collective-permute-done((bf16[512,1024]{1,0:T(8,128)(2,1)S(1)}, bf16[512,1024]{1,0:T(8,128)(2,1)}, u32[]{:S(2)}, u32[]{:S(2)}) %collective-permute-start.1) | collective-permute-done | bytes 1048608 | tf_op jit(solution)/shard_map/ppermute | solution.py:631
  41.8 1.6 %all-to-all-done.ends = f32[64,3,4,128]{3,2,1,0:T(4,128)S(1)} async-done(((f32[64,3,4,128]{3,2,1,0:T(4,128)}), f32[64,3,4,128]{3,2,1,0:T(4,128)S(1)}, u32[]{:S(2)}, u32[]{:S(2)}) %all-to-all-start) | async-done | bytes 393248 | tf_op jit(solution)/shard_map/all_to_all | solution.py:607
  43.4 0.8 shard_map.99
  44.2 8.1 %all-to-all-start.1 = ((bf16[64,3,4,128]{3,2,1,0:T(4,128)(2,1)}), bf16[64,3,4,128]{3,2,1,0:T(4,128)(2,1)S(1)}, u32[]{:S(2)}, u32[]{:S(2)}) async-start(bf16[64,3,4,128]{3,2,1,0:T(4,128)(2,1)} %shard_map.99), calls=%async_computation.1 | async-start | bytes 393216 | tf_op jit(solution)/shard_map/all_to_all | solution.py:607
  52.3 0.1 collective-permute-start.7
  52.4 11.3 %all-to-all-done.1 = bf16[64,3,4,128]{3,2,1,0:T(4,128)(2,1)S(1)} async-done(((bf16[64,3,4,128]{3,2,1,0:T(4,128)(2,1)}), bf16[64,3,4,128]{3,2,1,0:T(4,128)(2,1)S(1)}, u32[]{:S(2)}, u32[]{:S(2)}) %all-to-all-start.1) | async-done | bytes 196640 | tf_op jit(solution)/shard_map/all_to_all | solution.py:607
  63.7 0.5 collective-permute-start.9
  64.3 0.9 collective-permute-start.5
  65.2 2.0 %collective-permute-start.6 = (bf16[256,1024]{1,0:T(8,128)(2,1)S(1)}, bf16[256,1024]{1,0:T(8,128)(2,1)S(1)}, u32[]{:S(2)}, u32[]{:S(2)}) collective-permute-start(bf16[256,1024]{1,0:T(8,128)(2,1)S(1)} %slice.7), channel_id=1, source_target_pairs={{0,4},{1,5},{2,6},{3,7},{4,0},{5,1},{6,2},{7,3},{8,12},{9,13},{10,... | collective-permute-start | bytes 1572872 | tf_op jit(solution)/shard_map/ppermute | solution.py:631
  67.1 6.1 %shard_map.100 = (bf16[192,2048]{1,0:T(8,128)(2,1)S(1)}, bf16[2,64,2048]{2,1,0:T(8,128)(2,1)}, f32[2,192,1024]{2,1,0:T(8,128)S(1)}, bf16[2,2048,1024]{2,1,0:T(8,128)(2,1)S(1)}) custom-call(bf16[16,4,3,4,128]{4,3,2,1,0:T(4,128)(2,1)S(1)} %bitcast.24, f32[3,64,2048]{2,1,0:T(8,128)} %shard_map.98.inner_far, bf16[3,64,2048]{2,1,0:T(8,128)(2,1)} %get-tuple-element.45.query_far, ...), custom_call_target="tpu_custom_call" | custom-call | flops 5000000000 | bytes 14000000 | tf_op jit(solution)/shard_map/pallas_call | solution.py:527
  73.3 0.3 collective-permute-done.5.refs_3_
  73.6 0.8 collective-permute-done.6.refs_4_
  74.4 2.2 %collective-permute-start.10 = (bf16[256,1024]{1,0:T(8,128)(2,1)S(1)}, bf16[256,1024]{1,0:T(8,128)(2,1)S(1)}, u32[]{:S(2)}, u32[]{:S(2)}) collective-permute-start(bf16[256,1024]{1,0:T(8,128)(2,1)S(1)} %collective-permute-done.5.refs_3_), channel_id=1, source_target_pairs={{0,64},{1,65},{2,66},{3,67},{4,68},{5,69},{6,70},{7,71},{8,72},{9,... | collective-permute-start | bytes 1572872 | tf_op jit(solution)/shard_map/ppermute | solution.py:631
  76.5 0.3 collective-permute-start.11
  76.8 3.6 %shard_map.101.begun = f32[2,192,1024]{2,1,0:T(8,128)S(1)} custom-call(bf16[192,2048]{1,0:T(8,128)(2,1)S(1)} %get-tuple-element.50.prod, bf16[512,1024]{1,0:T(8,128)(2,1)} %collective-permute-done.1.refs_0_, bf16[512,1024]{1,0:T(8,128)(2,1)S(1)} %collective-permute-done.2.refs_1_, bf16[512,1024]{1,0:T(8,128)(2,1)S(1)} %collective-permute-done.3.refs_2_, ...), custom_call_target="tpu_custom_call" | custom-call | flops 2400000000 | bytes 10000000 | tf_op jit(solution)/shard_map/pallas_call | solution.py:555
  80.4 13.6 %shard_map.102 = (f32[2,64,2048]{2,1,0:T(8,128)}, bf16[2,64,2048]{2,1,0:T(8,128)(2,1)}, bf16[2,8,2048]{2,1,0:T(8,128)(2,1)S(1)}, bf16[16,4,2,4,128]{4,3,2,1,0:T(4,128)(2,1)}) custom-call(bf16[192,2048]{1,0:T(8,128)(2,1)S(1)} %get-tuple-element.50.prod, f32[2,192,1024]{2,1,0:T(8,128)S(1)} %get-tuple-element.51.near_mixed, ...), custom_call_target="tpu_custom_call" | custom-call | tf_op jit(solution)/shard_map/pallas_call | solution.py:569
  94.0 7.3 %all-to-all-start.2 = ((bf16[64,2,4,128]{3,2,1,0:T(4,128)(2,1)}), bf16[64,2,4,128]{3,2,1,0:T(4,128)(2,1)S(1)}, u32[]{:S(2)}, u32[]{:S(2)}) async-start(bf16[64,2,4,128]{3,2,1,0:T(4,128)(2,1)} %bitcast.9), calls=%async_computation.2 | async-start | bytes 262144 | tf_op jit(solution)/shard_map/all_to_all | solution.py:607
  101.4 5.8 %shard_map.103.refs_1_ = f32[2,64,2048]{2,1,0:T(8,128)} custom-call(bf16[2,64,2048]{2,1,0:T(8,128)(2,1)} %get-tuple-element.58.data, f32[16,2048]{1,0:T(8,128)} %bitcast.15, f32[16,2048]{1,0:T(8,128)} %bitcast.20), custom_call_target="tpu_custom_call" | custom-call | flops 200000000 | bytes 1572864 | tf_op jit(solution)/shard_map/pallas_call | solution.py:486
  107.2 4.2 %all-to-all-done.2.ends = bf16[64,2,4,128]{3,2,1,0:T(4,128)(2,1)S(1)} async-done(((bf16[64,2,4,128]{3,2,1,0:T(4,128)(2,1)}), bf16[64,2,4,128]{3,2,1,0:T(4,128)(2,1)S(1)}, u32[]{:S(2)}, u32[]{:S(2)}) %all-to-all-start.2) | async-done | bytes 131104 | tf_op jit(solution)/shard_map/all_to_all | solution.py:607
  111.4 0.8 shard_map.104
  112.2 7.1 %all-to-all-start.3 = ((bf16[64,2,4,128]{3,2,1,0:T(4,128)(2,1)}), bf16[64,2,4,128]{3,2,1,0:T(4,128)(2,1)S(1)}, u32[]{:S(2)}, u32[]{:S(2)}) async-start(bf16[64,2,4,128]{3,2,1,0:T(4,128)(2,1)} %shard_map.104), calls=%async_computation.3 | async-start | bytes 262144 | tf_op jit(solution)/shard_map/all_to_all | solution.py:607
  119.3 6.7 %collective-permute-start.12 = (bf16[2,8,2048]{2,1,0:T(8,128)(2,1)S(1)}, bf16[2,8,2048]{2,1,0:T(8,128)(2,1)S(1)}, u32[]{:S(2)}, u32[]{:S(2)}) collective-permute-start(bf16[2,8,2048]{2,1,0:T(8,128)(2,1)S(1)} %get-tuple-element.63), channel_id=1, source_target_pairs={{1,0},{2,1},{3,2},{4,3},{5,4},{6,5},{7,6},{8,7},{9,8},{10,9},{11,1... | collective-permute-start | bytes 196616 | tf_op jit(solution)/shard_map/ppermute | solution.py:613
  126.0 1.9 %collective-permute-done.12.refs_3_ = bf16[2,8,2048]{2,1,0:T(8,128)(2,1)S(1)} collective-permute-done((bf16[2,8,2048]{2,1,0:T(8,128)(2,1)S(1)}, bf16[2,8,2048]{2,1,0:T(8,128)(2,1)S(1)}, u32[]{:S(2)}, u32[]{:S(2)}) %collective-permute-start.12) | collective-permute-done | bytes 65568 | tf_op jit(solution)/shard_map/ppermute | solution.py:613
  127.9 1.3 all-to-all-done.3
  129.1 6.0 %shard_map.105 = (bf16[64,6144]{1,0:T(8,128)(2,1)}, bf16[64,6144]{1,0:T(8,128)(2,1)}) custom-call(bf16[16,4,2,4,128]{4,3,2,1,0:T(4,128)(2,1)S(1)} %bitcast.23, f32[2,64,2048]{2,1,0:T(8,128)} %shard_map.103.refs_1_, f32[2,64,2048]{2,1,0:T(8,128)} %get-tuple-element.62.refs_2_, bf16[2,8,2048]{2,1,0:T(8,128)(2,1)S(1)} %collective-permute-done.12.refs_3_, ...), custom_call_target="tpu_custom_call" | custom-call | tf_op jit(solution)/shard_map/pallas_call | solution.py:721
  (24 shorter events, 0.2 us)
Async XLA Ops:
  2.3 12.5 %collective-permute-start = (bf16[3,2,6144]{2,1,0:T(2,128)(2,1)S(1)}, bf16[3,2,6144]{2,1,0:T(2,128)(2,1)S(1)}, u32[]{:S(2)}, u32[]{:S(2)}) collective-permute-start(bf16[3,2,6144]{2,1,0:T(2,128)(2,1)S(1)} %get-tuple-element.34), channel_id=1, source_target_pairs={{0,1},{1,2},{2,3},{3,4},{4,5},{5,6},{6,7},{7,8},{8,9},{9,10},{10,1... | collective-permute-start | bytes 221192 | tf_op jit(solution)/shard_map/ppermute | solution.py:613
  14.8 50.4 %collective-permute-start.4 = (bf16[2048,1024]{1,0:T(8,128)(2,1)}, bf16[2048,1024]{1,0:T(8,128)(2,1)}, u32[]{:S(2)}, u32[]{:S(2)}) collective-permute-start(bf16[2048,1024]{1,0:T(8,128)(2,1)} %own_weight.1), channel_id=1, source_target_pairs={{0,64},{1,65},{2,66},{3,67},{4,68},{5,69},{6,70},{7,71},{8,72},{9,... | collective-permute-start | bytes 12582920 | tf_op jit(solution)/shard_map/ppermute | solution.py:631
  14.8 26.9 %collective-permute-start.1 = (bf16[512,1024]{1,0:T(8,128)(2,1)S(1)}, bf16[512,1024]{1,0:T(8,128)(2,1)}, u32[]{:S(2)}, u32[]{:S(2)}) collective-permute-start(bf16[512,1024]{1,0:T(8,128)(2,1)S(1)} %shard_map.96), channel_id=1, source_target_pairs={{0,160},{1,161},{2,162},{3,163},{4,164},{5,165},{6,166},{7,167},{8... | collective-permute-start | bytes 3145736 | tf_op jit(solution)/shard_map/ppermute | solution.py:631
  14.8 26.9 %copy-start = (f32[2048,16]{0,1:T(8,128)S(1)}, f32[2048,16]{0,1:T(8,128)}, u32[]{:S(2)}) copy-start(f32[2048,16]{0,1:T(8,128)} %param.13) | copy-start | bytes 393220
  21.1 46.0 %copy-start.1 = (f32[2048,16]{0,1:T(8,128)S(1)}, f32[2048,16]{0,1:T(8,128)}, u32[]{:S(2)}) copy-start(f32[2048,16]{0,1:T(8,128)} %param.12) | copy-start | bytes 393220
  21.2 22.2 %all-to-all-start = ((f32[64,3,4,128]{3,2,1,0:T(4,128)}), f32[64,3,4,128]{3,2,1,0:T(4,128)S(1)}, u32[]{:S(2)}, u32[]{:S(2)}) async-start(f32[64,3,4,128]{3,2,1,0:T(4,128)} %bitcast.46), calls=%async_computation | async-start | bytes 786432 | tf_op jit(solution)/shard_map/all_to_all | solution.py:607
  41.7 22.0 %collective-permute-start.2 = (bf16[512,1024]{1,0:T(8,128)(2,1)}, bf16[512,1024]{1,0:T(8,128)(2,1)S(1)}, u32[]{:S(2)}, u32[]{:S(2)}) collective-permute-start(bf16[512,1024]{1,0:T(8,128)(2,1)} %collective-permute-done.1.refs_0_), channel_id=1, source_target_pairs={{0,1},{1,0},{2,3},{3,2},{4,5},{5,4},{6,7},{7,6},{8,9},{9,8},{10,11... | collective-permute-start | bytes 3145736 | tf_op jit(solution)/shard_map/ppermute | solution.py:631
  41.7 22.0 %collective-permute-start.3 = (bf16[512,1024]{1,0:T(8,128)(2,1)}, bf16[512,1024]{1,0:T(8,128)(2,1)S(1)}, u32[]{:S(2)}, u32[]{:S(2)}) collective-permute-start(bf16[512,1024]{1,0:T(8,128)(2,1)} %collective-permute-done.1.refs_0_), channel_id=1, source_target_pairs={{0,4},{1,5},{2,6},{3,7},{4,0},{5,1},{6,2},{7,3},{8,12},{9,13},{10,... | collective-permute-start | bytes 3145736 | tf_op jit(solution)/shard_map/ppermute | solution.py:631
  44.2 19.5 %all-to-all-start.1 = ((bf16[64,3,4,128]{3,2,1,0:T(4,128)(2,1)}), bf16[64,3,4,128]{3,2,1,0:T(4,128)(2,1)S(1)}, u32[]{:S(2)}, u32[]{:S(2)}) async-start(bf16[64,3,4,128]{3,2,1,0:T(4,128)(2,1)} %shard_map.99), calls=%async_computation.1 | async-start | bytes 393216 | tf_op jit(solution)/shard_map/all_to_all | solution.py:607
  52.3 24.5 %collective-permute-start.7 = (bf16[512,1024]{1,0:T(8,128)(2,1)}, bf16[512,1024]{1,0:T(8,128)(2,1)}, u32[]{:S(2)}, u32[]{:S(2)}) collective-permute-start(bf16[512,1024]{1,0:T(8,128)(2,1)} %collective-permute-done.1.refs_0_), channel_id=1, source_target_pairs={{0,64},{1,65},{2,66},{3,67},{4,68},{5,69},{6,70},{7,71},{8,72},{9,... | collective-permute-start | bytes 3145736 | tf_op jit(solution)/shard_map/ppermute | solution.py:631
  63.7 13.1 %collective-permute-start.8 = (bf16[512,1024]{1,0:T(8,128)(2,1)S(1)}, bf16[512,1024]{1,0:T(8,128)(2,1)S(1)}, u32[]{:S(2)}, u32[]{:S(2)}) collective-permute-start(bf16[512,1024]{1,0:T(8,128)(2,1)S(1)} %collective-permute-done.2.refs_1_), channel_id=1, source_target_pairs={{0,64},{1,65},{2,66},{3,67},{4,68},{5,69},{6,70},{7,71},{8,72},{9,... | collective-permute-start | bytes 3145736 | tf_op jit(solution)/shard_map/ppermute | solution.py:631
  63.7 13.1 %collective-permute-start.9 = (bf16[512,1024]{1,0:T(8,128)(2,1)S(1)}, bf16[512,1024]{1,0:T(8,128)(2,1)S(1)}, u32[]{:S(2)}, u32[]{:S(2)}) collective-permute-start(bf16[512,1024]{1,0:T(8,128)(2,1)S(1)} %collective-permute-done.3.refs_2_), channel_id=1, source_target_pairs={{0,64},{1,65},{2,66},{3,67},{4,68},{5,69},{6,70},{7,71},{8,72},{9,... | collective-permute-start | bytes 3145736 | tf_op jit(solution)/shard_map/ppermute | solution.py:631
  64.3 9.3 %collective-permute-start.5 = (bf16[256,1024]{1,0:T(8,128)(2,1)S(1)}, bf16[256,1024]{1,0:T(8,128)(2,1)S(1)}, u32[]{:S(2)}, u32[]{:S(2)}) collective-permute-start(bf16[256,1024]{1,0:T(8,128)(2,1)S(1)} %slice.6), channel_id=1, source_target_pairs={{0,1},{1,0},{2,3},{3,2},{4,5},{5,4},{6,7},{7,6},{8,9},{9,8},{10,11... | collective-permute-start | bytes 1572872 | tf_op jit(solution)/shard_map/ppermute | solution.py:631
  65.2 9.2 %collective-permute-start.6 = (bf16[256,1024]{1,0:T(8,128)(2,1)S(1)}, bf16[256,1024]{1,0:T(8,128)(2,1)S(1)}, u32[]{:S(2)}, u32[]{:S(2)}) collective-permute-start(bf16[256,1024]{1,0:T(8,128)(2,1)S(1)} %slice.7), channel_id=1, source_target_pairs={{0,4},{1,5},{2,6},{3,7},{4,0},{5,1},{6,2},{7,3},{8,12},{9,13},{10,... | collective-permute-start | bytes 1572872 | tf_op jit(solution)/shard_map/ppermute | solution.py:631
  74.4 6.1 %copy-start.2 = (bf16[2,2,4096]{2,1,0:T(2,128)(2,1)S(1)}, bf16[2,2,4096]{2,1,0:T(2,128)(2,1)}, u32[]{:S(2)}) copy-start(bf16[2,2,4096]{2,1,0:T(2,128)(2,1)} %get-tuple-element.53.first_rows) | copy-start | bytes 98308
  74.4 6.1 %copy-start.3 = (f32[4096]{0:T(1024)S(1)}, f32[4096]{0:T(1024)}, u32[]{:S(2)}) copy-start(f32[4096]{0:T(1024)} %param.15) | copy-start | bytes 49156
  74.4 6.0 %collective-permute-start.10 = (bf16[256,1024]{1,0:T(8,128)(2,1)S(1)}, bf16[256,1024]{1,0:T(8,128)(2,1)S(1)}, u32[]{:S(2)}, u32[]{:S(2)}) collective-permute-start(bf16[256,1024]{1,0:T(8,128)(2,1)S(1)} %collective-permute-done.5.refs_3_), channel_id=1, source_target_pairs={{0,64},{1,65},{2,66},{3,67},{4,68},{5,69},{6,70},{7,71},{8,72},{9,... | collective-permute-start | bytes 1572872 | tf_op jit(solution)/shard_map/ppermute | solution.py:631
  76.5 3.9 %collective-permute-start.11 = (bf16[256,1024]{1,0:T(8,128)(2,1)S(1)}, bf16[256,1024]{1,0:T(8,128)(2,1)S(1)}, u32[]{:S(2)}, u32[]{:S(2)}) collective-permute-start(bf16[256,1024]{1,0:T(8,128)(2,1)S(1)} %collective-permute-done.6.refs_4_), channel_id=1, source_target_pairs={{0,64},{1,65},{2,66},{3,67},{4,68},{5,69},{6,70},{7,71},{8,72},{9,... | collective-permute-start | bytes 1572872 | tf_op jit(solution)/shard_map/ppermute | solution.py:631
  94.0 17.4 %all-to-all-start.2 = ((bf16[64,2,4,128]{3,2,1,0:T(4,128)(2,1)}), bf16[64,2,4,128]{3,2,1,0:T(4,128)(2,1)S(1)}, u32[]{:S(2)}, u32[]{:S(2)}) async-start(bf16[64,2,4,128]{3,2,1,0:T(4,128)(2,1)} %bitcast.9), calls=%async_computation.2 | async-start | bytes 262144 | tf_op jit(solution)/shard_map/all_to_all | solution.py:607
  112.2 16.9 %all-to-all-start.3 = ((bf16[64,2,4,128]{3,2,1,0:T(4,128)(2,1)}), bf16[64,2,4,128]{3,2,1,0:T(4,128)(2,1)S(1)}, u32[]{:S(2)}, u32[]{:S(2)}) async-start(bf16[64,2,4,128]{3,2,1,0:T(4,128)(2,1)} %shard_map.104), calls=%async_computation.3 | async-start | bytes 262144 | tf_op jit(solution)/shard_map/all_to_all | solution.py:607
  119.3 8.6 %collective-permute-start.12 = (bf16[2,8,2048]{2,1,0:T(8,128)(2,1)S(1)}, bf16[2,8,2048]{2,1,0:T(8,128)(2,1)S(1)}, u32[]{:S(2)}, u32[]{:S(2)}) collective-permute-start(bf16[2,8,2048]{2,1,0:T(8,128)(2,1)S(1)} %get-tuple-element.63), channel_id=1, source_target_pairs={{1,0},{2,1},{3,2},{4,3},{5,4},{6,5},{7,6},{8,7},{9,8},{10,9},{11,1... | collective-permute-start | bytes 196616 | tf_op jit(solution)/shard_map/ppermute | solution.py:613

commit v10 on v9

--- a/solution.py
+++ b/solution.py
@@ -243,7 +243,7 @@
     return first, along_x, along_z, last, last + BAND // 2
 
 
-def mix_pieces(prod, pieces, starts, begun, mixed):
+def mix_pieces(prod, pieces, starts, mixed):
     left = jnp.concatenate(
         [
             prod[:, pl.ds(pl.multiple_of(start, BAND // 2), piece.shape[0])]
@@ -255,25 +255,18 @@
     def mix(t, carry):
         columns = pl.ds(pl.multiple_of(t * BLOCK, BLOCK), BLOCK)
         right = jnp.concatenate([piece[:, columns] for piece in pieces], axis=0)
-        total = jnp.dot(left, right, preferred_element_type=f32)
-        mixed[:, columns] = total if begun is None else total + begun[:, columns]
+        mixed[:, columns] = jnp.dot(left, right, preferred_element_type=f32)
         return carry
 
     lax.fori_loop(0, WIDTH // BLOCK, mix, 0)
 
 
-def far_kernel(prod, *refs):
-    pieces, mixed = (refs[:3], refs[3:6]), refs[6]
-    starts = piece_starts(lax.axis_index("ctx"))
-    for p in range(2):
-        mix_pieces(prod, pieces[p], starts, None, mixed.at[p])
-
-
 def slope_kernel(
-    prod, near_mixed, begun, conv_far, query_far, rate, gain, first_rows, held, *refs
+    prod, near_mixed, conv_far, query_far, rate, gain, first_rows, held, *refs
 ):
     pieces, refs = (refs[0:PIECES], refs[PIECES : 2 * PIECES]), refs[2 * PIECES :]
-    query_slope, conv_slope, edge, states, conv, query, far_mixed, slope, prod_slope, ends, sems = refs
+    query_slope_far, conv_slope_far, edge, states = refs[:4]
+    query_slope, conv_slope, conv, query, far_mixed, slope, prod_slope, ends, sems = refs[4:]
     dp, ctx = lax.axis_index("dp"), lax.axis_index("ctx")
     late = [
         pltpu.make_async_copy(conv_far, conv, sems.at[0]),
@@ -291,7 +284,7 @@
         return pl.ds(pl.multiple_of(starts[piece], BAND // 2), pieces[0][piece].shape[0])
 
     for p in range(2):
-        mix_pieces(prod, pieces[p][3:], starts[3:], begun.at[p], far_mixed.at[p])
+        mix_pieces(prod, pieces[p], starts, far_mixed.at[p])
 
     squares = jnp.zeros((3 * ROWS, LANES), f32)
     for p in range(shards):
@@ -379,8 +372,22 @@
                 ends[m, tile // QUARTER, s, pl.ds(tile % QUARTER, 1), :] = state
         return carry
 
-    lax.fori_loop(0, TILES, state_tile, 0)
+    leaving = []
+    for q in range(QUARTERS):
+        lax.fori_loop(q * QUARTER, q * QUARTER + QUARTER, state_tile, 0)
+        lanes = pl.ds(q * QUARTER * LANES, QUARTER * LANES)
+        for n, (source, target) in enumerate(
+            ((query_slope, query_slope_far), (conv_slope, conv_slope_far))
+        ):
+            leaving.append(
+                pltpu.make_async_copy(
+                    source.at[:, :, lanes], target.at[:, :, lanes], sems.at[2 + 2 * q + n]
+                )
+            )
+            leaving[-1].start()
     states[...] = ends[...].astype(bf16)
+    for copy in leaving:
+        copy.wait()
 
 
 def final_kernel(*refs):
@@ -550,21 +557,7 @@
     )
 
 
-def far_call(prod, *pieces):
-    near = pl.BlockSpec(memory_space=pltpu.VMEM)
-    return pl.pallas_call(
-        far_kernel,
-        out_shape=pltpu.VMEM((2, 3 * ROWS, WIDTH), f32),
-        in_specs=[near] * 7,
-        out_specs=near,
-        compiler_params=params(4),
-        cost_estimate=pl.CostEstimate(
-            flops=2_400_000_000, bytes_accessed=10_000_000, transcendentals=0
-        ),
-    )(*map(in_vmem, (prod, *pieces)))
-
-
-def slope_call(prod, near_mixed, begun, conv, query, rate, gain, first_rows, held, *pieces):
+def slope_call(prod, near_mixed, conv, query, rate, gain, first_rows, held, *pieces):
     near = pl.BlockSpec(memory_space=pltpu.VMEM)
     return pl.pallas_call(
         slope_kernel,
@@ -574,20 +567,22 @@
             array(2, 8, C, dtype=bf16),
             array(M, QUARTERS, 2, QUARTER, LANES, dtype=bf16),
         ),
-        in_specs=[near] * 3 + [far()] * 2 + [pl.BlockSpec()] * 3 + [near] * (1 + 2 * PIECES),
-        out_specs=(pl.BlockSpec(),) * 4,
+        in_specs=[near] * 2 + [far()] * 2 + [pl.BlockSpec()] * 3 + [near] * (1 + 2 * PIECES),
+        out_specs=(far(), far(), pl.BlockSpec(), pl.BlockSpec()),
         scratch_shapes=[
+            pltpu.VMEM((2, ROWS, C), f32),
+            pltpu.VMEM((2, ROWS, C), bf16),
             pltpu.VMEM((2, ROWS, C), bf16),
             pltpu.VMEM((2, ROWS, C), bf16),
             pltpu.VMEM((2, 3 * ROWS, WIDTH), f32),
             pltpu.VMEM((2 * ROWS, D), bf16),
             pltpu.VMEM((2 * ROWS, C), f32),
             pltpu.VMEM((M, QUARTERS, 2, QUARTER, LANES), f32),
-            pltpu.SemaphoreType.DMA((2,)),
+            pltpu.SemaphoreType.DMA((2 + 2 * QUARTERS,)),
         ],
         compiler_params=params(10),
     )(
-        in_vmem(prod), in_vmem(near_mixed), in_vmem(begun), in_hbm(conv), in_hbm(query), rate, gain,
+        in_vmem(prod), in_vmem(near_mixed), in_hbm(conv), in_hbm(query), rate, gain,
         first_rows, in_vmem(held), *map(in_vmem, pieces),
     )
 
@@ -704,12 +699,10 @@
         reaching, inner, query, rate, res, out_weight, core_weight
     )
     prod, last_x, last_z = tied(prod, last_x, last_z)
-    begun = far_call(prod, *far_pieces, *core_pieces)
     far_pieces += [last_x, last_z]
     core_pieces += [swapped(last_x, "core"), swapped(last_z, "core")]
     query_slope, conv_slope, edge, ends = slope_call(
-        prod, near_mixed, begun, conv, query, rate, gain, first_rows, held, *far_pieces,
-        *core_pieces,
+        prod, near_mixed, conv, query, rate, gain, first_rows, held, *far_pieces, *core_pieces,
     )
 
     ends = exchanged(ends)

time: 137 us -> 137 us (level)
  blocking collectives: 0 us -> 20.1 us
  waiting for transfers between devices: 34.1 us -> 24.3 us
  starting transfers between devices: 46.4 us -> 38.5 us
  Pallas kernels: 53.6 us -> 50.8 us
    all_to_all x0 -> x1, blocking collectives: none -> 20.1 us  [exchanged(): return lax.all_to_all(flat, 'ctx', split_axis=0, concat_axis=0, tiled=True)]
    all_to_all x4 -> x3, waiting for transfers between devices: 18.4 us -> 6.97 us  [exchanged(): return lax.all_to_all(flat, 'ctx', split_axis=0, concat_axis=0, tiled=True)]
    all_to_all x4 -> x3, starting transfers between devices: 30.5 us -> 24.5 us  [exchanged(): return lax.all_to_all(flat, 'ctx', split_axis=0, concat_axis=0, tiled=True)]
    pallas_call x1 -> x0, Pallas kernels: 3.56 us -> none  [far_call(): pl.pallas_call(far_kernel, out_shape=pltpu.VMEM((2, 3 * ROWS, WIDTH), f32...]
    ppermute x11, starting transfers between devices: 5.9 us -> 3.96 us  [swapped(): lax.ppermute(value, ('dp', 'ctx'), [(device, partner(device, kind)) for d...]
    ppermute x11, waiting for transfers between devices: 6.04 us -> 7.59 us  [swapped(): lax.ppermute(value, ('dp', 'ctx'), [(device, partner(device, kind)) for d...]
    pallas_call x1, Pallas kernels: 13.6 us -> 15 us  [slope_call(): pl.pallas_call(slope_kernel, out_shape=(pltpu.HBM((2, ROWS, C), f32), plt...]
  transfers between devices with their start and end apart: 17 -> 16, of which waited for: 9 -> 9; matrix products, arithmetic and copies ran while one was open for 0% -> 0% of each run, Pallas kernels for 23% -> 20%
where the time goes in v10:
time: 137 us; the launch traced here: 135 us
  Pallas kernels  50.8 us (37%)
  starting transfers between devices  38.5 us (28%)
  waiting for transfers between devices  24.3 us (18%)
  blocking collectives  20.1 us (15%)
    all_to_all x3, starting transfers between devices, exchanged(): return lax.all_to_all(flat, 'ctx', split_axis=0, concat_axis=0, tiled=True)  24.5 us
    all_to_all x1, blocking collectives, exchanged(): return lax.all_to_all(flat, 'ctx', split_axis=0, concat_axis=0, tiled=True)  20.1 us
    pallas_call x1, Pallas kernels, slope_call(): pl.pallas_call(slope_kernel, out_shape=(pltpu.HBM((2, ROWS, C), f32), plt...  15 us
    pallas_call x2, Pallas kernels, within(): pl.pallas_call(functools.partial(within_kernel, streams, reverse), out_sh...  13.4 us
    ppermute x2, starting transfers between devices, passed_along(): lax.ppermute(value, 'ctx', [(source, source + steps) for source in range(...  10.1 us
    ppermute x2, waiting for transfers between devices, passed_along(): lax.ppermute(value, 'ctx', [(source, source + steps) for source in range(...  9.7 us
    ppermute x11, waiting for transfers between devices, swapped(): lax.ppermute(value, ('dp', 'ctx'), [(device, partner(device, kind)) for d...  7.59 us
    all_to_all x3, waiting for transfers between devices, exchanged(): return lax.all_to_all(flat, 'ctx', split_axis=0, concat_axis=0, tiled=True)  6.97 us
  transfers between devices with their start and end apart: 16, of which 9 were waited for; matrix products, arithmetic and copies ran while one was open for 0% of the time, Pallas kernels for 20%

profile of v10, /device:TPU:24, one launch (start us, length us, event | category | flops | bytes accessed | tf_op | source)
XLA Modules:
  0.0 134.8 jit_solution(5474772907454344697)
XLA Ops:
  0.6 1.7 %shard_map.95 = (bf16[3,2,6144]{2,1,0:T(2,128)(2,1)S(1)}, bf16[2,2,4096]{2,1,0:T(2,128)(2,1)}) custom-call(bf16[64,6144]{1,0:T(8,128)(2,1)} %bitcast.28, bf16[64,6144]{1,0:T(8,128)(2,1)} %bitcast.35, bf16[64,6144]{1,0:T(8,128)(2,1)} %bitcast.42, bf16[64,6144]{1,0:T(8,128)(2,1)} %bitcast.29, bf16[64,6144]{1,0:T(8,128)(2,1)} %bitcast.36), custom_call_target="tpu_custom_call" | custom-call | tf_op jit(solution)/shard_map/pallas_call | solution.py:648
  2.3 3.4 %collective-permute-start = (bf16[3,2,6144]{2,1,0:T(2,128)(2,1)S(1)}, bf16[3,2,6144]{2,1,0:T(2,128)(2,1)S(1)}, u32[]{:S(2)}, u32[]{:S(2)}) collective-permute-start(bf16[3,2,6144]{2,1,0:T(2,128)(2,1)S(1)} %get-tuple-element.34), channel_id=1, source_target_pairs={{0,1},{1,2},{2,3},{3,4},{4,5},{5,6},{6,7},{7,8},{8,9},{9,10},{10,1... | collective-permute-start | bytes 221192 | tf_op jit(solution)/shard_map/ppermute | solution.py:608
  5.7 1.2 shard_map.96
  7.0 7.8 %collective-permute-done.refs_9_.refs_10_.refs_11_.refs_8_ = bf16[3,2,6144]{2,1,0:T(2,128)(2,1)S(1)} collective-permute-done((bf16[3,2,6144]{2,1,0:T(2,128)(2,1)S(1)}, bf16[3,2,6144]{2,1,0:T(2,128)(2,1)S(1)}, u32[]{:S(2)}, u32[]{:S(2)}) %collective-permute-start) | collective-permute-done | bytes 73760 | tf_op jit(solution)/shard_map/ppermute | solution.py:608
  14.8 6.4 %shard_map.97 = (bf16[3,64,2048]{2,1,0:T(8,128)(2,1)}, bf16[3,64,2048]{2,1,0:T(8,128)(2,1)}, f32[16,4,3,4,128]{4,3,2,1,0:T(4,128)}) custom-call(bf16[64,6144]{1,0:T(8,128)(2,1)} %bitcast.30, bf16[64,6144]{1,0:T(8,128)(2,1)} %bitcast.31, bf16[64,6144]{1,0:T(8,128)(2,1)} %bitcast.32, bf16[64,6144]{1,0:T(8,128)(2,1)} %bitcast.37, bf16[64,6144]{1,0:T(8,128)(2,1)} %bitcast.38, ...), custom_call_target="tpu_custom_call" | custom-call | tf_op jit(solution)/shard_map/pallas_call | solution.py:666
  21.2 0.0 copy-start.1
  21.2 8.0 %all-to-all-start = ((f32[64,3,4,128]{3,2,1,0:T(4,128)}), f32[64,3,4,128]{3,2,1,0:T(4,128)S(1)}, u32[]{:S(2)}, u32[]{:S(2)}) async-start(f32[64,3,4,128]{3,2,1,0:T(4,128)} %bitcast.46), calls=%async_computation | async-start | bytes 786432 | tf_op jit(solution)/shard_map/all_to_all | solution.py:602
  29.2 7.6 %shard_map.98.inner_far = f32[3,64,2048]{2,1,0:T(8,128)} custom-call(bf16[3,64,2048]{2,1,0:T(8,128)(2,1)} %get-tuple-element.38.data, f32[16,2048]{1,0:T(8,128)} %bitcast.14, f32[16,2048]{1,0:T(8,128)} %bitcast.19), custom_call_target="tpu_custom_call" | custom-call | flops 300000000 | bytes 2359296 | tf_op jit(solution)/shard_map/pallas_call | solution.py:493
  36.8 4.9 %collective-permute-done.1.refs_0_ = bf16[512,1024]{1,0:T(8,128)(2,1)} collective-permute-done((bf16[512,1024]{1,0:T(8,128)(2,1)S(1)}, bf16[512,1024]{1,0:T(8,128)(2,1)}, u32[]{:S(2)}, u32[]{:S(2)}) %collective-permute-start.1) | collective-permute-done | bytes 1048608 | tf_op jit(solution)/shard_map/ppermute | solution.py:626
  41.7 0.1 dynamic-slice.3
  41.8 1.6 %all-to-all-done.ends = f32[64,3,4,128]{3,2,1,0:T(4,128)S(1)} async-done(((f32[64,3,4,128]{3,2,1,0:T(4,128)}), f32[64,3,4,128]{3,2,1,0:T(4,128)S(1)}, u32[]{:S(2)}, u32[]{:S(2)}) %all-to-all-start) | async-done | bytes 393248 | tf_op jit(solution)/shard_map/all_to_all | solution.py:602
  43.4 0.1 shard_map.99
  43.5 20.1 %all_to_all.20 = bf16[64,3,4,128]{3,2,1,0:T(4,128)(2,1)S(1)} all-to-all(bf16[64,3,4,128]{3,2,1,0:T(4,128)(2,1)S(1)} %shard_map.99), channel_id=1, replica_groups=mesh['dp'=4,'ctx'=64] {'ctx'}, dimensions={0} | all-to-all | bytes 393216 | tf_op jit(solution)/shard_map/all_to_all | solution.py:602
  63.7 0.9 collective-permute-start.5
  64.6 2.0 %collective-permute-start.6 = (bf16[256,1024]{1,0:T(8,128)(2,1)S(1)}, bf16[256,1024]{1,0:T(8,128)(2,1)S(1)}, u32[]{:S(2)}, u32[]{:S(2)}) collective-permute-start(bf16[256,1024]{1,0:T(8,128)(2,1)S(1)} %slice.7), channel_id=1, source_target_pairs={{0,4},{1,5},{2,6},{3,7},{4,0},{5,1},{6,2},{7,3},{8,12},{9,13},{10,... | collective-permute-start | bytes 1572872 | tf_op jit(solution)/shard_map/ppermute | solution.py:626
  66.7 0.5 collective-permute-start.8
  67.2 6.1 %shard_map.100 = (bf16[192,2048]{1,0:T(8,128)(2,1)S(1)}, bf16[2,64,2048]{2,1,0:T(8,128)(2,1)}, f32[2,192,1024]{2,1,0:T(8,128)S(1)}, bf16[2,2048,1024]{2,1,0:T(8,128)(2,1)S(1)}) custom-call(bf16[16,4,3,4,128]{4,3,2,1,0:T(4,128)(2,1)S(1)} %bitcast.24, f32[3,64,2048]{2,1,0:T(8,128)} %shard_map.98.inner_far, bf16[3,64,2048]{2,1,0:T(8,128)(2,1)} %get-tuple-element.45.query_far, ...), custom_call_target="tpu_custom_call" | custom-call | flops 5000000000 | bytes 14000000 | tf_op jit(solution)/shard_map/pallas_call | solution.py:534
  73.4 0.6 collective-permute-done.6.refs_4_
  73.9 0.0 collective-permute-start.10
  73.9 0.5 collective-permute-start.11
  74.4 1.4 %collective-permute-done.10.refs_8_ = bf16[256,1024]{1,0:T(8,128)(2,1)S(1)} collective-permute-done((bf16[256,1024]{1,0:T(8,128)(2,1)S(1)}, bf16[256,1024]{1,0:T(8,128)(2,1)S(1)}, u32[]{:S(2)}, u32[]{:S(2)}) %collective-permute-start.10) | collective-permute-done | bytes 524320 | tf_op jit(solution)/shard_map/ppermute | solution.py:626
  75.8 0.7 collective-permute-done.11.refs_9_
  76.6 15.0 %shard_map.101 = (f32[2,64,2048]{2,1,0:T(8,128)}, bf16[2,64,2048]{2,1,0:T(8,128)(2,1)}, bf16[2,8,2048]{2,1,0:T(8,128)(2,1)S(1)}, bf16[16,4,2,4,128]{4,3,2,1,0:T(4,128)(2,1)}) custom-call(bf16[192,2048]{1,0:T(8,128)(2,1)S(1)} %get-tuple-element.50.prod, f32[2,192,1024]{2,1,0:T(8,128)S(1)} %get-tuple-element.51.near_mixed, ...), custom_call_target="tpu_custom_call" | custom-call | tf_op jit(solution)/shard_map/pallas_call | solution.py:562
  91.6 9.3 %all-to-all-start.2 = ((bf16[64,2,4,128]{3,2,1,0:T(4,128)(2,1)}), bf16[64,2,4,128]{3,2,1,0:T(4,128)(2,1)S(1)}, u32[]{:S(2)}, u32[]{:S(2)}) async-start(bf16[64,2,4,128]{3,2,1,0:T(4,128)(2,1)} %bitcast.9), calls=%async_computation.2 | async-start | bytes 262144 | tf_op jit(solution)/shard_map/all_to_all | solution.py:602
  100.8 5.8 %shard_map.102.refs_1_ = f32[2,64,2048]{2,1,0:T(8,128)} custom-call(bf16[2,64,2048]{2,1,0:T(8,128)(2,1)} %get-tuple-element.58.data, f32[16,2048]{1,0:T(8,128)} %bitcast.15, f32[16,2048]{1,0:T(8,128)} %bitcast.20), custom_call_target="tpu_custom_call" | custom-call | flops 200000000 | bytes 1572864 | tf_op jit(solution)/shard_map/pallas_call | solution.py:493
  106.7 4.1 %all-to-all-done.2.ends = bf16[64,2,4,128]{3,2,1,0:T(4,128)(2,1)S(1)} async-done(((bf16[64,2,4,128]{3,2,1,0:T(4,128)(2,1)}), bf16[64,2,4,128]{3,2,1,0:T(4,128)(2,1)S(1)}, u32[]{:S(2)}, u32[]{:S(2)}) %all-to-all-start.2) | async-done | bytes 131104 | tf_op jit(solution)/shard_map/all_to_all | solution.py:602
  110.8 0.8 shard_map.103
  111.6 7.2 %all-to-all-start.3 = ((bf16[64,2,4,128]{3,2,1,0:T(4,128)(2,1)}), bf16[64,2,4,128]{3,2,1,0:T(4,128)(2,1)S(1)}, u32[]{:S(2)}, u32[]{:S(2)}) async-start(bf16[64,2,4,128]{3,2,1,0:T(4,128)(2,1)} %shard_map.103), calls=%async_computation.3 | async-start | bytes 262144 | tf_op jit(solution)/shard_map/all_to_all | solution.py:602
  118.8 6.7 %collective-permute-start.12 = (bf16[2,8,2048]{2,1,0:T(8,128)(2,1)S(1)}, bf16[2,8,2048]{2,1,0:T(8,128)(2,1)S(1)}, u32[]{:S(2)}, u32[]{:S(2)}) collective-permute-start(bf16[2,8,2048]{2,1,0:T(8,128)(2,1)S(1)} %get-tuple-element.63), channel_id=1, source_target_pairs={{1,0},{2,1},{3,2},{4,3},{5,4},{6,5},{7,6},{8,7},{9,8},{10,9},{11,1... | collective-permute-start | bytes 196616 | tf_op jit(solution)/shard_map/ppermute | solution.py:608
  125.5 1.9 %collective-permute-done.12.refs_3_ = bf16[2,8,2048]{2,1,0:T(8,128)(2,1)S(1)} collective-permute-done((bf16[2,8,2048]{2,1,0:T(8,128)(2,1)S(1)}, bf16[2,8,2048]{2,1,0:T(8,128)(2,1)S(1)}, u32[]{:S(2)}, u32[]{:S(2)}) %collective-permute-start.12) | collective-permute-done | bytes 65568 | tf_op jit(solution)/shard_map/ppermute | solution.py:608
  127.4 1.3 all-to-all-done.3
  128.6 6.0 %shard_map.104 = (bf16[64,6144]{1,0:T(8,128)(2,1)}, bf16[64,6144]{1,0:T(8,128)(2,1)}) custom-call(bf16[16,4,2,4,128]{4,3,2,1,0:T(4,128)(2,1)S(1)} %bitcast.23, f32[2,64,2048]{2,1,0:T(8,128)} %shard_map.102.refs_1_, f32[2,64,2048]{2,1,0:T(8,128)} %get-tuple-element.62.refs_2_, bf16[2,8,2048]{2,1,0:T(8,128)(2,1)S(1)} %collective-permute-done.12.refs_3_, ...), custom_call_target="tpu_custom_call" | custom-call | tf_op jit(solution)/shard_map/pallas_call | solution.py:714
  (22 shorter events, 0.1 us)
Async XLA Ops:
  2.3 12.5 %collective-permute-start = (bf16[3,2,6144]{2,1,0:T(2,128)(2,1)S(1)}, bf16[3,2,6144]{2,1,0:T(2,128)(2,1)S(1)}, u32[]{:S(2)}, u32[]{:S(2)}) collective-permute-start(bf16[3,2,6144]{2,1,0:T(2,128)(2,1)S(1)} %get-tuple-element.34), channel_id=1, source_target_pairs={{0,1},{1,2},{2,3},{3,4},{4,5},{5,6},{6,7},{7,8},{8,9},{9,10},{10,1... | collective-permute-start | bytes 221192 | tf_op jit(solution)/shard_map/ppermute | solution.py:608
  14.8 52.4 %collective-permute-start.4 = (bf16[2048,1024]{1,0:T(8,128)(2,1)}, bf16[2048,1024]{1,0:T(8,128)(2,1)}, u32[]{:S(2)}, u32[]{:S(2)}) collective-permute-start(bf16[2048,1024]{1,0:T(8,128)(2,1)} %own_weight.1), channel_id=1, source_target_pairs={{0,64},{1,65},{2,66},{3,67},{4,68},{5,69},{6,70},{7,71},{8,72},{9,... | collective-permute-start | bytes 12582920 | tf_op jit(solution)/shard_map/ppermute | solution.py:626
  14.8 26.9 %collective-permute-start.1 = (bf16[512,1024]{1,0:T(8,128)(2,1)S(1)}, bf16[512,1024]{1,0:T(8,128)(2,1)}, u32[]{:S(2)}, u32[]{:S(2)}) collective-permute-start(bf16[512,1024]{1,0:T(8,128)(2,1)S(1)} %shard_map.96), channel_id=1, source_target_pairs={{0,160},{1,161},{2,162},{3,163},{4,164},{5,165},{6,166},{7,167},{8... | collective-permute-start | bytes 3145736 | tf_op jit(solution)/shard_map/ppermute | solution.py:626
  14.8 26.9 %copy-start = (f32[2048,16]{0,1:T(8,128)S(1)}, f32[2048,16]{0,1:T(8,128)}, u32[]{:S(2)}) copy-start(f32[2048,16]{0,1:T(8,128)} %param.13) | copy-start | bytes 393220
  21.2 46.1 %copy-start.1 = (f32[2048,16]{0,1:T(8,128)S(1)}, f32[2048,16]{0,1:T(8,128)}, u32[]{:S(2)}) copy-start(f32[2048,16]{0,1:T(8,128)} %param.12) | copy-start | bytes 393220
  21.2 22.2 %all-to-all-start = ((f32[64,3,4,128]{3,2,1,0:T(4,128)}), f32[64,3,4,128]{3,2,1,0:T(4,128)S(1)}, u32[]{:S(2)}, u32[]{:S(2)}) async-start(f32[64,3,4,128]{3,2,1,0:T(4,128)} %bitcast.46), calls=%async_computation | async-start | bytes 786432 | tf_op jit(solution)/shard_map/all_to_all | solution.py:602
  41.7 22.0 %collective-permute-start.2 = (bf16[512,1024]{1,0:T(8,128)(2,1)}, bf16[512,1024]{1,0:T(8,128)(2,1)S(1)}, u32[]{:S(2)}, u32[]{:S(2)}) collective-permute-start(bf16[512,1024]{1,0:T(8,128)(2,1)} %collective-permute-done.1.refs_0_), channel_id=1, source_target_pairs={{0,1},{1,0},{2,3},{3,2},{4,5},{5,4},{6,7},{7,6},{8,9},{9,8},{10,11... | collective-permute-start | bytes 3145736 | tf_op jit(solution)/shard_map/ppermute | solution.py:626
  41.7 22.0 %collective-permute-start.3 = (bf16[512,1024]{1,0:T(8,128)(2,1)}, bf16[512,1024]{1,0:T(8,128)(2,1)S(1)}, u32[]{:S(2)}, u32[]{:S(2)}) collective-permute-start(bf16[512,1024]{1,0:T(8,128)(2,1)} %collective-permute-done.1.refs_0_), channel_id=1, source_target_pairs={{0,4},{1,5},{2,6},{3,7},{4,0},{5,1},{6,2},{7,3},{8,12},{9,13},{10,... | collective-permute-start | bytes 3145736 | tf_op jit(solution)/shard_map/ppermute | solution.py:626
  63.7 9.6 %collective-permute-start.5 = (bf16[256,1024]{1,0:T(8,128)(2,1)S(1)}, bf16[256,1024]{1,0:T(8,128)(2,1)S(1)}, u32[]{:S(2)}, u32[]{:S(2)}) collective-permute-start(bf16[256,1024]{1,0:T(8,128)(2,1)S(1)} %slice.6), channel_id=1, source_target_pairs={{0,1},{1,0},{2,3},{3,2},{4,5},{5,4},{6,7},{7,6},{8,9},{9,8},{10,11... | collective-permute-start | bytes 1572872 | tf_op jit(solution)/shard_map/ppermute | solution.py:626
  64.6 9.3 %collective-permute-start.6 = (bf16[256,1024]{1,0:T(8,128)(2,1)S(1)}, bf16[256,1024]{1,0:T(8,128)(2,1)S(1)}, u32[]{:S(2)}, u32[]{:S(2)}) collective-permute-start(bf16[256,1024]{1,0:T(8,128)(2,1)S(1)} %slice.7), channel_id=1, source_target_pairs={{0,4},{1,5},{2,6},{3,7},{4,0},{5,1},{6,2},{7,3},{8,12},{9,13},{10,... | collective-permute-start | bytes 1572872 | tf_op jit(solution)/shard_map/ppermute | solution.py:626
  66.7 7.7 %collective-permute-start.7 = (bf16[512,1024]{1,0:T(8,128)(2,1)}, bf16[512,1024]{1,0:T(8,128)(2,1)S(1)}, u32[]{:S(2)}, u32[]{:S(2)}) collective-permute-start(bf16[512,1024]{1,0:T(8,128)(2,1)} %collective-permute-done.1.refs_0_), channel_id=1, source_target_pairs={{0,64},{1,65},{2,66},{3,67},{4,68},{5,69},{6,70},{7,71},{8,72},{9,... | collective-permute-start | bytes 3145736 | tf_op jit(solution)/shard_map/ppermute | solution.py:626
  66.7 7.7 %collective-permute-start.8 = (bf16[512,1024]{1,0:T(8,128)(2,1)S(1)}, bf16[512,1024]{1,0:T(8,128)(2,1)S(1)}, u32[]{:S(2)}, u32[]{:S(2)}) collective-permute-start(bf16[512,1024]{1,0:T(8,128)(2,1)S(1)} %collective-permute-done.2.refs_1_), channel_id=1, source_target_pairs={{0,64},{1,65},{2,66},{3,67},{4,68},{5,69},{6,70},{7,71},{8,72},{9,... | collective-permute-start | bytes 3145736 | tf_op jit(solution)/shard_map/ppermute | solution.py:626
  67.2 7.2 %collective-permute-start.9 = (bf16[512,1024]{1,0:T(8,128)(2,1)S(1)}, bf16[512,1024]{1,0:T(8,128)(2,1)S(1)}, u32[]{:S(2)}, u32[]{:S(2)}) collective-permute-start(bf16[512,1024]{1,0:T(8,128)(2,1)S(1)} %collective-permute-done.3.refs_2_), channel_id=1, source_target_pairs={{0,64},{1,65},{2,66},{3,67},{4,68},{5,69},{6,70},{7,71},{8,72},{9,... | collective-permute-start | bytes 3145736 | tf_op jit(solution)/shard_map/ppermute | solution.py:626
  67.2 9.4 %copy-start.2 = (bf16[2,2,4096]{2,1,0:T(2,128)(2,1)S(1)}, bf16[2,2,4096]{2,1,0:T(2,128)(2,1)}, u32[]{:S(2)}) copy-start(bf16[2,2,4096]{2,1,0:T(2,128)(2,1)} %get-tuple-element.53.first_rows) | copy-start | bytes 98308
  67.2 9.4 %copy-start.3 = (f32[4096]{0:T(1024)S(1)}, f32[4096]{0:T(1024)}, u32[]{:S(2)}) copy-start(f32[4096]{0:T(1024)} %param.15) | copy-start | bytes 49156
  73.9 1.9 %collective-permute-start.10 = (bf16[256,1024]{1,0:T(8,128)(2,1)S(1)}, bf16[256,1024]{1,0:T(8,128)(2,1)S(1)}, u32[]{:S(2)}, u32[]{:S(2)}) collective-permute-start(bf16[256,1024]{1,0:T(8,128)(2,1)S(1)} %collective-permute-done.5.refs_3_), channel_id=1, source_target_pairs={{0,64},{1,65},{2,66},{3,67},{4,68},{5,69},{6,70},{7,71},{8,72},{9,... | collective-permute-start | bytes 1572872 | tf_op jit(solution)/shard_map/ppermute | solution.py:626
  73.9 2.7 %collective-permute-start.11 = (bf16[256,1024]{1,0:T(8,128)(2,1)S(1)}, bf16[256,1024]{1,0:T(8,128)(2,1)S(1)}, u32[]{:S(2)}, u32[]{:S(2)}) collective-permute-start(bf16[256,1024]{1,0:T(8,128)(2,1)S(1)} %collective-permute-done.6.refs_4_), channel_id=1, source_target_pairs={{0,64},{1,65},{2,66},{3,67},{4,68},{5,69},{6,70},{7,71},{8,72},{9,... | collective-permute-start | bytes 1572872 | tf_op jit(solution)/shard_map/ppermute | solution.py:626
  91.6 19.2 %all-to-all-start.2 = ((bf16[64,2,4,128]{3,2,1,0:T(4,128)(2,1)}), bf16[64,2,4,128]{3,2,1,0:T(4,128)(2,1)S(1)}, u32[]{:S(2)}, u32[]{:S(2)}) async-start(bf16[64,2,4,128]{3,2,1,0:T(4,128)(2,1)} %bitcast.9), calls=%async_computation.2 | async-start | bytes 262144 | tf_op jit(solution)/shard_map/all_to_all | solution.py:602
  111.6 17.1 %all-to-all-start.3 = ((bf16[64,2,4,128]{3,2,1,0:T(4,128)(2,1)}), bf16[64,2,4,128]{3,2,1,0:T(4,128)(2,1)S(1)}, u32[]{:S(2)}, u32[]{:S(2)}) async-start(bf16[64,2,4,128]{3,2,1,0:T(4,128)(2,1)} %shard_map.103), calls=%async_computation.3 | async-start | bytes 262144 | tf_op jit(solution)/shard_map/all_to_all | solution.py:602
  118.8 8.6 %collective-permute-start.12 = (bf16[2,8,2048]{2,1,0:T(8,128)(2,1)S(1)}, bf16[2,8,2048]{2,1,0:T(8,128)(2,1)S(1)}, u32[]{:S(2)}, u32[]{:S(2)}) collective-permute-start(bf16[2,8,2048]{2,1,0:T(8,128)(2,1)S(1)} %get-tuple-element.63), channel_id=1, source_target_pairs={{1,0},{2,1},{3,2},{4,3},{5,4},{6,5},{7,6},{8,7},{9,8},{10,9},{11,1... | collective-permute-start | bytes 196616 | tf_op jit(solution)/shard_map/ppermute | solution.py:608

commit v11 on v10

--- a/solution.py
+++ b/solution.py
@@ -182,15 +182,20 @@
     prod, conv, mixed, held,
     reaching, inner, query, sems,
 ):
-    copies = []
+    def entering(q):
+        lanes = pl.ds(pl.multiple_of(q * QUARTER * LANES, LANES), QUARTER * LANES)
+        return [
+            pltpu.make_async_copy(source.at[:, :, lanes], target.at[:, :, lanes], sems.at[2 * q + n])
+            for n, (source, target) in enumerate(((inner_far, inner), (query_far, query)))
+        ]
+
     for q in range(QUARTERS):
-        lanes = pl.ds(q * QUARTER * LANES, QUARTER * LANES)
-        copies += [
-            pltpu.make_async_copy(inner_far.at[:, :, lanes], inner.at[:, :, lanes], sems.at[2 * q]),
-            pltpu.make_async_copy(query_far.at[:, :, lanes], query.at[:, :, lanes], sems.at[2 * q + 1]),
-        ]
-    for p, weight in enumerate((own_weight, core_weight)):
-        copies.append(pltpu.make_async_copy(weight, held.at[p], sems.at[2 * QUARTERS + p]))
+        for copy in entering(q):
+            copy.start()
+    copies = [
+        pltpu.make_async_copy(weight, held.at[p], sems.at[2 * QUARTERS + p])
+        for p, weight in enumerate((own_weight, core_weight))
+    ]
     for copy in copies:
         copy.start()
     reaching[...] = arriving[...].astype(f32)
@@ -219,13 +224,16 @@
             prod[pl.ds(s * ROWS, ROWS), lanes] = product.astype(bf16)
         return carry
 
-    for q in range(QUARTERS):
-        for copy in copies[2 * q : 2 * q + 2]:
+    def conv_quarter(q, carry):
+        for copy in entering(q):
             copy.wait()
         lax.fori_loop(QUARTER * q, QUARTER * q + QUARTER, conv_tile, 0)
+        return carry
+
+    lax.fori_loop(0, QUARTERS, conv_quarter, 0)
 
     for p in range(2):
-        copies[2 * QUARTERS + p].wait()
+        copies[p].wait()
         mix_shard(prod, held.at[p], mixed.at[p])
 
 
@@ -372,22 +380,28 @@
                 ends[m, tile // QUARTER, s, pl.ds(tile % QUARTER, 1), :] = state
         return carry
 
-    leaving = []
+    def leaving(q):
+        lanes = pl.ds(pl.multiple_of(q * QUARTER * LANES, LANES), QUARTER * LANES)
+        return [
+            pltpu.make_async_copy(
+                source.at[:, :, lanes], target.at[:, :, lanes], sems.at[2 + 2 * q + n]
+            )
+            for n, (source, target) in enumerate(
+                ((query_slope, query_slope_far), (conv_slope, conv_slope_far))
+            )
+        ]
+
+    def state_quarter(q, carry):
+        lax.fori_loop(q * QUARTER, q * QUARTER + QUARTER, state_tile, 0)
+        for copy in leaving(q):
+            copy.start()
+        return carry
+
+    lax.fori_loop(0, QUARTERS, state_quarter, 0)
+    states[...] = ends[...].astype(bf16)
     for q in range(QUARTERS):
-        lax.fori_loop(q * QUARTER, q * QUARTER + QUARTER, state_tile, 0)
-        lanes = pl.ds(q * QUARTER * LANES, QUARTER * LANES)
-        for n, (source, target) in enumerate(
-            ((query_slope, query_slope_far), (conv_slope, conv_slope_far))
-        ):
-            leaving.append(
-                pltpu.make_async_copy(
-                    source.at[:, :, lanes], target.at[:, :, lanes], sems.at[2 + 2 * q + n]
-                )
-            )
-            leaving[-1].start()
-    states[...] = ends[...].astype(bf16)
-    for copy in leaving:
-        copy.wait()
+        for copy in leaving(q):
+            copy.wait()
 
 
 def final_kernel(*refs):

time: 137 us -> 137 us (level)
  no operation moved by 1% of the time
where the time goes in v11:
time: 137 us; the launch traced here: 135 us
  Pallas kernels  50.9 us (37%)
  starting transfers between devices  38.5 us (28%)
  waiting for transfers between devices  24.2 us (18%)
  blocking collectives  20.1 us (15%)
    all_to_all x3, starting transfers between devices, exchanged(): return lax.all_to_all(flat, 'ctx', split_axis=0, concat_axis=0, tiled=True)  24.5 us
    all_to_all x1, blocking collectives, exchanged(): return lax.all_to_all(flat, 'ctx', split_axis=0, concat_axis=0, tiled=True)  20.1 us
    pallas_call x1, Pallas kernels, slope_call(): pl.pallas_call(slope_kernel, out_shape=(pltpu.HBM((2, ROWS, C), f32), plt...  15.1 us
    pallas_call x2, Pallas kernels, within(): pl.pallas_call(functools.partial(within_kernel, streams, reverse), out_sh...  13.4 us
    ppermute x2, starting transfers between devices, passed_along(): lax.ppermute(value, 'ctx', [(source, source + steps) for source in range(...  10.1 us
    ppermute x2, waiting for transfers between devices, passed_along(): lax.ppermute(value, 'ctx', [(source, source + steps) for source in range(...  9.7 us
    ppermute x11, waiting for transfers between devices, swapped(): lax.ppermute(value, ('dp', 'ctx'), [(device, partner(device, kind)) for d...  7.55 us
    all_to_all x3, waiting for transfers between devices, exchanged(): return lax.all_to_all(flat, 'ctx', split_axis=0, concat_axis=0, tiled=True)  6.97 us
  transfers between devices with their start and end apart: 16, of which 9 were waited for; matrix products, arithmetic and copies ran while one was open for 0% of the time, Pallas kernels for 20%

profile of v11, /device:TPU:24, one launch (start us, length us, event | category | flops | bytes accessed | tf_op | source)
XLA Modules:
  0.0 134.9 jit_solution(11032665991315566605)
XLA Ops:
  0.6 1.7 %shard_map.95 = (bf16[3,2,6144]{2,1,0:T(2,128)(2,1)S(1)}, bf16[2,2,4096]{2,1,0:T(2,128)(2,1)}) custom-call(bf16[64,6144]{1,0:T(8,128)(2,1)} %bitcast.28, bf16[64,6144]{1,0:T(8,128)(2,1)} %bitcast.35, bf16[64,6144]{1,0:T(8,128)(2,1)} %bitcast.42, bf16[64,6144]{1,0:T(8,128)(2,1)} %bitcast.29, bf16[64,6144]{1,0:T(8,128)(2,1)} %bitcast.36), custom_call_target="tpu_custom_call" | custom-call | tf_op jit(solution)/shard_map/pallas_call | solution.py:662
  2.3 3.4 %collective-permute-start = (bf16[3,2,6144]{2,1,0:T(2,128)(2,1)S(1)}, bf16[3,2,6144]{2,1,0:T(2,128)(2,1)S(1)}, u32[]{:S(2)}, u32[]{:S(2)}) collective-permute-start(bf16[3,2,6144]{2,1,0:T(2,128)(2,1)S(1)} %get-tuple-element.34), channel_id=1, source_target_pairs={{0,1},{1,2},{2,3},{3,4},{4,5},{5,6},{6,7},{7,8},{8,9},{9,10},{10,1... | collective-permute-start | bytes 221192 | tf_op jit(solution)/shard_map/ppermute | solution.py:622
  5.7 1.2 shard_map.96
  7.0 7.8 %collective-permute-done.refs_9_.refs_10_.refs_11_.refs_8_ = bf16[3,2,6144]{2,1,0:T(2,128)(2,1)S(1)} collective-permute-done((bf16[3,2,6144]{2,1,0:T(2,128)(2,1)S(1)}, bf16[3,2,6144]{2,1,0:T(2,128)(2,1)S(1)}, u32[]{:S(2)}, u32[]{:S(2)}) %collective-permute-start) | collective-permute-done | bytes 73760 | tf_op jit(solution)/shard_map/ppermute | solution.py:622
  14.8 6.4 %shard_map.97 = (bf16[3,64,2048]{2,1,0:T(8,128)(2,1)}, bf16[3,64,2048]{2,1,0:T(8,128)(2,1)}, f32[16,4,3,4,128]{4,3,2,1,0:T(4,128)}) custom-call(bf16[64,6144]{1,0:T(8,128)(2,1)} %bitcast.30, bf16[64,6144]{1,0:T(8,128)(2,1)} %bitcast.31, bf16[64,6144]{1,0:T(8,128)(2,1)} %bitcast.32, bf16[64,6144]{1,0:T(8,128)(2,1)} %bitcast.37, bf16[64,6144]{1,0:T(8,128)(2,1)} %bitcast.38, ...), custom_call_target="tpu_custom_call" | custom-call | tf_op jit(solution)/shard_map/pallas_call | solution.py:680
  21.2 0.0 copy-start.1
  21.2 8.0 %all-to-all-start = ((f32[64,3,4,128]{3,2,1,0:T(4,128)}), f32[64,3,4,128]{3,2,1,0:T(4,128)S(1)}, u32[]{:S(2)}, u32[]{:S(2)}) async-start(f32[64,3,4,128]{3,2,1,0:T(4,128)} %bitcast.46), calls=%async_computation | async-start | bytes 786432 | tf_op jit(solution)/shard_map/all_to_all | solution.py:616
  29.2 7.6 %shard_map.98.inner_far = f32[3,64,2048]{2,1,0:T(8,128)} custom-call(bf16[3,64,2048]{2,1,0:T(8,128)(2,1)} %get-tuple-element.38.data, f32[16,2048]{1,0:T(8,128)} %bitcast.14, f32[16,2048]{1,0:T(8,128)} %bitcast.19), custom_call_target="tpu_custom_call" | custom-call | flops 300000000 | bytes 2359296 | tf_op jit(solution)/shard_map/pallas_call | solution.py:507
  36.8 4.9 %collective-permute-done.1.refs_0_ = bf16[512,1024]{1,0:T(8,128)(2,1)} collective-permute-done((bf16[512,1024]{1,0:T(8,128)(2,1)S(1)}, bf16[512,1024]{1,0:T(8,128)(2,1)}, u32[]{:S(2)}, u32[]{:S(2)}) %collective-permute-start.1) | collective-permute-done | bytes 1048608 | tf_op jit(solution)/shard_map/ppermute | solution.py:640
  41.7 0.1 dynamic-slice.3
  41.8 1.6 %all-to-all-done.ends = f32[64,3,4,128]{3,2,1,0:T(4,128)S(1)} async-done(((f32[64,3,4,128]{3,2,1,0:T(4,128)}), f32[64,3,4,128]{3,2,1,0:T(4,128)S(1)}, u32[]{:S(2)}, u32[]{:S(2)}) %all-to-all-start) | async-done | bytes 393248 | tf_op jit(solution)/shard_map/all_to_all | solution.py:616
  43.4 0.1 shard_map.99
  43.5 20.1 %all_to_all.20 = bf16[64,3,4,128]{3,2,1,0:T(4,128)(2,1)S(1)} all-to-all(bf16[64,3,4,128]{3,2,1,0:T(4,128)(2,1)S(1)} %shard_map.99), channel_id=1, replica_groups=mesh['dp'=4,'ctx'=64] {'ctx'}, dimensions={0} | all-to-all | bytes 393216 | tf_op jit(solution)/shard_map/all_to_all | solution.py:616
  63.7 0.9 collective-permute-start.5
  64.6 2.0 %collective-permute-start.6 = (bf16[256,1024]{1,0:T(8,128)(2,1)S(1)}, bf16[256,1024]{1,0:T(8,128)(2,1)S(1)}, u32[]{:S(2)}, u32[]{:S(2)}) collective-permute-start(bf16[256,1024]{1,0:T(8,128)(2,1)S(1)} %slice.7), channel_id=1, source_target_pairs={{0,4},{1,5},{2,6},{3,7},{4,0},{5,1},{6,2},{7,3},{8,12},{9,13},{10,... | collective-permute-start | bytes 1572872 | tf_op jit(solution)/shard_map/ppermute | solution.py:640
  66.7 0.5 collective-permute-start.8
  67.2 6.1 %shard_map.100 = (bf16[192,2048]{1,0:T(8,128)(2,1)S(1)}, bf16[2,64,2048]{2,1,0:T(8,128)(2,1)}, f32[2,192,1024]{2,1,0:T(8,128)S(1)}, bf16[2,2048,1024]{2,1,0:T(8,128)(2,1)S(1)}) custom-call(bf16[16,4,3,4,128]{4,3,2,1,0:T(4,128)(2,1)S(1)} %bitcast.24, f32[3,64,2048]{2,1,0:T(8,128)} %shard_map.98.inner_far, bf16[3,64,2048]{2,1,0:T(8,128)(2,1)} %get-tuple-element.45.query_far, ...), custom_call_target="tpu_custom_call" | custom-call | flops 5000000000 | bytes 14000000 | tf_op jit(solution)/shard_map/pallas_call | solution.py:548
  73.4 0.5 collective-permute-done.6.refs_4_
  73.9 0.1 collective-permute-start.10
  74.0 0.4 collective-permute-start.11
  74.4 1.4 %collective-permute-done.10.refs_8_ = bf16[256,1024]{1,0:T(8,128)(2,1)S(1)} collective-permute-done((bf16[256,1024]{1,0:T(8,128)(2,1)S(1)}, bf16[256,1024]{1,0:T(8,128)(2,1)S(1)}, u32[]{:S(2)}, u32[]{:S(2)}) %collective-permute-start.10) | collective-permute-done | bytes 524320 | tf_op jit(solution)/shard_map/ppermute | solution.py:640
  75.8 0.7 collective-permute-done.11.refs_9_
  76.6 15.1 %shard_map.101 = (f32[2,64,2048]{2,1,0:T(8,128)}, bf16[2,64,2048]{2,1,0:T(8,128)(2,1)}, bf16[2,8,2048]{2,1,0:T(8,128)(2,1)S(1)}, bf16[16,4,2,4,128]{4,3,2,1,0:T(4,128)(2,1)}) custom-call(bf16[192,2048]{1,0:T(8,128)(2,1)S(1)} %get-tuple-element.50.prod, f32[2,192,1024]{2,1,0:T(8,128)S(1)} %get-tuple-element.51.near_mixed, ...), custom_call_target="tpu_custom_call" | custom-call | tf_op jit(solution)/shard_map/pallas_call | solution.py:576
  91.7 9.3 %all-to-all-start.2 = ((bf16[64,2,4,128]{3,2,1,0:T(4,128)(2,1)}), bf16[64,2,4,128]{3,2,1,0:T(4,128)(2,1)S(1)}, u32[]{:S(2)}, u32[]{:S(2)}) async-start(bf16[64,2,4,128]{3,2,1,0:T(4,128)(2,1)} %bitcast.9), calls=%async_computation.2 | async-start | bytes 262144 | tf_op jit(solution)/shard_map/all_to_all | solution.py:616
  100.9 5.8 %shard_map.102.refs_1_ = f32[2,64,2048]{2,1,0:T(8,128)} custom-call(bf16[2,64,2048]{2,1,0:T(8,128)(2,1)} %get-tuple-element.58.data, f32[16,2048]{1,0:T(8,128)} %bitcast.15, f32[16,2048]{1,0:T(8,128)} %bitcast.20), custom_call_target="tpu_custom_call" | custom-call | flops 200000000 | bytes 1572864 | tf_op jit(solution)/shard_map/pallas_call | solution.py:507
  106.8 4.1 %all-to-all-done.2.ends = bf16[64,2,4,128]{3,2,1,0:T(4,128)(2,1)S(1)} async-done(((bf16[64,2,4,128]{3,2,1,0:T(4,128)(2,1)}), bf16[64,2,4,128]{3,2,1,0:T(4,128)(2,1)S(1)}, u32[]{:S(2)}, u32[]{:S(2)}) %all-to-all-start.2) | async-done | bytes 131104 | tf_op jit(solution)/shard_map/all_to_all | solution.py:616
  110.9 0.8 shard_map.103
  111.6 7.2 %all-to-all-start.3 = ((bf16[64,2,4,128]{3,2,1,0:T(4,128)(2,1)}), bf16[64,2,4,128]{3,2,1,0:T(4,128)(2,1)S(1)}, u32[]{:S(2)}, u32[]{:S(2)}) async-start(bf16[64,2,4,128]{3,2,1,0:T(4,128)(2,1)} %shard_map.103), calls=%async_computation.3 | async-start | bytes 262144 | tf_op jit(solution)/shard_map/all_to_all | solution.py:616
  118.9 6.7 %collective-permute-start.12 = (bf16[2,8,2048]{2,1,0:T(8,128)(2,1)S(1)}, bf16[2,8,2048]{2,1,0:T(8,128)(2,1)S(1)}, u32[]{:S(2)}, u32[]{:S(2)}) collective-permute-start(bf16[2,8,2048]{2,1,0:T(8,128)(2,1)S(1)} %get-tuple-element.63), channel_id=1, source_target_pairs={{1,0},{2,1},{3,2},{4,3},{5,4},{6,5},{7,6},{8,7},{9,8},{10,9},{11,1... | collective-permute-start | bytes 196616 | tf_op jit(solution)/shard_map/ppermute | solution.py:622
  125.6 1.9 %collective-permute-done.12.refs_3_ = bf16[2,8,2048]{2,1,0:T(8,128)(2,1)S(1)} collective-permute-done((bf16[2,8,2048]{2,1,0:T(8,128)(2,1)S(1)}, bf16[2,8,2048]{2,1,0:T(8,128)(2,1)S(1)}, u32[]{:S(2)}, u32[]{:S(2)}) %collective-permute-start.12) | collective-permute-done | bytes 65568 | tf_op jit(solution)/shard_map/ppermute | solution.py:622
  127.5 1.3 all-to-all-done.3
  128.7 6.0 %shard_map.104 = (bf16[64,6144]{1,0:T(8,128)(2,1)}, bf16[64,6144]{1,0:T(8,128)(2,1)}) custom-call(bf16[16,4,2,4,128]{4,3,2,1,0:T(4,128)(2,1)S(1)} %bitcast.23, f32[2,64,2048]{2,1,0:T(8,128)} %shard_map.102.refs_1_, f32[2,64,2048]{2,1,0:T(8,128)} %get-tuple-element.62.refs_2_, bf16[2,8,2048]{2,1,0:T(8,128)(2,1)S(1)} %collective-permute-done.12.refs_3_, ...), custom_call_target="tpu_custom_call" | custom-call | tf_op jit(solution)/shard_map/pallas_call | solution.py:728
  (22 shorter events, 0.1 us)
Async XLA Ops:
  2.3 12.5 %collective-permute-start = (bf16[3,2,6144]{2,1,0:T(2,128)(2,1)S(1)}, bf16[3,2,6144]{2,1,0:T(2,128)(2,1)S(1)}, u32[]{:S(2)}, u32[]{:S(2)}) collective-permute-start(bf16[3,2,6144]{2,1,0:T(2,128)(2,1)S(1)} %get-tuple-element.34), channel_id=1, source_target_pairs={{0,1},{1,2},{2,3},{3,4},{4,5},{5,6},{6,7},{7,8},{8,9},{9,10},{10,1... | collective-permute-start | bytes 221192 | tf_op jit(solution)/shard_map/ppermute | solution.py:622
  14.8 52.4 %collective-permute-start.4 = (bf16[2048,1024]{1,0:T(8,128)(2,1)}, bf16[2048,1024]{1,0:T(8,128)(2,1)}, u32[]{:S(2)}, u32[]{:S(2)}) collective-permute-start(bf16[2048,1024]{1,0:T(8,128)(2,1)} %own_weight.1), channel_id=1, source_target_pairs={{0,64},{1,65},{2,66},{3,67},{4,68},{5,69},{6,70},{7,71},{8,72},{9,... | collective-permute-start | bytes 12582920 | tf_op jit(solution)/shard_map/ppermute | solution.py:640
  14.8 26.9 %collective-permute-start.1 = (bf16[512,1024]{1,0:T(8,128)(2,1)S(1)}, bf16[512,1024]{1,0:T(8,128)(2,1)}, u32[]{:S(2)}, u32[]{:S(2)}) collective-permute-start(bf16[512,1024]{1,0:T(8,128)(2,1)S(1)} %shard_map.96), channel_id=1, source_target_pairs={{0,160},{1,161},{2,162},{3,163},{4,164},{5,165},{6,166},{7,167},{8... | collective-permute-start | bytes 3145736 | tf_op jit(solution)/shard_map/ppermute | solution.py:640
  14.8 26.9 %copy-start = (f32[2048,16]{0,1:T(8,128)S(1)}, f32[2048,16]{0,1:T(8,128)}, u32[]{:S(2)}) copy-start(f32[2048,16]{0,1:T(8,128)} %param.13) | copy-start | bytes 393220
  21.2 46.1 %copy-start.1 = (f32[2048,16]{0,1:T(8,128)S(1)}, f32[2048,16]{0,1:T(8,128)}, u32[]{:S(2)}) copy-start(f32[2048,16]{0,1:T(8,128)} %param.12) | copy-start | bytes 393220
  21.2 22.2 %all-to-all-start = ((f32[64,3,4,128]{3,2,1,0:T(4,128)}), f32[64,3,4,128]{3,2,1,0:T(4,128)S(1)}, u32[]{:S(2)}, u32[]{:S(2)}) async-start(f32[64,3,4,128]{3,2,1,0:T(4,128)} %bitcast.46), calls=%async_computation | async-start | bytes 786432 | tf_op jit(solution)/shard_map/all_to_all | solution.py:616
  41.7 22.0 %collective-permute-start.2 = (bf16[512,1024]{1,0:T(8,128)(2,1)}, bf16[512,1024]{1,0:T(8,128)(2,1)S(1)}, u32[]{:S(2)}, u32[]{:S(2)}) collective-permute-start(bf16[512,1024]{1,0:T(8,128)(2,1)} %collective-permute-done.1.refs_0_), channel_id=1, source_target_pairs={{0,1},{1,0},{2,3},{3,2},{4,5},{5,4},{6,7},{7,6},{8,9},{9,8},{10,11... | collective-permute-start | bytes 3145736 | tf_op jit(solution)/shard_map/ppermute | solution.py:640
  41.7 22.0 %collective-permute-start.3 = (bf16[512,1024]{1,0:T(8,128)(2,1)}, bf16[512,1024]{1,0:T(8,128)(2,1)S(1)}, u32[]{:S(2)}, u32[]{:S(2)}) collective-permute-start(bf16[512,1024]{1,0:T(8,128)(2,1)} %collective-permute-done.1.refs_0_), channel_id=1, source_target_pairs={{0,4},{1,5},{2,6},{3,7},{4,0},{5,1},{6,2},{7,3},{8,12},{9,13},{10,... | collective-permute-start | bytes 3145736 | tf_op jit(solution)/shard_map/ppermute | solution.py:640
  63.7 9.7 %collective-permute-start.5 = (bf16[256,1024]{1,0:T(8,128)(2,1)S(1)}, bf16[256,1024]{1,0:T(8,128)(2,1)S(1)}, u32[]{:S(2)}, u32[]{:S(2)}) collective-permute-start(bf16[256,1024]{1,0:T(8,128)(2,1)S(1)} %slice.6), channel_id=1, source_target_pairs={{0,1},{1,0},{2,3},{3,2},{4,5},{5,4},{6,7},{7,6},{8,9},{9,8},{10,11... | collective-permute-start | bytes 1572872 | tf_op jit(solution)/shard_map/ppermute | solution.py:640
  64.6 9.3 %collective-permute-start.6 = (bf16[256,1024]{1,0:T(8,128)(2,1)S(1)}, bf16[256,1024]{1,0:T(8,128)(2,1)S(1)}, u32[]{:S(2)}, u32[]{:S(2)}) collective-permute-start(bf16[256,1024]{1,0:T(8,128)(2,1)S(1)} %slice.7), channel_id=1, source_target_pairs={{0,4},{1,5},{2,6},{3,7},{4,0},{5,1},{6,2},{7,3},{8,12},{9,13},{10,... | collective-permute-start | bytes 1572872 | tf_op jit(solution)/shard_map/ppermute | solution.py:640
  66.7 7.7 %collective-permute-start.7 = (bf16[512,1024]{1,0:T(8,128)(2,1)}, bf16[512,1024]{1,0:T(8,128)(2,1)S(1)}, u32[]{:S(2)}, u32[]{:S(2)}) collective-permute-start(bf16[512,1024]{1,0:T(8,128)(2,1)} %collective-permute-done.1.refs_0_), channel_id=1, source_target_pairs={{0,64},{1,65},{2,66},{3,67},{4,68},{5,69},{6,70},{7,71},{8,72},{9,... | collective-permute-start | bytes 3145736 | tf_op jit(solution)/shard_map/ppermute | solution.py:640
  66.7 7.7 %collective-permute-start.8 = (bf16[512,1024]{1,0:T(8,128)(2,1)S(1)}, bf16[512,1024]{1,0:T(8,128)(2,1)S(1)}, u32[]{:S(2)}, u32[]{:S(2)}) collective-permute-start(bf16[512,1024]{1,0:T(8,128)(2,1)S(1)} %collective-permute-done.2.refs_1_), channel_id=1, source_target_pairs={{0,64},{1,65},{2,66},{3,67},{4,68},{5,69},{6,70},{7,71},{8,72},{9,... | collective-permute-start | bytes 3145736 | tf_op jit(solution)/shard_map/ppermute | solution.py:640
  67.2 7.2 %collective-permute-start.9 = (bf16[512,1024]{1,0:T(8,128)(2,1)S(1)}, bf16[512,1024]{1,0:T(8,128)(2,1)S(1)}, u32[]{:S(2)}, u32[]{:S(2)}) collective-permute-start(bf16[512,1024]{1,0:T(8,128)(2,1)S(1)} %collective-permute-done.3.refs_2_), channel_id=1, source_target_pairs={{0,64},{1,65},{2,66},{3,67},{4,68},{5,69},{6,70},{7,71},{8,72},{9,... | collective-permute-start | bytes 3145736 | tf_op jit(solution)/shard_map/ppermute | solution.py:640
  67.2 9.4 %copy-start.2 = (bf16[2,2,4096]{2,1,0:T(2,128)(2,1)S(1)}, bf16[2,2,4096]{2,1,0:T(2,128)(2,1)}, u32[]{:S(2)}) copy-start(bf16[2,2,4096]{2,1,0:T(2,128)(2,1)} %get-tuple-element.53.first_rows) | copy-start | bytes 98308
  67.2 9.4 %copy-start.3 = (f32[4096]{0:T(1024)S(1)}, f32[4096]{0:T(1024)}, u32[]{:S(2)}) copy-start(f32[4096]{0:T(1024)} %param.15) | copy-start | bytes 49156
  73.9 1.9 %collective-permute-start.10 = (bf16[256,1024]{1,0:T(8,128)(2,1)S(1)}, bf16[256,1024]{1,0:T(8,128)(2,1)S(1)}, u32[]{:S(2)}, u32[]{:S(2)}) collective-permute-start(bf16[256,1024]{1,0:T(8,128)(2,1)S(1)} %collective-permute-done.5.refs_3_), channel_id=1, source_target_pairs={{0,64},{1,65},{2,66},{3,67},{4,68},{5,69},{6,70},{7,71},{8,72},{9,... | collective-permute-start | bytes 1572872 | tf_op jit(solution)/shard_map/ppermute | solution.py:640
  74.0 2.6 %collective-permute-start.11 = (bf16[256,1024]{1,0:T(8,128)(2,1)S(1)}, bf16[256,1024]{1,0:T(8,128)(2,1)S(1)}, u32[]{:S(2)}, u32[]{:S(2)}) collective-permute-start(bf16[256,1024]{1,0:T(8,128)(2,1)S(1)} %collective-permute-done.6.refs_4_), channel_id=1, source_target_pairs={{0,64},{1,65},{2,66},{3,67},{4,68},{5,69},{6,70},{7,71},{8,72},{9,... | collective-permute-start | bytes 1572872 | tf_op jit(solution)/shard_map/ppermute | solution.py:640
  91.7 19.2 %all-to-all-start.2 = ((bf16[64,2,4,128]{3,2,1,0:T(4,128)(2,1)}), bf16[64,2,4,128]{3,2,1,0:T(4,128)(2,1)S(1)}, u32[]{:S(2)}, u32[]{:S(2)}) async-start(bf16[64,2,4,128]{3,2,1,0:T(4,128)(2,1)} %bitcast.9), calls=%async_computation.2 | async-start | bytes 262144 | tf_op jit(solution)/shard_map/all_to_all | solution.py:616
  111.6 17.1 %all-to-all-start.3 = ((bf16[64,2,4,128]{3,2,1,0:T(4,128)(2,1)}), bf16[64,2,4,128]{3,2,1,0:T(4,128)(2,1)S(1)}, u32[]{:S(2)}, u32[]{:S(2)}) async-start(bf16[64,2,4,128]{3,2,1,0:T(4,128)(2,1)} %shard_map.103), calls=%async_computation.3 | async-start | bytes 262144 | tf_op jit(solution)/shard_map/all_to_all | solution.py:616
  118.9 8.6 %collective-permute-start.12 = (bf16[2,8,2048]{2,1,0:T(8,128)(2,1)S(1)}, bf16[2,8,2048]{2,1,0:T(8,128)(2,1)S(1)}, u32[]{:S(2)}, u32[]{:S(2)}) collective-permute-start(bf16[2,8,2048]{2,1,0:T(8,128)(2,1)S(1)} %get-tuple-element.63), channel_id=1, source_target_pairs={{1,0},{2,1},{3,2},{4,3},{5,4},{6,5},{7,6},{8,7},{9,8},{10,9},{11,1... | collective-permute-start | bytes 196616 | tf_op jit(solution)/shard_map/ppermute | solution.py:622

commit v12 on v11

--- a/solution.py
+++ b/solution.py
@@ -20,7 +20,7 @@
 TILES = C // LANES
 WIDTH = D // 4
 BAND = C // 4
-BLOCK = 512
+BLOCK = 1024
 PIECES = 5
 QUARTERS = 4
 QUARTER = TILES // QUARTERS

time: 137 us -> 136 us (level)
  no operation moved by 1% of the time
where the time goes in v12:
time: 136 us; the launch traced here: 134 us
  Pallas kernels  50.3 us (37%)
  starting transfers between devices  38.5 us (28%)
  waiting for transfers between devices  24.2 us (18%)
  blocking collectives  20.1 us (15%)
    all_to_all x3, starting transfers between devices, exchanged(): return lax.all_to_all(flat, 'ctx', split_axis=0, concat_axis=0, tiled=True)  24.5 us
    all_to_all x1, blocking collectives, exchanged(): return lax.all_to_all(flat, 'ctx', split_axis=0, concat_axis=0, tiled=True)  20.1 us
    pallas_call x1, Pallas kernels, slope_call(): pl.pallas_call(slope_kernel, out_shape=(pltpu.HBM((2, ROWS, C), f32), plt...  14.4 us
    pallas_call x2, Pallas kernels, within(): pl.pallas_call(functools.partial(within_kernel, streams, reverse), out_sh...  13.4 us
    ppermute x2, starting transfers between devices, passed_along(): lax.ppermute(value, 'ctx', [(source, source + steps) for source in range(...  10.1 us
    ppermute x2, waiting for transfers between devices, passed_along(): lax.ppermute(value, 'ctx', [(source, source + steps) for source in range(...  9.7 us
    ppermute x11, waiting for transfers between devices, swapped(): lax.ppermute(value, ('dp', 'ctx'), [(device, partner(device, kind)) for d...  7.55 us
    all_to_all x3, waiting for transfers between devices, exchanged(): return lax.all_to_all(flat, 'ctx', split_axis=0, concat_axis=0, tiled=True)  6.97 us
  transfers between devices with their start and end apart: 16, of which 9 were waited for; matrix products, arithmetic and copies ran while one was open for 0% of the time, Pallas kernels for 20%

profile of v12, /device:TPU:24, one launch (start us, length us, event | category | flops | bytes accessed | tf_op | source)
XLA Modules:
  0.0 134.3 jit_solution(7206168630236795483)
XLA Ops:
  0.6 1.7 %shard_map.95 = (bf16[3,2,6144]{2,1,0:T(2,128)(2,1)S(1)}, bf16[2,2,4096]{2,1,0:T(2,128)(2,1)}) custom-call(bf16[64,6144]{1,0:T(8,128)(2,1)} %bitcast.28, bf16[64,6144]{1,0:T(8,128)(2,1)} %bitcast.35, bf16[64,6144]{1,0:T(8,128)(2,1)} %bitcast.42, bf16[64,6144]{1,0:T(8,128)(2,1)} %bitcast.29, bf16[64,6144]{1,0:T(8,128)(2,1)} %bitcast.36), custom_call_target="tpu_custom_call" | custom-call | tf_op jit(solution)/shard_map/pallas_call | solution.py:662
  2.3 3.4 %collective-permute-start = (bf16[3,2,6144]{2,1,0:T(2,128)(2,1)S(1)}, bf16[3,2,6144]{2,1,0:T(2,128)(2,1)S(1)}, u32[]{:S(2)}, u32[]{:S(2)}) collective-permute-start(bf16[3,2,6144]{2,1,0:T(2,128)(2,1)S(1)} %get-tuple-element.34), channel_id=1, source_target_pairs={{0,1},{1,2},{2,3},{3,4},{4,5},{5,6},{6,7},{7,8},{8,9},{9,10},{10,1... | collective-permute-start | bytes 221192 | tf_op jit(solution)/shard_map/ppermute | solution.py:622
  5.7 1.2 shard_map.96
  7.0 7.8 %collective-permute-done.refs_9_.refs_10_.refs_11_.refs_8_ = bf16[3,2,6144]{2,1,0:T(2,128)(2,1)S(1)} collective-permute-done((bf16[3,2,6144]{2,1,0:T(2,128)(2,1)S(1)}, bf16[3,2,6144]{2,1,0:T(2,128)(2,1)S(1)}, u32[]{:S(2)}, u32[]{:S(2)}) %collective-permute-start) | collective-permute-done | bytes 73760 | tf_op jit(solution)/shard_map/ppermute | solution.py:622
  14.8 6.4 %shard_map.97 = (bf16[3,64,2048]{2,1,0:T(8,128)(2,1)}, bf16[3,64,2048]{2,1,0:T(8,128)(2,1)}, f32[16,4,3,4,128]{4,3,2,1,0:T(4,128)}) custom-call(bf16[64,6144]{1,0:T(8,128)(2,1)} %bitcast.30, bf16[64,6144]{1,0:T(8,128)(2,1)} %bitcast.31, bf16[64,6144]{1,0:T(8,128)(2,1)} %bitcast.32, bf16[64,6144]{1,0:T(8,128)(2,1)} %bitcast.37, bf16[64,6144]{1,0:T(8,128)(2,1)} %bitcast.38, ...), custom_call_target="tpu_custom_call" | custom-call | tf_op jit(solution)/shard_map/pallas_call | solution.py:680
  21.2 0.0 copy-start.1
  21.2 8.0 %all-to-all-start = ((f32[64,3,4,128]{3,2,1,0:T(4,128)}), f32[64,3,4,128]{3,2,1,0:T(4,128)S(1)}, u32[]{:S(2)}, u32[]{:S(2)}) async-start(f32[64,3,4,128]{3,2,1,0:T(4,128)} %bitcast.46), calls=%async_computation | async-start | bytes 786432 | tf_op jit(solution)/shard_map/all_to_all | solution.py:616
  29.2 7.6 %shard_map.98.inner_far = f32[3,64,2048]{2,1,0:T(8,128)} custom-call(bf16[3,64,2048]{2,1,0:T(8,128)(2,1)} %get-tuple-element.38.data, f32[16,2048]{1,0:T(8,128)} %bitcast.14, f32[16,2048]{1,0:T(8,128)} %bitcast.19), custom_call_target="tpu_custom_call" | custom-call | flops 300000000 | bytes 2359296 | tf_op jit(solution)/shard_map/pallas_call | solution.py:507
  36.8 4.9 %collective-permute-done.1.refs_0_ = bf16[512,1024]{1,0:T(8,128)(2,1)} collective-permute-done((bf16[512,1024]{1,0:T(8,128)(2,1)S(1)}, bf16[512,1024]{1,0:T(8,128)(2,1)}, u32[]{:S(2)}, u32[]{:S(2)}) %collective-permute-start.1) | collective-permute-done | bytes 1048608 | tf_op jit(solution)/shard_map/ppermute | solution.py:640
  41.7 0.1 dynamic-slice.3
  41.8 1.6 %all-to-all-done.ends = f32[64,3,4,128]{3,2,1,0:T(4,128)S(1)} async-done(((f32[64,3,4,128]{3,2,1,0:T(4,128)}), f32[64,3,4,128]{3,2,1,0:T(4,128)S(1)}, u32[]{:S(2)}, u32[]{:S(2)}) %all-to-all-start) | async-done | bytes 393248 | tf_op jit(solution)/shard_map/all_to_all | solution.py:616
  43.4 0.1 shard_map.99
  43.5 20.1 %all_to_all.20 = bf16[64,3,4,128]{3,2,1,0:T(4,128)(2,1)S(1)} all-to-all(bf16[64,3,4,128]{3,2,1,0:T(4,128)(2,1)S(1)} %shard_map.99), channel_id=1, replica_groups=mesh['dp'=4,'ctx'=64] {'ctx'}, dimensions={0} | all-to-all | bytes 393216 | tf_op jit(solution)/shard_map/all_to_all | solution.py:616
  63.7 0.9 collective-permute-start.5
  64.6 2.0 %collective-permute-start.6 = (bf16[256,1024]{1,0:T(8,128)(2,1)S(1)}, bf16[256,1024]{1,0:T(8,128)(2,1)S(1)}, u32[]{:S(2)}, u32[]{:S(2)}) collective-permute-start(bf16[256,1024]{1,0:T(8,128)(2,1)S(1)} %slice.7), channel_id=1, source_target_pairs={{0,4},{1,5},{2,6},{3,7},{4,0},{5,1},{6,2},{7,3},{8,12},{9,13},{10,... | collective-permute-start | bytes 1572872 | tf_op jit(solution)/shard_map/ppermute | solution.py:640
  66.7 0.5 collective-permute-start.8
  67.2 6.1 %shard_map.100 = (bf16[192,2048]{1,0:T(8,128)(2,1)S(1)}, bf16[2,64,2048]{2,1,0:T(8,128)(2,1)}, f32[2,192,1024]{2,1,0:T(8,128)S(1)}, bf16[2,2048,1024]{2,1,0:T(8,128)(2,1)S(1)}) custom-call(bf16[16,4,3,4,128]{4,3,2,1,0:T(4,128)(2,1)S(1)} %bitcast.24, f32[3,64,2048]{2,1,0:T(8,128)} %shard_map.98.inner_far, bf16[3,64,2048]{2,1,0:T(8,128)(2,1)} %get-tuple-element.45.query_far, ...), custom_call_target="tpu_custom_call" | custom-call | flops 5000000000 | bytes 14000000 | tf_op jit(solution)/shard_map/pallas_call | solution.py:548
  73.4 0.5 collective-permute-done.6.refs_4_
  73.9 0.0 collective-permute-start.10
  74.0 0.5 collective-permute-start.11
  74.4 1.4 %collective-permute-done.10.refs_8_ = bf16[256,1024]{1,0:T(8,128)(2,1)S(1)} collective-permute-done((bf16[256,1024]{1,0:T(8,128)(2,1)S(1)}, bf16[256,1024]{1,0:T(8,128)(2,1)S(1)}, u32[]{:S(2)}, u32[]{:S(2)}) %collective-permute-start.10) | collective-permute-done | bytes 524320 | tf_op jit(solution)/shard_map/ppermute | solution.py:640
  75.8 0.7 collective-permute-done.11.refs_9_
  76.6 14.4 %shard_map.101 = (f32[2,64,2048]{2,1,0:T(8,128)}, bf16[2,64,2048]{2,1,0:T(8,128)(2,1)}, bf16[2,8,2048]{2,1,0:T(8,128)(2,1)S(1)}, bf16[16,4,2,4,128]{4,3,2,1,0:T(4,128)(2,1)}) custom-call(bf16[192,2048]{1,0:T(8,128)(2,1)S(1)} %get-tuple-element.50.prod, f32[2,192,1024]{2,1,0:T(8,128)S(1)} %get-tuple-element.51.near_mixed, ...), custom_call_target="tpu_custom_call" | custom-call | tf_op jit(solution)/shard_map/pallas_call | solution.py:576
  91.0 9.3 %all-to-all-start.2 = ((bf16[64,2,4,128]{3,2,1,0:T(4,128)(2,1)}), bf16[64,2,4,128]{3,2,1,0:T(4,128)(2,1)S(1)}, u32[]{:S(2)}, u32[]{:S(2)}) async-start(bf16[64,2,4,128]{3,2,1,0:T(4,128)(2,1)} %bitcast.9), calls=%async_computation.2 | async-start | bytes 262144 | tf_op jit(solution)/shard_map/all_to_all | solution.py:616
  100.3 5.8 %shard_map.102.refs_1_ = f32[2,64,2048]{2,1,0:T(8,128)} custom-call(bf16[2,64,2048]{2,1,0:T(8,128)(2,1)} %get-tuple-element.58.data, f32[16,2048]{1,0:T(8,128)} %bitcast.15, f32[16,2048]{1,0:T(8,128)} %bitcast.20), custom_call_target="tpu_custom_call" | custom-call | flops 200000000 | bytes 1572864 | tf_op jit(solution)/shard_map/pallas_call | solution.py:507
  106.1 4.1 %all-to-all-done.2.ends = bf16[64,2,4,128]{3,2,1,0:T(4,128)(2,1)S(1)} async-done(((bf16[64,2,4,128]{3,2,1,0:T(4,128)(2,1)}), bf16[64,2,4,128]{3,2,1,0:T(4,128)(2,1)S(1)}, u32[]{:S(2)}, u32[]{:S(2)}) %all-to-all-start.2) | async-done | bytes 131104 | tf_op jit(solution)/shard_map/all_to_all | solution.py:616
  110.2 0.8 shard_map.103
  111.0 7.2 %all-to-all-start.3 = ((bf16[64,2,4,128]{3,2,1,0:T(4,128)(2,1)}), bf16[64,2,4,128]{3,2,1,0:T(4,128)(2,1)S(1)}, u32[]{:S(2)}, u32[]{:S(2)}) async-start(bf16[64,2,4,128]{3,2,1,0:T(4,128)(2,1)} %shard_map.103), calls=%async_computation.3 | async-start | bytes 262144 | tf_op jit(solution)/shard_map/all_to_all | solution.py:616
  118.2 6.7 %collective-permute-start.12 = (bf16[2,8,2048]{2,1,0:T(8,128)(2,1)S(1)}, bf16[2,8,2048]{2,1,0:T(8,128)(2,1)S(1)}, u32[]{:S(2)}, u32[]{:S(2)}) collective-permute-start(bf16[2,8,2048]{2,1,0:T(8,128)(2,1)S(1)} %get-tuple-element.63), channel_id=1, source_target_pairs={{1,0},{2,1},{3,2},{4,3},{5,4},{6,5},{7,6},{8,7},{9,8},{10,9},{11,1... | collective-permute-start | bytes 196616 | tf_op jit(solution)/shard_map/ppermute | solution.py:622
  124.9 1.9 %collective-permute-done.12.refs_3_ = bf16[2,8,2048]{2,1,0:T(8,128)(2,1)S(1)} collective-permute-done((bf16[2,8,2048]{2,1,0:T(8,128)(2,1)S(1)}, bf16[2,8,2048]{2,1,0:T(8,128)(2,1)S(1)}, u32[]{:S(2)}, u32[]{:S(2)}) %collective-permute-start.12) | collective-permute-done | bytes 65568 | tf_op jit(solution)/shard_map/ppermute | solution.py:622
  126.8 1.3 all-to-all-done.3
  128.1 6.0 %shard_map.104 = (bf16[64,6144]{1,0:T(8,128)(2,1)}, bf16[64,6144]{1,0:T(8,128)(2,1)}) custom-call(bf16[16,4,2,4,128]{4,3,2,1,0:T(4,128)(2,1)S(1)} %bitcast.23, f32[2,64,2048]{2,1,0:T(8,128)} %shard_map.102.refs_1_, f32[2,64,2048]{2,1,0:T(8,128)} %get-tuple-element.62.refs_2_, bf16[2,8,2048]{2,1,0:T(8,128)(2,1)S(1)} %collective-permute-done.12.refs_3_, ...), custom_call_target="tpu_custom_call" | custom-call | tf_op jit(solution)/shard_map/pallas_call | solution.py:728
  (22 shorter events, 0.1 us)
Async XLA Ops:
  2.3 12.5 %collective-permute-start = (bf16[3,2,6144]{2,1,0:T(2,128)(2,1)S(1)}, bf16[3,2,6144]{2,1,0:T(2,128)(2,1)S(1)}, u32[]{:S(2)}, u32[]{:S(2)}) collective-permute-start(bf16[3,2,6144]{2,1,0:T(2,128)(2,1)S(1)} %get-tuple-element.34), channel_id=1, source_target_pairs={{0,1},{1,2},{2,3},{3,4},{4,5},{5,6},{6,7},{7,8},{8,9},{9,10},{10,1... | collective-permute-start | bytes 221192 | tf_op jit(solution)/shard_map/ppermute | solution.py:622
  14.8 52.4 %collective-permute-start.4 = (bf16[2048,1024]{1,0:T(8,128)(2,1)}, bf16[2048,1024]{1,0:T(8,128)(2,1)}, u32[]{:S(2)}, u32[]{:S(2)}) collective-permute-start(bf16[2048,1024]{1,0:T(8,128)(2,1)} %own_weight.1), channel_id=1, source_target_pairs={{0,64},{1,65},{2,66},{3,67},{4,68},{5,69},{6,70},{7,71},{8,72},{9,... | collective-permute-start | bytes 12582920 | tf_op jit(solution)/shard_map/ppermute | solution.py:640
  14.8 26.9 %collective-permute-start.1 = (bf16[512,1024]{1,0:T(8,128)(2,1)S(1)}, bf16[512,1024]{1,0:T(8,128)(2,1)}, u32[]{:S(2)}, u32[]{:S(2)}) collective-permute-start(bf16[512,1024]{1,0:T(8,128)(2,1)S(1)} %shard_map.96), channel_id=1, source_target_pairs={{0,160},{1,161},{2,162},{3,163},{4,164},{5,165},{6,166},{7,167},{8... | collective-permute-start | bytes 3145736 | tf_op jit(solution)/shard_map/ppermute | solution.py:640
  14.8 26.9 %copy-start = (f32[2048,16]{0,1:T(8,128)S(1)}, f32[2048,16]{0,1:T(8,128)}, u32[]{:S(2)}) copy-start(f32[2048,16]{0,1:T(8,128)} %param.13) | copy-start | bytes 393220
  21.2 46.1 %copy-start.1 = (f32[2048,16]{0,1:T(8,128)S(1)}, f32[2048,16]{0,1:T(8,128)}, u32[]{:S(2)}) copy-start(f32[2048,16]{0,1:T(8,128)} %param.12) | copy-start | bytes 393220
  21.2 22.2 %all-to-all-start = ((f32[64,3,4,128]{3,2,1,0:T(4,128)}), f32[64,3,4,128]{3,2,1,0:T(4,128)S(1)}, u32[]{:S(2)}, u32[]{:S(2)}) async-start(f32[64,3,4,128]{3,2,1,0:T(4,128)} %bitcast.46), calls=%async_computation | async-start | bytes 786432 | tf_op jit(solution)/shard_map/all_to_all | solution.py:616
  41.7 22.0 %collective-permute-start.2 = (bf16[512,1024]{1,0:T(8,128)(2,1)}, bf16[512,1024]{1,0:T(8,128)(2,1)S(1)}, u32[]{:S(2)}, u32[]{:S(2)}) collective-permute-start(bf16[512,1024]{1,0:T(8,128)(2,1)} %collective-permute-done.1.refs_0_), channel_id=1, source_target_pairs={{0,1},{1,0},{2,3},{3,2},{4,5},{5,4},{6,7},{7,6},{8,9},{9,8},{10,11... | collective-permute-start | bytes 3145736 | tf_op jit(solution)/shard_map/ppermute | solution.py:640
  41.7 22.0 %collective-permute-start.3 = (bf16[512,1024]{1,0:T(8,128)(2,1)}, bf16[512,1024]{1,0:T(8,128)(2,1)S(1)}, u32[]{:S(2)}, u32[]{:S(2)}) collective-permute-start(bf16[512,1024]{1,0:T(8,128)(2,1)} %collective-permute-done.1.refs_0_), channel_id=1, source_target_pairs={{0,4},{1,5},{2,6},{3,7},{4,0},{5,1},{6,2},{7,3},{8,12},{9,13},{10,... | collective-permute-start | bytes 3145736 | tf_op jit(solution)/shard_map/ppermute | solution.py:640
  63.7 9.6 %collective-permute-start.5 = (bf16[256,1024]{1,0:T(8,128)(2,1)S(1)}, bf16[256,1024]{1,0:T(8,128)(2,1)S(1)}, u32[]{:S(2)}, u32[]{:S(2)}) collective-permute-start(bf16[256,1024]{1,0:T(8,128)(2,1)S(1)} %slice.6), channel_id=1, source_target_pairs={{0,1},{1,0},{2,3},{3,2},{4,5},{5,4},{6,7},{7,6},{8,9},{9,8},{10,11... | collective-permute-start | bytes 1572872 | tf_op jit(solution)/shard_map/ppermute | solution.py:640
  64.6 9.3 %collective-permute-start.6 = (bf16[256,1024]{1,0:T(8,128)(2,1)S(1)}, bf16[256,1024]{1,0:T(8,128)(2,1)S(1)}, u32[]{:S(2)}, u32[]{:S(2)}) collective-permute-start(bf16[256,1024]{1,0:T(8,128)(2,1)S(1)} %slice.7), channel_id=1, source_target_pairs={{0,4},{1,5},{2,6},{3,7},{4,0},{5,1},{6,2},{7,3},{8,12},{9,13},{10,... | collective-permute-start | bytes 1572872 | tf_op jit(solution)/shard_map/ppermute | solution.py:640
  66.7 7.7 %collective-permute-start.7 = (bf16[512,1024]{1,0:T(8,128)(2,1)}, bf16[512,1024]{1,0:T(8,128)(2,1)S(1)}, u32[]{:S(2)}, u32[]{:S(2)}) collective-permute-start(bf16[512,1024]{1,0:T(8,128)(2,1)} %collective-permute-done.1.refs_0_), channel_id=1, source_target_pairs={{0,64},{1,65},{2,66},{3,67},{4,68},{5,69},{6,70},{7,71},{8,72},{9,... | collective-permute-start | bytes 3145736 | tf_op jit(solution)/shard_map/ppermute | solution.py:640
  66.7 7.7 %collective-permute-start.8 = (bf16[512,1024]{1,0:T(8,128)(2,1)S(1)}, bf16[512,1024]{1,0:T(8,128)(2,1)S(1)}, u32[]{:S(2)}, u32[]{:S(2)}) collective-permute-start(bf16[512,1024]{1,0:T(8,128)(2,1)S(1)} %collective-permute-done.2.refs_1_), channel_id=1, source_target_pairs={{0,64},{1,65},{2,66},{3,67},{4,68},{5,69},{6,70},{7,71},{8,72},{9,... | collective-permute-start | bytes 3145736 | tf_op jit(solution)/shard_map/ppermute | solution.py:640
  67.2 7.2 %collective-permute-start.9 = (bf16[512,1024]{1,0:T(8,128)(2,1)S(1)}, bf16[512,1024]{1,0:T(8,128)(2,1)S(1)}, u32[]{:S(2)}, u32[]{:S(2)}) collective-permute-start(bf16[512,1024]{1,0:T(8,128)(2,1)S(1)} %collective-permute-done.3.refs_2_), channel_id=1, source_target_pairs={{0,64},{1,65},{2,66},{3,67},{4,68},{5,69},{6,70},{7,71},{8,72},{9,... | collective-permute-start | bytes 3145736 | tf_op jit(solution)/shard_map/ppermute | solution.py:640
  67.2 9.4 %copy-start.2 = (bf16[2,2,4096]{2,1,0:T(2,128)(2,1)S(1)}, bf16[2,2,4096]{2,1,0:T(2,128)(2,1)}, u32[]{:S(2)}) copy-start(bf16[2,2,4096]{2,1,0:T(2,128)(2,1)} %get-tuple-element.53.first_rows) | copy-start | bytes 98308
  67.2 9.4 %copy-start.3 = (f32[4096]{0:T(1024)S(1)}, f32[4096]{0:T(1024)}, u32[]{:S(2)}) copy-start(f32[4096]{0:T(1024)} %param.15) | copy-start | bytes 49156
  73.9 1.9 %collective-permute-start.10 = (bf16[256,1024]{1,0:T(8,128)(2,1)S(1)}, bf16[256,1024]{1,0:T(8,128)(2,1)S(1)}, u32[]{:S(2)}, u32[]{:S(2)}) collective-permute-start(bf16[256,1024]{1,0:T(8,128)(2,1)S(1)} %collective-permute-done.5.refs_3_), channel_id=1, source_target_pairs={{0,64},{1,65},{2,66},{3,67},{4,68},{5,69},{6,70},{7,71},{8,72},{9,... | collective-permute-start | bytes 1572872 | tf_op jit(solution)/shard_map/ppermute | solution.py:640
  74.0 2.6 %collective-permute-start.11 = (bf16[256,1024]{1,0:T(8,128)(2,1)S(1)}, bf16[256,1024]{1,0:T(8,128)(2,1)S(1)}, u32[]{:S(2)}, u32[]{:S(2)}) collective-permute-start(bf16[256,1024]{1,0:T(8,128)(2,1)S(1)} %collective-permute-done.6.refs_4_), channel_id=1, source_target_pairs={{0,64},{1,65},{2,66},{3,67},{4,68},{5,69},{6,70},{7,71},{8,72},{9,... | collective-permute-start | bytes 1572872 | tf_op jit(solution)/shard_map/ppermute | solution.py:640
  91.0 19.2 %all-to-all-start.2 = ((bf16[64,2,4,128]{3,2,1,0:T(4,128)(2,1)}), bf16[64,2,4,128]{3,2,1,0:T(4,128)(2,1)S(1)}, u32[]{:S(2)}, u32[]{:S(2)}) async-start(bf16[64,2,4,128]{3,2,1,0:T(4,128)(2,1)} %bitcast.9), calls=%async_computation.2 | async-start | bytes 262144 | tf_op jit(solution)/shard_map/all_to_all | solution.py:616
  111.0 17.1 %all-to-all-start.3 = ((bf16[64,2,4,128]{3,2,1,0:T(4,128)(2,1)}), bf16[64,2,4,128]{3,2,1,0:T(4,128)(2,1)S(1)}, u32[]{:S(2)}, u32[]{:S(2)}) async-start(bf16[64,2,4,128]{3,2,1,0:T(4,128)(2,1)} %shard_map.103), calls=%async_computation.3 | async-start | bytes 262144 | tf_op jit(solution)/shard_map/all_to_all | solution.py:616
  118.2 8.6 %collective-permute-start.12 = (bf16[2,8,2048]{2,1,0:T(8,128)(2,1)S(1)}, bf16[2,8,2048]{2,1,0:T(8,128)(2,1)S(1)}, u32[]{:S(2)}, u32[]{:S(2)}) collective-permute-start(bf16[2,8,2048]{2,1,0:T(8,128)(2,1)S(1)} %get-tuple-element.63), channel_id=1, source_target_pairs={{1,0},{2,1},{3,2},{4,3},{5,4},{6,5},{7,6},{8,7},{9,8},{10,9},{11,1... | collective-permute-start | bytes 196616 | tf_op jit(solution)/shard_map/ppermute | solution.py:622
